TPU v7x, 32 devices: a whole 2x2x4 slice. The times are simulated.
32 devices in a mesh: groups: 2 (over y), seq: 4 (over z), head: 2 (over x), dp: 2 (over core).
Axes of the slice: x: 2, y: 2, z: 4, core: 2. Of those that a mesh axis runs over, the one named last changes fastest.
Arguments:
- queries: bfloat16 [4, 2048, 512], P(('groups', 'dp'), 'seq', 'head'), parts along dimension 0, may hold values from -6 to 6
- key_rows: bfloat16 [4, 2048, 512], P(('groups', 'dp'), 'seq', 'head'), parts along dimension 0, may hold values from -6 to 6
- value_rows: bfloat16 [4, 2048, 512], P(('groups', 'dp'), 'seq', 'head'), parts along dimension 0, may hold values from -6 to 6
- layout: int32 [4, 8, 4], P('head'), may hold values from 0 to 7
- out_weight: bfloat16 [4096, 512], P(None, 'head'), may hold values from -0.25 to 0.25
- out_grad: bfloat16 [4, 2048, 4096], P(('groups', 'dp'), 'seq', 'head'), parts along dimension 0, may hold values from -6 to 6
Outputs:
- attn: bfloat16 [4, 2048, 512], P(('groups', 'dp'), 'seq', 'head'), parts along dimension 0
- query_grad: bfloat16 [4, 2048, 512], P(('groups', 'dp'), 'seq', 'head'), parts along dimension 0
- key_grad: bfloat16 [4, 2048, 512], P(('groups', 'dp'), 'seq', 'head'), parts along dimension 0
- value_grad: bfloat16 [4, 2048, 512], P(('groups', 'dp'), 'seq', 'head'), parts along dimension 0
- weight_grad: float32 [8192, 512], P(('groups', 'seq', 'dp'), 'head'), parts along dimension 0
There are 2 independent parts, one for each index of `groups`. A program takes and returns all parts, laid end to end along the dimension named above; an argument that names none is the same for every part. Nothing has to cross between parts.
Inputs may be any that keep to these rules, and one draw needn't show every extreme that they name: layout[h, i, j] names a key-value block of the same sequence that query block i of head h reads; entries may repeat and may name any block.
All inputs are finite; a program needn't handle non-finite values.
Results may differ from a plain program's by a relative error of at most 0.018.
Values may be sent and summed in bfloat16 or wider, within the bound.
No kernel may reach another device: no remote copies, remote signals or barrier semaphores. Data moves between devices by JAX's collectives and lax.ppermute only.
A program may use at most 64 MiB of HBM per device.

v0:
```python
import jax
import jax.numpy as jnp
from jax import lax
from jax.sharding import PartitionSpec as P

DH = 128
BLK = 256


epsilon = 1e-06


def feature_map(inputs):
    return jnp.where(inputs > 0, inputs + 1.0, jnp.exp(jnp.minimum(inputs, 0.0)))


def feature_slope(inputs):
    return jnp.where(inputs > 0, 1.0, jnp.exp(jnp.minimum(inputs, 0.0)))


def per_device(queries, key_rows, value_rows, layout, out_weight, out_grad):
    highest = lax.Precision.HIGHEST
    f32 = jnp.float32
    bf16 = jnp.bfloat16
    seq_count = lax.axis_size("seq")
    seq_index = lax.axis_index("seq")
    heads_here = layout.shape[0]
    block_total = layout.shape[1]
    tokens_here = queries.shape[1]
    block_count = tokens_here // BLK
    my_first = seq_index * block_count
    counts = jnp.sum(
        (layout[..., None] == jnp.arange(block_total, dtype=jnp.int32)).astype(f32), axis=2
    )
    owner_cols = lax.dynamic_slice_in_dim(counts, my_first, block_count, 2)
    causal = jnp.tril(jnp.ones((BLK, BLK), f32))
    query_in = queries[0].astype(f32).reshape(block_count, BLK, heads_here, DH)
    key_in = key_rows[0].astype(f32).reshape(block_count, BLK, heads_here, DH)
    value_b = value_rows[0].reshape(block_count, BLK, heads_here, DH)
    query_feat = feature_map(query_in).astype(bf16)
    key_feat = feature_map(key_in).astype(bf16)
    states = jnp.einsum("nthd,nthe->nhde", key_feat, value_b, preferred_element_type=f32)
    presum = jnp.einsum("hqm,mhde->qhde", owner_cols, states, precision=highest)
    presum = presum.reshape(seq_count, block_count, heads_here, DH, DH)
    arrived = lax.all_to_all(presum, "seq", split_axis=0, concat_axis=0, tiled=True)
    carried = jnp.sum(arrived, axis=0)
    carried_b = carried.astype(bf16)
    scores = (
        jnp.einsum("nthd,nshd->nhts", query_feat, key_feat, preferred_element_type=f32) * causal
    )
    scores_b = scores.astype(bf16)
    numer = jnp.einsum("nthd,nhde->nthe", query_feat, carried_b, preferred_element_type=f32)
    numer = numer + jnp.einsum("nhts,nshe->nthe", scores_b, value_b, preferred_element_type=f32)
    rinv = lax.rsqrt(jnp.mean(numer * numer, axis=-1, keepdims=True) + epsilon)
    attn_out = (numer * rinv).astype(bf16)
    attn_flat = attn_out.reshape(tokens_here, heads_here * DH)
    gathered = lax.all_gather(out_grad, "head", axis=2, tiled=True)
    grad_rows = gathered[0]
    d_attn = jnp.dot(grad_rows, out_weight, preferred_element_type=f32).astype(bf16)
    grad_f = d_attn.astype(f32).reshape(block_count, BLK, heads_here, DH)
    d_numer = rinv * grad_f - numer * rinv**3 * jnp.mean(grad_f * numer, axis=-1, keepdims=True)
    d_numer = d_numer.astype(bf16)
    c_grad = jnp.einsum("nthd,nthe->nhde", query_feat, d_numer, preferred_element_type=f32)
    s_grad = jnp.einsum(
        "hmk,mhde->khde",
        owner_cols,
        lax.all_gather(c_grad, "seq", axis=0, tiled=True),
        precision=highest,
    )
    s_grad_b = s_grad.astype(bf16)
    p_grad = (
        jnp.einsum("nthe,nshe->nhts", d_numer, value_b, preferred_element_type=f32) * causal
    ).astype(bf16)
    dq_feat = jnp.einsum("nthe,nhde->nthd", d_numer, carried_b, preferred_element_type=f32)
    dq_feat = dq_feat + jnp.einsum("nhts,nshd->nthd", p_grad, key_feat, preferred_element_type=f32)
    dk_feat = jnp.einsum("nshe,nhde->nshd", value_b, s_grad_b, preferred_element_type=f32)
    dk_feat = dk_feat + jnp.einsum(
        "nhts,nthd->nshd", p_grad, query_feat, preferred_element_type=f32
    )
    dv_full = jnp.einsum("nshd,nhde->nshe", key_feat, s_grad_b, preferred_element_type=f32)
    dv_full = dv_full + jnp.einsum("nhts,nthe->nshe", scores_b, d_numer, preferred_element_type=f32)
    flat_shape = (1, tokens_here, heads_here * DH)
    query_grad = (dq_feat * feature_slope(query_in)).astype(bf16).reshape(flat_shape)
    key_grad = (dk_feat * feature_slope(key_in)).astype(bf16).reshape(flat_shape)
    value_grad = dv_full.astype(bf16).reshape(flat_shape)
    weight_grad = lax.psum_scatter(
        lax.dot_general(
            grad_rows, attn_flat, (((0,), (0,)), ((), ())), preferred_element_type=f32
        ).astype(jnp.bfloat16),
        ("seq", "dp"),
        scatter_dimension=0,
        tiled=True,
    ).astype(jnp.float32)
    return (attn_flat.reshape(flat_shape), query_grad, key_grad, value_grad, weight_grad)


def solution(mesh):
    placed = (
        P(("groups", "dp"), "seq", "head"),
        P(("groups", "dp"), "seq", "head"),
        P(("groups", "dp"), "seq", "head"),
        P("head", None, None),
        P(None, "head"),
        P(("groups", "dp"), "seq", "head"),
    )
    return jax.shard_map(
        per_device,
        mesh=mesh,
        in_specs=placed,
        out_specs=(
            P(("groups", "dp"), "seq", "head"),
            P(("groups", "dp"), "seq", "head"),
            P(("groups", "dp"), "seq", "head"),
            P(("groups", "dp"), "seq", "head"),
            P(("groups", "seq", "dp"), "head"),
        ),
        check_vma=False,
    )
```

profile of v0, /device:TPU:0, one launch (start us, length us, event | category | flops | bytes accessed | tf_op | source)
XLA Modules:
  0.0 156.0 jit_solution(2445478102337339927)
XLA Ops:
  7.9 1.9 %fusion.26 = (f32[1,512,256]{2,1,0:T(8,128)}, bf16[1,512,256]{2,1,0:T(8,128)(2,1)S(1)}) fusion(bf16[1,512,256]{2,1,0:T(8,128)(2,1)} %param.7), kind=kLoop, calls=%fused_computation.37 | loop fusion | flops 917504 | bytes 1048576 | tf_op jit(solution)/shard_map/jit(_where)/select_n | solution.py:18
  10.5 1.1 fusion.33
  11.6 1.4 copy.90
  13.0 6.3 %all-to-all-start = ((f32[4,2,2,128,128]{4,1,3,2,0:T(2,128)}), f32[4,2,2,128,128]{4,1,3,2,0:T(2,128)}, u32[]{:S(2)}, u32[]{:S(2)}) async-start(f32[4,2,2,128,128]{4,1,3,2,0:T(2,128)} %copy.90), calls=%async_computation | async-start | bytes 2097152 | tf_op jit(solution)/shard_map/all_to_all | solution.py:45
  19.3 2.0 %fusion.30 = (f32[1,512,256]{2,1,0:T(8,128)}, bf16[1,512,256]{2,1,0:T(8,128)(2,1)S(1)}) fusion(bf16[1,512,256]{2,1,0:T(8,128)(2,1)} %param.6), kind=kLoop, calls=%fused_computation.41 | loop fusion | flops 917504 | bytes 1048576 | tf_op jit(solution)/shard_map/jit(_where)/select_n | solution.py:18
  22.2 1.1 convolution_bitcast_fusion
  23.4 21.7 %all-to-all-done = f32[4,2,2,128,128]{4,1,3,2,0:T(2,128)} async-done(((f32[4,2,2,128,128]{4,1,3,2,0:T(2,128)}), f32[4,2,2,128,128]{4,1,3,2,0:T(2,128)}, u32[]{:S(2)}, u32[]{:S(2)}) %all-to-all-start) | async-done | bytes 1048608 | tf_op jit(solution)/shard_map/all_to_all | solution.py:45
  45.1 1.7 %reduce_sum.37 = bf16[2,2,128,128]{3,0,2,1:T(2,128)(2,1)S(1)} reduce(f32[4,2,2,128,128]{4,1,3,2,0:T(2,128)} %all-to-all-done, f32[]{:T(128)} %constant.9.clone.1), dimensions={0}, to_apply=%region_1.2 | reduce | flops 196608 | bytes 1179652 | tf_op jit(solution)/shard_map/reduce_sum | solution.py:46
  46.8 22.2 %all-gather.3.cloned.1.call-done = bf16[1,512,4096]{2,1,0:T(8,128)(2,1)} async-done(((bf16[1,512,2048]{2,1,0:T(8,128)(2,1)}), bf16[1,512,4096]{2,1,0:T(8,128)(2,1)}) %all-gather.3.cloned.1.call-update) | async-done | bytes 4194320 | tf_op jit(solution)/shard_map/all_gather | solution.py:57
  69.1 4.2 %fusion.16 = f32[512,256]{1,0:T(8,128)} fusion(bf16[4096,256]{1,0:T(8,128)(2,1)S(1)} %copy-done, bf16[1,512,4096]{2,1,0:T(8,128)(2,1)} %all-gather.3.cloned.1.call-done), kind=kOutput, calls=%fused_computation.22 | convolution fusion | flops 1074003968 | bytes 6815744 | tf_op jit(solution)/shard_map/dot_general | solution.py:59
  73.3 2.1 %reshape.94 = f32[2,256,2,128]{3,2,1,0:T(2,128)} reshape(f32[512,256]{1,0:T(8,128)} %fusion.16) | data formatting | bytes 1048576 | tf_op jit(solution)/shard_map/reshape | solution.py:60
  75.4 2.0 %copy.98 = f32[2,256,2,128]{1,3,2,0:T(8,128)} copy(f32[2,256,2,128]{3,2,1,0:T(2,128)} %reshape.94) | data formatting | bytes 1048576 | tf_op jit(solution)/shard_map/reshape | solution.py:60
  77.4 1.5 multiply_reduce_fusion
  79.0 1.9 %subtract_convert_fusion = (bf16[2,256,2,128]{1,3,2,0:T(8,128)(2,1)S(1)}, bf16[2,256,2,128]{1,3,2,0:T(8,128)(2,1)}) fusion(f32[2,256,2,128]{1,3,2,0:T(8,128)S(1)} %get-tuple-element.35, f32[2,256,2,128]{1,3,2,0:T(8,128)} %copy.98, f32[2,256,2]{1,2,0:T(2,128)S(1)} %get-tuple-element.36, f32[2,256,2]{1,2,0:T(2,128)S(1)} %get-tuple-element.33, ...), kind=kLoop, calls=%fused_computation.42 | loop fusion | flops 917504 | bytes 1585152 | tf_op jit(solution)/shard_map/convert_element_type | solution.py:62
  82.1 1.8 %copy.97 = bf16[2,256,2,128]{3,2,1,0:T(2,128)(2,1)} copy(bf16[2,256,2,128]{1,3,2,0:T(8,128)(2,1)} %get-tuple-element.28) | data formatting | bytes 524288 | tf_op jit(solution)/shard_map/convert_element_type | solution.py:55
  83.9 4.9 %fusion = bf16[4096,256]{0,1:T(8,128)(2,1)} fusion(bf16[1,512,4096]{2,1,0:T(8,128)(2,1)} %all-gather.3.cloned.1.call-done, bf16[64,8,2,128]{3,2,1,0:T(2,128)(2,1)} %bitcast.68), kind=kOutput, calls=%fused_computation.1 | convolution fusion | flops 1074790400 | bytes 6553600 | tf_op jit(solution)/shard_map/dot_general | solution.py:87
  88.8 2.1 %select_n.48 = f32[2,256,2,128]{3,2,1,0:T(2,128)} reshape(f32[1,512,256]{2,1,0:T(8,128)} %get-tuple-element.29) | data formatting | bytes 1048576 | tf_op jit(solution)/shard_map/jit(_where)/select_n | solution.py:18
  90.9 2.0 %copy.113 = f32[2,256,2,128]{1,3,2,0:T(8,128)} copy(f32[2,256,2,128]{3,2,1,0:T(2,128)} %select_n.48) | data formatting | bytes 1048576 | tf_op jit(solution)/shard_map/jit(_where)/select_n | solution.py:18
  92.9 2.1 %select_n.46 = f32[2,256,2,128]{3,2,1,0:T(2,128)} reshape(f32[1,512,256]{2,1,0:T(8,128)} %get-tuple-element.31) | data formatting | bytes 1048576 | tf_op jit(solution)/shard_map/jit(_where)/select_n | solution.py:18
  95.0 2.0 %copy.105 = f32[2,256,2,128]{1,3,2,0:T(8,128)} copy(f32[2,256,2,128]{3,2,1,0:T(2,128)} %select_n.46) | data formatting | bytes 1048576 | tf_op jit(solution)/shard_map/jit(_where)/select_n | solution.py:18
  97.1 1.8 %reshape_reshape.3 = bf16[1,512,256]{2,1,0:T(8,128)(2,1)} reshape(bf16[2,256,2,128]{3,2,1,0:T(2,128)(2,1)} %copy.97) | data formatting | bytes 524288 | tf_op jit(solution)/shard_map/reshape;reshape | solution.py:94
  98.9 1.3 fusion.5
  101.0 1.3 fusion.51
  102.2 2.0 %fusion.11 = bf16[2,256,2,128]{1,3,2,0:T(8,128)(2,1)} fusion(f32[2,256,2,128]{1,3,2,0:T(8,128)} %copy.105, f32[2,2,128,256]{3,2,1,0:T(8,128)S(1)} %fusion.51, bf16[2,256,2,128]{1,3,2,0:T(8,128)(2,1)S(1)} %get-tuple-element.27, bf16[2,2,128,128]{3,0,2,1:T(2,128)(2,1)S(1)} %reduce_sum.37), kind=kOutput, calls=%fused_computation.19 | convolution fusion | flops 33947648 | bytes 1703936 | tf_op jit(solution)/shard_map/nthe,nhde->nthd/dot_general | solution.py:74
  104.2 1.8 %copy.106 = bf16[2,256,2,128]{3,2,1,0:T(2,128)(2,1)} copy(bf16[2,256,2,128]{1,3,2,0:T(8,128)(2,1)} %fusion.11) | data formatting | bytes 524288 | tf_op jit(solution)/shard_map/convert_element_type | solution.py:83
  106.0 1.8 %reshape.89 = bf16[1,512,256]{2,1,0:T(8,128)(2,1)} reshape(bf16[2,256,2,128]{3,2,1,0:T(2,128)(2,1)} %copy.106) | data formatting | bytes 524288 | tf_op jit(solution)/shard_map/reshape | solution.py:83
  108.9 2.1 %fusion.53 = f32[2,2,128,256]{3,2,1,0:T(8,128)} fusion(bf16[2,256,2,128]{1,3,2,0:T(8,128)(2,1)S(1)} %copy.107, bf16[2,2,256,256]{3,2,1,0:T(8,128)(2,1)} %copy-done.1), kind=kOutput, calls=%fused_computation.74 | convolution fusion | flops 67108864 | bytes 1310720 | tf_op jit(solution)/shard_map/nhts,nthd->nshd/dot_general | solution.py:77
  111.0 2.9 %fusion.21 = bf16[2,2,128,128]{3,0,2,1:T(2,128)(2,1)S(1)} fusion(f32[8,2,128,128]{3,2,1,0:T(8,128)} %all-gather.5.cloned.1.call-done, f32[2,8,8]{2,1,0:T(8,128)S(1)} %convert_reduce_fusion, s32[]{:T(128)S(6)} %select_n.41), kind=kOutput, calls=%fused_computation.26 | convolution fusion | flops 6356992 | bytes 1180164 | tf_op jit(solution)/shard_map/hmk,mhde->khde/dot_general | solution.py:64
  114.0 2.1 %fusion.20 = bf16[2,256,2,128]{1,3,2,0:T(8,128)(2,1)} fusion(f32[2,2,128,256]{3,2,1,0:T(8,128)} %fusion.54, bf16[2,2,128,128]{2,3,1,0:T(8,128)(2,1)S(1)} %copy.115, bf16[2,256,2,128]{3,2,1,0:T(2,128)(2,1)} %copy-done.2), kind=kOutput, calls=%fused_computation.24 | convolution fusion | flops 33816576 | bytes 1179648 | tf_op jit(solution)/shard_map/nshd,nhde->nshe/dot_general | solution.py:80
  118.1 1.3 fusion.12
  120.4 27.1 %reduce-scatter.2.cloned.1.call-done = bf16[512,256]{0,1:T(8,128)(2,1)} async-done(((bf16[4096,256]{0,1:T(8,128)(2,1)}), bf16[512,256]{0,1:T(8,128)(2,1)}) %reduce-scatter.2.cloned.1.call-update) | async-done | bytes 262160 | tf_op jit(solution)/shard_map/reduce_scatter | solution.py:86
  147.6 1.9 %copy.119 = f32[512,256]{1,0:T(8,128)} copy(bf16[512,256]{0,1:T(8,128)(2,1)} %reduce-scatter.2.cloned.1.call-done) | data formatting | bytes 786432
  (40 shorter events, 8.4 us)
Async XLA Ops:
  7.2 61.9 %copy-start = (bf16[4096,256]{1,0:T(8,128)(2,1)S(1)}, bf16[4096,256]{1,0:T(8,128)(2,1)}, u32[]{:S(2)}) copy-start(bf16[4096,256]{1,0:T(8,128)(2,1)} %param.10) | copy-start | bytes 6291460
  7.2 2.9 %copy-start.6 = (bf16[1,512,256]{2,1,0:T(8,128)(2,1)S(1)}, bf16[1,512,256]{2,1,0:T(8,128)(2,1)}, u32[]{:S(2)}) copy-start(bf16[1,512,256]{2,1,0:T(8,128)(2,1)} %param.8) | copy-start | bytes 786436
  7.2 3.0 %copy-start.7 = (s32[2,8,4]{1,2,0:T(4,128)S(1)}, s32[2,8,4]{1,2,0:T(4,128)}, u32[]{:S(2)}) copy-start(s32[2,8,4]{1,2,0:T(4,128)} %param.9) | copy-start | bytes 772
  7.2 61.9 %all-gather.3.cloned.1.call-start = ((), (), s32[]{:S(2)}) async-start(), calls=%async_computation.2 | async-start | bytes 6291456 | tf_op jit(solution)/shard_map/all_gather | solution.py:57
  9.9 11.6 %copy-start.2 = (bf16[2,256,2,128]{3,2,1,0:T(2,128)(2,1)}, bf16[2,256,2,128]{3,2,1,0:T(2,128)(2,1)S(1)}, u32[]{:S(2)}) copy-start(bf16[2,256,2,128]{3,2,1,0:T(2,128)(2,1)S(1)} %select_n.40) | copy-start | bytes 786436
  10.1 11.2 %copy-start.3 = (bf16[2,256,2,128]{1,3,2,0:T(8,128)(2,1)}, bf16[2,256,2,128]{1,3,2,0:T(8,128)(2,1)S(1)}, u32[]{:S(2)}) copy-start(bf16[2,256,2,128]{1,3,2,0:T(8,128)(2,1)S(1)} %copy.86) | copy-start | bytes 786436
  13.0 32.1 %all-to-all-start = ((f32[4,2,2,128,128]{4,1,3,2,0:T(2,128)}), f32[4,2,2,128,128]{4,1,3,2,0:T(2,128)}, u32[]{:S(2)}, u32[]{:S(2)}) async-start(f32[4,2,2,128,128]{4,1,3,2,0:T(2,128)} %copy.90), calls=%async_computation | async-start | bytes 2097152 | tf_op jit(solution)/shard_map/all_to_all | solution.py:45
  19.3 91.7 %all-gather.5.cloned.1.call-start = ((), (), s32[]{:S(2)}) async-start(), calls=%async_computation.3 | async-start | bytes 1310720 | tf_op jit(solution)/shard_map/all_gather | solution.py:67
  21.5 0.7 copy-start.4
  81.8 65.8 %reduce-scatter.2.cloned.1.call-start = ((), (), s32[]{:S(2)}) async-start(), calls=%async_computation.4 | async-start | bytes 2359296 | tf_op jit(solution)/shard_map/reduce_scatter | solution.py:86
  100.2 0.8 copy-start.1
  108.9 9.2 %copy-start.5 = (f32[2,256,2,128]{1,3,2,0:T(8,128)S(1)}, f32[2,256,2,128]{1,3,2,0:T(8,128)}, u32[]{:S(2)}) copy-start(f32[2,256,2,128]{1,3,2,0:T(8,128)} %copy.113) | copy-start | bytes 1572868
Sparse Core Ops, SparseCore 0:
  9.6 59.4 all-gather.2
  81.9 27.9 all-gather.4
  112.2 35.3 reduce-scatter.1
where the time goes:
time: 157 us; the launch traced here: 156 us
  waiting for transfers between devices  71.8 us (46%)
  matrix products  28.3 us (18%)
  local copies, waits for them, and re-layouts  27.8 us (18%)
  between operations  14 us (9%)
  other arithmetic  7.58 us (5%)
  starting transfers between devices  6.58 us (4%)
    reduce_scatter x1, waiting for transfers between devices, per_device(): lax.psum_scatter(lax.dot_general(grad_rows, attn_flat, (((0,), (0,)), (()...  27.1 us
    all_gather x1, waiting for transfers between devices, per_device(): gathered = lax.all_gather(out_grad, 'head', axis=2, tiled=True)  22.2 us
    all_to_all x1, waiting for transfers between devices, per_device(): lax.all_to_all(presum, 'seq', split_axis=0, concat_axis=0, tiled=True)  21.7 us
    select_n x4, local copies, waits for them, and re-layouts, feature_slope(): return jnp.where(inputs > 0, 1.0, jnp.exp(jnp.minimum(inputs, 0.0)))  8.28 us
    all_to_all x1, starting transfers between devices, per_device(): lax.all_to_all(presum, 'seq', split_axis=0, concat_axis=0, tiled=True)  6.32 us
    dot_general x1, matrix products, per_device(): lax.dot_general(grad_rows, attn_flat, (((0,), (0,)), ((), ())), preferred...  4.88 us
    dot_general x1, matrix products, per_device(): jnp.dot(grad_rows, out_weight, preferred_element_type=f32).astype(bf16)  4.23 us
    reshape x2, local copies, waits for them, and re-layouts, per_device(): grad_f = d_attn.astype(f32).reshape(block_count, BLK, heads_here, DH)  4.13 us
  transfers between devices with their start and end apart: 4, of which 3 were waited for; matrix products, arithmetic and copies ran while one was open for 31% of the time, Pallas kernels for 0%

commit v1 on v0

v1 whole, which is shorter than its diff:
```python
import functools

import jax
import jax.numpy as jnp
from jax import lax
from jax.experimental import pallas as pl
from jax.experimental.pallas import tpu as pltpu
from jax.sharding import PartitionSpec as P

DH = 128
BLK = 256
EPS = 1e-06
F32 = jnp.float32
BF16 = jnp.bfloat16
VM = pl.BlockSpec(memory_space=pltpu.VMEM)
SM = pl.BlockSpec(memory_space=pltpu.SMEM)
TN = (((0,), (0,)), ((), ()))
NT = (((1,), (1,)), ((), ()))
NN = (((1,), (0,)), ((), ()))


def sds(shape, dtype):
    return jax.ShapeDtypeStruct(shape, dtype)


def mm(a, b, dims):
    return lax.dot_general(a, b, dims, preferred_element_type=F32)


def feature(x):
    return jnp.where(x > 0, x + 1.0, jnp.exp(jnp.minimum(x, 0.0)))


def slope(x):
    return jnp.where(x > 0, 1.0, jnp.exp(jnp.minimum(x, 0.0)))


def call(body, outs, ins, flops, name):
    read = sum(a.size * a.dtype.itemsize for a in ins)
    wrote = sum(s.size * s.dtype.itemsize for s in outs)
    return pl.pallas_call(
        body,
        out_shape=outs,
        in_specs=[SM if a.dtype == jnp.int32 else VM for a in ins],
        out_specs=[VM] * len(outs),
        name=name,
        cost_estimate=pl.CostEstimate(flops=flops, bytes_accessed=read + wrote, transcendentals=0),
    )(*ins)


def tiles(tokens, heads):
    for n in range(tokens // BLK):
        for h in range(heads):
            yield n * heads + h, slice(n * BLK, (n + 1) * BLK), slice(h * DH, (h + 1) * DH)


def mat(i):
    return slice(i * DH, (i + 1) * DH)


def states_body(k_ref, v_ref, kf_ref, st_ref):
    for i, r, c in tiles(k_ref.shape[0], k_ref.shape[1] // DH):
        kf = feature(k_ref[r, c].astype(F32)).astype(BF16)
        kf_ref[r, c] = kf
        st_ref[mat(i), :] = mm(kf, v_ref[r, c], TN).astype(BF16)


def causal():
    rows = lax.broadcasted_iota(jnp.int32, (BLK, BLK), 0)
    cols = lax.broadcasted_iota(jnp.int32, (BLK, BLK), 1)
    return rows >= cols


def scores_body(q_ref, kf_ref, v_ref, qf_ref, sc_ref, intra_ref):
    keep = causal()
    for i, r, c in tiles(q_ref.shape[0], q_ref.shape[1] // DH):
        qf = feature(q_ref[r, c].astype(F32)).astype(BF16)
        qf_ref[r, c] = qf
        sc = jnp.where(keep, mm(qf, kf_ref[r, c], NT), 0.0).astype(BF16)
        sc_ref[i * BLK : (i + 1) * BLK, :] = sc
        intra_ref[r, c] = mm(sc, v_ref[r, c], NN)


def count(lay_ref, nsel, nb_all, h, i, b):
    total = jnp.int32(0)
    base = (h * nb_all + i) * nsel
    for j in range(nsel):
        total = total + jnp.where(lay_ref[base + j] == b, 1, 0)
    return total.astype(F32)


def numer_body(dims, np_, *refs):
    nb, heads, nb_all, nsel = dims
    pos_ref, base_ref, lay_ref = refs[:3]
    parts = refs[3 : 3 + np_]
    qf_ref, intra_ref, carried_ref, num_ref, attn_ref = refs[3 + np_ :]
    for i, r, c in tiles(qf_ref.shape[0], heads):
        n, h = divmod(i, heads)
        query_block = pos_ref[0] * nb + n
        total = jnp.zeros((DH, DH), F32)
        for s, part in enumerate(parts):
            for b in range(part.shape[0] // (heads * DH)):
                times = count(lay_ref, nsel, nb_all, h, query_block, base_ref[s] + b)
                total = total + times * part[mat(b * heads + h), :].astype(F32)
        carried = total.astype(BF16)
        carried_ref[mat(i), :] = carried
        num = mm(qf_ref[r, c], carried, NN) + intra_ref[r, c]
        num_ref[r, c] = num
        rinv = lax.rsqrt(jnp.mean(num * num, axis=-1, keepdims=True) + EPS)
        attn_ref[r, c] = (num * rinv).astype(BF16)


def dnum_body(n_d, *refs):
    d_refs = refs[:n_d]
    num_ref, qf_ref, dnum_ref, cg_ref = refs[n_d:]
    for i, r, c in tiles(num_ref.shape[0], num_ref.shape[1] // DH):
        num = num_ref[r, c]
        grad = d_refs[0][r, c].astype(F32)
        for d in d_refs[1:]:
            grad = grad + d[r, c].astype(F32)
        grad = grad.astype(BF16).astype(F32)
        rinv = lax.rsqrt(jnp.mean(num * num, axis=-1, keepdims=True) + EPS)
        lean = jnp.mean(grad * num, axis=-1, keepdims=True)
        dnum = (rinv * grad - num * (rinv * rinv * rinv * lean)).astype(BF16)
        dnum_ref[r, c] = dnum
        cg_ref[mat(i), :] = mm(qf_ref[r, c], dnum, TN).astype(BF16)


def query_body(q_ref, qf_ref, kf_ref, v_ref, dnum_ref, carried_ref, sc_ref, dq_ref, dk_ref, dv_ref):
    keep = causal()
    for i, r, c in tiles(q_ref.shape[0], q_ref.shape[1] // DH):
        dnum = dnum_ref[r, c]
        pg = jnp.where(keep, mm(dnum, v_ref[r, c], NT), 0.0).astype(BF16)
        dq = mm(dnum, carried_ref[mat(i), :], NT) + mm(pg, kf_ref[r, c], NN)
        dq_ref[r, c] = (dq * slope(q_ref[r, c].astype(F32))).astype(BF16)
        dk_ref[r, c] = mm(pg, qf_ref[r, c], TN)
        dv_ref[r, c] = mm(sc_ref[i * BLK : (i + 1) * BLK, :], dnum, TN)


def key_body(dims, np_, *refs):
    nb, heads, nb_all, nsel = dims
    pos_ref, base_ref, lay_ref = refs[:3]
    parts = refs[3 : 3 + np_]
    k_ref, kf_ref, v_ref, dkp_ref, dvp_ref, dk_ref, dv_ref = refs[3 + np_ :]
    for i, r, c in tiles(k_ref.shape[0], heads):
        n, h = divmod(i, heads)
        key_block = pos_ref[0] * nb + n
        total = jnp.zeros((DH, DH), F32)
        for s, part in enumerate(parts):
            for b in range(part.shape[0] // (heads * DH)):
                times = count(lay_ref, nsel, nb_all, h, base_ref[s] + b, key_block)
                total = total + times * part[mat(b * heads + h), :].astype(F32)
        sg = total.astype(BF16)
        dk = mm(v_ref[r, c], sg, NT) + dkp_ref[r, c]
        dk_ref[r, c] = (dk * slope(k_ref[r, c].astype(F32))).astype(BF16)
        dv_ref[r, c] = (mm(kf_ref[r, c], sg, NN) + dvp_ref[r, c]).astype(BF16)


def own_body(at_ref, og_ref, w_ref, out_ref):
    part = mm(og_ref[...], w_ref[...], NN)

    @pl.when(pl.program_id(0) == 0)
    def _():
        out_ref[...] = part

    @pl.when(pl.program_id(0) > 0)
    def _():
        out_ref[...] += part


def own_partial(at, og, w, steps=4):
    tokens, width = og.shape
    cols = w.shape[1]
    bk = width // steps
    return pl.pallas_call(
        own_body,
        out_shape=sds((tokens, cols), F32),
        grid_spec=pltpu.PrefetchScalarGridSpec(
            num_scalar_prefetch=1,
            grid=(steps,),
            in_specs=[
                pl.BlockSpec((tokens, bk), lambda g, at: (0, g)),
                pl.BlockSpec((bk, cols), lambda g, at: (at[0] * steps + g, 0)),
            ],
            out_specs=pl.BlockSpec((tokens, cols), lambda g, at: (0, 0)),
        ),
        name="own_partial",
        cost_estimate=pl.CostEstimate(
            flops=2 * tokens * width * cols,
            bytes_accessed=2 * tokens * width + 2 * width * cols + 4 * tokens * cols,
            transcendentals=0,
        ),
    )(at, og, w)


def other_body(at_ref, og_ref, first_ref, second_ref, out_ref, acc_ref):
    @pl.when(pl.program_id(0) == 0)
    def _():
        acc_ref[...] = mm(og_ref[...], first_ref[...], NN)

    @pl.when(pl.program_id(0) == 1)
    def _():
        out_ref[...] = (acc_ref[...] + mm(og_ref[...], second_ref[...], NN)).astype(BF16)


def other_partial(at, og, first, second):
    tokens, width = og.shape
    half, cols = first.shape
    return pl.pallas_call(
        other_body,
        out_shape=sds((tokens, cols), BF16),
        grid_spec=pltpu.PrefetchScalarGridSpec(
            num_scalar_prefetch=1,
            grid=(2,),
            in_specs=[
                pl.BlockSpec((tokens, half), lambda g, at: (0, at[g])),
                pl.BlockSpec((half, cols), lambda g, at: (0, 0)),
                pl.BlockSpec((half, cols), lambda g, at: (0, 0)),
            ],
            out_specs=pl.BlockSpec((tokens, cols), lambda g, at: (0, 0)),
            scratch_shapes=[pltpu.VMEM((tokens, cols), F32)],
        ),
        name="other_partial",
        cost_estimate=pl.CostEstimate(
            flops=2 * tokens * width * cols,
            bytes_accessed=2 * tokens * width + 2 * width * cols + 2 * tokens * cols,
            transcendentals=0,
        ),
    )(at, og, first, second)


def wg_send_body(at_ref, attn_ref, og_ref, out_ref):
    out_ref[...] = mm(attn_ref[...], og_ref[...], TN).astype(BF16)


def wg_keep_body(at_ref, attn_ref, og_ref, got_ref, give_ref, keep_ref):
    total = mm(attn_ref[...], og_ref[...], TN) + got_ref[...].astype(F32)

    @pl.when(pl.program_id(0) == 0)
    def _():
        give_ref[...] = total.astype(BF16)

    @pl.when(pl.program_id(0) == 1)
    def _():
        keep_ref[...] = total


def weight_part(at, attn, og, got=None):
    tokens, cols = attn.shape
    rows = og.shape[1] // 4
    whole = pl.BlockSpec((cols, rows), lambda g, at: (0, 0))
    specs = [
        pl.BlockSpec((tokens, cols), lambda g, at: (0, 0)),
        pl.BlockSpec((tokens, rows), lambda g, at: (0, at[g])),
    ]
    if got is None:
        body, args = wg_send_body, (at, attn, og)
        outs = sds((2 * cols, rows), BF16)
        out_specs = pl.BlockSpec((cols, rows), lambda g, at: (g, 0))
    else:
        body, args = wg_keep_body, (at, attn, og, got)
        specs.append(pl.BlockSpec((cols, rows), lambda g, at: (g, 0)))
        outs = (sds((cols, rows), BF16), sds((cols, rows), F32))
        out_specs = (whole, whole)
    return pl.pallas_call(
        body,
        out_shape=outs,
        grid_spec=pltpu.PrefetchScalarGridSpec(
            num_scalar_prefetch=1, grid=(2,), in_specs=specs, out_specs=out_specs
        ),
        name="weight_send" if got is None else "weight_keep",
        cost_estimate=pl.CostEstimate(
            flops=4 * tokens * rows * cols,
            bytes_accessed=2 * tokens * (cols + 2 * rows) + 6 * cols * rows,
            transcendentals=0,
        ),
    )(*args)


def pair_body(keep_ref, got_ref, out_ref):
    out_ref[...] = (keep_ref[...] + got_ref[...].astype(F32)).astype(BF16)


def final_body(pos_ref, mine_ref, a_ref, b_ref, c_ref, out_ref):
    mine = jnp.where(pos_ref[1] > 0, mine_ref[...].astype(F32), 0.0)
    total = mine + a_ref[...].astype(F32) + b_ref[...].astype(F32) + c_ref[...].astype(F32)
    out_ref[...] = total.T


def swap(x, axis):
    return lax.ppermute(x, axis, [(0, 1), (1, 0)])


def gather_parts(x, size):
    if size > 4:
        return [lax.all_gather(x, "seq", axis=0, tiled=True)]
    parts = [x]
    for shift in range(1, size):
        pairs = [(i, (i + shift) % size) for i in range(size)]
        parts.append(lax.ppermute(x, "seq", pairs))
    return parts


def per_device(queries, key_rows, value_rows, layout, out_weight, out_grad):
    seq_size = lax.axis_size("seq")
    head_size = lax.axis_size("head")
    dp_size = lax.axis_size("dp")
    z = lax.axis_index("seq").astype(jnp.int32)
    x = lax.axis_index("head").astype(jnp.int32)
    core = lax.axis_index("dp").astype(jnp.int32)
    heads, nb_all, nsel = layout.shape
    q, k, v, og = queries[0], key_rows[0], value_rows[0], out_grad[0]
    tokens, cols = q.shape
    nb = tokens // BLK
    dims = (nb, heads, nb_all, nsel)
    paired = seq_size == 4 and head_size == 2 and dp_size == 2
    home = (z // 2 == x).astype(jnp.int32)
    pos = jnp.stack([z, home])
    lay = layout.reshape(-1)
    if seq_size > 4:
        bases = jnp.zeros((1,), jnp.int32)
    else:
        bases = ((z - jnp.arange(seq_size, dtype=jnp.int32)) % seq_size) * nb
    flat = sds((tokens, cols), F32)
    rows16 = sds((tokens, cols), BF16)
    mats = sds((nb * heads * DH, DH), BF16)
    unit = 2 * tokens * cols * DH

    if paired:
        width = og.shape[1]
        half = width // 2
        far = lax.dynamic_slice_in_dim(out_weight, (1 - x) * width + core * half, half, 0)
        w_first = swap(far, "head")
    kf, st = call(states_body, (rows16, mats), (k, v), unit, "states")
    parts = gather_parts(st, seq_size)
    qf, sc, intra = call(
        scores_body,
        (rows16, sds((nb * heads * BLK, BLK), BF16), flat),
        (q, kf, v),
        4 * unit,
        "scores",
    )
    if paired:
        d_own = own_partial(x[None], og, out_weight)
        w_second = swap(w_first, "dp")
        d_other = other_partial(jnp.stack([core, 1 - core]), og, w_first, w_second)
    else:
        og = lax.all_gather(og, "head", axis=1, tiled=True)
        d_own = jnp.dot(og, out_weight, preferred_element_type=F32)
    carried, num, attn = call(
        functools.partial(numer_body, dims, len(parts)),
        (mats, flat, rows16),
        (pos, bases, lay, *parts, qf, intra),
        unit,
        "numer",
    )
    if paired:
        attn_other = swap(attn, "head")
        d_parts = (d_own, swap(d_other, "head"))
    else:
        d_parts = (d_own,)
    dnum, cg = call(
        functools.partial(dnum_body, len(d_parts)),
        (rows16, mats),
        (*d_parts, num, qf),
        unit,
        "dnum",
    )
    cparts = gather_parts(cg, seq_size)
    dq, dkp, dvp = call(
        query_body,
        (rows16, flat, flat),
        (q, qf, kf, v, dnum, carried, sc),
        9 * unit,
        "query",
    )
    dk, dv = call(
        functools.partial(key_body, dims, len(cparts)),
        (rows16, rows16),
        (pos, bases, lay, *cparts, k, kf, v, dkp, dvp),
        2 * unit,
        "key",
    )
    if paired:
        parity = z % 2
        order = jnp.stack([1 - parity, parity])
        give_at = 2 * order + (1 - core)
        keep_at = 2 * order + core
        neighbours = [(0, 1), (1, 0), (2, 3), (3, 2)]
        sums = []
        for block in (attn, attn_other):
            got = swap(weight_part(give_at, block, og), "dp")
            give, keep = weight_part(keep_at, block, og, got)
            got = lax.ppermute(give, "seq", neighbours)
            sums.append(call(pair_body, (sds(keep.shape, BF16),), (keep, got), 0, "pair")[0])
        mine, cross = sums
        to_line, to_side, to_both = [], [], []
        for s in range(4):
            for h in range(2):
                if s // 2 == h:
                    to_side.append((s * 2 + h, s * 2 + 1 - h))
                else:
                    to_line.append((s * 2 + h, (s ^ 2) * 2 + h))
                    to_both.append((s * 2 + h, (s ^ 2) * 2 + 1 - h))
        axes = ("seq", "head")
        arrived = (
            lax.ppermute(mine, axes, to_line),
            lax.ppermute(cross, axes, to_both),
            lax.ppermute(cross, axes, to_side),
        )
        (weight_grad,) = call(
            final_body, (sds(mine.shape[::-1], F32),), (pos, mine, *arrived), 0, "final"
        )
    else:
        weight_grad = lax.psum_scatter(
            lax.dot_general(og, attn, TN, preferred_element_type=F32).astype(BF16),
            ("seq", "dp"),
            scatter_dimension=0,
            tiled=True,
        ).astype(F32)
    return attn[None], dq[None], dk[None], dv[None], weight_grad


def solution(mesh):
    rows = P(("groups", "dp"), "seq", "head")
    return jax.shard_map(
        per_device,
        mesh=mesh,
        in_specs=(rows, rows, rows, P("head", None, None), P(None, "head"), rows),
        out_specs=(rows, rows, rows, rows, P(("groups", "seq", "dp"), "head")),
        check_vma=False,
    )
```

time: 157 us -> 109 us (0.69)
  waiting for transfers between devices: 71.8 us -> 24.8 us
  Pallas kernels: 0 us -> 43.9 us
  matrix products: 28.3 us -> 0 us
  starting transfers between devices: 6.58 us -> 24.9 us
  local copies, waits for them, and re-layouts: 27.8 us -> 10.6 us
  between operations: 14 us -> 0.78 us
  other arithmetic: 7.58 us -> 3 us
    pallas_call x0 -> x15, Pallas kernels: none -> 43.9 us  [the longest x9 22.6 us: call(): pl.pallas_call(body, out_shape=outs, in_specs=[SM if a.dtype == jnp.int32...]
    dot_general x16 -> x0, matrix products: 28.3 us -> none  [the longest x1 4.88 us: per_device(): lax.dot_general(grad_rows, attn_flat, (((0,), (0,)), ((), ())), preferred...]
    reduce_scatter x1 -> x0, waiting for transfers between devices: 27.1 us -> none  [per_device(): lax.psum_scatter(lax.dot_general(grad_rows, attn_flat, (((0,), (0,)), (()...]
    ppermute x0 -> x17, starting transfers between devices: none -> 24.9 us  [the longest x6 11.8 us: gather_parts(): parts.append(lax.ppermute(x, 'seq', pairs))]
    ppermute x0 -> x17, waiting for transfers between devices: none -> 24.8 us  [the longest x6 21.9 us: gather_parts(): parts.append(lax.ppermute(x, 'seq', pairs))]
    all_gather x2 -> x0, waiting for transfers between devices: 22.2 us -> none  [the longest x1 22.2 us: per_device(): gathered = lax.all_gather(out_grad, 'head', axis=2, tiled=True)]
    all_to_all x1 -> x0, waiting for transfers between devices: 21.7 us -> none  [per_device(): lax.all_to_all(presum, 'seq', split_axis=0, concat_axis=0, tiled=True)]
    select_n x8 -> x0, local copies, waits for them, and re-layouts: 8.69 us -> none  [the longest x4 8.28 us: feature_slope(): return jnp.where(inputs > 0, 1.0, jnp.exp(jnp.minimum(inputs, 0.0)))]
  transfers between devices with their start and end apart: 4 -> 17, of which waited for: 3 -> 3; matrix products, arithmetic and copies ran while one was open for 31% -> 4% of each run, Pallas kernels for 0% -> 39%
where the time goes in v1:
time: 109 us; the launch traced here: 108 us
  Pallas kernels  43.9 us (40%)
  starting transfers between devices  24.9 us (23%)
  waiting for transfers between devices  24.8 us (23%)
  local copies, waits for them, and re-layouts  10.6 us (10%)
  other arithmetic  3 us (3%)
    pallas_call x9, Pallas kernels, call(): pl.pallas_call(body, out_shape=outs, in_specs=[SM if a.dtype == jnp.int32...  22.6 us
    ppermute x6, waiting for transfers between devices, gather_parts(): parts.append(lax.ppermute(x, 'seq', pairs))  21.9 us
    pallas_call x4, Pallas kernels, weight_part(): pl.pallas_call(body, out_shape=outs, grid_spec=pltpu.PrefetchScalarGridSp...  13.4 us
    ppermute x6, starting transfers between devices, gather_parts(): parts.append(lax.ppermute(x, 'seq', pairs))  11.8 us
    unnamed x37, local copies, waits for them, and re-layouts  8.82 us
    ppermute x1, starting transfers between devices, per_device(): lax.ppermute(cross, axes, to_side)  4.58 us
    ppermute x6, starting transfers between devices, swap(): return lax.ppermute(x, axis, [(0, 1), (1, 0)])  4.58 us
    pallas_call x1, Pallas kernels, own_partial(): pl.pallas_call(own_body, out_shape=sds((tokens, cols), F32), grid_spec=pl...  4.13 us
  transfers between devices with their start and end apart: 17, of which 3 were waited for; matrix products, arithmetic and copies ran while one was open for 4% of the time, Pallas kernels for 39%

profile of v1, /device:TPU:0, one launch (start us, length us, event | category | flops | bytes accessed | tf_op | source)
XLA Modules:
  0.0 108.0 jit_solution(2950326451160037863)
XLA Ops:
  0.6 1.1 %constant_dynamic-slice_fusion = bf16[1024,256]{1,0:T(8,128)(2,1)S(1)} fusion(bf16[4096,256]{1,0:T(8,128)(2,1)} %w_ref.1, s32[]{:T(128)S(6)} %select_n.22), kind=kLoop, calls=%fused_computation.10 | loop fusion | bytes 1048580 | tf_op jit(solution)/shard_map/dynamic_slice | solution.py:332
  1.7 3.0 %collective-permute-start.3 = (bf16[1024,256]{1,0:T(8,128)(2,1)S(1)}, bf16[1024,256]{1,0:T(8,128)(2,1)S(1)}, u32[]{:S(2)}, u32[]{:S(2)}) collective-permute-start(bf16[1024,256]{1,0:T(8,128)(2,1)S(1)} %constant_dynamic-slice_fusion), channel_id=1, source_target_pairs={{0,2},{2,0},{1,3},{3,1},{4,6},{6,4},{5,7},{7,5},{8,10},{10,8},{9,1... | collective-permute-start | bytes 1572872 | tf_op jit(solution)/shard_map/ppermute | solution.py:291
  4.7 2.0 %states.1 = (bf16[512,256]{1,0:T(8,128)(2,1)}, bf16[512,128]{1,0:T(8,128)(2,1)}) custom-call(bf16[512,256]{1,0:T(8,128)(2,1)} %bitcast.28, bf16[512,256]{1,0:T(8,128)(2,1)} %bitcast.21), custom_call_target="tpu_custom_call" | custom-call | flops 33554432 | bytes 917504 | tf_op jit(solution)/shard_map/states/pallas_call | solution.py:41
  6.8 3.6 %collective-permute-start.2 = (bf16[512,128]{1,0:T(8,128)(2,1)}, bf16[512,128]{1,0:T(8,128)(2,1)S(1)}, u32[]{:S(2)}, u32[]{:S(2)}) collective-permute-start(bf16[512,128]{1,0:T(8,128)(2,1)} %get-tuple-element.24.refs_3_), channel_id=1, source_target_pairs={{0,12},{4,0},{8,4},{12,8},{1,13},{5,1},{9,5},{13,9},{2,14},{6,2},{... | collective-permute-start | bytes 393224 | tf_op jit(solution)/shard_map/ppermute | solution.py:300
  10.4 1.0 collective-permute-start
  13.3 2.7 %scores.1 = (bf16[512,256]{1,0:T(8,128)(2,1)}, bf16[1024,256]{1,0:T(8,128)(2,1)}, f32[512,256]{1,0:T(8,128)}) custom-call(bf16[512,256]{1,0:T(8,128)(2,1)} %bitcast.25, bf16[512,256]{1,0:T(8,128)(2,1)} %get-tuple-element.25.kf_ref.refs_8_, bf16[512,256]{1,0:T(8,128)(2,1)} %bitcast.22), custom_call_target="tpu_custom_call" | custom-call | flops 134217728 | bytes 2097152 | tf_op jit(solution)/shard_map/scores/pallas_call | solution.py:41
  16.6 4.8 %collective-permute-done.1.refs_5_ = bf16[512,128]{1,0:T(8,128)(2,1)S(1)} collective-permute-done((bf16[512,128]{1,0:T(8,128)(2,1)}, bf16[512,128]{1,0:T(8,128)(2,1)S(1)}, u32[]{:S(2)}, u32[]{:S(2)}) %collective-permute-start.1) | collective-permute-done | bytes 131104 | tf_op jit(solution)/shard_map/ppermute | solution.py:300
  22.1 2.7 %numer.1 = (bf16[512,128]{1,0:T(8,128)(2,1)}, f32[512,256]{1,0:T(8,128)}, bf16[512,256]{1,0:T(8,128)(2,1)}) custom-call(s32[2]{0:T(128)} %pad_add_fusion.refs_0_.pos_ref, s32[4]{0:T(128)} %fusion.refs_1_, s32[64]{0:T(128)} %reshape.13.refs_2_, bf16[512,128]{1,0:T(8,128)(2,1)} %get-tuple-element.24.refs_3_, bf16[512,128]{1,0:T(8,128)(2,1)} %copy-done.17, ...), custom_call_target="tpu_custom_call" | custom-call | flops 33554432 | bytes 2228504 | tf_op jit(solution)/shard_map/numer/pallas_call | solution.py:41
  25.9 3.2 %weight_send.2 = bf16[512,512]{1,0:T(8,128)(2,1)} custom-call(s32[2]{0:T(128)} %broadcast_add_fusion.at_ref, bf16[512,256]{1,0:T(8,128)(2,1)} %get-tuple-element.28.attn_ref, bf16[512,2048]{1,0:T(8,128)(2,1)} %bitcast.15), custom_call_target="tpu_custom_call" | custom-call | flops 268435456 | bytes 2097152 | tf_op jit(solution)/shard_map/weight_send/pallas_call | solution.py:265
  29.6 2.8 %collective-permute-done.12.attn_ref = bf16[512,256]{1,0:T(8,128)(2,1)S(1)} collective-permute-done((bf16[512,256]{1,0:T(8,128)(2,1)}, bf16[512,256]{1,0:T(8,128)(2,1)S(1)}, u32[]{:S(2)}, u32[]{:S(2)}) %collective-permute-start.12) | collective-permute-done | bytes 262176 | tf_op jit(solution)/shard_map/ppermute | solution.py:291
  33.1 3.2 %weight_send.3 = bf16[512,512]{1,0:T(8,128)(2,1)} custom-call(s32[2]{0:T(128)} %broadcast_add_fusion.at_ref, bf16[512,256]{1,0:T(8,128)(2,1)} %copy-done, bf16[512,2048]{1,0:T(8,128)(2,1)} %bitcast.16), custom_call_target="tpu_custom_call" | custom-call | flops 268435456 | bytes 2097152 | tf_op jit(solution)/shard_map/weight_send/pallas_call | solution.py:265
  37.6 0.8 copy-done.4
  38.4 3.5 %weight_keep.2 = (bf16[256,512]{1,0:T(8,128)(2,1)}, f32[256,512]{1,0:T(8,128)}) custom-call(s32[2]{0:T(128)} %broadcast_add_fusion.1.at_ref, bf16[512,256]{1,0:T(8,128)(2,1)} %get-tuple-element.28.attn_ref, bf16[512,2048]{1,0:T(8,128)(2,1)} %bitcast.17, bf16[512,512]{1,0:T(8,128)(2,1)} %copy-done.4), custom_call_target="tpu_custom_call" | custom-call | flops 268435456 | bytes 2097152 | tf_op jit(solution)/shard_map/weight_keep/pallas_call | solution.py:265
  41.9 0.9 collective-permute-start.10
  42.8 0.8 copy-done.3
  43.6 3.8 %other_partial.1 = bf16[512,256]{1,0:T(8,128)(2,1)} custom-call(s32[2]{0:T(128)} %pad_add_fusion.1.at_ref, bf16[512,2048]{1,0:T(8,128)(2,1)} %bitcast.18, bf16[1024,256]{1,0:T(8,128)(2,1)} %copy-done.1, bf16[1024,256]{1,0:T(8,128)(2,1)} %copy-done.3), custom_call_target="tpu_custom_call" | custom-call | flops 536870912 | bytes 3407872 | tf_op jit(solution)/shard_map/other_partial/pallas_call | solution.py:209
  48.0 0.8 copy-done.2
  48.8 3.5 %weight_keep.3 = (bf16[256,512]{1,0:T(8,128)(2,1)}, f32[256,512]{1,0:T(8,128)}) custom-call(s32[2]{0:T(128)} %broadcast_add_fusion.1.at_ref, bf16[512,256]{1,0:T(8,128)(2,1)} %copy-done, bf16[512,2048]{1,0:T(8,128)(2,1)} %bitcast.19, bf16[512,512]{1,0:T(8,128)(2,1)} %copy-done.2), custom_call_target="tpu_custom_call" | custom-call | flops 268435456 | bytes 2097152 | tf_op jit(solution)/shard_map/weight_keep/pallas_call | solution.py:265
  52.3 1.1 %collective-permute-start.14 = (bf16[256,512]{1,0:T(8,128)(2,1)}, bf16[256,512]{1,0:T(8,128)(2,1)S(1)}, u32[]{:S(2)}, u32[]{:S(2)}) collective-permute-start(bf16[256,512]{1,0:T(8,128)(2,1)} %get-tuple-element.42), channel_id=1, source_target_pairs={{0,4},{4,0},{8,12},{12,8},{1,5},{5,1},{9,13},{13,9},{2,6},{6,2},{1... | collective-permute-start | bytes 786440 | tf_op jit(solution)/shard_map/ppermute | solution.py:394
  53.5 4.1 %own_partial.1.refs_0_ = f32[512,256]{1,0:T(8,128)} custom-call(s32[1]{0:T(128)} %bitcast.6.at_ref, bf16[512,2048]{1,0:T(8,128)(2,1)} %bitcast.20, bf16[4096,256]{1,0:T(8,128)(2,1)} %w_ref.1), custom_call_target="tpu_custom_call" | custom-call | flops 536870912 | bytes 3670016 | tf_op jit(solution)/shard_map/own_partial/pallas_call | solution.py:175
  58.3 2.6 %dnum.1 = (bf16[512,256]{1,0:T(8,128)(2,1)}, bf16[512,128]{1,0:T(8,128)(2,1)}) custom-call(f32[512,256]{1,0:T(8,128)} %own_partial.1.refs_0_, bf16[512,256]{1,0:T(8,128)(2,1)} %copy-done.10, f32[512,256]{1,0:T(8,128)} %get-tuple-element.29.refs_2_, bf16[512,256]{1,0:T(8,128)(2,1)} %get-tuple-element.26.refs_7_.refs_3_.qf_ref), custom_call_target="tpu_custom_call" | custom-call | flops 33554432 | bytes 1966080 | tf_op jit(solution)/shard_map/dnum/pallas_call | solution.py:41
  60.9 2.1 %collective-permute-start.8 = (bf16[512,128]{1,0:T(8,128)(2,1)}, bf16[512,128]{1,0:T(8,128)(2,1)S(1)}, u32[]{:S(2)}, u32[]{:S(2)}) collective-permute-start(bf16[512,128]{1,0:T(8,128)(2,1)} %get-tuple-element.34.refs_3_), channel_id=1, source_target_pairs={{0,12},{4,0},{8,4},{12,8},{1,13},{5,1},{9,5},{13,9},{2,14},{6,2},{... | collective-permute-start | bytes 393224 | tf_op jit(solution)/shard_map/ppermute | solution.py:300
  63.7 1.9 %pair.2.mine_ref = bf16[256,512]{1,0:T(8,128)(2,1)} custom-call(f32[256,512]{1,0:T(8,128)} %get-tuple-element.39.keep_ref, bf16[256,512]{1,0:T(8,128)(2,1)} %copy-done.8), custom_call_target="tpu_custom_call" | custom-call | bytes 1048576 | tf_op jit(solution)/shard_map/pair/pallas_call | solution.py:41
  65.6 1.3 %collective-permute-start.11 = (bf16[256,512]{1,0:T(8,128)(2,1)}, bf16[256,512]{1,0:T(8,128)(2,1)S(1)}, u32[]{:S(2)}, u32[]{:S(2)}) collective-permute-start(bf16[256,512]{1,0:T(8,128)(2,1)} %pair.2.mine_ref), channel_id=1, source_target_pairs={{2,10},{6,14},{8,0},{12,4},{3,11},{7,15},{9,1},{13,5},{18,26},{22,... | collective-permute-start | bytes 786440 | tf_op jit(solution)/shard_map/ppermute | solution.py:407
  67.6 1.9 %pair.3 = bf16[256,512]{1,0:T(8,128)(2,1)} custom-call(f32[256,512]{1,0:T(8,128)} %get-tuple-element.41.keep_ref, bf16[256,512]{1,0:T(8,128)(2,1)} %copy-done.9), custom_call_target="tpu_custom_call" | custom-call | bytes 1048576 | tf_op jit(solution)/shard_map/pair/pallas_call | solution.py:41
  69.4 4.6 %collective-permute-start.16 = (bf16[256,512]{1,0:T(8,128)(2,1)}, bf16[256,512]{1,0:T(8,128)(2,1)S(1)}, u32[]{:S(2)}, u32[]{:S(2)}) collective-permute-start(bf16[256,512]{1,0:T(8,128)(2,1)} %pair.3), channel_id=1, source_target_pairs={{0,2},{4,6},{10,8},{14,12},{1,3},{5,7},{11,9},{15,13},{16,18},{20,... | collective-permute-start | bytes 786440 | tf_op jit(solution)/shard_map/ppermute | solution.py:409
  74.7 3.0 %collective-permute-start.7 = (bf16[512,128]{1,0:T(8,128)(2,1)S(1)}, bf16[512,128]{1,0:T(8,128)(2,1)S(1)}, u32[]{:S(2)}, u32[]{:S(2)}) collective-permute-start(bf16[512,128]{1,0:T(8,128)(2,1)S(1)} %copy-done.11), channel_id=1, source_target_pairs={{0,8},{4,12},{8,0},{12,4},{1,9},{5,13},{9,1},{13,5},{2,10},{6,14},... | collective-permute-start | bytes 393224 | tf_op jit(solution)/shard_map/ppermute | solution.py:300
  77.7 2.0 %collective-permute-start.6 = (bf16[512,128]{1,0:T(8,128)(2,1)S(1)}, bf16[512,128]{1,0:T(8,128)(2,1)S(1)}, u32[]{:S(2)}, u32[]{:S(2)}) collective-permute-start(bf16[512,128]{1,0:T(8,128)(2,1)S(1)} %copy-done.11), channel_id=1, source_target_pairs={{0,4},{4,8},{8,12},{12,0},{1,5},{5,9},{9,13},{13,1},{2,6},{6,10},{... | collective-permute-start | bytes 393224 | tf_op jit(solution)/shard_map/ppermute | solution.py:300
  79.8 3.8 %query.1 = (bf16[512,256]{1,0:T(8,128)(2,1)}, f32[512,256]{1,0:T(8,128)}, f32[512,256]{1,0:T(8,128)}) custom-call(bf16[512,256]{1,0:T(8,128)(2,1)} %bitcast.26, bf16[512,256]{1,0:T(8,128)(2,1)} %get-tuple-element.26.refs_7_.refs_3_.qf_ref, bf16[512,256]{1,0:T(8,128)(2,1)} %get-tuple-element.25.kf_ref.refs_8_, bf16[512,256]{1,0:T(8,128)(2,1)} %bitcast.23, ...), custom_call_target="tpu_custom_call" | custom-call | flops 301989888 | bytes 3276800 | tf_op jit(solution)/shard_map/query/pallas_call | solution.py:41
  83.6 17.2 %collective-permute-done.7.refs_5_ = bf16[512,128]{1,0:T(8,128)(2,1)S(1)} collective-permute-done((bf16[512,128]{1,0:T(8,128)(2,1)S(1)}, bf16[512,128]{1,0:T(8,128)(2,1)S(1)}, u32[]{:S(2)}, u32[]{:S(2)}) %collective-permute-start.7) | collective-permute-done | bytes 131104 | tf_op jit(solution)/shard_map/ppermute | solution.py:300
  101.5 2.9 %key.1 = (bf16[512,256]{1,0:T(8,128)(2,1)}, bf16[512,256]{1,0:T(8,128)(2,1)}) custom-call(s32[2]{0:T(128)} %pad_add_fusion.refs_0_.pos_ref, s32[4]{0:T(128)} %fusion.refs_1_, s32[64]{0:T(128)} %reshape.13.refs_2_, bf16[512,128]{1,0:T(8,128)(2,1)} %get-tuple-element.34.refs_3_, bf16[512,128]{1,0:T(8,128)(2,1)} %copy-done.14, bf16[512,128]{1,0:T(8,128)(2,1)} %copy-done.13, ...), custom_call_target="tpu_custom_call" | custom-call | flops 67108864 | bytes 2883864 | tf_op jit(solution)/shard_map/key/pallas_call | solution.py:41
  105.8 2.2 %final.1 = f32[512,256]{1,0:T(8,128)} custom-call(s32[2]{0:T(128)} %pad_add_fusion.refs_0_.pos_ref, bf16[256,512]{1,0:T(8,128)(2,1)} %pair.2.mine_ref, bf16[256,512]{1,0:T(8,128)(2,1)} %copy-done.5, bf16[256,512]{1,0:T(8,128)(2,1)} %copy-done.7, bf16[256,512]{1,0:T(8,128)(2,1)} %copy-done.6), custom_call_target="tpu_custom_call" | custom-call | bytes 1572872 | tf_op jit(solution)/shard_map/final/pallas_call | solution.py:41
  (61 shorter events, 12.4 us)
Async XLA Ops:
  1.7 27.3 %collective-permute-start.3 = (bf16[1024,256]{1,0:T(8,128)(2,1)S(1)}, bf16[1024,256]{1,0:T(8,128)(2,1)S(1)}, u32[]{:S(2)}, u32[]{:S(2)}) collective-permute-start(bf16[1024,256]{1,0:T(8,128)(2,1)S(1)} %constant_dynamic-slice_fusion), channel_id=1, source_target_pairs={{0,2},{2,0},{1,3},{3,1},{4,6},{6,4},{5,7},{7,5},{8,10},{10,8},{9,1... | collective-permute-start | bytes 1572872 | tf_op jit(solution)/shard_map/ppermute | solution.py:291
  6.8 9.8 %collective-permute-start.2 = (bf16[512,128]{1,0:T(8,128)(2,1)}, bf16[512,128]{1,0:T(8,128)(2,1)S(1)}, u32[]{:S(2)}, u32[]{:S(2)}) collective-permute-start(bf16[512,128]{1,0:T(8,128)(2,1)} %get-tuple-element.24.refs_3_), channel_id=1, source_target_pairs={{0,12},{4,0},{8,4},{12,8},{1,13},{5,1},{9,5},{13,9},{2,14},{6,2},{... | collective-permute-start | bytes 393224 | tf_op jit(solution)/shard_map/ppermute | solution.py:300
  10.4 11.0 %collective-permute-start.1 = (bf16[512,128]{1,0:T(8,128)(2,1)}, bf16[512,128]{1,0:T(8,128)(2,1)S(1)}, u32[]{:S(2)}, u32[]{:S(2)}) collective-permute-start(bf16[512,128]{1,0:T(8,128)(2,1)} %get-tuple-element.24.refs_3_), channel_id=1, source_target_pairs={{0,8},{4,12},{8,0},{12,4},{1,9},{5,13},{9,1},{13,5},{2,10},{6,14},... | collective-permute-start | bytes 393224 | tf_op jit(solution)/shard_map/ppermute | solution.py:300
  10.4 11.0 %collective-permute-start = (bf16[512,128]{1,0:T(8,128)(2,1)}, bf16[512,128]{1,0:T(8,128)(2,1)S(1)}, u32[]{:S(2)}, u32[]{:S(2)}) collective-permute-start(bf16[512,128]{1,0:T(8,128)(2,1)} %get-tuple-element.24.refs_3_), channel_id=1, source_target_pairs={{0,4},{4,8},{8,12},{12,0},{1,5},{5,9},{9,13},{13,1},{2,6},{6,10},{... | collective-permute-start | bytes 393224 | tf_op jit(solution)/shard_map/ppermute | solution.py:300
  16.6 4.8 %copy-start.15 = (bf16[512,128]{1,0:T(8,128)(2,1)}, bf16[512,128]{1,0:T(8,128)(2,1)S(1)}, u32[]{:S(2)}) copy-start(bf16[512,128]{1,0:T(8,128)(2,1)S(1)} %collective-permute-done.2.refs_6_) | copy-start | bytes 393220
  21.4 0.7 copy-start.17
  24.8 7.7 %collective-permute-start.12 = (bf16[512,256]{1,0:T(8,128)(2,1)}, bf16[512,256]{1,0:T(8,128)(2,1)S(1)}, u32[]{:S(2)}, u32[]{:S(2)}) collective-permute-start(bf16[512,256]{1,0:T(8,128)(2,1)} %get-tuple-element.28.attn_ref), channel_id=1, source_target_pairs={{0,2},{2,0},{1,3},{3,1},{4,6},{6,4},{5,7},{7,5},{8,10},{10,8},{9,1... | collective-permute-start | bytes 786440 | tf_op jit(solution)/shard_map/ppermute | solution.py:291
  29.0 8.6 %collective-permute-start.9 = (bf16[512,512]{1,0:T(8,128)(2,1)}, bf16[512,512]{1,0:T(8,128)(2,1)S(1)}, u32[]{:S(2)}, u32[]{:S(2)}) collective-permute-start(bf16[512,512]{1,0:T(8,128)(2,1)} %weight_send.2), channel_id=1, source_target_pairs={{0,1},{1,0},{2,3},{3,2},{4,5},{5,4},{6,7},{7,6},{8,9},{9,8},{10,11... | collective-permute-start | bytes 1572872 | tf_op jit(solution)/shard_map/ppermute | solution.py:291
  29.1 13.8 %copy-start.1 = (bf16[1024,256]{1,0:T(8,128)(2,1)}, bf16[1024,256]{1,0:T(8,128)(2,1)S(1)}, u32[]{:S(2)}) copy-start(bf16[1024,256]{1,0:T(8,128)(2,1)S(1)} %collective-permute-done.3.first_ref) | copy-start | bytes 1572868
  29.1 13.8 %collective-permute-start.4 = (bf16[1024,256]{1,0:T(8,128)(2,1)S(1)}, bf16[1024,256]{1,0:T(8,128)(2,1)S(1)}, u32[]{:S(2)}, u32[]{:S(2)}) collective-permute-start(bf16[1024,256]{1,0:T(8,128)(2,1)S(1)} %collective-permute-done.3.first_ref), channel_id=1, source_target_pairs={{0,1},{1,0},{2,3},{3,2},{4,5},{5,4},{6,7},{7,6},{8,9},{9,8},{10,11... | collective-permute-start | bytes 1572872 | tf_op jit(solution)/shard_map/ppermute | solution.py:291
  32.4 0.7 copy-start
  36.3 11.7 %collective-permute-start.13 = (bf16[512,512]{1,0:T(8,128)(2,1)}, bf16[512,512]{1,0:T(8,128)(2,1)S(1)}, u32[]{:S(2)}, u32[]{:S(2)}) collective-permute-start(bf16[512,512]{1,0:T(8,128)(2,1)} %weight_send.3), channel_id=1, source_target_pairs={{0,1},{1,0},{2,3},{3,2},{4,5},{5,4},{6,7},{7,6},{8,9},{9,8},{10,11... | collective-permute-start | bytes 1572872 | tf_op jit(solution)/shard_map/ppermute | solution.py:291
  37.6 0.8 copy-start.4
  41.9 21.1 %collective-permute-start.10 = (bf16[256,512]{1,0:T(8,128)(2,1)}, bf16[256,512]{1,0:T(8,128)(2,1)S(1)}, u32[]{:S(2)}, u32[]{:S(2)}) collective-permute-start(bf16[256,512]{1,0:T(8,128)(2,1)} %get-tuple-element.40), channel_id=1, source_target_pairs={{0,4},{4,0},{8,12},{12,8},{1,5},{5,1},{9,13},{13,9},{2,6},{6,2},{1... | collective-permute-start | bytes 786440 | tf_op jit(solution)/shard_map/ppermute | solution.py:394
  42.8 0.8 copy-start.3
  47.4 10.2 %collective-permute-start.5 = (bf16[512,256]{1,0:T(8,128)(2,1)}, bf16[512,256]{1,0:T(8,128)(2,1)S(1)}, u32[]{:S(2)}, u32[]{:S(2)}) collective-permute-start(bf16[512,256]{1,0:T(8,128)(2,1)} %other_partial.1), channel_id=1, source_target_pairs={{0,2},{2,0},{1,3},{3,1},{4,6},{6,4},{5,7},{7,5},{8,10},{10,8},{9,1... | collective-permute-start | bytes 786440 | tf_op jit(solution)/shard_map/ppermute | solution.py:291
  48.0 0.8 copy-start.2
  52.3 14.5 %collective-permute-start.14 = (bf16[256,512]{1,0:T(8,128)(2,1)}, bf16[256,512]{1,0:T(8,128)(2,1)S(1)}, u32[]{:S(2)}, u32[]{:S(2)}) collective-permute-start(bf16[256,512]{1,0:T(8,128)(2,1)} %get-tuple-element.42), channel_id=1, source_target_pairs={{0,4},{4,0},{8,12},{12,8},{1,5},{5,1},{9,13},{13,9},{2,6},{6,2},{1... | collective-permute-start | bytes 786440 | tf_op jit(solution)/shard_map/ppermute | solution.py:394
  57.6 0.7 copy-start.10
  60.9 13.8 %copy-start.11 = (bf16[512,128]{1,0:T(8,128)(2,1)S(1)}, bf16[512,128]{1,0:T(8,128)(2,1)}, u32[]{:S(2)}) copy-start(bf16[512,128]{1,0:T(8,128)(2,1)} %get-tuple-element.34.refs_3_) | copy-start | bytes 393220
  60.9 16.9 %collective-permute-start.8 = (bf16[512,128]{1,0:T(8,128)(2,1)}, bf16[512,128]{1,0:T(8,128)(2,1)S(1)}, u32[]{:S(2)}, u32[]{:S(2)}) collective-permute-start(bf16[512,128]{1,0:T(8,128)(2,1)} %get-tuple-element.34.refs_3_), channel_id=1, source_target_pairs={{0,12},{4,0},{8,4},{12,8},{1,13},{5,1},{9,5},{13,9},{2,14},{6,2},{... | collective-permute-start | bytes 393224 | tf_op jit(solution)/shard_map/ppermute | solution.py:300
  63.0 0.7 copy-start.8
  65.6 38.8 %collective-permute-start.11 = (bf16[256,512]{1,0:T(8,128)(2,1)}, bf16[256,512]{1,0:T(8,128)(2,1)S(1)}, u32[]{:S(2)}, u32[]{:S(2)}) collective-permute-start(bf16[256,512]{1,0:T(8,128)(2,1)} %pair.2.mine_ref), channel_id=1, source_target_pairs={{2,10},{6,14},{8,0},{12,4},{3,11},{7,15},{9,1},{13,5},{18,26},{22,... | collective-permute-start | bytes 786440 | tf_op jit(solution)/shard_map/ppermute | solution.py:407
  66.9 0.7 copy-start.9
  69.4 34.9 %collective-permute-start.16 = (bf16[256,512]{1,0:T(8,128)(2,1)}, bf16[256,512]{1,0:T(8,128)(2,1)S(1)}, u32[]{:S(2)}, u32[]{:S(2)}) collective-permute-start(bf16[256,512]{1,0:T(8,128)(2,1)} %pair.3), channel_id=1, source_target_pairs={{0,2},{4,6},{10,8},{14,12},{1,3},{5,7},{11,9},{15,13},{16,18},{20,... | collective-permute-start | bytes 786440 | tf_op jit(solution)/shard_map/ppermute | solution.py:409
  74.0 30.4 %collective-permute-start.15 = (bf16[256,512]{1,0:T(8,128)(2,1)}, bf16[256,512]{1,0:T(8,128)(2,1)S(1)}, u32[]{:S(2)}, u32[]{:S(2)}) collective-permute-start(bf16[256,512]{1,0:T(8,128)(2,1)} %pair.3), channel_id=1, source_target_pairs={{2,8},{6,12},{8,2},{12,6},{3,9},{7,13},{9,3},{13,7},{18,24},{22,28... | collective-permute-start | bytes 786440 | tf_op jit(solution)/shard_map/ppermute | solution.py:408
  74.7 26.0 %collective-permute-start.7 = (bf16[512,128]{1,0:T(8,128)(2,1)S(1)}, bf16[512,128]{1,0:T(8,128)(2,1)S(1)}, u32[]{:S(2)}, u32[]{:S(2)}) collective-permute-start(bf16[512,128]{1,0:T(8,128)(2,1)S(1)} %copy-done.11), channel_id=1, source_target_pairs={{0,8},{4,12},{8,0},{12,4},{1,9},{5,13},{9,1},{13,5},{2,10},{6,14},... | collective-permute-start | bytes 393224 | tf_op jit(solution)/shard_map/ppermute | solution.py:300
  77.7 23.0 %copy-start.12 = (bf16[512,128]{1,0:T(8,128)(2,1)}, bf16[512,128]{1,0:T(8,128)(2,1)S(1)}, u32[]{:S(2)}) copy-start(bf16[512,128]{1,0:T(8,128)(2,1)S(1)} %collective-permute-done.8.refs_6_) | copy-start | bytes 393220
  77.7 23.0 %collective-permute-start.6 = (bf16[512,128]{1,0:T(8,128)(2,1)S(1)}, bf16[512,128]{1,0:T(8,128)(2,1)S(1)}, u32[]{:S(2)}, u32[]{:S(2)}) collective-permute-start(bf16[512,128]{1,0:T(8,128)(2,1)S(1)} %copy-done.11), channel_id=1, source_target_pairs={{0,4},{4,8},{8,12},{12,0},{1,5},{5,9},{9,13},{13,1},{2,6},{6,10},{... | collective-permute-start | bytes 393224 | tf_op jit(solution)/shard_map/ppermute | solution.py:300
  104.4 0.7 copy-start.5
  104.4 0.8 copy-start.6
  105.1 0.7 copy-start.7
  (3 other events, 2.0 us)

commit v2 on v1

--- a/solution.py
+++ b/solution.py
@@ -10,6 +10,7 @@
 DH = 128
 BLK = 256
 EPS = 1e-06
+LIMIT = 16 << 20
 F32 = jnp.float32
 BF16 = jnp.bfloat16
 VM = pl.BlockSpec(memory_space=pltpu.VMEM)
@@ -44,6 +45,7 @@
         in_specs=[SM if a.dtype == jnp.int32 else VM for a in ins],
         out_specs=[VM] * len(outs),
         name=name,
+        compiler_params=pltpu.CompilerParams(vmem_limit_bytes=LIMIT),
         cost_estimate=pl.CostEstimate(flops=flops, bytes_accessed=read + wrote, transcendentals=0),
     )(*ins)
 
@@ -185,6 +187,7 @@
             out_specs=pl.BlockSpec((tokens, cols), lambda g, at: (0, 0)),
         ),
         name="own_partial",
+        compiler_params=pltpu.CompilerParams(vmem_limit_bytes=LIMIT),
         cost_estimate=pl.CostEstimate(
             flops=2 * tokens * width * cols,
             bytes_accessed=2 * tokens * width + 2 * width * cols + 4 * tokens * cols,
@@ -221,6 +224,7 @@
             scratch_shapes=[pltpu.VMEM((tokens, cols), F32)],
         ),
         name="other_partial",
+        compiler_params=pltpu.CompilerParams(vmem_limit_bytes=LIMIT),
         cost_estimate=pl.CostEstimate(
             flops=2 * tokens * width * cols,
             bytes_accessed=2 * tokens * width + 2 * width * cols + 2 * tokens * cols,
@@ -269,6 +273,7 @@
             num_scalar_prefetch=1, grid=(2,), in_specs=specs, out_specs=out_specs
         ),
         name="weight_send" if got is None else "weight_keep",
+        compiler_params=pltpu.CompilerParams(vmem_limit_bytes=LIMIT),
         cost_estimate=pl.CostEstimate(
             flops=4 * tokens * rows * cols,
             bytes_accessed=2 * tokens * (cols + 2 * rows) + 6 * cols * rows,

time: 109 us -> 91 us (0.83)
  Pallas kernels: 43.9 us -> 18.3 us
  waiting for transfers between devices: 24.8 us -> 37.3 us
  other arithmetic: 3 us -> 0.32 us
    pallas_call x9, Pallas kernels: 22.6 us -> 8.73 us  [call(): pl.pallas_call(body, out_shape=outs, in_specs=[SM if a.dtype == jnp.int32...]
    pallas_call x4, Pallas kernels: 13.4 us -> 5.38 us  [weight_part(): pl.pallas_call(body, out_shape=outs, grid_spec=pltpu.PrefetchScalarGridSp...]
    ppermute x6, waiting for transfers between devices: 21.9 us -> 29.5 us  [gather_parts(): parts.append(lax.ppermute(x, 'seq', pairs))]
    ppermute x6, waiting for transfers between devices: 2.86 us -> 7.78 us  [swap(): return lax.ppermute(x, axis, [(0, 1), (1, 0)])]
    pallas_call x1, Pallas kernels: 4.13 us -> 1.57 us  [own_partial(): pl.pallas_call(own_body, out_shape=sds((tokens, cols), F32), grid_spec=pl...]
    ppermute x1, starting transfers between devices: 4.58 us -> 2.46 us  [per_device(): lax.ppermute(cross, axes, to_side)]
    pallas_call x1, Pallas kernels: 3.8 us -> 2.6 us  [other_partial(): pl.pallas_call(other_body, out_shape=sds((tokens, cols), BF16), grid_spec...]
    unnamed x37 -> x35, local copies, waits for them, and re-layouts: 8.82 us -> 7.78 us
  transfers between devices with their start and end apart: 17 -> 17, of which waited for: 3 -> 4; matrix products, arithmetic and copies ran while one was open for 4% -> 1% of each run, Pallas kernels for 39% -> 18%
where the time goes in v2:
time: 91 us; the launch traced here: 90.6 us
  waiting for transfers between devices  37.3 us (41%)
  starting transfers between devices  23.9 us (26%)
  Pallas kernels  18.3 us (20%)
  local copies, waits for them, and re-layouts  9.88 us (11%)
    ppermute x6, waiting for transfers between devices, gather_parts(): parts.append(lax.ppermute(x, 'seq', pairs))  29.5 us
    ppermute x6, starting transfers between devices, gather_parts(): parts.append(lax.ppermute(x, 'seq', pairs))  12.6 us
    pallas_call x9, Pallas kernels, call(): pl.pallas_call(body, out_shape=outs, in_specs=[SM if a.dtype == jnp.int32...  8.73 us
    ppermute x6, waiting for transfers between devices, swap(): return lax.ppermute(x, axis, [(0, 1), (1, 0)])  7.78 us
    unnamed x35, local copies, waits for them, and re-layouts  7.78 us
    pallas_call x4, Pallas kernels, weight_part(): pl.pallas_call(body, out_shape=outs, grid_spec=pltpu.PrefetchScalarGridSp...  5.38 us
    ppermute x6, starting transfers between devices, swap(): return lax.ppermute(x, axis, [(0, 1), (1, 0)])  4.7 us
    pallas_call x1, Pallas kernels, other_partial(): pl.pallas_call(other_body, out_shape=sds((tokens, cols), BF16), grid_spec...  2.6 us
  transfers between devices with their start and end apart: 17, of which 4 were waited for; matrix products, arithmetic and copies ran while one was open for 1% of the time, Pallas kernels for 18%

profile of v2, /device:TPU:0, one launch (start us, length us, event | category | flops | bytes accessed | tf_op | source)
XLA Modules:
  0.0 90.6 jit_solution(7774696983819436287)
XLA Ops:
  0.7 2.0 %constant_dynamic-slice_fusion = bf16[1024,256]{1,0:T(8,128)(2,1)} fusion(bf16[4096,256]{1,0:T(8,128)(2,1)} %w_ref.1, s32[]{:T(128)S(6)} %select_n.22), kind=kLoop, calls=%fused_computation.10 | loop fusion | bytes 1048580 | tf_op jit(solution)/shard_map/dynamic_slice | solution.py:337
  2.7 2.9 %collective-permute-start.3 = (bf16[1024,256]{1,0:T(8,128)(2,1)}, bf16[1024,256]{1,0:T(8,128)(2,1)}, u32[]{:S(2)}, u32[]{:S(2)}) collective-permute-start(bf16[1024,256]{1,0:T(8,128)(2,1)} %constant_dynamic-slice_fusion), channel_id=1, source_target_pairs={{0,2},{2,0},{1,3},{3,1},{4,6},{6,4},{5,7},{7,5},{8,10},{10,8},{9,1... | collective-permute-start | bytes 1572872 | tf_op jit(solution)/shard_map/ppermute | solution.py:296
  5.6 0.9 %copy-done.1 = bf16[1,512,256]{2,1,0:T(8,128)(2,1)S(1)} copy-done((bf16[1,512,256]{2,1,0:T(8,128)(2,1)S(1)}, bf16[1,512,256]{2,1,0:T(8,128)(2,1)}, u32[]{:S(2)}) %copy-start.1) | copy-done | bytes 262168
  6.6 0.9 %copy-done.9 = bf16[1,512,256]{2,1,0:T(8,128)(2,1)S(1)} copy-done((bf16[1,512,256]{2,1,0:T(8,128)(2,1)S(1)}, bf16[1,512,256]{2,1,0:T(8,128)(2,1)}, u32[]{:S(2)}) %copy-start.9) | copy-done | bytes 262168
  7.9 3.7 %collective-permute-start.2 = (bf16[512,128]{1,0:T(8,128)(2,1)S(1)}, bf16[512,128]{1,0:T(8,128)(2,1)S(1)}, u32[]{:S(2)}, u32[]{:S(2)}) collective-permute-start(bf16[512,128]{1,0:T(8,128)(2,1)S(1)} %get-tuple-element.24.refs_3_), channel_id=1, source_target_pairs={{0,12},{4,0},{8,4},{12,8},{1,13},{5,1},{9,5},{13,9},{2,14},{6,2},{... | collective-permute-start | bytes 393224 | tf_op jit(solution)/shard_map/ppermute | solution.py:305
  11.5 1.0 %collective-permute-start = (bf16[512,128]{1,0:T(8,128)(2,1)S(1)}, bf16[512,128]{1,0:T(8,128)(2,1)S(1)}, u32[]{:S(2)}, u32[]{:S(2)}) collective-permute-start(bf16[512,128]{1,0:T(8,128)(2,1)S(1)} %get-tuple-element.24.refs_3_), channel_id=1, source_target_pairs={{0,4},{4,8},{8,12},{12,0},{1,5},{5,9},{9,13},{13,1},{2,6},{6,10},{... | collective-permute-start | bytes 393224 | tf_op jit(solution)/shard_map/ppermute | solution.py:305
  12.6 0.8 copy.12
  13.4 0.9 %copy-done.2 = bf16[1,512,256]{2,1,0:T(8,128)(2,1)S(1)} copy-done((bf16[1,512,256]{2,1,0:T(8,128)(2,1)S(1)}, bf16[1,512,256]{2,1,0:T(8,128)(2,1)}, u32[]{:S(2)}) %copy-start.2) | copy-done | bytes 262168
  14.4 0.9 %copy-done.5 = bf16[1,512,256]{2,1,0:T(8,128)(2,1)S(1)} copy-done((bf16[1,512,256]{2,1,0:T(8,128)(2,1)S(1)}, bf16[1,512,256]{2,1,0:T(8,128)(2,1)}, u32[]{:S(2)}) %copy-start.5) | copy-done | bytes 262168
  16.1 6.3 %collective-permute-done.1.refs_5_ = bf16[512,128]{1,0:T(8,128)(2,1)S(1)} collective-permute-done((bf16[512,128]{1,0:T(8,128)(2,1)S(1)}, bf16[512,128]{1,0:T(8,128)(2,1)S(1)}, u32[]{:S(2)}, u32[]{:S(2)}) %collective-permute-start.1) | collective-permute-done | bytes 131104 | tf_op jit(solution)/shard_map/ppermute | solution.py:305
  23.0 0.9 copy-done.14
  23.9 1.8 %numer.1 = (bf16[512,128]{1,0:T(8,128)(2,1)S(1)}, f32[512,256]{1,0:T(8,128)S(1)}, bf16[512,256]{1,0:T(8,128)(2,1)}) custom-call(s32[2]{0:T(128)S(1)} %pad_add_fusion.refs_0_.pos_ref, s32[4]{0:T(128)S(1)} %fusion.refs_1_, s32[64]{0:T(128)S(1)} %reshape.13.refs_2_, bf16[512,128]{1,0:T(8,128)(2,1)S(1)} %get-tuple-element.24.refs_3_, ...), custom_call_target="tpu_custom_call" | custom-call | flops 33554432 | bytes 2228504 | tf_op jit(solution)/shard_map/numer/pallas_call | solution.py:42
  26.9 0.9 %copy-done.7 = bf16[512,256]{1,0:T(8,128)(2,1)S(1)} copy-done((bf16[512,256]{1,0:T(8,128)(2,1)S(1)}, bf16[512,256]{1,0:T(8,128)(2,1)}, u32[]{:S(2)}) %copy-start.7) | copy-done | bytes 262168
  27.9 1.3 %weight_send.2 = bf16[512,512]{1,0:T(8,128)(2,1)S(1)} custom-call(s32[2]{0:T(128)S(1)} %broadcast_add_fusion.at_ref, bf16[512,256]{1,0:T(8,128)(2,1)S(1)} %copy-done.7, bf16[512,2048]{1,0:T(8,128)(2,1)S(1)} %bitcast.15), custom_call_target="tpu_custom_call" | custom-call | flops 268435456 | bytes 2097152 | tf_op jit(solution)/shard_map/weight_send/pallas_call | solution.py:269
  29.8 4.2 %collective-permute-done.12.attn_ref = bf16[512,256]{1,0:T(8,128)(2,1)S(1)} collective-permute-done((bf16[512,256]{1,0:T(8,128)(2,1)}, bf16[512,256]{1,0:T(8,128)(2,1)S(1)}, u32[]{:S(2)}, u32[]{:S(2)}) %collective-permute-start.12) | collective-permute-done | bytes 262176 | tf_op jit(solution)/shard_map/ppermute | solution.py:296
  34.0 1.3 %weight_send.3 = bf16[512,512]{1,0:T(8,128)(2,1)S(1)} custom-call(s32[2]{0:T(128)S(1)} %broadcast_add_fusion.at_ref, bf16[512,256]{1,0:T(8,128)(2,1)S(1)} %collective-permute-done.12.attn_ref, bf16[512,2048]{1,0:T(8,128)(2,1)S(1)} %bitcast.16), custom_call_target="tpu_custom_call" | custom-call | flops 268435456 | bytes 2097152 | tf_op jit(solution)/shard_map/weight_send/pallas_call | solution.py:269
  35.5 1.4 %weight_keep.2 = (bf16[256,512]{1,0:T(8,128)(2,1)S(1)}, f32[256,512]{1,0:T(8,128)S(1)}) custom-call(s32[2]{0:T(128)S(1)} %broadcast_add_fusion.1.at_ref, bf16[512,256]{1,0:T(8,128)(2,1)S(1)} %copy-done.8, bf16[512,2048]{1,0:T(8,128)(2,1)S(1)} %bitcast.17, bf16[512,512]{1,0:T(8,128)(2,1)S(1)} %collective-permute-done.9.got_ref), custom_call_target="tpu_custom_call" | custom-call | flops 268435456 | bytes 2097152 | tf_op jit(solution)/shard_map/weight_keep/pallas_call | solution.py:269
  36.9 0.9 collective-permute-start.10
  37.8 2.6 %other_partial.1 = bf16[512,256]{1,0:T(8,128)(2,1)S(1)} custom-call(s32[2]{0:T(128)S(1)} %pad_add_fusion.1.at_ref, bf16[512,2048]{1,0:T(8,128)(2,1)S(1)} %bitcast.18, bf16[1024,256]{1,0:T(8,128)(2,1)} %collective-permute-done.3.first_ref, bf16[1024,256]{1,0:T(8,128)(2,1)S(1)} %collective-permute-done.4.second_ref), custom_call_target="tpu_custom_call" | custom-call | flops 536870912 | bytes 3407872 | tf_op jit(solution)/shard_map/other_partial/pallas_call | solution.py:212
  41.0 1.4 %weight_keep.3 = (bf16[256,512]{1,0:T(8,128)(2,1)S(1)}, f32[256,512]{1,0:T(8,128)S(1)}) custom-call(s32[2]{0:T(128)S(1)} %broadcast_add_fusion.1.at_ref, bf16[512,256]{1,0:T(8,128)(2,1)S(1)} %collective-permute-done.12.attn_ref, bf16[512,2048]{1,0:T(8,128)(2,1)S(1)} %bitcast.19, bf16[512,512]{1,0:T(8,128)(2,1)S(1)} %collective-permute-done.13.got_ref), custom_call_target="tpu_custom_call" | custom-call | flops 268435456 | bytes 2097152 | tf_op jit(solution)/shard_map/weight_keep/pallas_call | solution.py:269
  42.4 1.3 %collective-permute-start.14 = (bf16[256,512]{1,0:T(8,128)(2,1)S(1)}, bf16[256,512]{1,0:T(8,128)(2,1)S(1)}, u32[]{:S(2)}, u32[]{:S(2)}) collective-permute-start(bf16[256,512]{1,0:T(8,128)(2,1)S(1)} %get-tuple-element.42), channel_id=1, source_target_pairs={{0,4},{4,0},{8,12},{12,8},{1,5},{5,1},{9,13},{13,9},{2,6},{6,2},{1... | collective-permute-start | bytes 786440 | tf_op jit(solution)/shard_map/ppermute | solution.py:399
  43.7 1.6 %own_partial.1.refs_0_ = f32[512,256]{1,0:T(8,128)S(1)} custom-call(s32[1]{0:T(128)} %bitcast.6.at_ref, bf16[512,2048]{1,0:T(8,128)(2,1)S(1)} %bitcast.20, bf16[4096,256]{1,0:T(8,128)(2,1)S(1)} %copy-done.4), custom_call_target="tpu_custom_call" | custom-call | flops 536870912 | bytes 3670016 | tf_op jit(solution)/shard_map/own_partial/pallas_call | solution.py:177
  45.3 3.6 %collective-permute-done.5.refs_1_ = bf16[512,256]{1,0:T(8,128)(2,1)S(1)} collective-permute-done((bf16[512,256]{1,0:T(8,128)(2,1)S(1)}, bf16[512,256]{1,0:T(8,128)(2,1)S(1)}, u32[]{:S(2)}, u32[]{:S(2)}) %collective-permute-start.5) | collective-permute-done | bytes 262176 | tf_op jit(solution)/shard_map/ppermute | solution.py:296
  49.5 3.4 %collective-permute-start.8 = (bf16[512,128]{1,0:T(8,128)(2,1)S(1)}, bf16[512,128]{1,0:T(8,128)(2,1)S(1)}, u32[]{:S(2)}, u32[]{:S(2)}) collective-permute-start(bf16[512,128]{1,0:T(8,128)(2,1)S(1)} %get-tuple-element.34.refs_3_), channel_id=1, source_target_pairs={{0,12},{4,0},{8,4},{12,8},{1,13},{5,1},{9,5},{13,9},{2,14},{6,2},{... | collective-permute-start | bytes 393224 | tf_op jit(solution)/shard_map/ppermute | solution.py:305
  53.0 1.3 %collective-permute-start.11 = (bf16[256,512]{1,0:T(8,128)(2,1)S(1)}, bf16[256,512]{1,0:T(8,128)(2,1)S(1)}, u32[]{:S(2)}, u32[]{:S(2)}) collective-permute-start(bf16[256,512]{1,0:T(8,128)(2,1)S(1)} %pair.2.mine_ref), channel_id=1, source_target_pairs={{2,10},{6,14},{8,0},{12,4},{3,11},{7,15},{9,1},{13,5},{18,26},{22,... | collective-permute-start | bytes 786440 | tf_op jit(solution)/shard_map/ppermute | solution.py:412
  54.4 2.5 %collective-permute-start.16 = (bf16[256,512]{1,0:T(8,128)(2,1)S(1)}, bf16[256,512]{1,0:T(8,128)(2,1)S(1)}, u32[]{:S(2)}, u32[]{:S(2)}) collective-permute-start(bf16[256,512]{1,0:T(8,128)(2,1)S(1)} %pair.3), channel_id=1, source_target_pairs={{0,2},{4,6},{10,8},{14,12},{1,3},{5,7},{11,9},{15,13},{16,18},{20,... | collective-permute-start | bytes 786440 | tf_op jit(solution)/shard_map/ppermute | solution.py:414
  57.5 3.7 %collective-permute-start.7 = (bf16[512,128]{1,0:T(8,128)(2,1)S(1)}, bf16[512,128]{1,0:T(8,128)(2,1)S(1)}, u32[]{:S(2)}, u32[]{:S(2)}) collective-permute-start(bf16[512,128]{1,0:T(8,128)(2,1)S(1)} %get-tuple-element.34.refs_3_), channel_id=1, source_target_pairs={{0,8},{4,12},{8,0},{12,4},{1,9},{5,13},{9,1},{13,5},{2,10},{6,14},... | collective-permute-start | bytes 393224 | tf_op jit(solution)/shard_map/ppermute | solution.py:305
  61.2 0.8 collective-permute-start.6
  62.1 1.9 %query.1 = (bf16[512,256]{1,0:T(8,128)(2,1)}, f32[512,256]{1,0:T(8,128)S(1)}, f32[512,256]{1,0:T(8,128)S(1)}) custom-call(bf16[512,256]{1,0:T(8,128)(2,1)S(1)} %bitcast.26, bf16[512,256]{1,0:T(8,128)(2,1)S(1)} %get-tuple-element.26.refs_7_.refs_3_.qf_ref, bf16[512,256]{1,0:T(8,128)(2,1)S(1)} %get-tuple-element.25.kf_ref.refs_8_, ...), custom_call_target="tpu_custom_call" | custom-call | flops 301989888 | bytes 3276800 | tf_op jit(solution)/shard_map/query/pallas_call | solution.py:42
  64.0 23.2 %collective-permute-done.7.refs_5_ = bf16[512,128]{1,0:T(8,128)(2,1)S(1)} collective-permute-done((bf16[512,128]{1,0:T(8,128)(2,1)S(1)}, bf16[512,128]{1,0:T(8,128)(2,1)S(1)}, u32[]{:S(2)}, u32[]{:S(2)}) %collective-permute-start.7) | collective-permute-done | bytes 131104 | tf_op jit(solution)/shard_map/ppermute | solution.py:305
  87.2 1.8 %key.1 = (bf16[512,256]{1,0:T(8,128)(2,1)}, bf16[512,256]{1,0:T(8,128)(2,1)}) custom-call(s32[2]{0:T(128)S(1)} %pad_add_fusion.refs_0_.pos_ref, s32[4]{0:T(128)S(1)} %fusion.refs_1_, s32[64]{0:T(128)S(1)} %reshape.13.refs_2_, bf16[512,128]{1,0:T(8,128)(2,1)S(1)} %get-tuple-element.34.refs_3_, bf16[512,128]{1,0:T(8,128)(2,1)S(1)} %collective-permute-done.6.refs_4_, ...), custom_call_target="tpu_custom_call" | custom-call | flops 67108864 | bytes 2883864 | tf_op jit(solution)/shard_map/key/pallas_call | solution.py:42
  89.0 1.5 %final.1 = f32[512,256]{1,0:T(8,128)} custom-call(s32[2]{0:T(128)S(1)} %pad_add_fusion.refs_0_.pos_ref, bf16[256,512]{1,0:T(8,128)(2,1)S(1)} %pair.2.mine_ref, bf16[256,512]{1,0:T(8,128)(2,1)S(1)} %collective-permute-done.11.a_ref, bf16[256,512]{1,0:T(8,128)(2,1)S(1)} %collective-permute-done.15.b_ref, bf16[256,512]{1,0:T(8,128)(2,1)S(1)} %collective-permute-done.16.c_ref), custom_call_target="tpu_custom_call" | custom-call | bytes 1572872 | tf_op jit(solution)/shard_map/final/pallas_call | solution.py:42
  (59 shorter events, 5.9 us)
Async XLA Ops:
  0.6 26.3 %copy-start = (bf16[1,512,2048]{2,1,0:T(8,128)(2,1)S(1)}, bf16[1,512,2048]{2,1,0:T(8,128)(2,1)}, u32[]{:S(2)}) copy-start(bf16[1,512,2048]{2,1,0:T(8,128)(2,1)} %param.11) | copy-start | bytes 6291460
  2.7 26.6 %collective-permute-start.3 = (bf16[1024,256]{1,0:T(8,128)(2,1)}, bf16[1024,256]{1,0:T(8,128)(2,1)}, u32[]{:S(2)}, u32[]{:S(2)}) collective-permute-start(bf16[1024,256]{1,0:T(8,128)(2,1)} %constant_dynamic-slice_fusion), channel_id=1, source_target_pairs={{0,2},{2,0},{1,3},{3,1},{4,6},{6,4},{5,7},{7,5},{8,10},{10,8},{9,1... | collective-permute-start | bytes 1572872 | tf_op jit(solution)/shard_map/ppermute | solution.py:296
  5.6 0.9 %copy-start.1 = (bf16[1,512,256]{2,1,0:T(8,128)(2,1)S(1)}, bf16[1,512,256]{2,1,0:T(8,128)(2,1)}, u32[]{:S(2)}) copy-start(bf16[1,512,256]{2,1,0:T(8,128)(2,1)} %param.8) | copy-start | bytes 786436
  6.6 0.9 %copy-start.9 = (bf16[1,512,256]{2,1,0:T(8,128)(2,1)S(1)}, bf16[1,512,256]{2,1,0:T(8,128)(2,1)}, u32[]{:S(2)}) copy-start(bf16[1,512,256]{2,1,0:T(8,128)(2,1)} %param.7) | copy-start | bytes 786436
  7.9 8.2 %collective-permute-start.2 = (bf16[512,128]{1,0:T(8,128)(2,1)S(1)}, bf16[512,128]{1,0:T(8,128)(2,1)S(1)}, u32[]{:S(2)}, u32[]{:S(2)}) collective-permute-start(bf16[512,128]{1,0:T(8,128)(2,1)S(1)} %get-tuple-element.24.refs_3_), channel_id=1, source_target_pairs={{0,12},{4,0},{8,4},{12,8},{1,13},{5,1},{9,5},{13,9},{2,14},{6,2},{... | collective-permute-start | bytes 393224 | tf_op jit(solution)/shard_map/ppermute | solution.py:305
  11.5 10.8 %collective-permute-start.1 = (bf16[512,128]{1,0:T(8,128)(2,1)S(1)}, bf16[512,128]{1,0:T(8,128)(2,1)S(1)}, u32[]{:S(2)}, u32[]{:S(2)}) collective-permute-start(bf16[512,128]{1,0:T(8,128)(2,1)S(1)} %get-tuple-element.24.refs_3_), channel_id=1, source_target_pairs={{0,8},{4,12},{8,0},{12,4},{1,9},{5,13},{9,1},{13,5},{2,10},{6,14},... | collective-permute-start | bytes 393224 | tf_op jit(solution)/shard_map/ppermute | solution.py:305
  11.5 10.8 %collective-permute-start = (bf16[512,128]{1,0:T(8,128)(2,1)S(1)}, bf16[512,128]{1,0:T(8,128)(2,1)S(1)}, u32[]{:S(2)}, u32[]{:S(2)}) collective-permute-start(bf16[512,128]{1,0:T(8,128)(2,1)S(1)} %get-tuple-element.24.refs_3_), channel_id=1, source_target_pairs={{0,4},{4,8},{8,12},{12,0},{1,5},{5,9},{9,13},{13,1},{2,6},{6,10},{... | collective-permute-start | bytes 393224 | tf_op jit(solution)/shard_map/ppermute | solution.py:305
  13.4 1.0 %copy-start.2 = (bf16[1,512,256]{2,1,0:T(8,128)(2,1)S(1)}, bf16[1,512,256]{2,1,0:T(8,128)(2,1)}, u32[]{:S(2)}) copy-start(bf16[1,512,256]{2,1,0:T(8,128)(2,1)} %param.8) | copy-start | bytes 786436
  14.4 0.9 %copy-start.5 = (bf16[1,512,256]{2,1,0:T(8,128)(2,1)S(1)}, bf16[1,512,256]{2,1,0:T(8,128)(2,1)}, u32[]{:S(2)}) copy-start(bf16[1,512,256]{2,1,0:T(8,128)(2,1)} %param.6) | copy-start | bytes 786436
  16.0 9.7 %copy-start.11 = (bf16[1024,256]{1,0:T(8,128)(2,1)}, bf16[1024,256]{1,0:T(8,128)(2,1)S(1)}, u32[]{:S(2)}) copy-start(bf16[1024,256]{1,0:T(8,128)(2,1)S(1)} %get-tuple-element.32.sc_ref) | copy-start | bytes 1572868
  23.0 0.9 copy-start.14
  26.3 7.7 %collective-permute-start.12 = (bf16[512,256]{1,0:T(8,128)(2,1)}, bf16[512,256]{1,0:T(8,128)(2,1)S(1)}, u32[]{:S(2)}, u32[]{:S(2)}) collective-permute-start(bf16[512,256]{1,0:T(8,128)(2,1)} %get-tuple-element.28.attn_ref), channel_id=1, source_target_pairs={{0,2},{2,0},{1,3},{3,1},{4,6},{6,4},{5,7},{7,5},{8,10},{10,8},{9,1... | collective-permute-start | bytes 786440 | tf_op jit(solution)/shard_map/ppermute | solution.py:296
  26.9 1.0 %copy-start.7 = (bf16[512,256]{1,0:T(8,128)(2,1)S(1)}, bf16[512,256]{1,0:T(8,128)(2,1)}, u32[]{:S(2)}) copy-start(bf16[512,256]{1,0:T(8,128)(2,1)} %get-tuple-element.28.attn_ref) | copy-start | bytes 786436
  29.2 6.3 %copy-start.8 = (bf16[512,256]{1,0:T(8,128)(2,1)S(1)}, bf16[512,256]{1,0:T(8,128)(2,1)}, u32[]{:S(2)}) copy-start(bf16[512,256]{1,0:T(8,128)(2,1)} %get-tuple-element.28.attn_ref) | copy-start | bytes 786436
  29.2 6.3 %collective-permute-start.9 = (bf16[512,512]{1,0:T(8,128)(2,1)S(1)}, bf16[512,512]{1,0:T(8,128)(2,1)S(1)}, u32[]{:S(2)}, u32[]{:S(2)}) collective-permute-start(bf16[512,512]{1,0:T(8,128)(2,1)S(1)} %weight_send.2), channel_id=1, source_target_pairs={{0,1},{1,0},{2,3},{3,2},{4,5},{5,4},{6,7},{7,6},{8,9},{9,8},{10,11... | collective-permute-start | bytes 1572872 | tf_op jit(solution)/shard_map/ppermute | solution.py:296
  29.3 8.5 %collective-permute-start.4 = (bf16[1024,256]{1,0:T(8,128)(2,1)}, bf16[1024,256]{1,0:T(8,128)(2,1)S(1)}, u32[]{:S(2)}, u32[]{:S(2)}) collective-permute-start(bf16[1024,256]{1,0:T(8,128)(2,1)} %collective-permute-done.3.first_ref), channel_id=1, source_target_pairs={{0,1},{1,0},{2,3},{3,2},{4,5},{5,4},{6,7},{7,6},{8,9},{9,8},{10,11... | collective-permute-start | bytes 1572872 | tf_op jit(solution)/shard_map/ppermute | solution.py:296
  35.3 5.7 %collective-permute-start.13 = (bf16[512,512]{1,0:T(8,128)(2,1)S(1)}, bf16[512,512]{1,0:T(8,128)(2,1)S(1)}, u32[]{:S(2)}, u32[]{:S(2)}) collective-permute-start(bf16[512,512]{1,0:T(8,128)(2,1)S(1)} %weight_send.3), channel_id=1, source_target_pairs={{0,1},{1,0},{2,3},{3,2},{4,5},{5,4},{6,7},{7,6},{8,9},{9,8},{10,11... | collective-permute-start | bytes 1572872 | tf_op jit(solution)/shard_map/ppermute | solution.py:296
  36.9 16.0 %collective-permute-start.10 = (bf16[256,512]{1,0:T(8,128)(2,1)S(1)}, bf16[256,512]{1,0:T(8,128)(2,1)S(1)}, u32[]{:S(2)}, u32[]{:S(2)}) collective-permute-start(bf16[256,512]{1,0:T(8,128)(2,1)S(1)} %get-tuple-element.40), channel_id=1, source_target_pairs={{0,4},{4,0},{8,12},{12,8},{1,5},{5,1},{9,13},{13,9},{2,6},{6,2},{1... | collective-permute-start | bytes 786440 | tf_op jit(solution)/shard_map/ppermute | solution.py:399
  40.4 3.3 %copy-start.4 = (bf16[4096,256]{1,0:T(8,128)(2,1)S(1)}, bf16[4096,256]{1,0:T(8,128)(2,1)}, u32[]{:S(2)}) copy-start(bf16[4096,256]{1,0:T(8,128)(2,1)} %w_ref.1) | copy-start | bytes 6291460
  40.4 8.5 %collective-permute-start.5 = (bf16[512,256]{1,0:T(8,128)(2,1)S(1)}, bf16[512,256]{1,0:T(8,128)(2,1)S(1)}, u32[]{:S(2)}, u32[]{:S(2)}) collective-permute-start(bf16[512,256]{1,0:T(8,128)(2,1)S(1)} %other_partial.1), channel_id=1, source_target_pairs={{0,2},{2,0},{1,3},{3,1},{4,6},{6,4},{5,7},{7,5},{8,10},{10,8},{9,1... | collective-permute-start | bytes 786440 | tf_op jit(solution)/shard_map/ppermute | solution.py:296
  42.4 11.9 %collective-permute-start.14 = (bf16[256,512]{1,0:T(8,128)(2,1)S(1)}, bf16[256,512]{1,0:T(8,128)(2,1)S(1)}, u32[]{:S(2)}, u32[]{:S(2)}) collective-permute-start(bf16[256,512]{1,0:T(8,128)(2,1)S(1)} %get-tuple-element.42), channel_id=1, source_target_pairs={{0,4},{4,0},{8,12},{12,8},{1,5},{5,1},{9,13},{13,9},{2,6},{6,2},{1... | collective-permute-start | bytes 786440 | tf_op jit(solution)/shard_map/ppermute | solution.py:399
  45.3 16.8 %copy-start.3 = (bf16[1,512,256]{2,1,0:T(8,128)(2,1)S(1)}, bf16[1,512,256]{2,1,0:T(8,128)(2,1)}, u32[]{:S(2)}) copy-start(bf16[1,512,256]{2,1,0:T(8,128)(2,1)} %param.8) | copy-start | bytes 786436
  45.3 16.8 %copy-start.6 = (bf16[1,512,256]{2,1,0:T(8,128)(2,1)S(1)}, bf16[1,512,256]{2,1,0:T(8,128)(2,1)}, u32[]{:S(2)}) copy-start(bf16[1,512,256]{2,1,0:T(8,128)(2,1)} %param.6) | copy-start | bytes 786436
  45.3 16.7 %copy-start.12 = (bf16[1024,256]{1,0:T(8,128)(2,1)S(1)}, bf16[1024,256]{1,0:T(8,128)(2,1)}, u32[]{:S(2)}) copy-start(bf16[1024,256]{1,0:T(8,128)(2,1)} %copy-done.11) | copy-start | bytes 1572868
  45.3 16.7 %copy-start.16 = (bf16[512,128]{1,0:T(8,128)(2,1)S(1)}, bf16[512,128]{1,0:T(8,128)(2,1)}, u32[]{:S(2)}) copy-start(bf16[512,128]{1,0:T(8,128)(2,1)} %copy-done.15) | copy-start | bytes 393220
  49.5 37.7 %copy-start.10 = (bf16[1,512,256]{2,1,0:T(8,128)(2,1)S(1)}, bf16[1,512,256]{2,1,0:T(8,128)(2,1)}, u32[]{:S(2)}) copy-start(bf16[1,512,256]{2,1,0:T(8,128)(2,1)} %param.7) | copy-start | bytes 786436
  49.5 11.7 %collective-permute-start.8 = (bf16[512,128]{1,0:T(8,128)(2,1)S(1)}, bf16[512,128]{1,0:T(8,128)(2,1)S(1)}, u32[]{:S(2)}, u32[]{:S(2)}) collective-permute-start(bf16[512,128]{1,0:T(8,128)(2,1)S(1)} %get-tuple-element.34.refs_3_), channel_id=1, source_target_pairs={{0,12},{4,0},{8,4},{12,8},{1,13},{5,1},{9,5},{13,9},{2,14},{6,2},{... | collective-permute-start | bytes 393224 | tf_op jit(solution)/shard_map/ppermute | solution.py:305
  53.0 36.0 %collective-permute-start.11 = (bf16[256,512]{1,0:T(8,128)(2,1)S(1)}, bf16[256,512]{1,0:T(8,128)(2,1)S(1)}, u32[]{:S(2)}, u32[]{:S(2)}) collective-permute-start(bf16[256,512]{1,0:T(8,128)(2,1)S(1)} %pair.2.mine_ref), channel_id=1, source_target_pairs={{2,10},{6,14},{8,0},{12,4},{3,11},{7,15},{9,1},{13,5},{18,26},{22,... | collective-permute-start | bytes 786440 | tf_op jit(solution)/shard_map/ppermute | solution.py:412
  54.4 34.7 %collective-permute-start.16 = (bf16[256,512]{1,0:T(8,128)(2,1)S(1)}, bf16[256,512]{1,0:T(8,128)(2,1)S(1)}, u32[]{:S(2)}, u32[]{:S(2)}) collective-permute-start(bf16[256,512]{1,0:T(8,128)(2,1)S(1)} %pair.3), channel_id=1, source_target_pairs={{0,2},{4,6},{10,8},{14,12},{1,3},{5,7},{11,9},{15,13},{16,18},{20,... | collective-permute-start | bytes 786440 | tf_op jit(solution)/shard_map/ppermute | solution.py:414
  56.8 32.2 %collective-permute-start.15 = (bf16[256,512]{1,0:T(8,128)(2,1)S(1)}, bf16[256,512]{1,0:T(8,128)(2,1)S(1)}, u32[]{:S(2)}, u32[]{:S(2)}) collective-permute-start(bf16[256,512]{1,0:T(8,128)(2,1)S(1)} %pair.3), channel_id=1, source_target_pairs={{2,8},{6,12},{8,2},{12,6},{3,9},{7,13},{9,3},{13,7},{18,24},{22,28... | collective-permute-start | bytes 786440 | tf_op jit(solution)/shard_map/ppermute | solution.py:413
  57.5 29.7 %collective-permute-start.7 = (bf16[512,128]{1,0:T(8,128)(2,1)S(1)}, bf16[512,128]{1,0:T(8,128)(2,1)S(1)}, u32[]{:S(2)}, u32[]{:S(2)}) collective-permute-start(bf16[512,128]{1,0:T(8,128)(2,1)S(1)} %get-tuple-element.34.refs_3_), channel_id=1, source_target_pairs={{0,8},{4,12},{8,0},{12,4},{1,9},{5,13},{9,1},{13,5},{2,10},{6,14},... | collective-permute-start | bytes 393224 | tf_op jit(solution)/shard_map/ppermute | solution.py:305
  61.2 26.0 %collective-permute-start.6 = (bf16[512,128]{1,0:T(8,128)(2,1)S(1)}, bf16[512,128]{1,0:T(8,128)(2,1)S(1)}, u32[]{:S(2)}, u32[]{:S(2)}) collective-permute-start(bf16[512,128]{1,0:T(8,128)(2,1)S(1)} %get-tuple-element.34.refs_3_), channel_id=1, source_target_pairs={{0,4},{4,8},{8,12},{12,0},{1,5},{5,9},{9,13},{13,1},{2,6},{6,10},{... | collective-permute-start | bytes 393224 | tf_op jit(solution)/shard_map/ppermute | solution.py:305
  (2 other events, 1.3 us)

commit v3 on v2

--- a/solution.py
+++ b/solution.py
@@ -11,6 +11,8 @@
 BLK = 256
 EPS = 1e-06
 LIMIT = 16 << 20
+SHORT = pl.CostEstimate(flops=1, bytes_accessed=1, transcendentals=0)
+LONG = pl.CostEstimate(flops=10**11, bytes_accessed=1, transcendentals=0)
 F32 = jnp.float32
 BF16 = jnp.bfloat16
 VM = pl.BlockSpec(memory_space=pltpu.VMEM)
@@ -46,7 +48,7 @@
         out_specs=[VM] * len(outs),
         name=name,
         compiler_params=pltpu.CompilerParams(vmem_limit_bytes=LIMIT),
-        cost_estimate=pl.CostEstimate(flops=flops, bytes_accessed=read + wrote, transcendentals=0),
+        cost_estimate=LONG if name in ("key", "numer") else SHORT,
     )(*ins)
 
 
@@ -83,16 +85,15 @@
         intra_ref[r, c] = mm(sc, v_ref[r, c], NN)
 
 
-def count(lay_ref, nsel, nb_all, h, i, b):
+def count(lay_ref, h, i, b):
     total = jnp.int32(0)
-    base = (h * nb_all + i) * nsel
-    for j in range(nsel):
-        total = total + jnp.where(lay_ref[base + j] == b, 1, 0)
+    for j in range(lay_ref.shape[2]):
+        total = total + jnp.where(lay_ref[h, i, j] == b, 1, 0)
     return total.astype(F32)
 
 
 def numer_body(dims, np_, *refs):
-    nb, heads, nb_all, nsel = dims
+    nb, heads = dims
     pos_ref, base_ref, lay_ref = refs[:3]
     parts = refs[3 : 3 + np_]
     qf_ref, intra_ref, carried_ref, num_ref, attn_ref = refs[3 + np_ :]
@@ -102,7 +103,7 @@
         total = jnp.zeros((DH, DH), F32)
         for s, part in enumerate(parts):
             for b in range(part.shape[0] // (heads * DH)):
-                times = count(lay_ref, nsel, nb_all, h, query_block, base_ref[s] + b)
+                times = count(lay_ref, h, query_block, base_ref[s] + b)
                 total = total + times * part[mat(b * heads + h), :].astype(F32)
         carried = total.astype(BF16)
         carried_ref[mat(i), :] = carried
@@ -112,14 +113,16 @@
         attn_ref[r, c] = (num * rinv).astype(BF16)
 
 
-def dnum_body(n_d, *refs):
+def dnum_body(n_d, pos_ref, *refs):
     d_refs = refs[:n_d]
     num_ref, qf_ref, dnum_ref, cg_ref = refs[n_d:]
+    heads = num_ref.shape[1] // DH
     for i, r, c in tiles(num_ref.shape[0], num_ref.shape[1] // DH):
         num = num_ref[r, c]
         grad = d_refs[0][r, c].astype(F32)
-        for d in d_refs[1:]:
-            grad = grad + d[r, c].astype(F32)
+        if n_d == 3:
+            same, sib = d_refs[1][r, :].astype(F32), d_refs[2][r, :].astype(F32)
+            grad = grad + jnp.where(pos_ref[3] == i % heads, same, sib)
         grad = grad.astype(BF16).astype(F32)
         rinv = lax.rsqrt(jnp.mean(num * num, axis=-1, keepdims=True) + EPS)
         lean = jnp.mean(grad * num, axis=-1, keepdims=True)
@@ -140,7 +143,7 @@
 
 
 def key_body(dims, np_, *refs):
-    nb, heads, nb_all, nsel = dims
+    nb, heads = dims
     pos_ref, base_ref, lay_ref = refs[:3]
     parts = refs[3 : 3 + np_]
     k_ref, kf_ref, v_ref, dkp_ref, dvp_ref, dk_ref, dv_ref = refs[3 + np_ :]
@@ -150,7 +153,7 @@
         total = jnp.zeros((DH, DH), F32)
         for s, part in enumerate(parts):
             for b in range(part.shape[0] // (heads * DH)):
-                times = count(lay_ref, nsel, nb_all, h, base_ref[s] + b, key_block)
+                times = count(lay_ref, h, base_ref[s] + b, key_block)
                 total = total + times * part[mat(b * heads + h), :].astype(F32)
         sg = total.astype(BF16)
         dk = mm(v_ref[r, c], sg, NT) + dkp_ref[r, c]
@@ -188,98 +191,25 @@
         ),
         name="own_partial",
         compiler_params=pltpu.CompilerParams(vmem_limit_bytes=LIMIT),
-        cost_estimate=pl.CostEstimate(
-            flops=2 * tokens * width * cols,
-            bytes_accessed=2 * tokens * width + 2 * width * cols + 4 * tokens * cols,
-            transcendentals=0,
-        ),
+        cost_estimate=SHORT,
     )(at, og, w)
 
 
-def other_body(at_ref, og_ref, first_ref, second_ref, out_ref, acc_ref):
-    @pl.when(pl.program_id(0) == 0)
-    def _():
-        acc_ref[...] = mm(og_ref[...], first_ref[...], NN)
-
-    @pl.when(pl.program_id(0) == 1)
-    def _():
-        out_ref[...] = (acc_ref[...] + mm(og_ref[...], second_ref[...], NN)).astype(BF16)
-
-
-def other_partial(at, og, first, second):
-    tokens, width = og.shape
-    half, cols = first.shape
-    return pl.pallas_call(
-        other_body,
-        out_shape=sds((tokens, cols), BF16),
-        grid_spec=pltpu.PrefetchScalarGridSpec(
-            num_scalar_prefetch=1,
-            grid=(2,),
-            in_specs=[
-                pl.BlockSpec((tokens, half), lambda g, at: (0, at[g])),
-                pl.BlockSpec((half, cols), lambda g, at: (0, 0)),
-                pl.BlockSpec((half, cols), lambda g, at: (0, 0)),
-            ],
-            out_specs=pl.BlockSpec((tokens, cols), lambda g, at: (0, 0)),
-            scratch_shapes=[pltpu.VMEM((tokens, cols), F32)],
-        ),
-        name="other_partial",
-        compiler_params=pltpu.CompilerParams(vmem_limit_bytes=LIMIT),
-        cost_estimate=pl.CostEstimate(
-            flops=2 * tokens * width * cols,
-            bytes_accessed=2 * tokens * width + 2 * width * cols + 2 * tokens * cols,
-            transcendentals=0,
-        ),
-    )(at, og, first, second)
-
-
-def wg_send_body(at_ref, attn_ref, og_ref, out_ref):
-    out_ref[...] = mm(attn_ref[...], og_ref[...], TN).astype(BF16)
-
-
-def wg_keep_body(at_ref, attn_ref, og_ref, got_ref, give_ref, keep_ref):
-    total = mm(attn_ref[...], og_ref[...], TN) + got_ref[...].astype(F32)
-
-    @pl.when(pl.program_id(0) == 0)
-    def _():
-        give_ref[...] = total.astype(BF16)
-
-    @pl.when(pl.program_id(0) == 1)
-    def _():
-        keep_ref[...] = total
-
-
-def weight_part(at, attn, og, got=None):
-    tokens, cols = attn.shape
-    rows = og.shape[1] // 4
-    whole = pl.BlockSpec((cols, rows), lambda g, at: (0, 0))
-    specs = [
-        pl.BlockSpec((tokens, cols), lambda g, at: (0, 0)),
-        pl.BlockSpec((tokens, rows), lambda g, at: (0, at[g])),
-    ]
-    if got is None:
-        body, args = wg_send_body, (at, attn, og)
-        outs = sds((2 * cols, rows), BF16)
-        out_specs = pl.BlockSpec((cols, rows), lambda g, at: (g, 0))
-    else:
-        body, args = wg_keep_body, (at, attn, og, got)
-        specs.append(pl.BlockSpec((cols, rows), lambda g, at: (g, 0)))
-        outs = (sds((cols, rows), BF16), sds((cols, rows), F32))
-        out_specs = (whole, whole)
-    return pl.pallas_call(
-        body,
-        out_shape=outs,
-        grid_spec=pltpu.PrefetchScalarGridSpec(
-            num_scalar_prefetch=1, grid=(2,), in_specs=specs, out_specs=out_specs
-        ),
-        name="weight_send" if got is None else "weight_keep",
-        compiler_params=pltpu.CompilerParams(vmem_limit_bytes=LIMIT),
-        cost_estimate=pl.CostEstimate(
-            flops=4 * tokens * rows * cols,
-            bytes_accessed=2 * tokens * (cols + 2 * rows) + 6 * cols * rows,
-            transcendentals=0,
-        ),
-    )(*args)
+def other_body(og_ref, og_sib_ref, w_ref, same_ref, sib_ref):
+    same_ref[...] = mm(og_ref[...], w_ref[...], NN).astype(BF16)
+    sib_ref[...] = mm(og_sib_ref[...], w_ref[...], NN).astype(BF16)
+
+
+def weight_body(pos_ref, attn_ref, attn_sib_ref, og_ref, og_sib_ref, give_ref, keep_ref):
+    rows = give_ref.shape[1]
+    parity, core = pos_ref[2], pos_ref[3]
+
+    def part(pair):
+        at = pl.ds(pl.multiple_of((2 * pair + core) * rows, rows), rows)
+        return mm(attn_ref[...], og_ref[:, at], TN) + mm(attn_sib_ref[...], og_sib_ref[:, at], TN)
+
+    give_ref[...] = part(1 - parity).astype(BF16)
+    keep_ref[...] = part(parity)
 
 
 def pair_body(keep_ref, got_ref, out_ref):
@@ -290,6 +220,10 @@
     mine = jnp.where(pos_ref[1] > 0, mine_ref[...].astype(F32), 0.0)
     total = mine + a_ref[...].astype(F32) + b_ref[...].astype(F32) + c_ref[...].astype(F32)
     out_ref[...] = total.T
+
+
+def after(x, *deps):
+    return lax.optimization_barrier((x, *deps))[0]
 
 
 def swap(x, axis):
@@ -313,15 +247,14 @@
     z = lax.axis_index("seq").astype(jnp.int32)
     x = lax.axis_index("head").astype(jnp.int32)
     core = lax.axis_index("dp").astype(jnp.int32)
-    heads, nb_all, nsel = layout.shape
+    heads = layout.shape[0]
     q, k, v, og = queries[0], key_rows[0], value_rows[0], out_grad[0]
     tokens, cols = q.shape
     nb = tokens // BLK
-    dims = (nb, heads, nb_all, nsel)
+    dims = (nb, heads)
     paired = seq_size == 4 and head_size == 2 and dp_size == 2
     home = (z // 2 == x).astype(jnp.int32)
-    pos = jnp.stack([z, home])
-    lay = layout.reshape(-1)
+    pos = jnp.stack([z, home, z % 2, core])
     if seq_size > 4:
         bases = jnp.zeros((1,), jnp.int32)
     else:
@@ -331,13 +264,13 @@
     mats = sds((nb * heads * DH, DH), BF16)
     unit = 2 * tokens * cols * DH
 
+    kf, st = call(states_body, (rows16, mats), (k, v), unit, "states")
+    parts = gather_parts(st, seq_size)
     if paired:
         width = og.shape[1]
-        half = width // 2
-        far = lax.dynamic_slice_in_dim(out_weight, (1 - x) * width + core * half, half, 0)
-        w_first = swap(far, "head")
-    kf, st = call(states_body, (rows16, mats), (k, v), unit, "states")
-    parts = gather_parts(st, seq_size)
+        og_sib = swap(og, "dp")
+        far = lax.dynamic_slice(after(out_weight, st), ((1 - x) * width, core * DH), (width, DH))
+        w_other = swap(far, "head")
     qf, sc, intra = call(
         scores_body,
         (rows16, sds((nb * heads * BLK, BLK), BF16), flat),
@@ -345,29 +278,37 @@
         4 * unit,
         "scores",
     )
-    if paired:
-        d_own = own_partial(x[None], og, out_weight)
-        w_second = swap(w_first, "dp")
-        d_other = other_partial(jnp.stack([core, 1 - core]), og, w_first, w_second)
-    else:
+    if not paired:
         og = lax.all_gather(og, "head", axis=1, tiled=True)
         d_own = jnp.dot(og, out_weight, preferred_element_type=F32)
     carried, num, attn = call(
         functools.partial(numer_body, dims, len(parts)),
         (mats, flat, rows16),
-        (pos, bases, lay, *parts, qf, intra),
+        (pos, bases, layout, *parts, qf, intra),
         unit,
         "numer",
     )
     if paired:
         attn_other = swap(attn, "head")
-        d_parts = (d_own, swap(d_other, "head"))
+        og_late, sib_late = lax.optimization_barrier((og, og_sib, attn))[:2]
+        d_own = own_partial(x[None], og_late, out_weight)
+        column = sds((tokens, DH), BF16)
+        d_same, d_sib = call(other_body, (column, column), (og_late, sib_late, w_other), 0, "other")
+        across = [(h * 2 + c, (1 - h) * 2 + 1 - c) for h in range(2) for c in range(2)]
+        d_same = swap(d_same, "head")
+        d_sib = lax.ppermute(d_sib, ("head", "dp"), across)
+        block = (cols, width // 4)
+        outs = (sds(block, BF16), sds(block, F32))
+        neighbours = [(0, 1), (1, 0), (2, 3), (3, 2)]
+        give_a, keep_a = call(weight_body, outs, (pos, attn, swap(attn, "dp"), og, og_sib), 0, "weight")
+        got_a = lax.ppermute(give_a, "seq", neighbours)
+        d_parts = (d_own, after(d_same, give_a), d_sib)
     else:
         d_parts = (d_own,)
     dnum, cg = call(
         functools.partial(dnum_body, len(d_parts)),
         (rows16, mats),
-        (*d_parts, num, qf),
+        (pos, *d_parts, num, qf),
         unit,
         "dnum",
     )
@@ -382,23 +323,18 @@
     dk, dv = call(
         functools.partial(key_body, dims, len(cparts)),
         (rows16, rows16),
-        (pos, bases, lay, *cparts, k, kf, v, dkp, dvp),
+        (pos, bases, layout, *cparts, k, kf, v, dkp, dvp),
         2 * unit,
         "key",
     )
     if paired:
-        parity = z % 2
-        order = jnp.stack([1 - parity, parity])
-        give_at = 2 * order + (1 - core)
-        keep_at = 2 * order + core
-        neighbours = [(0, 1), (1, 0), (2, 3), (3, 2)]
-        sums = []
-        for block in (attn, attn_other):
-            got = swap(weight_part(give_at, block, og), "dp")
-            give, keep = weight_part(keep_at, block, og, got)
-            got = lax.ppermute(give, "seq", neighbours)
-            sums.append(call(pair_body, (sds(keep.shape, BF16),), (keep, got), 0, "pair")[0])
-        mine, cross = sums
+        attn_other = after(attn_other, cg)
+        give_b, keep_b = call(
+            weight_body, outs, (pos, attn_other, swap(attn_other, "dp"), og, og_sib), 0, "weight"
+        )
+        got_b = lax.ppermute(give_b, "seq", neighbours)
+        (mine,) = call(pair_body, (sds(keep_a.shape, BF16),), (keep_a, got_a), 0, "pair")
+        (cross,) = call(pair_body, (sds(keep_b.shape, BF16),), (keep_b, got_b), 0, "pair")
         to_line, to_side, to_both = [], [], []
         for s in range(4):
             for h in range(2):

time: 91 us -> 81.7 us (0.90)
  the two profiles are of different devices: /device:TPU:0 before, /device:TPU:3 now
where the time goes in v3:
time: 81.7 us; the launch traced here: 81.3 us
  waiting for transfers between devices  34.5 us (42%)
  starting transfers between devices  22.1 us (27%)
  Pallas kernels  15.3 us (19%)
  local copies, waits for them, and re-layouts  8.42 us (10%)
  between operations  0.85 us (1%)
    ppermute x1, waiting for transfers between devices, per_device(): lax.ppermute(cross, axes, to_both)  16.3 us
    pallas_call x12, Pallas kernels, call(): pl.pallas_call(body, out_shape=outs, in_specs=[SM if a.dtype == jnp.int32...  13.8 us
    ppermute x6, starting transfers between devices, gather_parts(): parts.append(lax.ppermute(x, 'seq', pairs))  8.33 us
    ppermute x1, waiting for transfers between devices, per_device(): got_b = lax.ppermute(give_b, 'seq', neighbours)  7.05 us
    unnamed x31, local copies, waits for them, and re-layouts  6.52 us
    ppermute x6, waiting for transfers between devices, swap(): return lax.ppermute(x, axis, [(0, 1), (1, 0)])  6.4 us
    ppermute x6, starting transfers between devices, swap(): return lax.ppermute(x, axis, [(0, 1), (1, 0)])  3.72 us
    ppermute x1, starting transfers between devices, per_device(): lax.ppermute(mine, axes, to_line)  3.05 us
  transfers between devices with their start and end apart: 18, of which 8 were waited for; matrix products, arithmetic and copies ran while one was open for 3% of the time, Pallas kernels for 17%

profile of v3, /device:TPU:3, one launch (start us, length us, event | category | flops | bytes accessed | tf_op | source)
XLA Modules:
  0.0 81.3 jit_solution(14083233882781633531)
XLA Ops:
  0.6 0.9 %copy-done.2 = bf16[1,512,256]{2,1,0:T(8,128)(2,1)S(1)} copy-done((bf16[1,512,256]{2,1,0:T(8,128)(2,1)S(1)}, bf16[1,512,256]{2,1,0:T(8,128)(2,1)}, u32[]{:S(2)}) %copy-start.2) | copy-done | bytes 262168
  1.6 0.9 %copy-done.10 = bf16[1,512,256]{2,1,0:T(8,128)(2,1)S(1)} copy-done((bf16[1,512,256]{2,1,0:T(8,128)(2,1)S(1)}, bf16[1,512,256]{2,1,0:T(8,128)(2,1)}, u32[]{:S(2)}) %copy-start.10) | copy-done | bytes 262168
  2.9 1.3 %collective-permute-start = (bf16[512,128]{1,0:T(8,128)(2,1)S(1)}, bf16[512,128]{1,0:T(8,128)(2,1)S(1)}, u32[]{:S(2)}, u32[]{:S(2)}) collective-permute-start(bf16[512,128]{1,0:T(8,128)(2,1)S(1)} %get-tuple-element.31.refs_3_), channel_id=1, source_target_pairs={{0,4},{4,8},{8,12},{12,0},{1,5},{5,9},{9,13},{13,1},{2,6},{6,10},{... | collective-permute-start | bytes 393224 | tf_op jit(solution)/shard_map/ppermute | solution.py:239
  4.2 2.3 %collective-permute-start.1 = (bf16[512,128]{1,0:T(8,128)(2,1)S(1)}, bf16[512,128]{1,0:T(8,128)(2,1)S(1)}, u32[]{:S(2)}, u32[]{:S(2)}) collective-permute-start(bf16[512,128]{1,0:T(8,128)(2,1)S(1)} %get-tuple-element.31.refs_3_), channel_id=1, source_target_pairs={{0,8},{4,12},{8,0},{12,4},{1,9},{5,13},{9,1},{13,5},{2,10},{6,14},... | collective-permute-start | bytes 393224 | tf_op jit(solution)/shard_map/ppermute | solution.py:239
  6.6 1.1 %collective-permute-start.2 = (bf16[512,128]{1,0:T(8,128)(2,1)S(1)}, bf16[512,128]{1,0:T(8,128)(2,1)}, u32[]{:S(2)}, u32[]{:S(2)}) collective-permute-start(bf16[512,128]{1,0:T(8,128)(2,1)S(1)} %get-tuple-element.31.refs_3_), channel_id=1, source_target_pairs={{0,12},{4,0},{8,4},{12,8},{1,13},{5,1},{9,5},{13,9},{2,14},{6,2},{... | collective-permute-start | bytes 393224 | tf_op jit(solution)/shard_map/ppermute | solution.py:239
  7.6 1.5 %collective-permute-start.3 = (bf16[512,2048]{1,0:T(8,128)(2,1)}, bf16[512,2048]{1,0:T(8,128)(2,1)S(1)}, u32[]{:S(2)}, u32[]{:S(2)}) collective-permute-start(bf16[512,2048]{1,0:T(8,128)(2,1)} %bitcast.13), channel_id=1, source_target_pairs={{0,1},{1,0},{2,3},{3,2},{4,5},{5,4},{6,7},{7,6},{8,9},{9,8},{10,11... | collective-permute-start | bytes 6291464 | tf_op jit(solution)/shard_map/ppermute | solution.py:230
  9.1 1.9 %dynamic_slice.3 = bf16[2048,128]{1,0:T(8,128)(2,1)} dynamic-slice(bf16[4096,256]{1,0:T(8,128)(2,1)} %w_ref.1, s32[]{:T(128)S(6)} %select_n.26, s32[]{:T(128)S(6)} %select_n.27), dynamic_slice_sizes={2048,128} | dynamic-slice | bytes 1048580 | tf_op jit(solution)/shard_map/dynamic_slice | solution.py:272
  11.3 0.9 %copy-done.3 = bf16[1,512,256]{2,1,0:T(8,128)(2,1)S(1)} copy-done((bf16[1,512,256]{2,1,0:T(8,128)(2,1)S(1)}, bf16[1,512,256]{2,1,0:T(8,128)(2,1)}, u32[]{:S(2)}) %copy-start.3) | copy-done | bytes 262168
  12.3 0.9 %copy-done.5 = bf16[1,512,256]{2,1,0:T(8,128)(2,1)S(1)} copy-done((bf16[1,512,256]{2,1,0:T(8,128)(2,1)S(1)}, bf16[1,512,256]{2,1,0:T(8,128)(2,1)}, u32[]{:S(2)}) %copy-start.5) | copy-done | bytes 262168
  14.7 0.8 copy-done.12
  15.9 1.0 %copy-done.13 = f32[512,256]{1,0:T(8,128)S(1)} copy-done((f32[512,256]{1,0:T(8,128)S(1)}, f32[512,256]{1,0:T(8,128)}, u32[]{:S(2)}) %copy-start.13) | copy-done | bytes 524312
  16.9 2.3 %numer.1 = (bf16[512,128]{1,0:T(8,128)(2,1)S(1)}, f32[512,256]{1,0:T(8,128)S(1)}, bf16[512,256]{1,0:T(8,128)(2,1)}) custom-call(s32[4]{0:T(128)S(1)} %pad_add_fusion.refs_0_.pos_ref, s32[4]{0:T(128)S(1)} %fusion.refs_1_, s32[2,8,4]{2,1,0:T(8,128)S(1)} %copy.11.refs_2_, bf16[512,128]{1,0:T(8,128)(2,1)S(1)} %get-tuple-element.31.refs_3_, ...), custom_call_target="tpu_custom_call" | custom-call | flops 99999997952 | bytes 1 | tf_op jit(solution)/shard_map/numer/pallas_call | solution.py:44
  20.5 4.3 %collective-permute-done.4.w_ref = bf16[2048,128]{1,0:T(8,128)(2,1)S(1)} collective-permute-done((bf16[2048,128]{1,0:T(8,128)(2,1)}, bf16[2048,128]{1,0:T(8,128)(2,1)S(1)}, u32[]{:S(2)}, u32[]{:S(2)}) %collective-permute-start.4) | collective-permute-done | bytes 524320 | tf_op jit(solution)/shard_map/ppermute | solution.py:230
  24.8 1.2 %other.1 = (bf16[512,128]{1,0:T(8,128)(2,1)S(1)}, bf16[512,128]{1,0:T(8,128)(2,1)S(1)}) custom-call(bf16[512,2048]{1,0:T(8,128)(2,1)S(1)} %bitcast.14, bf16[512,2048]{1,0:T(8,128)(2,1)S(1)} %collective-permute-done.3.og_sib_ref, bf16[2048,128]{1,0:T(8,128)(2,1)S(1)} %collective-permute-done.4.w_ref), custom_call_target="tpu_custom_call" | custom-call | flops 1 | bytes 1 | tf_op jit(solution)/shard_map/other/pallas_call | solution.py:44
  26.4 2.5 %collective-permute-start.7 = (bf16[512,128]{1,0:T(8,128)(2,1)S(1)}, bf16[512,128]{1,0:T(8,128)(2,1)S(1)}, u32[]{:S(2)}, u32[]{:S(2)}) collective-permute-start(bf16[512,128]{1,0:T(8,128)(2,1)S(1)} %get-tuple-element.42), channel_id=1, source_target_pairs={{0,3},{1,2},{2,1},{3,0},{4,7},{5,6},{6,5},{7,4},{8,11},{9,10},{10,... | collective-permute-start | bytes 393224 | tf_op jit(solution)/shard_map/ppermute | solution.py:299
  28.9 1.6 %own_partial.1.refs_0_ = f32[512,256]{1,0:T(8,128)S(1)} custom-call(s32[1]{0:T(128)} %bitcast.8.at_ref, bf16[512,2048]{1,0:T(8,128)(2,1)S(1)} %bitcast.15, bf16[4096,256]{1,0:T(8,128)(2,1)S(1)} %copy-done.1), custom_call_target="tpu_custom_call" | custom-call | flops 1 | bytes 1 | tf_op jit(solution)/shard_map/own_partial/pallas_call | solution.py:180
  30.5 1.3 %weight.2 = (bf16[256,512]{1,0:T(8,128)(2,1)S(1)}, f32[256,512]{1,0:T(8,128)S(1)}) custom-call(s32[4]{0:T(128)S(1)} %pad_add_fusion.refs_0_.pos_ref, bf16[512,256]{1,0:T(8,128)(2,1)S(1)} %copy-done.9, bf16[512,256]{1,0:T(8,128)(2,1)S(1)} %collective-permute-done.6.attn_sib_ref, bf16[512,2048]{1,0:T(8,128)(2,1)S(1)} %bitcast.16, ...), custom_call_target="tpu_custom_call" | custom-call | flops 1 | bytes 1 | tf_op jit(solution)/shard_map/weight/pallas_call | solution.py:44
  31.8 1.4 %collective-permute-done.5.refs_1_ = bf16[512,128]{1,0:T(8,128)(2,1)S(1)} collective-permute-done((bf16[512,128]{1,0:T(8,128)(2,1)S(1)}, bf16[512,128]{1,0:T(8,128)(2,1)S(1)}, u32[]{:S(2)}, u32[]{:S(2)}) %collective-permute-start.5) | collective-permute-done | bytes 131104 | tf_op jit(solution)/shard_map/ppermute | solution.py:230
  33.2 2.9 %collective-permute-done.7.refs_2_ = bf16[512,128]{1,0:T(8,128)(2,1)S(1)} collective-permute-done((bf16[512,128]{1,0:T(8,128)(2,1)S(1)}, bf16[512,128]{1,0:T(8,128)(2,1)S(1)}, u32[]{:S(2)}, u32[]{:S(2)}) %collective-permute-start.7) | collective-permute-done | bytes 131104 | tf_op jit(solution)/shard_map/ppermute | solution.py:299
  36.1 1.1 %dnum.1 = (bf16[512,256]{1,0:T(8,128)(2,1)S(1)}, bf16[512,128]{1,0:T(8,128)(2,1)S(1)}) custom-call(s32[4]{0:T(128)S(1)} %pad_add_fusion.refs_0_.pos_ref, f32[512,256]{1,0:T(8,128)S(1)} %own_partial.1.refs_0_, bf16[512,128]{1,0:T(8,128)(2,1)S(1)} %collective-permute-done.5.refs_1_, bf16[512,128]{1,0:T(8,128)(2,1)S(1)} %collective-permute-done.7.refs_2_, ...), custom_call_target="tpu_custom_call" | custom-call | flops 1 | bytes 1 | tf_op jit(solution)/shard_map/dnum/pallas_call | solution.py:44
  38.9 1.3 %weight.3 = (bf16[256,512]{1,0:T(8,128)(2,1)S(1)}, f32[256,512]{1,0:T(8,128)S(1)}) custom-call(s32[4]{0:T(128)S(1)} %pad_add_fusion.refs_0_.pos_ref, bf16[512,256]{1,0:T(8,128)(2,1)S(1)} %collective-permute-done.13.attn_ref, bf16[512,256]{1,0:T(8,128)(2,1)S(1)} %collective-permute-done.14.attn_sib_ref, bf16[512,2048]{1,0:T(8,128)(2,1)S(1)} %bitcast.17, ...), custom_call_target="tpu_custom_call" | custom-call | flops 1 | bytes 1 | tf_op jit(solution)/shard_map/weight/pallas_call | solution.py:44
  40.9 0.9 %collective-permute-start.8 = (bf16[512,128]{1,0:T(8,128)(2,1)S(1)}, bf16[512,128]{1,0:T(8,128)(2,1)S(1)}, u32[]{:S(2)}, u32[]{:S(2)}) collective-permute-start(bf16[512,128]{1,0:T(8,128)(2,1)S(1)} %get-tuple-element.48.refs_3_), channel_id=1, source_target_pairs={{0,4},{4,8},{8,12},{12,0},{1,5},{5,9},{9,13},{13,1},{2,6},{6,10},{... | collective-permute-start | bytes 393224 | tf_op jit(solution)/shard_map/ppermute | solution.py:239
  42.4 2.1 %collective-permute-start.10 = (bf16[512,128]{1,0:T(8,128)(2,1)S(1)}, bf16[512,128]{1,0:T(8,128)(2,1)S(1)}, u32[]{:S(2)}, u32[]{:S(2)}) collective-permute-start(bf16[512,128]{1,0:T(8,128)(2,1)S(1)} %get-tuple-element.48.refs_3_), channel_id=1, source_target_pairs={{0,12},{4,0},{8,4},{12,8},{1,13},{5,1},{9,5},{13,9},{2,14},{6,2},{... | collective-permute-start | bytes 393224 | tf_op jit(solution)/shard_map/ppermute | solution.py:239
  44.5 2.0 %query.1 = (bf16[512,256]{1,0:T(8,128)(2,1)}, f32[512,256]{1,0:T(8,128)S(1)}, f32[512,256]{1,0:T(8,128)S(1)}) custom-call(bf16[512,256]{1,0:T(8,128)(2,1)S(1)} %bitcast.23, bf16[512,256]{1,0:T(8,128)(2,1)S(1)} %get-tuple-element.33.refs_7_.refs_4_.qf_ref, bf16[512,256]{1,0:T(8,128)(2,1)S(1)} %get-tuple-element.32.kf_ref.refs_8_, ...), custom_call_target="tpu_custom_call" | custom-call | flops 1 | bytes 1 | tf_op jit(solution)/shard_map/query/pallas_call | solution.py:44
  46.5 3.0 %collective-permute-start.12 = (bf16[256,512]{1,0:T(8,128)(2,1)S(1)}, bf16[256,512]{1,0:T(8,128)(2,1)S(1)}, u32[]{:S(2)}, u32[]{:S(2)}) collective-permute-start(bf16[256,512]{1,0:T(8,128)(2,1)S(1)} %pair.2.mine_ref), channel_id=1, source_target_pairs={{2,10},{6,14},{8,0},{12,4},{3,11},{7,15},{9,1},{13,5},{18,26},{22,... | collective-permute-start | bytes 786440 | tf_op jit(solution)/shard_map/ppermute | solution.py:348
  49.6 7.0 %collective-permute-done.15.got_ref = bf16[256,512]{1,0:T(8,128)(2,1)S(1)} collective-permute-done((bf16[256,512]{1,0:T(8,128)(2,1)S(1)}, bf16[256,512]{1,0:T(8,128)(2,1)S(1)}, u32[]{:S(2)}, u32[]{:S(2)}) %collective-permute-start.15) | collective-permute-done | bytes 262176 | tf_op jit(solution)/shard_map/ppermute | solution.py:335
  56.7 1.9 %collective-permute-start.16 = (bf16[256,512]{1,0:T(8,128)(2,1)S(1)}, bf16[256,512]{1,0:T(8,128)(2,1)S(1)}, u32[]{:S(2)}, u32[]{:S(2)}) collective-permute-start(bf16[256,512]{1,0:T(8,128)(2,1)S(1)} %pair.3), channel_id=1, source_target_pairs={{2,8},{6,12},{8,2},{12,6},{3,9},{7,13},{9,3},{13,7},{18,24},{22,28... | collective-permute-start | bytes 786440 | tf_op jit(solution)/shard_map/ppermute | solution.py:349
  58.6 1.3 %collective-permute-start.17 = (bf16[256,512]{1,0:T(8,128)(2,1)S(1)}, bf16[256,512]{1,0:T(8,128)(2,1)S(1)}, u32[]{:S(2)}, u32[]{:S(2)}) collective-permute-start(bf16[256,512]{1,0:T(8,128)(2,1)S(1)} %pair.3), channel_id=1, source_target_pairs={{0,2},{4,6},{10,8},{14,12},{1,3},{5,7},{11,9},{15,13},{16,18},{20,... | collective-permute-start | bytes 786440 | tf_op jit(solution)/shard_map/ppermute | solution.py:350
  59.9 1.9 %key.1 = (bf16[512,256]{1,0:T(8,128)(2,1)}, bf16[512,256]{1,0:T(8,128)(2,1)}) custom-call(s32[4]{0:T(128)S(1)} %pad_add_fusion.refs_0_.pos_ref, s32[4]{0:T(128)S(1)} %fusion.refs_1_, s32[2,8,4]{2,1,0:T(8,128)S(1)} %copy.11.refs_2_, bf16[512,128]{1,0:T(8,128)(2,1)S(1)} %get-tuple-element.48.refs_3_, bf16[512,128]{1,0:T(8,128)(2,1)S(1)} %collective-permute-done.8.refs_4_, ...), custom_call_target="tpu_custom_call" | custom-call | flops 99999997952 | bytes 1 | tf_op jit(solution)/shard_map/key/pallas_call | solution.py:44
  61.9 1.6 %collective-permute-done.12.a_ref = bf16[256,512]{1,0:T(8,128)(2,1)S(1)} collective-permute-done((bf16[256,512]{1,0:T(8,128)(2,1)S(1)}, bf16[256,512]{1,0:T(8,128)(2,1)S(1)}, u32[]{:S(2)}, u32[]{:S(2)}) %collective-permute-start.12) | collective-permute-done | bytes 262176 | tf_op jit(solution)/shard_map/ppermute | solution.py:348
  63.5 16.3 %collective-permute-done.16.b_ref = bf16[256,512]{1,0:T(8,128)(2,1)S(1)} collective-permute-done((bf16[256,512]{1,0:T(8,128)(2,1)S(1)}, bf16[256,512]{1,0:T(8,128)(2,1)S(1)}, u32[]{:S(2)}, u32[]{:S(2)}) %collective-permute-start.16) | collective-permute-done | bytes 262176 | tf_op jit(solution)/shard_map/ppermute | solution.py:349
  79.8 1.5 %final.1 = f32[512,256]{1,0:T(8,128)} custom-call(s32[4]{0:T(128)S(1)} %pad_add_fusion.refs_0_.pos_ref, bf16[256,512]{1,0:T(8,128)(2,1)S(1)} %pair.2.mine_ref, bf16[256,512]{1,0:T(8,128)(2,1)S(1)} %collective-permute-done.12.a_ref, bf16[256,512]{1,0:T(8,128)(2,1)S(1)} %collective-permute-done.16.b_ref, bf16[256,512]{1,0:T(8,128)(2,1)S(1)} %collective-permute-done.17.c_ref), custom_call_target="tpu_custom_call" | custom-call | flops 1 | bytes 1 | tf_op jit(solution)/shard_map/final/pallas_call | solution.py:44
  (51 shorter events, 7.1 us)
Async XLA Ops:
  0.6 1.0 %copy-start.2 = (bf16[1,512,256]{2,1,0:T(8,128)(2,1)S(1)}, bf16[1,512,256]{2,1,0:T(8,128)(2,1)}, u32[]{:S(2)}) copy-start(bf16[1,512,256]{2,1,0:T(8,128)(2,1)} %param.8) | copy-start | bytes 786436
  1.6 0.9 %copy-start.10 = (bf16[1,512,256]{2,1,0:T(8,128)(2,1)S(1)}, bf16[1,512,256]{2,1,0:T(8,128)(2,1)}, u32[]{:S(2)}) copy-start(bf16[1,512,256]{2,1,0:T(8,128)(2,1)} %param.7) | copy-start | bytes 786436
  2.5 12.9 %copy-start.14 = (s32[2,8,4]{1,2,0:T(4,128)S(1)}, s32[2,8,4]{1,2,0:T(4,128)}, u32[]{:S(2)}) copy-start(s32[2,8,4]{1,2,0:T(4,128)} %param.9) | copy-start | bytes 772
  2.9 12.7 %collective-permute-start = (bf16[512,128]{1,0:T(8,128)(2,1)S(1)}, bf16[512,128]{1,0:T(8,128)(2,1)S(1)}, u32[]{:S(2)}, u32[]{:S(2)}) collective-permute-start(bf16[512,128]{1,0:T(8,128)(2,1)S(1)} %get-tuple-element.31.refs_3_), channel_id=1, source_target_pairs={{0,4},{4,8},{8,12},{12,0},{1,5},{5,9},{9,13},{13,1},{2,6},{6,10},{... | collective-permute-start | bytes 393224 | tf_op jit(solution)/shard_map/ppermute | solution.py:239
  4.2 11.6 %collective-permute-start.1 = (bf16[512,128]{1,0:T(8,128)(2,1)S(1)}, bf16[512,128]{1,0:T(8,128)(2,1)S(1)}, u32[]{:S(2)}, u32[]{:S(2)}) collective-permute-start(bf16[512,128]{1,0:T(8,128)(2,1)S(1)} %get-tuple-element.31.refs_3_), channel_id=1, source_target_pairs={{0,8},{4,12},{8,0},{12,4},{1,9},{5,13},{9,1},{13,5},{2,10},{6,14},... | collective-permute-start | bytes 393224 | tf_op jit(solution)/shard_map/ppermute | solution.py:239
  6.6 9.3 %collective-permute-start.2 = (bf16[512,128]{1,0:T(8,128)(2,1)S(1)}, bf16[512,128]{1,0:T(8,128)(2,1)}, u32[]{:S(2)}, u32[]{:S(2)}) collective-permute-start(bf16[512,128]{1,0:T(8,128)(2,1)S(1)} %get-tuple-element.31.refs_3_), channel_id=1, source_target_pairs={{0,12},{4,0},{8,4},{12,8},{1,13},{5,1},{9,5},{13,9},{2,14},{6,2},{... | collective-permute-start | bytes 393224 | tf_op jit(solution)/shard_map/ppermute | solution.py:239
  7.6 12.8 %collective-permute-start.3 = (bf16[512,2048]{1,0:T(8,128)(2,1)}, bf16[512,2048]{1,0:T(8,128)(2,1)S(1)}, u32[]{:S(2)}, u32[]{:S(2)}) collective-permute-start(bf16[512,2048]{1,0:T(8,128)(2,1)} %bitcast.13), channel_id=1, source_target_pairs={{0,1},{1,0},{2,3},{3,2},{4,5},{5,4},{6,7},{7,6},{8,9},{9,8},{10,11... | collective-permute-start | bytes 6291464 | tf_op jit(solution)/shard_map/ppermute | solution.py:230
  11.0 13.8 %collective-permute-start.4 = (bf16[2048,128]{1,0:T(8,128)(2,1)}, bf16[2048,128]{1,0:T(8,128)(2,1)S(1)}, u32[]{:S(2)}, u32[]{:S(2)}) collective-permute-start(bf16[2048,128]{1,0:T(8,128)(2,1)} %dynamic_slice.3), channel_id=1, source_target_pairs={{0,2},{2,0},{1,3},{3,1},{4,6},{6,4},{5,7},{7,5},{8,10},{10,8},{9,1... | collective-permute-start | bytes 1572872 | tf_op jit(solution)/shard_map/ppermute | solution.py:230
  11.3 0.9 %copy-start.3 = (bf16[1,512,256]{2,1,0:T(8,128)(2,1)S(1)}, bf16[1,512,256]{2,1,0:T(8,128)(2,1)}, u32[]{:S(2)}) copy-start(bf16[1,512,256]{2,1,0:T(8,128)(2,1)} %param.8) | copy-start | bytes 786436
  12.3 0.9 %copy-start.5 = (bf16[1,512,256]{2,1,0:T(8,128)(2,1)S(1)}, bf16[1,512,256]{2,1,0:T(8,128)(2,1)}, u32[]{:S(2)}) copy-start(bf16[1,512,256]{2,1,0:T(8,128)(2,1)} %param.6) | copy-start | bytes 786436
  14.6 0.8 copy-start.12
  15.9 1.0 %copy-start.13 = (f32[512,256]{1,0:T(8,128)S(1)}, f32[512,256]{1,0:T(8,128)}, u32[]{:S(2)}) copy-start(f32[512,256]{1,0:T(8,128)} %copy-done.12) | copy-start | bytes 1572868
  16.9 7.9 %copy-start = (bf16[1,512,2048]{2,1,0:T(8,128)(2,1)S(1)}, bf16[1,512,2048]{2,1,0:T(8,128)(2,1)}, u32[]{:S(2)}) copy-start(bf16[1,512,2048]{2,1,0:T(8,128)(2,1)} %param.11) | copy-start | bytes 6291460
  19.2 9.7 %copy-start.1 = (bf16[4096,256]{1,0:T(8,128)(2,1)S(1)}, bf16[4096,256]{1,0:T(8,128)(2,1)}, u32[]{:S(2)}) copy-start(bf16[4096,256]{1,0:T(8,128)(2,1)} %w_ref.1) | copy-start | bytes 6291460
  19.2 11.3 %collective-permute-start.6 = (bf16[512,256]{1,0:T(8,128)(2,1)}, bf16[512,256]{1,0:T(8,128)(2,1)S(1)}, u32[]{:S(2)}, u32[]{:S(2)}) collective-permute-start(bf16[512,256]{1,0:T(8,128)(2,1)} %get-tuple-element.35.attn_ref), channel_id=1, source_target_pairs={{0,1},{1,0},{2,3},{3,2},{4,5},{5,4},{6,7},{7,6},{8,9},{9,8},{10,11... | collective-permute-start | bytes 786440 | tf_op jit(solution)/shard_map/ppermute | solution.py:230
  19.8 17.5 %collective-permute-start.13 = (bf16[512,256]{1,0:T(8,128)(2,1)}, bf16[512,256]{1,0:T(8,128)(2,1)S(1)}, u32[]{:S(2)}, u32[]{:S(2)}) collective-permute-start(bf16[512,256]{1,0:T(8,128)(2,1)} %get-tuple-element.35.attn_ref), channel_id=1, source_target_pairs={{0,2},{2,0},{1,3},{3,1},{4,6},{6,4},{5,7},{7,5},{8,10},{10,8},{9,1... | collective-permute-start | bytes 786440 | tf_op jit(solution)/shard_map/ppermute | solution.py:230
  26.1 7.2 %collective-permute-start.5 = (bf16[512,128]{1,0:T(8,128)(2,1)S(1)}, bf16[512,128]{1,0:T(8,128)(2,1)S(1)}, u32[]{:S(2)}, u32[]{:S(2)}) collective-permute-start(bf16[512,128]{1,0:T(8,128)(2,1)S(1)} %get-tuple-element.39), channel_id=1, source_target_pairs={{0,2},{2,0},{1,3},{3,1},{4,6},{6,4},{5,7},{7,5},{8,10},{10,8},{9,1... | collective-permute-start | bytes 393224 | tf_op jit(solution)/shard_map/ppermute | solution.py:230
  26.4 9.8 %collective-permute-start.7 = (bf16[512,128]{1,0:T(8,128)(2,1)S(1)}, bf16[512,128]{1,0:T(8,128)(2,1)S(1)}, u32[]{:S(2)}, u32[]{:S(2)}) collective-permute-start(bf16[512,128]{1,0:T(8,128)(2,1)S(1)} %get-tuple-element.42), channel_id=1, source_target_pairs={{0,3},{1,2},{2,1},{3,0},{4,7},{5,6},{6,5},{7,4},{8,11},{9,10},{10,... | collective-permute-start | bytes 393224 | tf_op jit(solution)/shard_map/ppermute | solution.py:299
  28.9 1.6 %copy-start.9 = (bf16[512,256]{1,0:T(8,128)(2,1)S(1)}, bf16[512,256]{1,0:T(8,128)(2,1)}, u32[]{:S(2)}) copy-start(bf16[512,256]{1,0:T(8,128)(2,1)} %get-tuple-element.35.attn_ref) | copy-start | bytes 786436
  37.3 7.2 %copy-start.4 = (bf16[1,512,256]{2,1,0:T(8,128)(2,1)S(1)}, bf16[1,512,256]{2,1,0:T(8,128)(2,1)}, u32[]{:S(2)}) copy-start(bf16[1,512,256]{2,1,0:T(8,128)(2,1)} %param.8) | copy-start | bytes 786436
  37.3 7.2 %copy-start.6 = (bf16[1,512,256]{2,1,0:T(8,128)(2,1)S(1)}, bf16[1,512,256]{2,1,0:T(8,128)(2,1)}, u32[]{:S(2)}) copy-start(bf16[1,512,256]{2,1,0:T(8,128)(2,1)} %param.6) | copy-start | bytes 786436
  37.3 7.2 %copy-start.8 = (bf16[1024,256]{1,0:T(8,128)(2,1)S(1)}, bf16[1024,256]{1,0:T(8,128)(2,1)}, u32[]{:S(2)}) copy-start(bf16[1024,256]{1,0:T(8,128)(2,1)} %copy-done.7) | copy-start | bytes 1572868
  37.3 1.6 %collective-permute-start.14 = (bf16[512,256]{1,0:T(8,128)(2,1)S(1)}, bf16[512,256]{1,0:T(8,128)(2,1)S(1)}, u32[]{:S(2)}, u32[]{:S(2)}) collective-permute-start(bf16[512,256]{1,0:T(8,128)(2,1)S(1)} %collective-permute-done.13.attn_ref), channel_id=1, source_target_pairs={{0,1},{1,0},{2,3},{3,2},{4,5},{5,4},{6,7},{7,6},{8,9},{9,8},{10,11... | collective-permute-start | bytes 786440 | tf_op jit(solution)/shard_map/ppermute | solution.py:230
  37.7 8.8 %collective-permute-start.11 = (bf16[256,512]{1,0:T(8,128)(2,1)S(1)}, bf16[256,512]{1,0:T(8,128)(2,1)S(1)}, u32[]{:S(2)}, u32[]{:S(2)}) collective-permute-start(bf16[256,512]{1,0:T(8,128)(2,1)S(1)} %get-tuple-element.40), channel_id=1, source_target_pairs={{0,4},{4,0},{8,12},{12,8},{1,5},{5,1},{9,13},{13,9},{2,6},{6,2},{1... | collective-permute-start | bytes 786440 | tf_op jit(solution)/shard_map/ppermute | solution.py:304
  40.2 19.7 %copy-start.11 = (bf16[1,512,256]{2,1,0:T(8,128)(2,1)S(1)}, bf16[1,512,256]{2,1,0:T(8,128)(2,1)}, u32[]{:S(2)}) copy-start(bf16[1,512,256]{2,1,0:T(8,128)(2,1)} %param.7) | copy-start | bytes 786436
  40.2 16.4 %collective-permute-start.15 = (bf16[256,512]{1,0:T(8,128)(2,1)S(1)}, bf16[256,512]{1,0:T(8,128)(2,1)S(1)}, u32[]{:S(2)}, u32[]{:S(2)}) collective-permute-start(bf16[256,512]{1,0:T(8,128)(2,1)S(1)} %get-tuple-element.56), channel_id=1, source_target_pairs={{0,4},{4,0},{8,12},{12,8},{1,5},{5,1},{9,13},{13,9},{2,6},{6,2},{1... | collective-permute-start | bytes 786440 | tf_op jit(solution)/shard_map/ppermute | solution.py:335
  40.9 17.7 %collective-permute-start.8 = (bf16[512,128]{1,0:T(8,128)(2,1)S(1)}, bf16[512,128]{1,0:T(8,128)(2,1)S(1)}, u32[]{:S(2)}, u32[]{:S(2)}) collective-permute-start(bf16[512,128]{1,0:T(8,128)(2,1)S(1)} %get-tuple-element.48.refs_3_), channel_id=1, source_target_pairs={{0,4},{4,8},{8,12},{12,0},{1,5},{5,9},{9,13},{13,1},{2,6},{6,10},{... | collective-permute-start | bytes 393224 | tf_op jit(solution)/shard_map/ppermute | solution.py:239
  41.8 18.1 %collective-permute-start.9 = (bf16[512,128]{1,0:T(8,128)(2,1)S(1)}, bf16[512,128]{1,0:T(8,128)(2,1)S(1)}, u32[]{:S(2)}, u32[]{:S(2)}) collective-permute-start(bf16[512,128]{1,0:T(8,128)(2,1)S(1)} %get-tuple-element.48.refs_3_), channel_id=1, source_target_pairs={{0,8},{4,12},{8,0},{12,4},{1,9},{5,13},{9,1},{13,5},{2,10},{6,14},... | collective-permute-start | bytes 393224 | tf_op jit(solution)/shard_map/ppermute | solution.py:239
  42.4 17.6 %collective-permute-start.10 = (bf16[512,128]{1,0:T(8,128)(2,1)S(1)}, bf16[512,128]{1,0:T(8,128)(2,1)S(1)}, u32[]{:S(2)}, u32[]{:S(2)}) collective-permute-start(bf16[512,128]{1,0:T(8,128)(2,1)S(1)} %get-tuple-element.48.refs_3_), channel_id=1, source_target_pairs={{0,12},{4,0},{8,4},{12,8},{1,13},{5,1},{9,5},{13,9},{2,14},{6,2},{... | collective-permute-start | bytes 393224 | tf_op jit(solution)/shard_map/ppermute | solution.py:239
  46.5 17.0 %collective-permute-start.12 = (bf16[256,512]{1,0:T(8,128)(2,1)S(1)}, bf16[256,512]{1,0:T(8,128)(2,1)S(1)}, u32[]{:S(2)}, u32[]{:S(2)}) collective-permute-start(bf16[256,512]{1,0:T(8,128)(2,1)S(1)} %pair.2.mine_ref), channel_id=1, source_target_pairs={{2,10},{6,14},{8,0},{12,4},{3,11},{7,15},{9,1},{13,5},{18,26},{22,... | collective-permute-start | bytes 786440 | tf_op jit(solution)/shard_map/ppermute | solution.py:348
  56.7 23.1 %collective-permute-start.16 = (bf16[256,512]{1,0:T(8,128)(2,1)S(1)}, bf16[256,512]{1,0:T(8,128)(2,1)S(1)}, u32[]{:S(2)}, u32[]{:S(2)}) collective-permute-start(bf16[256,512]{1,0:T(8,128)(2,1)S(1)} %pair.3), channel_id=1, source_target_pairs={{2,8},{6,12},{8,2},{12,6},{3,9},{7,13},{9,3},{13,7},{18,24},{22,28... | collective-permute-start | bytes 786440 | tf_op jit(solution)/shard_map/ppermute | solution.py:349
  58.6 21.2 %collective-permute-start.17 = (bf16[256,512]{1,0:T(8,128)(2,1)S(1)}, bf16[256,512]{1,0:T(8,128)(2,1)S(1)}, u32[]{:S(2)}, u32[]{:S(2)}) collective-permute-start(bf16[256,512]{1,0:T(8,128)(2,1)S(1)} %pair.3), channel_id=1, source_target_pairs={{0,2},{4,6},{10,8},{14,12},{1,3},{5,7},{11,9},{15,13},{16,18},{20,... | collective-permute-start | bytes 786440 | tf_op jit(solution)/shard_map/ppermute | solution.py:350
  (1 other events, 0.8 us)

commit v4 on v3

--- a/solution.py
+++ b/solution.py
@@ -48,7 +48,7 @@
         out_specs=[VM] * len(outs),
         name=name,
         compiler_params=pltpu.CompilerParams(vmem_limit_bytes=LIMIT),
-        cost_estimate=LONG if name in ("key", "numer") else SHORT,
+        cost_estimate=LONG if name in ("query", "dnum", "numer") else SHORT,
     )(*ins)
 
 
@@ -67,6 +67,44 @@
         kf = feature(k_ref[r, c].astype(F32)).astype(BF16)
         kf_ref[r, c] = kf
         st_ref[mat(i), :] = mm(kf, v_ref[r, c], TN).astype(BF16)
+
+
+def begin_body(at_ref, k_ref, v_ref, w_ref, kf_ref, st_ref, far_ref):
+    far_ref[...] = w_ref[...]
+    states_body(k_ref, v_ref, kf_ref, st_ref)
+
+
+def begin(at, k, v, w, width):
+    tokens, cols = k.shape
+    count = tokens // BLK * (cols // DH)
+    whole = pl.BlockSpec((tokens, cols), lambda g, at: (0, 0))
+    return pl.pallas_call(
+        begin_body,
+        out_shape=(
+            sds((tokens, cols), BF16),
+            sds((count * DH, DH), BF16),
+            sds((width, DH), BF16),
+        ),
+        grid_spec=pltpu.PrefetchScalarGridSpec(
+            num_scalar_prefetch=1,
+            grid=(1,),
+            in_specs=[whole, whole, pl.BlockSpec((width, DH), lambda g, at: (at[0], at[1]))],
+            out_specs=[
+                whole,
+                pl.BlockSpec((count * DH, DH), lambda g, at: (0, 0)),
+                pl.BlockSpec((width, DH), lambda g, at: (0, 0)),
+            ],
+        ),
+        name="begin",
+        compiler_params=pltpu.CompilerParams(vmem_limit_bytes=56 << 20),
+        cost_estimate=SHORT,
+    )(at, k, v, w)
+
+
+def split_body(x_ref, *outs):
+    rows = outs[0].shape[0]
+    for i, out in enumerate(outs):
+        out[...] = x_ref[i * rows : (i + 1) * rows, :]
 
 
 def causal():
@@ -200,13 +238,18 @@
     sib_ref[...] = mm(og_sib_ref[...], w_ref[...], NN).astype(BF16)
 
 
-def weight_body(pos_ref, attn_ref, attn_sib_ref, og_ref, og_sib_ref, give_ref, keep_ref):
+def weight_body(pos_ref, attn_ref, og_ref, og_sib_ref, *refs):
+    *sib_refs, give_ref, keep_ref = refs
+    step = sib_refs[0].shape[0]
     rows = give_ref.shape[1]
     parity, core = pos_ref[2], pos_ref[3]
 
     def part(pair):
         at = pl.ds(pl.multiple_of((2 * pair + core) * rows, rows), rows)
-        return mm(attn_ref[...], og_ref[:, at], TN) + mm(attn_sib_ref[...], og_sib_ref[:, at], TN)
+        total = mm(attn_ref[...], og_ref[:, at], TN)
+        for i, sib in enumerate(sib_refs):
+            total = total + mm(sib[...], og_sib_ref[i * step : (i + 1) * step, at], TN)
+        return total
 
     give_ref[...] = part(1 - parity).astype(BF16)
     keep_ref[...] = part(parity)
@@ -264,13 +307,14 @@
     mats = sds((nb * heads * DH, DH), BF16)
     unit = 2 * tokens * cols * DH
 
-    kf, st = call(states_body, (rows16, mats), (k, v), unit, "states")
-    parts = gather_parts(st, seq_size)
     if paired:
         width = og.shape[1]
+        kf, st, far = begin(jnp.stack([1 - x, core]), k, v, out_weight, width)
+        w_other = swap(far, "head")
         og_sib = swap(og, "dp")
-        far = lax.dynamic_slice(after(out_weight, st), ((1 - x) * width, core * DH), (width, DH))
-        w_other = swap(far, "head")
+    else:
+        kf, st = call(states_body, (rows16, mats), (k, v), unit, "states")
+    parts = gather_parts(st, seq_size)
     qf, sc, intra = call(
         scores_body,
         (rows16, sds((nb * heads * BLK, BLK), BF16), flat),
@@ -290,19 +334,29 @@
     )
     if paired:
         attn_other = swap(attn, "head")
-        og_late, sib_late = lax.optimization_barrier((og, og_sib, attn))[:2]
-        d_own = own_partial(x[None], og_late, out_weight)
         column = sds((tokens, DH), BF16)
-        d_same, d_sib = call(other_body, (column, column), (og_late, sib_late, w_other), 0, "other")
+        sib_late = after(og_sib, attn)
+        d_same, d_sib = call(other_body, (column, column), (og, sib_late, w_other), 0, "other")
         across = [(h * 2 + c, (1 - h) * 2 + 1 - c) for h in range(2) for c in range(2)]
+        d_sib_sent = d_sib
         d_same = swap(d_same, "head")
         d_sib = lax.ppermute(d_sib, ("head", "dp"), across)
         block = (cols, width // 4)
         outs = (sds(block, BF16), sds(block, F32))
         neighbours = [(0, 1), (1, 0), (2, 3), (3, 2)]
-        give_a, keep_a = call(weight_body, outs, (pos, attn, swap(attn, "dp"), og, og_sib), 0, "weight")
+        give_a, keep_a = call(weight_body, outs, (pos, attn, og, og_sib, swap(attn, "dp")), 0, "weight")
         got_a = lax.ppermute(give_a, "seq", neighbours)
-        d_parts = (d_own, after(d_same, give_a), d_sib)
+        attn_other = after(attn_other, give_a, d_sib_sent)
+        quarter = sds((tokens // 4, cols), BF16)
+        pieces = call(split_body, (quarter,) * 4, (attn_other,), 0, "split")
+        pieces = [swap(piece, "dp") for piece in pieces]
+        give_b, keep_b = call(
+            weight_body, outs, (pos, attn_other, og, og_sib, *pieces), 0, "weight"
+        )
+        got_b = lax.ppermute(give_b, "seq", neighbours)
+        d_own = own_partial(x[None], after(og, give_b), out_weight)
+        (mine,) = call(pair_body, (sds(keep_a.shape, BF16),), (keep_a, got_a), 0, "pair")
+        d_parts = (d_own, after(d_same, give_b, mine), d_sib)
     else:
         d_parts = (d_own,)
     dnum, cg = call(
@@ -312,7 +366,13 @@
         unit,
         "dnum",
     )
-    cparts = gather_parts(cg, seq_size)
+    if paired:
+        two = lax.ppermute(cg, "seq", [(i, i ^ 2) for i in range(4)])
+        one = lax.ppermute(cg, "seq", neighbours)
+        cparts = [cg, one, two, lax.ppermute(after(two, one), "seq", neighbours)]
+        cbases = (z ^ jnp.arange(4, dtype=jnp.int32)) * nb
+    else:
+        cparts, cbases = gather_parts(cg, seq_size), bases
     dq, dkp, dvp = call(
         query_body,
         (rows16, flat, flat),
@@ -323,17 +383,11 @@
     dk, dv = call(
         functools.partial(key_body, dims, len(cparts)),
         (rows16, rows16),
-        (pos, bases, layout, *cparts, k, kf, v, dkp, dvp),
+        (pos, cbases, layout, *cparts, k, kf, v, dkp, dvp),
         2 * unit,
         "key",
     )
     if paired:
-        attn_other = after(attn_other, cg)
-        give_b, keep_b = call(
-            weight_body, outs, (pos, attn_other, swap(attn_other, "dp"), og, og_sib), 0, "weight"
-        )
-        got_b = lax.ppermute(give_b, "seq", neighbours)
-        (mine,) = call(pair_body, (sds(keep_a.shape, BF16),), (keep_a, got_a), 0, "pair")
         (cross,) = call(pair_body, (sds(keep_b.shape, BF16),), (keep_b, got_b), 0, "pair")
         to_line, to_side, to_both = [], [], []
         for s in range(4):

time: 81.7 us -> 77.2 us (0.945)
  the two profiles are of different devices: /device:TPU:3 before, /device:TPU:24 now
where the time goes in v4:
time: 77.2 us; the launch traced here: 76.7 us
  starting transfers between devices  26.4 us (34%)
  Pallas kernels  22.1 us (29%)
  waiting for transfers between devices  21.1 us (27%)
  local copies, waits for them, and re-layouts  5.58 us (7%)
  between operations  0.89 us (1%)
    pallas_call x12, Pallas kernels, call(): pl.pallas_call(body, out_shape=outs, in_specs=[SM if a.dtype == jnp.int32...  17.3 us
    ppermute x1, waiting for transfers between devices, per_device(): lax.ppermute(cross, axes, to_both)  7.83 us
    ppermute x1, waiting for transfers between devices, per_device(): cparts = [cg, one, two, lax.ppermute(after(two, one), 'seq', neighbours)]  7.09 us
    ppermute x9, starting transfers between devices, swap(): return lax.ppermute(x, axis, [(0, 1), (1, 0)])  5.77 us
    unnamed x29, local copies, waits for them, and re-layouts  5.58 us
    ppermute x1, starting transfers between devices, per_device(): lax.ppermute(mine, axes, to_line)  4.52 us
    ppermute x3, waiting for transfers between devices, gather_parts(): parts.append(lax.ppermute(x, 'seq', pairs))  4.35 us
    ppermute x3, starting transfers between devices, gather_parts(): parts.append(lax.ppermute(x, 'seq', pairs))  3.83 us
  transfers between devices with their start and end apart: 21, of which 7 were waited for; matrix products, arithmetic and copies ran while one was open for 0% of the time, Pallas kernels for 23%

profile of v4, /device:TPU:24, one launch (start us, length us, event | category | flops | bytes accessed | tf_op | source)
XLA Modules:
  0.0 76.7 jit_solution(13348250330027062409)
XLA Ops:
  1.3 3.2 %begin.1 = (bf16[512,256]{1,0:T(8,128)(2,1)}, bf16[512,128]{1,0:T(8,128)(2,1)}, bf16[2048,128]{1,0:T(8,128)(2,1)}) custom-call(s32[2]{0:T(128)} %pad_add_fusion.1.at_ref, bf16[512,256]{1,0:T(8,128)(2,1)} %bitcast.23, bf16[512,256]{1,0:T(8,128)(2,1)} %bitcast.19, bf16[4096,256]{1,0:T(8,128)(2,1)} %w_ref.3), custom_call_target="tpu_custom_call" | custom-call | flops 1 | bytes 1 | tf_op jit(solution)/shard_map/begin/pallas_call | solution.py:81
  4.9 3.4 %collective-permute-start = (bf16[512,128]{1,0:T(8,128)(2,1)}, bf16[512,128]{1,0:T(8,128)(2,1)}, u32[]{:S(2)}, u32[]{:S(2)}) collective-permute-start(bf16[512,128]{1,0:T(8,128)(2,1)} %get-tuple-element.36.refs_3_), channel_id=1, source_target_pairs={{0,4},{4,8},{8,12},{12,0},{1,5},{5,9},{9,13},{13,1},{2,6},{6,10},{... | collective-permute-start | bytes 393224 | tf_op jit(solution)/shard_map/ppermute | solution.py:282
  8.3 1.5 %collective-permute-start.6 = (bf16[2048,128]{1,0:T(8,128)(2,1)}, bf16[2048,128]{1,0:T(8,128)(2,1)S(1)}, u32[]{:S(2)}, u32[]{:S(2)}) collective-permute-start(bf16[2048,128]{1,0:T(8,128)(2,1)} %get-tuple-element.43), channel_id=1, source_target_pairs={{0,2},{2,0},{1,3},{3,1},{4,6},{6,4},{5,7},{7,5},{8,10},{10,8},{9,1... | collective-permute-start | bytes 1572872 | tf_op jit(solution)/shard_map/ppermute | solution.py:273
  9.8 0.9 %copy-done.3 = bf16[512,256]{1,0:T(8,128)(2,1)S(1)} copy-done((bf16[512,256]{1,0:T(8,128)(2,1)S(1)}, bf16[512,256]{1,0:T(8,128)(2,1)}, u32[]{:S(2)}) %copy-start.3) | copy-done | bytes 262168
  10.8 0.7 scores.1
  11.4 0.8 %copy-done.8 = bf16[1024,256]{1,0:T(8,128)(2,1)} copy-done((bf16[1024,256]{1,0:T(8,128)(2,1)}, bf16[1024,256]{1,0:T(8,128)(2,1)S(1)}, u32[]{:S(2)}) %copy-start.8) | copy-done | bytes 524312
  12.2 0.8 %copy-done.10 = f32[512,256]{1,0:T(8,128)} copy-done((f32[512,256]{1,0:T(8,128)}, f32[512,256]{1,0:T(8,128)S(1)}, u32[]{:S(2)}) %copy-start.10) | copy-done | bytes 524312
  13.2 4.3 %collective-permute-done.1.refs_5_ = bf16[512,128]{1,0:T(8,128)(2,1)} collective-permute-done((bf16[512,128]{1,0:T(8,128)(2,1)}, bf16[512,128]{1,0:T(8,128)(2,1)}, u32[]{:S(2)}, u32[]{:S(2)}) %collective-permute-start.1) | collective-permute-done | bytes 131104 | tf_op jit(solution)/shard_map/ppermute | solution.py:282
  17.6 1.0 %copy-done.11 = f32[512,256]{1,0:T(8,128)S(1)} copy-done((f32[512,256]{1,0:T(8,128)S(1)}, f32[512,256]{1,0:T(8,128)}, u32[]{:S(2)}) %copy-start.11) | copy-done | bytes 524312
  18.6 0.9 %copy-done.12 = bf16[512,128]{1,0:T(8,128)(2,1)S(1)} copy-done((bf16[512,128]{1,0:T(8,128)(2,1)S(1)}, bf16[512,128]{1,0:T(8,128)(2,1)}, u32[]{:S(2)}) %copy-start.12) | copy-done | bytes 131096
  19.5 2.2 %numer.1 = (bf16[512,128]{1,0:T(8,128)(2,1)S(1)}, f32[512,256]{1,0:T(8,128)S(1)}, bf16[512,256]{1,0:T(8,128)(2,1)}) custom-call(s32[4]{0:T(128)S(1)} %pad_add_fusion.refs_0_.pos_ref, s32[4]{0:T(128)S(1)} %fusion.refs_1_, s32[2,8,4]{2,1,0:T(8,128)S(1)} %copy.11.refs_2_, bf16[512,128]{1,0:T(8,128)(2,1)S(1)} %copy-done.12, ...), custom_call_target="tpu_custom_call" | custom-call | flops 99999997952 | bytes 1 | tf_op jit(solution)/shard_map/numer/pallas_call | solution.py:44
  21.7 1.5 %collective-permute-start.3 = (bf16[512,256]{1,0:T(8,128)(2,1)}, bf16[512,256]{1,0:T(8,128)(2,1)S(1)}, u32[]{:S(2)}, u32[]{:S(2)}) collective-permute-start(bf16[512,256]{1,0:T(8,128)(2,1)} %get-tuple-element.40.attn_ref), channel_id=1, source_target_pairs={{0,2},{2,0},{1,3},{3,1},{4,6},{6,4},{5,7},{7,5},{8,10},{10,8},{9,1... | collective-permute-start | bytes 786440 | tf_op jit(solution)/shard_map/ppermute | solution.py:273
  23.5 0.9 %copy-done.7 = bf16[512,256]{1,0:T(8,128)(2,1)S(1)} copy-done((bf16[512,256]{1,0:T(8,128)(2,1)S(1)}, bf16[512,256]{1,0:T(8,128)(2,1)}, u32[]{:S(2)}) %copy-start.7) | copy-done | bytes 262168
  24.4 2.3 %weight.2 = (bf16[256,512]{1,0:T(8,128)(2,1)S(1)}, f32[256,512]{1,0:T(8,128)S(1)}) custom-call(s32[4]{0:T(128)S(1)} %pad_add_fusion.refs_0_.pos_ref, bf16[512,256]{1,0:T(8,128)(2,1)S(1)} %copy-done.7, bf16[512,2048]{1,0:T(8,128)(2,1)S(1)} %bitcast.15, bf16[512,2048]{1,0:T(8,128)(2,1)} %collective-permute-done.4.og_sib_ref, ...), custom_call_target="tpu_custom_call" | custom-call | flops 1 | bytes 1 | tf_op jit(solution)/shard_map/weight/pallas_call | solution.py:44
  26.8 2.6 %collective-permute-start.12 = (bf16[256,512]{1,0:T(8,128)(2,1)S(1)}, bf16[256,512]{1,0:T(8,128)(2,1)S(1)}, u32[]{:S(2)}, u32[]{:S(2)}) collective-permute-start(bf16[256,512]{1,0:T(8,128)(2,1)S(1)} %get-tuple-element.41), channel_id=1, source_target_pairs={{0,4},{4,0},{8,12},{12,8},{1,5},{5,1},{9,13},{13,9},{2,6},{6,2},{1... | collective-permute-start | bytes 786440 | tf_op jit(solution)/shard_map/ppermute | solution.py:348
  29.3 2.8 %other.1 = (bf16[512,128]{1,0:T(8,128)(2,1)S(1)}, bf16[512,128]{1,0:T(8,128)(2,1)S(1)}) custom-call(bf16[512,2048]{1,0:T(8,128)(2,1)S(1)} %bitcast.16, bf16[512,2048]{1,0:T(8,128)(2,1)} %collective-permute-done.4.og_sib_ref, bf16[2048,128]{1,0:T(8,128)(2,1)S(1)} %collective-permute-done.6.w_ref), custom_call_target="tpu_custom_call" | custom-call | flops 1 | bytes 1 | tf_op jit(solution)/shard_map/other/pallas_call | solution.py:44
  32.8 1.5 %collective-permute-start.11 = (bf16[512,128]{1,0:T(8,128)(2,1)S(1)}, bf16[512,128]{1,0:T(8,128)(2,1)S(1)}, u32[]{:S(2)}, u32[]{:S(2)}) collective-permute-start(bf16[512,128]{1,0:T(8,128)(2,1)S(1)} %get-tuple-element.52), channel_id=1, source_target_pairs={{0,2},{2,0},{1,3},{3,1},{4,6},{6,4},{5,7},{7,5},{8,10},{10,8},{9,1... | collective-permute-start | bytes 393224 | tf_op jit(solution)/shard_map/ppermute | solution.py:273
  35.0 0.8 %collective-permute-done.9.refs_2_ = bf16[128,256]{1,0:T(8,128)(2,1)S(1)} collective-permute-done((bf16[128,256]{1,0:T(8,128)(2,1)S(1)}, bf16[128,256]{1,0:T(8,128)(2,1)S(1)}, u32[]{:S(2)}, u32[]{:S(2)}) %collective-permute-start.9) | collective-permute-done | bytes 65568 | tf_op jit(solution)/shard_map/ppermute | solution.py:273
  36.2 2.6 %weight.3 = (bf16[256,512]{1,0:T(8,128)(2,1)S(1)}, f32[256,512]{1,0:T(8,128)S(1)}) custom-call(s32[4]{0:T(128)S(1)} %pad_add_fusion.refs_0_.pos_ref, bf16[512,256]{1,0:T(8,128)(2,1)S(1)} %collective-permute-done.3.x_ref.attn_ref, bf16[512,2048]{1,0:T(8,128)(2,1)S(1)} %bitcast.17, bf16[512,2048]{1,0:T(8,128)(2,1)} %collective-permute-done.4.og_sib_ref, ...), custom_call_target="tpu_custom_call" | custom-call | flops 1 | bytes 1 | tf_op jit(solution)/shard_map/weight/pallas_call | solution.py:44
  38.8 1.0 %collective-permute-start.18 = (bf16[256,512]{1,0:T(8,128)(2,1)S(1)}, bf16[256,512]{1,0:T(8,128)(2,1)S(1)}, u32[]{:S(2)}, u32[]{:S(2)}) collective-permute-start(bf16[256,512]{1,0:T(8,128)(2,1)S(1)} %get-tuple-element.50), channel_id=1, source_target_pairs={{0,4},{4,0},{8,12},{12,8},{1,5},{5,1},{9,13},{13,9},{2,6},{6,2},{1... | collective-permute-start | bytes 786440 | tf_op jit(solution)/shard_map/ppermute | solution.py:356
  39.8 1.6 %own_partial.1.refs_0_ = f32[512,256]{1,0:T(8,128)S(1)} custom-call(s32[1]{0:T(128)} %bitcast.9.at_ref, bf16[512,2048]{1,0:T(8,128)(2,1)S(1)} %bitcast.18, bf16[4096,256]{1,0:T(8,128)(2,1)S(1)} %copy-done.1), custom_call_target="tpu_custom_call" | custom-call | flops 1 | bytes 1 | tf_op jit(solution)/shard_map/own_partial/pallas_call | solution.py:218
  41.5 1.1 %dnum.1 = (bf16[512,256]{1,0:T(8,128)(2,1)S(1)}, bf16[512,128]{1,0:T(8,128)(2,1)S(1)}) custom-call(s32[4]{0:T(128)S(1)} %pad_add_fusion.refs_0_.pos_ref, f32[512,256]{1,0:T(8,128)S(1)} %own_partial.1.refs_0_, bf16[512,128]{1,0:T(8,128)(2,1)S(1)} %collective-permute-done.11.refs_1_, bf16[512,128]{1,0:T(8,128)(2,1)S(1)} %collective-permute-done.13.refs_2_, ...), custom_call_target="tpu_custom_call" | custom-call | flops 99999997952 | bytes 1 | tf_op jit(solution)/shard_map/dnum/pallas_call | solution.py:44
  43.0 1.1 %collective-permute-start.14 = (bf16[512,128]{1,0:T(8,128)(2,1)S(1)}, bf16[512,128]{1,0:T(8,128)(2,1)S(1)}, u32[]{:S(2)}, u32[]{:S(2)}) collective-permute-start(bf16[512,128]{1,0:T(8,128)(2,1)S(1)} %get-tuple-element.60.refs_3_), channel_id=1, source_target_pairs={{0,4},{4,0},{8,12},{12,8},{1,5},{5,1},{9,13},{13,9},{2,6},{6,2},{1... | collective-permute-start | bytes 393224 | tf_op jit(solution)/shard_map/ppermute | solution.py:371
  44.1 4.5 %collective-permute-start.17 = (bf16[256,512]{1,0:T(8,128)(2,1)S(1)}, bf16[256,512]{1,0:T(8,128)(2,1)S(1)}, u32[]{:S(2)}, u32[]{:S(2)}) collective-permute-start(bf16[256,512]{1,0:T(8,128)(2,1)S(1)} %pair.2.mine_ref), channel_id=1, source_target_pairs={{2,10},{6,14},{8,0},{12,4},{3,11},{7,15},{9,1},{13,5},{18,26},{22,... | collective-permute-start | bytes 786440 | tf_op jit(solution)/shard_map/ppermute | solution.py:402
  49.0 1.3 %collective-permute-start.20 = (bf16[256,512]{1,0:T(8,128)(2,1)S(1)}, bf16[256,512]{1,0:T(8,128)(2,1)S(1)}, u32[]{:S(2)}, u32[]{:S(2)}) collective-permute-start(bf16[256,512]{1,0:T(8,128)(2,1)S(1)} %pair.3), channel_id=1, source_target_pairs={{0,2},{4,6},{10,8},{14,12},{1,3},{5,7},{11,9},{15,13},{16,18},{20,... | collective-permute-start | bytes 786440 | tf_op jit(solution)/shard_map/ppermute | solution.py:404
  50.3 3.5 %collective-permute-start.19 = (bf16[256,512]{1,0:T(8,128)(2,1)S(1)}, bf16[256,512]{1,0:T(8,128)(2,1)S(1)}, u32[]{:S(2)}, u32[]{:S(2)}) collective-permute-start(bf16[256,512]{1,0:T(8,128)(2,1)S(1)} %pair.3), channel_id=1, source_target_pairs={{2,8},{6,12},{8,2},{12,6},{3,9},{7,13},{9,3},{13,7},{18,24},{22,28... | collective-permute-start | bytes 786440 | tf_op jit(solution)/shard_map/ppermute | solution.py:403
  53.8 2.5 %collective-permute-start.16 = (bf16[512,128]{1,0:T(8,128)(2,1)S(1)}, bf16[512,128]{1,0:T(8,128)(2,1)S(1)}, u32[]{:S(2)}, u32[]{:S(2)}) collective-permute-start(bf16[512,128]{1,0:T(8,128)(2,1)S(1)} %collective-permute-done.15.refs_5_), channel_id=1, source_target_pairs={{0,4},{4,0},{8,12},{12,8},{1,5},{5,1},{9,13},{13,9},{2,6},{6,2},{1... | collective-permute-start | bytes 393224 | tf_op jit(solution)/shard_map/ppermute | solution.py:372
  56.4 2.0 %query.1 = (bf16[512,256]{1,0:T(8,128)(2,1)}, f32[512,256]{1,0:T(8,128)S(1)}, f32[512,256]{1,0:T(8,128)S(1)}) custom-call(bf16[512,256]{1,0:T(8,128)(2,1)S(1)} %bitcast.26, bf16[512,256]{1,0:T(8,128)(2,1)S(1)} %get-tuple-element.38.refs_7_.refs_4_.qf_ref, bf16[512,256]{1,0:T(8,128)(2,1)S(1)} %copy-done.4, bf16[512,256]{1,0:T(8,128)(2,1)S(1)} %bitcast.21, ...), custom_call_target="tpu_custom_call" | custom-call | flops 99999997952 | bytes 1 | tf_op jit(solution)/shard_map/query/pallas_call | solution.py:44
  58.3 7.1 %collective-permute-done.16.refs_6_ = bf16[512,128]{1,0:T(8,128)(2,1)S(1)} collective-permute-done((bf16[512,128]{1,0:T(8,128)(2,1)S(1)}, bf16[512,128]{1,0:T(8,128)(2,1)S(1)}, u32[]{:S(2)}, u32[]{:S(2)}) %collective-permute-start.16) | collective-permute-done | bytes 131104 | tf_op jit(solution)/shard_map/ppermute | solution.py:372
  65.4 1.9 %key.1 = (bf16[512,256]{1,0:T(8,128)(2,1)}, bf16[512,256]{1,0:T(8,128)(2,1)}) custom-call(s32[4]{0:T(128)S(1)} %pad_add_fusion.refs_0_.pos_ref, s32[4]{0:T(128)S(1)} %xor_multiply_fusion.refs_1_, s32[2,8,4]{2,1,0:T(8,128)S(1)} %copy.11.refs_2_, bf16[512,128]{1,0:T(8,128)(2,1)S(1)} %get-tuple-element.60.refs_3_, ...), custom_call_target="tpu_custom_call" | custom-call | flops 1 | bytes 1 | tf_op jit(solution)/shard_map/key/pallas_call | solution.py:44
  67.3 7.8 %collective-permute-done.19.b_ref = bf16[256,512]{1,0:T(8,128)(2,1)S(1)} collective-permute-done((bf16[256,512]{1,0:T(8,128)(2,1)S(1)}, bf16[256,512]{1,0:T(8,128)(2,1)S(1)}, u32[]{:S(2)}, u32[]{:S(2)}) %collective-permute-start.19) | collective-permute-done | bytes 262176 | tf_op jit(solution)/shard_map/ppermute | solution.py:403
  75.2 1.5 %final.1 = f32[512,256]{1,0:T(8,128)} custom-call(s32[4]{0:T(128)S(1)} %pad_add_fusion.refs_0_.pos_ref, bf16[256,512]{1,0:T(8,128)(2,1)S(1)} %pair.2.mine_ref, bf16[256,512]{1,0:T(8,128)(2,1)S(1)} %collective-permute-done.17.a_ref, bf16[256,512]{1,0:T(8,128)(2,1)S(1)} %collective-permute-done.19.b_ref, bf16[256,512]{1,0:T(8,128)(2,1)S(1)} %collective-permute-done.20.c_ref), custom_call_target="tpu_custom_call" | custom-call | flops 1 | bytes 1 | tf_op jit(solution)/shard_map/final/pallas_call | solution.py:44
  (57 shorter events, 4.0 us)
Async XLA Ops:
  0.6 9.2 %copy-start.2 = (bf16[1,512,256]{2,1,0:T(8,128)(2,1)S(1)}, bf16[1,512,256]{2,1,0:T(8,128)(2,1)}, u32[]{:S(2)}) copy-start(bf16[1,512,256]{2,1,0:T(8,128)(2,1)} %param.8) | copy-start | bytes 786436
  0.6 9.1 %copy-start = (bf16[1,512,2048]{2,1,0:T(8,128)(2,1)S(1)}, bf16[1,512,2048]{2,1,0:T(8,128)(2,1)}, u32[]{:S(2)}) copy-start(bf16[1,512,2048]{2,1,0:T(8,128)(2,1)} %param.11) | copy-start | bytes 6291460
  0.7 9.2 %copy-start.6 = (bf16[1,512,256]{2,1,0:T(8,128)(2,1)S(1)}, bf16[1,512,256]{2,1,0:T(8,128)(2,1)}, u32[]{:S(2)}) copy-start(bf16[1,512,256]{2,1,0:T(8,128)(2,1)} %param.6) | copy-start | bytes 786436
  0.7 12.4 %copy-start.13 = (s32[2,8,4]{1,2,0:T(4,128)S(1)}, s32[2,8,4]{1,2,0:T(4,128)}, u32[]{:S(2)}) copy-start(s32[2,8,4]{1,2,0:T(4,128)} %param.9) | copy-start | bytes 772
  4.5 8.8 %collective-permute-start.2 = (bf16[512,128]{1,0:T(8,128)(2,1)}, bf16[512,128]{1,0:T(8,128)(2,1)S(1)}, u32[]{:S(2)}, u32[]{:S(2)}) collective-permute-start(bf16[512,128]{1,0:T(8,128)(2,1)} %get-tuple-element.36.refs_3_), channel_id=1, source_target_pairs={{0,12},{4,0},{8,4},{12,8},{1,13},{5,1},{9,5},{13,9},{2,14},{6,2},{... | collective-permute-start | bytes 393224 | tf_op jit(solution)/shard_map/ppermute | solution.py:282
  4.9 12.7 %collective-permute-start.1 = (bf16[512,128]{1,0:T(8,128)(2,1)}, bf16[512,128]{1,0:T(8,128)(2,1)}, u32[]{:S(2)}, u32[]{:S(2)}) collective-permute-start(bf16[512,128]{1,0:T(8,128)(2,1)} %get-tuple-element.36.refs_3_), channel_id=1, source_target_pairs={{0,8},{4,12},{8,0},{12,4},{1,9},{5,13},{9,1},{13,5},{2,10},{6,14},... | collective-permute-start | bytes 393224 | tf_op jit(solution)/shard_map/ppermute | solution.py:282
  4.9 12.7 %collective-permute-start = (bf16[512,128]{1,0:T(8,128)(2,1)}, bf16[512,128]{1,0:T(8,128)(2,1)}, u32[]{:S(2)}, u32[]{:S(2)}) collective-permute-start(bf16[512,128]{1,0:T(8,128)(2,1)} %get-tuple-element.36.refs_3_), channel_id=1, source_target_pairs={{0,4},{4,8},{8,12},{12,0},{1,5},{5,9},{9,13},{13,1},{2,6},{6,10},{... | collective-permute-start | bytes 393224 | tf_op jit(solution)/shard_map/ppermute | solution.py:282
  8.3 21.1 %collective-permute-start.6 = (bf16[2048,128]{1,0:T(8,128)(2,1)}, bf16[2048,128]{1,0:T(8,128)(2,1)S(1)}, u32[]{:S(2)}, u32[]{:S(2)}) collective-permute-start(bf16[2048,128]{1,0:T(8,128)(2,1)} %get-tuple-element.43), channel_id=1, source_target_pairs={{0,2},{2,0},{1,3},{3,1},{4,6},{6,4},{5,7},{7,5},{8,10},{10,8},{9,1... | collective-permute-start | bytes 1572872 | tf_op jit(solution)/shard_map/ppermute | solution.py:273
  9.8 13.7 %collective-permute-start.4 = (bf16[512,2048]{1,0:T(8,128)(2,1)S(1)}, bf16[512,2048]{1,0:T(8,128)(2,1)}, u32[]{:S(2)}, u32[]{:S(2)}) collective-permute-start(bf16[512,2048]{1,0:T(8,128)(2,1)S(1)} %bitcast.14), channel_id=1, source_target_pairs={{0,1},{1,0},{2,3},{3,2},{4,5},{5,4},{6,7},{7,6},{8,9},{9,8},{10,11... | collective-permute-start | bytes 6291464 | tf_op jit(solution)/shard_map/ppermute | solution.py:273
  9.8 1.0 %copy-start.3 = (bf16[512,256]{1,0:T(8,128)(2,1)S(1)}, bf16[512,256]{1,0:T(8,128)(2,1)}, u32[]{:S(2)}) copy-start(bf16[512,256]{1,0:T(8,128)(2,1)} %get-tuple-element.37.kf_ref.refs_8_) | copy-start | bytes 786436
  17.6 1.0 %copy-start.11 = (f32[512,256]{1,0:T(8,128)S(1)}, f32[512,256]{1,0:T(8,128)}, u32[]{:S(2)}) copy-start(f32[512,256]{1,0:T(8,128)} %copy-done.10) | copy-start | bytes 1572868
  21.7 1.7 %collective-permute-start.5 = (bf16[512,256]{1,0:T(8,128)(2,1)}, bf16[512,256]{1,0:T(8,128)(2,1)S(1)}, u32[]{:S(2)}, u32[]{:S(2)}) collective-permute-start(bf16[512,256]{1,0:T(8,128)(2,1)} %get-tuple-element.40.attn_ref), channel_id=1, source_target_pairs={{0,1},{1,0},{2,3},{3,2},{4,5},{5,4},{6,7},{7,6},{8,9},{9,8},{10,11... | collective-permute-start | bytes 786440 | tf_op jit(solution)/shard_map/ppermute | solution.py:273
  21.7 10.4 %collective-permute-start.3 = (bf16[512,256]{1,0:T(8,128)(2,1)}, bf16[512,256]{1,0:T(8,128)(2,1)S(1)}, u32[]{:S(2)}, u32[]{:S(2)}) collective-permute-start(bf16[512,256]{1,0:T(8,128)(2,1)} %get-tuple-element.40.attn_ref), channel_id=1, source_target_pairs={{0,2},{2,0},{1,3},{3,1},{4,6},{6,4},{5,7},{7,5},{8,10},{10,8},{9,1... | collective-permute-start | bytes 786440 | tf_op jit(solution)/shard_map/ppermute | solution.py:273
  23.5 1.0 %copy-start.7 = (bf16[512,256]{1,0:T(8,128)(2,1)S(1)}, bf16[512,256]{1,0:T(8,128)(2,1)}, u32[]{:S(2)}) copy-start(bf16[512,256]{1,0:T(8,128)(2,1)} %get-tuple-element.40.attn_ref) | copy-start | bytes 786436
  26.8 14.6 %collective-permute-start.12 = (bf16[256,512]{1,0:T(8,128)(2,1)S(1)}, bf16[256,512]{1,0:T(8,128)(2,1)S(1)}, u32[]{:S(2)}, u32[]{:S(2)}) collective-permute-start(bf16[256,512]{1,0:T(8,128)(2,1)S(1)} %get-tuple-element.41), channel_id=1, source_target_pairs={{0,4},{4,0},{8,12},{12,8},{1,5},{5,1},{9,13},{13,9},{2,6},{6,2},{1... | collective-permute-start | bytes 786440 | tf_op jit(solution)/shard_map/ppermute | solution.py:348
  32.2 2.1 %collective-permute-start.7 = (bf16[128,256]{1,0:T(8,128)(2,1)S(1)}, bf16[128,256]{1,0:T(8,128)(2,1)S(1)}, u32[]{:S(2)}, u32[]{:S(2)}) collective-permute-start(bf16[128,256]{1,0:T(8,128)(2,1)S(1)} %get-tuple-element.46), channel_id=1, source_target_pairs={{0,1},{1,0},{2,3},{3,2},{4,5},{5,4},{6,7},{7,6},{8,9},{9,8},{10,11... | collective-permute-start | bytes 196616 | tf_op jit(solution)/shard_map/ppermute | solution.py:273
  32.3 2.6 %collective-permute-start.8 = (bf16[128,256]{1,0:T(8,128)(2,1)S(1)}, bf16[128,256]{1,0:T(8,128)(2,1)S(1)}, u32[]{:S(2)}, u32[]{:S(2)}) collective-permute-start(bf16[128,256]{1,0:T(8,128)(2,1)S(1)} %get-tuple-element.47), channel_id=1, source_target_pairs={{0,1},{1,0},{2,3},{3,2},{4,5},{5,4},{6,7},{7,6},{8,9},{9,8},{10,11... | collective-permute-start | bytes 196616 | tf_op jit(solution)/shard_map/ppermute | solution.py:273
  32.8 8.7 %collective-permute-start.11 = (bf16[512,128]{1,0:T(8,128)(2,1)S(1)}, bf16[512,128]{1,0:T(8,128)(2,1)S(1)}, u32[]{:S(2)}, u32[]{:S(2)}) collective-permute-start(bf16[512,128]{1,0:T(8,128)(2,1)S(1)} %get-tuple-element.52), channel_id=1, source_target_pairs={{0,2},{2,0},{1,3},{3,1},{4,6},{6,4},{5,7},{7,5},{8,10},{10,8},{9,1... | collective-permute-start | bytes 393224 | tf_op jit(solution)/shard_map/ppermute | solution.py:273
  34.3 7.2 %collective-permute-start.13 = (bf16[512,128]{1,0:T(8,128)(2,1)S(1)}, bf16[512,128]{1,0:T(8,128)(2,1)S(1)}, u32[]{:S(2)}, u32[]{:S(2)}) collective-permute-start(bf16[512,128]{1,0:T(8,128)(2,1)S(1)} %get-tuple-element.44), channel_id=1, source_target_pairs={{0,3},{1,2},{2,1},{3,0},{4,7},{5,6},{6,5},{7,4},{8,11},{9,10},{10,... | collective-permute-start | bytes 393224 | tf_op jit(solution)/shard_map/ppermute | solution.py:343
  34.3 1.6 %collective-permute-start.9 = (bf16[128,256]{1,0:T(8,128)(2,1)S(1)}, bf16[128,256]{1,0:T(8,128)(2,1)S(1)}, u32[]{:S(2)}, u32[]{:S(2)}) collective-permute-start(bf16[128,256]{1,0:T(8,128)(2,1)S(1)} %get-tuple-element.48), channel_id=1, source_target_pairs={{0,1},{1,0},{2,3},{3,2},{4,5},{5,4},{6,7},{7,6},{8,9},{9,8},{10,11... | collective-permute-start | bytes 196616 | tf_op jit(solution)/shard_map/ppermute | solution.py:273
  34.9 4.9 %copy-start.1 = (bf16[4096,256]{1,0:T(8,128)(2,1)S(1)}, bf16[4096,256]{1,0:T(8,128)(2,1)}, u32[]{:S(2)}) copy-start(bf16[4096,256]{1,0:T(8,128)(2,1)} %w_ref.3) | copy-start | bytes 6291460
  35.0 1.3 %collective-permute-start.10 = (bf16[128,256]{1,0:T(8,128)(2,1)S(1)}, bf16[128,256]{1,0:T(8,128)(2,1)S(1)}, u32[]{:S(2)}, u32[]{:S(2)}) collective-permute-start(bf16[128,256]{1,0:T(8,128)(2,1)S(1)} %get-tuple-element.49), channel_id=1, source_target_pairs={{0,1},{1,0},{2,3},{3,2},{4,5},{5,4},{6,7},{7,6},{8,9},{9,8},{10,11... | collective-permute-start | bytes 196616 | tf_op jit(solution)/shard_map/ppermute | solution.py:273
  38.8 10.2 %collective-permute-start.18 = (bf16[256,512]{1,0:T(8,128)(2,1)S(1)}, bf16[256,512]{1,0:T(8,128)(2,1)S(1)}, u32[]{:S(2)}, u32[]{:S(2)}) collective-permute-start(bf16[256,512]{1,0:T(8,128)(2,1)S(1)} %get-tuple-element.50), channel_id=1, source_target_pairs={{0,4},{4,0},{8,12},{12,8},{1,5},{5,1},{9,13},{13,9},{2,6},{6,2},{1... | collective-permute-start | bytes 786440 | tf_op jit(solution)/shard_map/ppermute | solution.py:356
  41.5 14.9 %copy-start.4 = (bf16[512,256]{1,0:T(8,128)(2,1)S(1)}, bf16[512,256]{1,0:T(8,128)(2,1)}, u32[]{:S(2)}) copy-start(bf16[512,256]{1,0:T(8,128)(2,1)} %get-tuple-element.37.kf_ref.refs_8_) | copy-start | bytes 786436
  41.5 14.9 %copy-start.9 = (bf16[1024,256]{1,0:T(8,128)(2,1)S(1)}, bf16[1024,256]{1,0:T(8,128)(2,1)}, u32[]{:S(2)}) copy-start(bf16[1024,256]{1,0:T(8,128)(2,1)} %copy-done.8) | copy-start | bytes 1572868
  42.7 11.1 %collective-permute-start.15 = (bf16[512,128]{1,0:T(8,128)(2,1)S(1)}, bf16[512,128]{1,0:T(8,128)(2,1)S(1)}, u32[]{:S(2)}, u32[]{:S(2)}) collective-permute-start(bf16[512,128]{1,0:T(8,128)(2,1)S(1)} %get-tuple-element.60.refs_3_), channel_id=1, source_target_pairs={{0,8},{4,12},{8,0},{12,4},{1,9},{5,13},{9,1},{13,5},{2,10},{6,14},... | collective-permute-start | bytes 393224 | tf_op jit(solution)/shard_map/ppermute | solution.py:370
  43.0 10.8 %collective-permute-start.14 = (bf16[512,128]{1,0:T(8,128)(2,1)S(1)}, bf16[512,128]{1,0:T(8,128)(2,1)S(1)}, u32[]{:S(2)}, u32[]{:S(2)}) collective-permute-start(bf16[512,128]{1,0:T(8,128)(2,1)S(1)} %get-tuple-element.60.refs_3_), channel_id=1, source_target_pairs={{0,4},{4,0},{8,12},{12,8},{1,5},{5,1},{9,13},{13,9},{2,6},{6,2},{1... | collective-permute-start | bytes 393224 | tf_op jit(solution)/shard_map/ppermute | solution.py:371
  44.1 23.2 %collective-permute-start.17 = (bf16[256,512]{1,0:T(8,128)(2,1)S(1)}, bf16[256,512]{1,0:T(8,128)(2,1)S(1)}, u32[]{:S(2)}, u32[]{:S(2)}) collective-permute-start(bf16[256,512]{1,0:T(8,128)(2,1)S(1)} %pair.2.mine_ref), channel_id=1, source_target_pairs={{2,10},{6,14},{8,0},{12,4},{3,11},{7,15},{9,1},{13,5},{18,26},{22,... | collective-permute-start | bytes 786440 | tf_op jit(solution)/shard_map/ppermute | solution.py:402
  49.0 18.3 %collective-permute-start.20 = (bf16[256,512]{1,0:T(8,128)(2,1)S(1)}, bf16[256,512]{1,0:T(8,128)(2,1)S(1)}, u32[]{:S(2)}, u32[]{:S(2)}) collective-permute-start(bf16[256,512]{1,0:T(8,128)(2,1)S(1)} %pair.3), channel_id=1, source_target_pairs={{0,2},{4,6},{10,8},{14,12},{1,3},{5,7},{11,9},{15,13},{16,18},{20,... | collective-permute-start | bytes 786440 | tf_op jit(solution)/shard_map/ppermute | solution.py:404
  50.3 24.8 %collective-permute-start.19 = (bf16[256,512]{1,0:T(8,128)(2,1)S(1)}, bf16[256,512]{1,0:T(8,128)(2,1)S(1)}, u32[]{:S(2)}, u32[]{:S(2)}) collective-permute-start(bf16[256,512]{1,0:T(8,128)(2,1)S(1)} %pair.3), channel_id=1, source_target_pairs={{2,8},{6,12},{8,2},{12,6},{3,9},{7,13},{9,3},{13,7},{18,24},{22,28... | collective-permute-start | bytes 786440 | tf_op jit(solution)/shard_map/ppermute | solution.py:403
  53.8 11.6 %collective-permute-start.16 = (bf16[512,128]{1,0:T(8,128)(2,1)S(1)}, bf16[512,128]{1,0:T(8,128)(2,1)S(1)}, u32[]{:S(2)}, u32[]{:S(2)}) collective-permute-start(bf16[512,128]{1,0:T(8,128)(2,1)S(1)} %collective-permute-done.15.refs_5_), channel_id=1, source_target_pairs={{0,4},{4,0},{8,12},{12,8},{1,5},{5,1},{9,13},{13,9},{2,6},{6,2},{1... | collective-permute-start | bytes 393224 | tf_op jit(solution)/shard_map/ppermute | solution.py:372
  56.4 9.0 %copy-start.5 = (bf16[1,512,256]{2,1,0:T(8,128)(2,1)S(1)}, bf16[1,512,256]{2,1,0:T(8,128)(2,1)}, u32[]{:S(2)}) copy-start(bf16[1,512,256]{2,1,0:T(8,128)(2,1)} %param.7) | copy-start | bytes 786436
  (3 other events, 2.5 us)

commit v5 on v4

--- a/solution.py
+++ b/solution.py
@@ -11,6 +11,7 @@
 BLK = 256
 EPS = 1e-06
 LIMIT = 16 << 20
+BEGIN = 56 << 20
 SHORT = pl.CostEstimate(flops=1, bytes_accessed=1, transcendentals=0)
 LONG = pl.CostEstimate(flops=10**11, bytes_accessed=1, transcendentals=0)
 F32 = jnp.float32
@@ -69,15 +70,29 @@
         st_ref[mat(i), :] = mm(kf, v_ref[r, c], TN).astype(BF16)
 
 
-def begin_body(at_ref, k_ref, v_ref, w_ref, kf_ref, st_ref, far_ref):
-    far_ref[...] = w_ref[...]
-    states_body(k_ref, v_ref, kf_ref, st_ref)
-
-
-def begin(at, k, v, w, width):
+def begin_body(k_ref, v_ref, w_ref, kf_ref, st_ref, far_ref, k_in, v_in, far_in, sems):
+    width, cols = far_ref.shape
+    rows = pl.ds(pl.multiple_of((1 - lax.axis_index("head")) * width, width), width)
+    lanes = pl.ds(pl.multiple_of(lax.axis_index("dp") * cols, cols), cols)
+    far_copy = pltpu.make_async_copy(w_ref.at[rows, lanes], far_in, sems.at[0])
+    k_copy = pltpu.make_async_copy(k_ref, k_in, sems.at[1])
+    v_copy = pltpu.make_async_copy(v_ref, v_in, sems.at[2])
+    k_copy.start()
+    v_copy.start()
+    far_copy.start()
+    k_copy.wait()
+    v_copy.wait()
+    states_body(k_in, v_in, kf_ref, st_ref)
+    far_copy.wait()
+    out_copy = pltpu.make_async_copy(far_in, far_ref, sems.at[3])
+    out_copy.start()
+    out_copy.wait()
+
+
+def begin(k, v, w, width):
     tokens, cols = k.shape
     count = tokens // BLK * (cols // DH)
-    whole = pl.BlockSpec((tokens, cols), lambda g, at: (0, 0))
+    hbm = pl.BlockSpec(memory_space=pl.ANY)
     return pl.pallas_call(
         begin_body,
         out_shape=(
@@ -85,20 +100,18 @@
             sds((count * DH, DH), BF16),
             sds((width, DH), BF16),
         ),
-        grid_spec=pltpu.PrefetchScalarGridSpec(
-            num_scalar_prefetch=1,
-            grid=(1,),
-            in_specs=[whole, whole, pl.BlockSpec((width, DH), lambda g, at: (at[0], at[1]))],
-            out_specs=[
-                whole,
-                pl.BlockSpec((count * DH, DH), lambda g, at: (0, 0)),
-                pl.BlockSpec((width, DH), lambda g, at: (0, 0)),
-            ],
-        ),
+        in_specs=[hbm, hbm, hbm],
+        out_specs=[VM, VM, hbm],
+        scratch_shapes=[
+            pltpu.VMEM((tokens, cols), BF16),
+            pltpu.VMEM((tokens, cols), BF16),
+            pltpu.VMEM((width, DH), BF16),
+            pltpu.SemaphoreType.DMA((4,)),
+        ],
         name="begin",
-        compiler_params=pltpu.CompilerParams(vmem_limit_bytes=56 << 20),
+        compiler_params=pltpu.CompilerParams(vmem_limit_bytes=BEGIN),
         cost_estimate=SHORT,
-    )(at, k, v, w)
+    )(k, v, w)
 
 
 def split_body(x_ref, *outs):
@@ -125,23 +138,36 @@
 
 def count(lay_ref, h, i, b):
     total = jnp.int32(0)
-    for j in range(lay_ref.shape[2]):
-        total = total + jnp.where(lay_ref[h, i, j] == b, 1, 0)
+    for j in range(lay_ref.shape[1]):
+        total = total + jnp.where(lay_ref[h, j, i] == b, 1, 0)
     return total.astype(F32)
 
 
+def in_order(z, s):
+    return 0
+
+
+def by_shift(z, s):
+    size = lax.axis_size("seq")
+    return lax.rem(z + size - s, size)
+
+
+def by_flip(z, s):
+    return lax.bitwise_xor(z, jnp.int32(s))
+
+
 def numer_body(dims, np_, *refs):
-    nb, heads = dims
-    pos_ref, base_ref, lay_ref = refs[:3]
-    parts = refs[3 : 3 + np_]
-    qf_ref, intra_ref, carried_ref, num_ref, attn_ref = refs[3 + np_ :]
+    nb, heads, owner_of = dims
+    lay_ref, *parts = refs[: 1 + np_]
+    qf_ref, intra_ref, carried_ref, num_ref, attn_ref = refs[1 + np_ :]
+    z = lax.axis_index("seq")
     for i, r, c in tiles(qf_ref.shape[0], heads):
         n, h = divmod(i, heads)
-        query_block = pos_ref[0] * nb + n
+        query_block = z * nb + n
         total = jnp.zeros((DH, DH), F32)
         for s, part in enumerate(parts):
             for b in range(part.shape[0] // (heads * DH)):
-                times = count(lay_ref, h, query_block, base_ref[s] + b)
+                times = count(lay_ref, h, query_block, owner_of(z, s) * nb + b)
                 total = total + times * part[mat(b * heads + h), :].astype(F32)
         carried = total.astype(BF16)
         carried_ref[mat(i), :] = carried
@@ -151,7 +177,7 @@
         attn_ref[r, c] = (num * rinv).astype(BF16)
 
 
-def dnum_body(n_d, pos_ref, *refs):
+def dnum_body(n_d, *refs):
     d_refs = refs[:n_d]
     num_ref, qf_ref, dnum_ref, cg_ref = refs[n_d:]
     heads = num_ref.shape[1] // DH
@@ -160,7 +186,7 @@
         grad = d_refs[0][r, c].astype(F32)
         if n_d == 3:
             same, sib = d_refs[1][r, :].astype(F32), d_refs[2][r, :].astype(F32)
-            grad = grad + jnp.where(pos_ref[3] == i % heads, same, sib)
+            grad = grad + jnp.where(lax.axis_index("dp") == i % heads, same, sib)
         grad = grad.astype(BF16).astype(F32)
         rinv = lax.rsqrt(jnp.mean(num * num, axis=-1, keepdims=True) + EPS)
         lean = jnp.mean(grad * num, axis=-1, keepdims=True)
@@ -181,17 +207,17 @@
 
 
 def key_body(dims, np_, *refs):
-    nb, heads = dims
-    pos_ref, base_ref, lay_ref = refs[:3]
-    parts = refs[3 : 3 + np_]
-    k_ref, kf_ref, v_ref, dkp_ref, dvp_ref, dk_ref, dv_ref = refs[3 + np_ :]
+    nb, heads, owner_of = dims
+    lay_ref, *parts = refs[: 1 + np_]
+    k_ref, kf_ref, v_ref, dkp_ref, dvp_ref, dk_ref, dv_ref = refs[1 + np_ :]
+    z = lax.axis_index("seq")
     for i, r, c in tiles(k_ref.shape[0], heads):
         n, h = divmod(i, heads)
-        key_block = pos_ref[0] * nb + n
+        key_block = z * nb + n
         total = jnp.zeros((DH, DH), F32)
         for s, part in enumerate(parts):
             for b in range(part.shape[0] // (heads * DH)):
-                times = count(lay_ref, h, base_ref[s] + b, key_block)
+                times = count(lay_ref, h, owner_of(z, s) * nb + b, key_block)
                 total = total + times * part[mat(b * heads + h), :].astype(F32)
         sg = total.astype(BF16)
         dk = mm(v_ref[r, c], sg, NT) + dkp_ref[r, c]
@@ -199,38 +225,28 @@
         dv_ref[r, c] = (mm(kf_ref[r, c], sg, NN) + dvp_ref[r, c]).astype(BF16)
 
 
-def own_body(at_ref, og_ref, w_ref, out_ref):
-    part = mm(og_ref[...], w_ref[...], NN)
-
-    @pl.when(pl.program_id(0) == 0)
-    def _():
-        out_ref[...] = part
-
-    @pl.when(pl.program_id(0) > 0)
-    def _():
-        out_ref[...] += part
-
-
-def own_partial(at, og, w, steps=4):
+def own_body(og_ref, w_ref, out_ref, w_in, sem):
+    width = w_in.shape[0]
+    rows = pl.ds(pl.multiple_of(lax.axis_index("head") * width, width), width)
+    copy = pltpu.make_async_copy(w_ref.at[rows, :], w_in, sem)
+    copy.start()
+    copy.wait()
+    out_ref[...] = mm(og_ref[...], w_in[...], NN)
+
+
+def own_partial(og, w):
     tokens, width = og.shape
     cols = w.shape[1]
-    bk = width // steps
     return pl.pallas_call(
         own_body,
         out_shape=sds((tokens, cols), F32),
-        grid_spec=pltpu.PrefetchScalarGridSpec(
-            num_scalar_prefetch=1,
-            grid=(steps,),
-            in_specs=[
-                pl.BlockSpec((tokens, bk), lambda g, at: (0, g)),
-                pl.BlockSpec((bk, cols), lambda g, at: (at[0] * steps + g, 0)),
-            ],
-            out_specs=pl.BlockSpec((tokens, cols), lambda g, at: (0, 0)),
-        ),
+        in_specs=[VM, pl.BlockSpec(memory_space=pl.ANY)],
+        out_specs=VM,
+        scratch_shapes=[pltpu.VMEM((width, cols), BF16), pltpu.SemaphoreType.DMA],
         name="own_partial",
         compiler_params=pltpu.CompilerParams(vmem_limit_bytes=LIMIT),
         cost_estimate=SHORT,
-    )(at, og, w)
+    )(og, w)
 
 
 def other_body(og_ref, og_sib_ref, w_ref, same_ref, sib_ref):
@@ -238,11 +254,11 @@
     sib_ref[...] = mm(og_sib_ref[...], w_ref[...], NN).astype(BF16)
 
 
-def weight_body(pos_ref, attn_ref, og_ref, og_sib_ref, *refs):
+def weight_body(attn_ref, og_ref, og_sib_ref, *refs):
     *sib_refs, give_ref, keep_ref = refs
     step = sib_refs[0].shape[0]
     rows = give_ref.shape[1]
-    parity, core = pos_ref[2], pos_ref[3]
+    parity, core = lax.rem(lax.axis_index("seq"), 2), lax.axis_index("dp")
 
     def part(pair):
         at = pl.ds(pl.multiple_of((2 * pair + core) * rows, rows), rows)
@@ -259,8 +275,9 @@
     out_ref[...] = (keep_ref[...] + got_ref[...].astype(F32)).astype(BF16)
 
 
-def final_body(pos_ref, mine_ref, a_ref, b_ref, c_ref, out_ref):
-    mine = jnp.where(pos_ref[1] > 0, mine_ref[...].astype(F32), 0.0)
+def final_body(mine_ref, a_ref, b_ref, c_ref, out_ref):
+    home = lax.axis_index("seq") // 2 == lax.axis_index("head")
+    mine = jnp.where(home, mine_ref[...].astype(F32), 0.0)
     total = mine + a_ref[...].astype(F32) + b_ref[...].astype(F32) + c_ref[...].astype(F32)
     out_ref[...] = total.T
 
@@ -287,21 +304,13 @@
     seq_size = lax.axis_size("seq")
     head_size = lax.axis_size("head")
     dp_size = lax.axis_size("dp")
-    z = lax.axis_index("seq").astype(jnp.int32)
-    x = lax.axis_index("head").astype(jnp.int32)
-    core = lax.axis_index("dp").astype(jnp.int32)
     heads = layout.shape[0]
     q, k, v, og = queries[0], key_rows[0], value_rows[0], out_grad[0]
     tokens, cols = q.shape
     nb = tokens // BLK
-    dims = (nb, heads)
     paired = seq_size == 4 and head_size == 2 and dp_size == 2
-    home = (z // 2 == x).astype(jnp.int32)
-    pos = jnp.stack([z, home, z % 2, core])
-    if seq_size > 4:
-        bases = jnp.zeros((1,), jnp.int32)
-    else:
-        bases = ((z - jnp.arange(seq_size, dtype=jnp.int32)) % seq_size) * nb
+    lay = layout.transpose(0, 2, 1)
+    first_owner = in_order if seq_size > 4 else by_shift
     flat = sds((tokens, cols), F32)
     rows16 = sds((tokens, cols), BF16)
     mats = sds((nb * heads * DH, DH), BF16)
@@ -309,7 +318,7 @@
 
     if paired:
         width = og.shape[1]
-        kf, st, far = begin(jnp.stack([1 - x, core]), k, v, out_weight, width)
+        kf, st, far = begin(k, v, out_weight, width)
         w_other = swap(far, "head")
         og_sib = swap(og, "dp")
     else:
@@ -326,9 +335,9 @@
         og = lax.all_gather(og, "head", axis=1, tiled=True)
         d_own = jnp.dot(og, out_weight, preferred_element_type=F32)
     carried, num, attn = call(
-        functools.partial(numer_body, dims, len(parts)),
+        functools.partial(numer_body, (nb, heads, first_owner), len(parts)),
         (mats, flat, rows16),
-        (pos, bases, layout, *parts, qf, intra),
+        (lay, *parts, qf, intra),
         unit,
         "numer",
     )
@@ -344,17 +353,17 @@
         block = (cols, width // 4)
         outs = (sds(block, BF16), sds(block, F32))
         neighbours = [(0, 1), (1, 0), (2, 3), (3, 2)]
-        give_a, keep_a = call(weight_body, outs, (pos, attn, og, og_sib, swap(attn, "dp")), 0, "weight")
+        give_a, keep_a = call(weight_body, outs, (attn, og, og_sib, swap(attn, "dp")), 0, "weight")
         got_a = lax.ppermute(give_a, "seq", neighbours)
         attn_other = after(attn_other, give_a, d_sib_sent)
         quarter = sds((tokens // 4, cols), BF16)
         pieces = call(split_body, (quarter,) * 4, (attn_other,), 0, "split")
         pieces = [swap(piece, "dp") for piece in pieces]
         give_b, keep_b = call(
-            weight_body, outs, (pos, attn_other, og, og_sib, *pieces), 0, "weight"
+            weight_body, outs, (attn_other, og, og_sib, *pieces), 0, "weight"
         )
         got_b = lax.ppermute(give_b, "seq", neighbours)
-        d_own = own_partial(x[None], after(og, give_b), out_weight)
+        d_own = own_partial(after(og, give_b), out_weight)
         (mine,) = call(pair_body, (sds(keep_a.shape, BF16),), (keep_a, got_a), 0, "pair")
         d_parts = (d_own, after(d_same, give_b, mine), d_sib)
     else:
@@ -362,7 +371,7 @@
     dnum, cg = call(
         functools.partial(dnum_body, len(d_parts)),
         (rows16, mats),
-        (pos, *d_parts, num, qf),
+        (*d_parts, num, qf),
         unit,
         "dnum",
     )
@@ -370,9 +379,9 @@
         two = lax.ppermute(cg, "seq", [(i, i ^ 2) for i in range(4)])
         one = lax.ppermute(cg, "seq", neighbours)
         cparts = [cg, one, two, lax.ppermute(after(two, one), "seq", neighbours)]
-        cbases = (z ^ jnp.arange(4, dtype=jnp.int32)) * nb
+        second_owner = by_flip
     else:
-        cparts, cbases = gather_parts(cg, seq_size), bases
+        cparts, second_owner = gather_parts(cg, seq_size), first_owner
     dq, dkp, dvp = call(
         query_body,
         (rows16, flat, flat),
@@ -381,9 +390,9 @@
         "query",
     )
     dk, dv = call(
-        functools.partial(key_body, dims, len(cparts)),
+        functools.partial(key_body, (nb, heads, second_owner), len(cparts)),
         (rows16, rows16),
-        (pos, cbases, layout, *cparts, k, kf, v, dkp, dvp),
+        (lay, *cparts, k, kf, v, dkp, dvp),
         2 * unit,
         "key",
     )
@@ -404,7 +413,7 @@
             lax.ppermute(cross, axes, to_side),
         )
         (weight_grad,) = call(
-            final_body, (sds(mine.shape[::-1], F32),), (pos, mine, *arrived), 0, "final"
+            final_body, (sds(mine.shape[::-1], F32),), (mine, *arrived), 0, "final"
         )
     else:
         weight_grad = lax.psum_scatter(

time: 77.2 us -> 73.3 us (0.949)
  the two profiles are of different devices: /device:TPU:24 before, /device:TPU:3 now
where the time goes in v5:
time: 73.3 us; the launch traced here: 73.1 us
  waiting for transfers between devices  31.1 us (42%)
  starting transfers between devices  23.4 us (32%)
  Pallas kernels  14.9 us (20%)
  local copies, waits for them, and re-layouts  2.83 us (4%)
  between operations  0.85 us (1%)
    pallas_call x12, Pallas kernels, call(): pl.pallas_call(body, out_shape=outs, in_specs=[SM if a.dtype == jnp.int32...  11 us
    ppermute x1, waiting for transfers between devices, per_device(): cparts = [cg, one, two, lax.ppermute(after(two, one), 'seq', neighbours)]  9.21 us
    ppermute x1, waiting for transfers between devices, per_device(): lax.ppermute(cross, axes, to_both)  7.19 us
    ppermute x3, waiting for transfers between devices, gather_parts(): parts.append(lax.ppermute(x, 'seq', pairs))  7.08 us
    ppermute x9, waiting for transfers between devices, swap(): return lax.ppermute(x, axis, [(0, 1), (1, 0)])  5.25 us
    ppermute x9, starting transfers between devices, swap(): return lax.ppermute(x, axis, [(0, 1), (1, 0)])  5.14 us
    ppermute x3, starting transfers between devices, gather_parts(): parts.append(lax.ppermute(x, 'seq', pairs))  3.83 us
    ppermute x1, starting transfers between devices, per_device(): lax.ppermute(cross, axes, to_both)  3.68 us
  transfers between devices with their start and end apart: 21, of which 8 were waited for; matrix products, arithmetic and copies ran while one was open for 0% of the time, Pallas kernels for 15%

profile of v5, /device:TPU:3, one launch (start us, length us, event | category | flops | bytes accessed | tf_op | source)
XLA Modules:
  0.0 73.1 jit_solution(17219150662558120487)
XLA Ops:
  0.7 3.1 %begin.1 = (bf16[512,256]{1,0:T(8,128)(2,1)}, bf16[512,128]{1,0:T(8,128)(2,1)}, bf16[2048,128]{1,0:T(8,128)(2,1)}) custom-call(bf16[512,256]{1,0:T(8,128)(2,1)} %bitcast.18, bf16[512,256]{1,0:T(8,128)(2,1)} %bitcast.14, bf16[4096,256]{1,0:T(8,128)(2,1)} %w_ref.3), custom_call_target="tpu_custom_call" | custom-call | flops 1 | bytes 1 | tf_op jit(solution)/shard_map/begin/pallas_call | solution.py:96
  3.8 3.4 %collective-permute-start.2 = (bf16[512,128]{1,0:T(8,128)(2,1)}, bf16[512,128]{1,0:T(8,128)(2,1)S(1)}, u32[]{:S(2)}, u32[]{:S(2)}) collective-permute-start(bf16[512,128]{1,0:T(8,128)(2,1)} %get-tuple-element.36.refs_1_), channel_id=1, source_target_pairs={{0,12},{4,0},{8,4},{12,8},{1,13},{5,1},{9,5},{13,9},{2,14},{6,2},{... | collective-permute-start | bytes 393224 | tf_op jit(solution)/shard_map/ppermute | solution.py:299
  7.9 1.8 %collective-permute-start.4 = (bf16[512,2048]{1,0:T(8,128)(2,1)S(1)}, bf16[512,2048]{1,0:T(8,128)(2,1)S(1)}, u32[]{:S(2)}, u32[]{:S(2)}) collective-permute-start(bf16[512,2048]{1,0:T(8,128)(2,1)S(1)} %bitcast.9), channel_id=1, source_target_pairs={{0,1},{1,0},{2,3},{3,2},{4,5},{5,4},{6,7},{7,6},{8,9},{9,8},{10,11... | collective-permute-start | bytes 6291464 | tf_op jit(solution)/shard_map/ppermute | solution.py:290
  9.7 0.9 %copy-done.4 = bf16[512,256]{1,0:T(8,128)(2,1)S(1)} copy-done((bf16[512,256]{1,0:T(8,128)(2,1)S(1)}, bf16[512,256]{1,0:T(8,128)(2,1)}, u32[]{:S(2)}) %copy-start.4) | copy-done | bytes 262168
  10.6 0.7 scores.1
  11.3 7.1 %collective-permute-done.1.refs_3_ = bf16[512,128]{1,0:T(8,128)(2,1)S(1)} collective-permute-done((bf16[512,128]{1,0:T(8,128)(2,1)}, bf16[512,128]{1,0:T(8,128)(2,1)S(1)}, u32[]{:S(2)}, u32[]{:S(2)}) %collective-permute-start.1) | collective-permute-done | bytes 131104 | tf_op jit(solution)/shard_map/ppermute | solution.py:299
  18.4 0.9 %copy-done.9 = bf16[512,128]{1,0:T(8,128)(2,1)S(1)} copy-done((bf16[512,128]{1,0:T(8,128)(2,1)S(1)}, bf16[512,128]{1,0:T(8,128)(2,1)}, u32[]{:S(2)}) %copy-start.9) | copy-done | bytes 131096
  19.3 1.8 %numer.1 = (bf16[512,128]{1,0:T(8,128)(2,1)S(1)}, f32[512,256]{1,0:T(8,128)S(1)}, bf16[512,256]{1,0:T(8,128)(2,1)}) custom-call(s32[2,4,8]{2,1,0:T(4,128)S(1)} %bitcast.23, bf16[512,128]{1,0:T(8,128)(2,1)S(1)} %copy-done.9, bf16[512,128]{1,0:T(8,128)(2,1)S(1)} %collective-permute-done.refs_2_, bf16[512,128]{1,0:T(8,128)(2,1)S(1)} %collective-permute-done.1.refs_3_, ...), custom_call_target="tpu_custom_call" | custom-call | flops 99999997952 | bytes 1 | tf_op jit(solution)/shard_map/numer/pallas_call | solution.py:45
  21.1 1.2 %collective-permute-start.5 = (bf16[512,256]{1,0:T(8,128)(2,1)}, bf16[512,256]{1,0:T(8,128)(2,1)S(1)}, u32[]{:S(2)}, u32[]{:S(2)}) collective-permute-start(bf16[512,256]{1,0:T(8,128)(2,1)} %get-tuple-element.40.attn_ref), channel_id=1, source_target_pairs={{0,1},{1,0},{2,3},{3,2},{4,5},{5,4},{6,7},{7,6},{8,9},{9,8},{10,11... | collective-permute-start | bytes 786440 | tf_op jit(solution)/shard_map/ppermute | solution.py:290
  22.5 1.1 %collective-permute-done.5.refs_0_ = bf16[512,256]{1,0:T(8,128)(2,1)S(1)} collective-permute-done((bf16[512,256]{1,0:T(8,128)(2,1)}, bf16[512,256]{1,0:T(8,128)(2,1)S(1)}, u32[]{:S(2)}, u32[]{:S(2)}) %collective-permute-start.5) | collective-permute-done | bytes 262176 | tf_op jit(solution)/shard_map/ppermute | solution.py:290
  23.7 0.9 %copy-done.7 = bf16[512,256]{1,0:T(8,128)(2,1)S(1)} copy-done((bf16[512,256]{1,0:T(8,128)(2,1)S(1)}, bf16[512,256]{1,0:T(8,128)(2,1)}, u32[]{:S(2)}) %copy-start.7) | copy-done | bytes 262168
  24.6 0.8 %weight.2 = (bf16[256,512]{1,0:T(8,128)(2,1)S(1)}, f32[256,512]{1,0:T(8,128)S(1)}) custom-call(bf16[512,256]{1,0:T(8,128)(2,1)S(1)} %copy-done.7, bf16[512,2048]{1,0:T(8,128)(2,1)S(1)} %bitcast.10, bf16[512,2048]{1,0:T(8,128)(2,1)S(1)} %collective-permute-done.4.og_sib_ref, bf16[512,256]{1,0:T(8,128)(2,1)S(1)} %collective-permute-done.5.refs_0_), custom_call_target="tpu_custom_call" | custom-call | flops 1 | bytes 1 | tf_op jit(solution)/shard_map/weight/pallas_call | solution.py:45
  25.4 0.6 collective-permute-start.12
  26.0 1.2 %other.1 = (bf16[512,128]{1,0:T(8,128)(2,1)S(1)}, bf16[512,128]{1,0:T(8,128)(2,1)S(1)}) custom-call(bf16[512,2048]{1,0:T(8,128)(2,1)S(1)} %bitcast.11, bf16[512,2048]{1,0:T(8,128)(2,1)S(1)} %collective-permute-done.4.og_sib_ref, bf16[2048,128]{1,0:T(8,128)(2,1)S(1)} %collective-permute-done.6.w_ref), custom_call_target="tpu_custom_call" | custom-call | flops 1 | bytes 1 | tf_op jit(solution)/shard_map/other/pallas_call | solution.py:45
  27.2 3.2 %collective-permute-done.3.x_ref.attn_ref = bf16[512,256]{1,0:T(8,128)(2,1)S(1)} collective-permute-done((bf16[512,256]{1,0:T(8,128)(2,1)}, bf16[512,256]{1,0:T(8,128)(2,1)S(1)}, u32[]{:S(2)}, u32[]{:S(2)}) %collective-permute-start.3) | collective-permute-done | bytes 262176 | tf_op jit(solution)/shard_map/ppermute | solution.py:290
  30.4 0.8 %collective-permute-start.7 = (bf16[128,256]{1,0:T(8,128)(2,1)S(1)}, bf16[128,256]{1,0:T(8,128)(2,1)S(1)}, u32[]{:S(2)}, u32[]{:S(2)}) collective-permute-start(bf16[128,256]{1,0:T(8,128)(2,1)S(1)} %get-tuple-element.46), channel_id=1, source_target_pairs={{0,1},{1,0},{2,3},{3,2},{4,5},{5,4},{6,7},{7,6},{8,9},{9,8},{10,11... | collective-permute-start | bytes 196616 | tf_op jit(solution)/shard_map/ppermute | solution.py:290
  31.6 1.8 %collective-permute-start.13 = (bf16[512,128]{1,0:T(8,128)(2,1)S(1)}, bf16[512,128]{1,0:T(8,128)(2,1)S(1)}, u32[]{:S(2)}, u32[]{:S(2)}) collective-permute-start(bf16[512,128]{1,0:T(8,128)(2,1)S(1)} %get-tuple-element.44), channel_id=1, source_target_pairs={{0,3},{1,2},{2,1},{3,0},{4,7},{5,6},{6,5},{7,4},{8,11},{9,10},{10,... | collective-permute-start | bytes 393224 | tf_op jit(solution)/shard_map/ppermute | solution.py:352
  34.0 0.7 %collective-permute-done.9.refs_2_ = bf16[128,256]{1,0:T(8,128)(2,1)S(1)} collective-permute-done((bf16[128,256]{1,0:T(8,128)(2,1)S(1)}, bf16[128,256]{1,0:T(8,128)(2,1)S(1)}, u32[]{:S(2)}, u32[]{:S(2)}) %collective-permute-start.9) | collective-permute-done | bytes 65568 | tf_op jit(solution)/shard_map/ppermute | solution.py:290
  34.9 1.0 %weight.3 = (bf16[256,512]{1,0:T(8,128)(2,1)S(1)}, f32[256,512]{1,0:T(8,128)S(1)}) custom-call(bf16[512,256]{1,0:T(8,128)(2,1)S(1)} %collective-permute-done.3.x_ref.attn_ref, bf16[512,2048]{1,0:T(8,128)(2,1)S(1)} %bitcast.12, bf16[512,2048]{1,0:T(8,128)(2,1)S(1)} %collective-permute-done.4.og_sib_ref, bf16[128,256]{1,0:T(8,128)(2,1)S(1)} %collective-permute-done.7.refs_0_, ...), custom_call_target="tpu_custom_call" | custom-call | flops 1 | bytes 1 | tf_op jit(solution)/shard_map/weight/pallas_call | solution.py:45
  35.9 0.6 collective-permute-start.18
  36.5 0.8 %own_partial.1.refs_0_ = f32[512,256]{1,0:T(8,128)S(1)} custom-call(bf16[512,2048]{1,0:T(8,128)(2,1)S(1)} %bitcast.13, bf16[4096,256]{1,0:T(8,128)(2,1)S(1)} %copy-done.1), custom_call_target="tpu_custom_call" | custom-call | flops 1 | bytes 1 | tf_op jit(solution)/shard_map/own_partial/pallas_call | solution.py:240
  37.3 2.4 %collective-permute-done.13.refs_2_ = bf16[512,128]{1,0:T(8,128)(2,1)S(1)} collective-permute-done((bf16[512,128]{1,0:T(8,128)(2,1)S(1)}, bf16[512,128]{1,0:T(8,128)(2,1)S(1)}, u32[]{:S(2)}, u32[]{:S(2)}) %collective-permute-start.13) | collective-permute-done | bytes 131104 | tf_op jit(solution)/shard_map/ppermute | solution.py:352
  40.3 2.4 %collective-permute-start.15 = (bf16[512,128]{1,0:T(8,128)(2,1)S(1)}, bf16[512,128]{1,0:T(8,128)(2,1)S(1)}, u32[]{:S(2)}, u32[]{:S(2)}) collective-permute-start(bf16[512,128]{1,0:T(8,128)(2,1)S(1)} %get-tuple-element.60.refs_1_), channel_id=1, source_target_pairs={{0,8},{4,12},{8,0},{12,4},{1,9},{5,13},{9,1},{13,5},{2,10},{6,14},... | collective-permute-start | bytes 393224 | tf_op jit(solution)/shard_map/ppermute | solution.py:379
  42.7 2.5 %collective-permute-start.17 = (bf16[256,512]{1,0:T(8,128)(2,1)S(1)}, bf16[256,512]{1,0:T(8,128)(2,1)S(1)}, u32[]{:S(2)}, u32[]{:S(2)}) collective-permute-start(bf16[256,512]{1,0:T(8,128)(2,1)S(1)} %pair.2.mine_ref), channel_id=1, source_target_pairs={{2,10},{6,14},{8,0},{12,4},{3,11},{7,15},{9,1},{13,5},{18,26},{22,... | collective-permute-start | bytes 786440 | tf_op jit(solution)/shard_map/ppermute | solution.py:411
  45.2 1.3 %collective-permute-start.20 = (bf16[256,512]{1,0:T(8,128)(2,1)S(1)}, bf16[256,512]{1,0:T(8,128)(2,1)S(1)}, u32[]{:S(2)}, u32[]{:S(2)}) collective-permute-start(bf16[256,512]{1,0:T(8,128)(2,1)S(1)} %pair.3), channel_id=1, source_target_pairs={{0,2},{4,6},{10,8},{14,12},{1,3},{5,7},{11,9},{15,13},{16,18},{20,... | collective-permute-start | bytes 786440 | tf_op jit(solution)/shard_map/ppermute | solution.py:413
  46.5 3.7 %collective-permute-start.19 = (bf16[256,512]{1,0:T(8,128)(2,1)S(1)}, bf16[256,512]{1,0:T(8,128)(2,1)S(1)}, u32[]{:S(2)}, u32[]{:S(2)}) collective-permute-start(bf16[256,512]{1,0:T(8,128)(2,1)S(1)} %pair.3), channel_id=1, source_target_pairs={{2,8},{6,12},{8,2},{12,6},{3,9},{7,13},{9,3},{13,7},{18,24},{22,28... | collective-permute-start | bytes 786440 | tf_op jit(solution)/shard_map/ppermute | solution.py:412
  50.3 1.5 %collective-permute-start.16 = (bf16[512,128]{1,0:T(8,128)(2,1)S(1)}, bf16[512,128]{1,0:T(8,128)(2,1)S(1)}, u32[]{:S(2)}, u32[]{:S(2)}) collective-permute-start(bf16[512,128]{1,0:T(8,128)(2,1)S(1)} %collective-permute-done.15.refs_3_), channel_id=1, source_target_pairs={{0,4},{4,0},{8,12},{12,8},{1,5},{5,1},{9,13},{13,9},{2,6},{6,2},{1... | collective-permute-start | bytes 393224 | tf_op jit(solution)/shard_map/ppermute | solution.py:381
  51.8 1.9 %query.1 = (bf16[512,256]{1,0:T(8,128)(2,1)}, f32[512,256]{1,0:T(8,128)S(1)}, f32[512,256]{1,0:T(8,128)S(1)}) custom-call(bf16[512,256]{1,0:T(8,128)(2,1)S(1)} %bitcast.21, bf16[512,256]{1,0:T(8,128)(2,1)S(1)} %get-tuple-element.38.refs_5_.refs_4_.qf_ref, bf16[512,256]{1,0:T(8,128)(2,1)S(1)} %copy-done.5, bf16[512,256]{1,0:T(8,128)(2,1)S(1)} %bitcast.16, ...), custom_call_target="tpu_custom_call" | custom-call | flops 99999997952 | bytes 1 | tf_op jit(solution)/shard_map/query/pallas_call | solution.py:45
  53.8 9.2 %collective-permute-done.16.refs_4_ = bf16[512,128]{1,0:T(8,128)(2,1)S(1)} collective-permute-done((bf16[512,128]{1,0:T(8,128)(2,1)S(1)}, bf16[512,128]{1,0:T(8,128)(2,1)S(1)}, u32[]{:S(2)}, u32[]{:S(2)}) %collective-permute-start.16) | collective-permute-done | bytes 131104 | tf_op jit(solution)/shard_map/ppermute | solution.py:381
  63.0 1.9 %key.1 = (bf16[512,256]{1,0:T(8,128)(2,1)}, bf16[512,256]{1,0:T(8,128)(2,1)}) custom-call(s32[2,4,8]{2,1,0:T(4,128)S(1)} %bitcast.24, bf16[512,128]{1,0:T(8,128)(2,1)S(1)} %get-tuple-element.60.refs_1_, bf16[512,128]{1,0:T(8,128)(2,1)S(1)} %collective-permute-done.14.refs_2_, bf16[512,128]{1,0:T(8,128)(2,1)S(1)} %collective-permute-done.15.refs_3_, ...), custom_call_target="tpu_custom_call" | custom-call | flops 1 | bytes 1 | tf_op jit(solution)/shard_map/key/pallas_call | solution.py:45
  64.9 7.2 %collective-permute-done.19.b_ref = bf16[256,512]{1,0:T(8,128)(2,1)S(1)} collective-permute-done((bf16[256,512]{1,0:T(8,128)(2,1)S(1)}, bf16[256,512]{1,0:T(8,128)(2,1)S(1)}, u32[]{:S(2)}, u32[]{:S(2)}) %collective-permute-start.19) | collective-permute-done | bytes 262176 | tf_op jit(solution)/shard_map/ppermute | solution.py:412
  72.1 1.0 %final.1 = f32[512,256]{1,0:T(8,128)} custom-call(bf16[256,512]{1,0:T(8,128)(2,1)S(1)} %pair.2.mine_ref, bf16[256,512]{1,0:T(8,128)(2,1)S(1)} %collective-permute-done.17.a_ref, bf16[256,512]{1,0:T(8,128)(2,1)S(1)} %collective-permute-done.19.b_ref, bf16[256,512]{1,0:T(8,128)(2,1)S(1)} %collective-permute-done.20.c_ref), custom_call_target="tpu_custom_call" | custom-call | flops 1 | bytes 1 | tf_op jit(solution)/shard_map/final/pallas_call | solution.py:45
  (44 shorter events, 2.7 us)
Async XLA Ops:
  0.6 9.0 %copy-start.2 = (bf16[1,512,256]{2,1,0:T(8,128)(2,1)S(1)}, bf16[1,512,256]{2,1,0:T(8,128)(2,1)}, u32[]{:S(2)}) copy-start(bf16[1,512,256]{2,1,0:T(8,128)(2,1)} %param.8) | copy-start | bytes 786436
  0.6 7.2 %copy-start = (bf16[1,512,2048]{2,1,0:T(8,128)(2,1)S(1)}, bf16[1,512,2048]{2,1,0:T(8,128)(2,1)}, u32[]{:S(2)}) copy-start(bf16[1,512,2048]{2,1,0:T(8,128)(2,1)} %param.11) | copy-start | bytes 6291460
  0.7 9.0 %copy-start.6 = (bf16[1,512,256]{2,1,0:T(8,128)(2,1)S(1)}, bf16[1,512,256]{2,1,0:T(8,128)(2,1)}, u32[]{:S(2)}) copy-start(bf16[1,512,256]{2,1,0:T(8,128)(2,1)} %param.6) | copy-start | bytes 786436
  0.7 17.7 %copy-start.8 = (s32[2,8,4]{1,2,0:T(4,128)S(1)}, s32[2,8,4]{1,2,0:T(4,128)}, u32[]{:S(2)}) copy-start(s32[2,8,4]{1,2,0:T(4,128)} %param.9) | copy-start | bytes 772
  3.8 7.5 %collective-permute-start.2 = (bf16[512,128]{1,0:T(8,128)(2,1)}, bf16[512,128]{1,0:T(8,128)(2,1)S(1)}, u32[]{:S(2)}, u32[]{:S(2)}) collective-permute-start(bf16[512,128]{1,0:T(8,128)(2,1)} %get-tuple-element.36.refs_1_), channel_id=1, source_target_pairs={{0,12},{4,0},{8,4},{12,8},{1,13},{5,1},{9,5},{13,9},{2,14},{6,2},{... | collective-permute-start | bytes 393224 | tf_op jit(solution)/shard_map/ppermute | solution.py:299
  7.2 11.2 %collective-permute-start.1 = (bf16[512,128]{1,0:T(8,128)(2,1)}, bf16[512,128]{1,0:T(8,128)(2,1)S(1)}, u32[]{:S(2)}, u32[]{:S(2)}) collective-permute-start(bf16[512,128]{1,0:T(8,128)(2,1)} %get-tuple-element.36.refs_1_), channel_id=1, source_target_pairs={{0,8},{4,12},{8,0},{12,4},{1,9},{5,13},{9,1},{13,5},{2,10},{6,14},... | collective-permute-start | bytes 393224 | tf_op jit(solution)/shard_map/ppermute | solution.py:299
  7.2 11.2 %collective-permute-start = (bf16[512,128]{1,0:T(8,128)(2,1)}, bf16[512,128]{1,0:T(8,128)(2,1)S(1)}, u32[]{:S(2)}, u32[]{:S(2)}) collective-permute-start(bf16[512,128]{1,0:T(8,128)(2,1)} %get-tuple-element.36.refs_1_), channel_id=1, source_target_pairs={{0,4},{4,8},{8,12},{12,0},{1,5},{5,9},{9,13},{13,1},{2,6},{6,10},{... | collective-permute-start | bytes 393224 | tf_op jit(solution)/shard_map/ppermute | solution.py:299
  7.6 18.4 %collective-permute-start.6 = (bf16[2048,128]{1,0:T(8,128)(2,1)}, bf16[2048,128]{1,0:T(8,128)(2,1)S(1)}, u32[]{:S(2)}, u32[]{:S(2)}) collective-permute-start(bf16[2048,128]{1,0:T(8,128)(2,1)} %get-tuple-element.43), channel_id=1, source_target_pairs={{0,2},{2,0},{1,3},{3,1},{4,6},{6,4},{5,7},{7,5},{8,10},{10,8},{9,1... | collective-permute-start | bytes 1572872 | tf_op jit(solution)/shard_map/ppermute | solution.py:290
  7.9 15.8 %collective-permute-start.4 = (bf16[512,2048]{1,0:T(8,128)(2,1)S(1)}, bf16[512,2048]{1,0:T(8,128)(2,1)S(1)}, u32[]{:S(2)}, u32[]{:S(2)}) collective-permute-start(bf16[512,2048]{1,0:T(8,128)(2,1)S(1)} %bitcast.9), channel_id=1, source_target_pairs={{0,1},{1,0},{2,3},{3,2},{4,5},{5,4},{6,7},{7,6},{8,9},{9,8},{10,11... | collective-permute-start | bytes 6291464 | tf_op jit(solution)/shard_map/ppermute | solution.py:290
  9.7 1.0 %copy-start.4 = (bf16[512,256]{1,0:T(8,128)(2,1)S(1)}, bf16[512,256]{1,0:T(8,128)(2,1)}, u32[]{:S(2)}) copy-start(bf16[512,256]{1,0:T(8,128)(2,1)} %get-tuple-element.37.kf_ref.refs_6_) | copy-start | bytes 786436
  18.4 0.9 %copy-start.9 = (bf16[512,128]{1,0:T(8,128)(2,1)S(1)}, bf16[512,128]{1,0:T(8,128)(2,1)}, u32[]{:S(2)}) copy-start(bf16[512,128]{1,0:T(8,128)(2,1)} %get-tuple-element.36.refs_1_) | copy-start | bytes 393220
  21.1 2.5 %collective-permute-start.5 = (bf16[512,256]{1,0:T(8,128)(2,1)}, bf16[512,256]{1,0:T(8,128)(2,1)S(1)}, u32[]{:S(2)}, u32[]{:S(2)}) collective-permute-start(bf16[512,256]{1,0:T(8,128)(2,1)} %get-tuple-element.40.attn_ref), channel_id=1, source_target_pairs={{0,1},{1,0},{2,3},{3,2},{4,5},{5,4},{6,7},{7,6},{8,9},{9,8},{10,11... | collective-permute-start | bytes 786440 | tf_op jit(solution)/shard_map/ppermute | solution.py:290
  22.3 8.1 %collective-permute-start.3 = (bf16[512,256]{1,0:T(8,128)(2,1)}, bf16[512,256]{1,0:T(8,128)(2,1)S(1)}, u32[]{:S(2)}, u32[]{:S(2)}) collective-permute-start(bf16[512,256]{1,0:T(8,128)(2,1)} %get-tuple-element.40.attn_ref), channel_id=1, source_target_pairs={{0,2},{2,0},{1,3},{3,1},{4,6},{6,4},{5,7},{7,5},{8,10},{10,8},{9,1... | collective-permute-start | bytes 786440 | tf_op jit(solution)/shard_map/ppermute | solution.py:290
  23.7 1.0 %copy-start.7 = (bf16[512,256]{1,0:T(8,128)(2,1)S(1)}, bf16[512,256]{1,0:T(8,128)(2,1)}, u32[]{:S(2)}) copy-start(bf16[512,256]{1,0:T(8,128)(2,1)} %get-tuple-element.40.attn_ref) | copy-start | bytes 786436
  25.4 11.9 %collective-permute-start.12 = (bf16[256,512]{1,0:T(8,128)(2,1)S(1)}, bf16[256,512]{1,0:T(8,128)(2,1)S(1)}, u32[]{:S(2)}, u32[]{:S(2)}) collective-permute-start(bf16[256,512]{1,0:T(8,128)(2,1)S(1)} %get-tuple-element.41), channel_id=1, source_target_pairs={{0,4},{4,0},{8,12},{12,8},{1,5},{5,1},{9,13},{13,9},{2,6},{6,2},{1... | collective-permute-start | bytes 786440 | tf_op jit(solution)/shard_map/ppermute | solution.py:357
  30.4 3.0 %collective-permute-start.7 = (bf16[128,256]{1,0:T(8,128)(2,1)S(1)}, bf16[128,256]{1,0:T(8,128)(2,1)S(1)}, u32[]{:S(2)}, u32[]{:S(2)}) collective-permute-start(bf16[128,256]{1,0:T(8,128)(2,1)S(1)} %get-tuple-element.46), channel_id=1, source_target_pairs={{0,1},{1,0},{2,3},{3,2},{4,5},{5,4},{6,7},{7,6},{8,9},{9,8},{10,11... | collective-permute-start | bytes 196616 | tf_op jit(solution)/shard_map/ppermute | solution.py:290
  31.3 2.2 %collective-permute-start.8 = (bf16[128,256]{1,0:T(8,128)(2,1)S(1)}, bf16[128,256]{1,0:T(8,128)(2,1)S(1)}, u32[]{:S(2)}, u32[]{:S(2)}) collective-permute-start(bf16[128,256]{1,0:T(8,128)(2,1)S(1)} %get-tuple-element.47), channel_id=1, source_target_pairs={{0,1},{1,0},{2,3},{3,2},{4,5},{5,4},{6,7},{7,6},{8,9},{9,8},{10,11... | collective-permute-start | bytes 196616 | tf_op jit(solution)/shard_map/ppermute | solution.py:290
  31.4 6.0 %collective-permute-start.11 = (bf16[512,128]{1,0:T(8,128)(2,1)S(1)}, bf16[512,128]{1,0:T(8,128)(2,1)S(1)}, u32[]{:S(2)}, u32[]{:S(2)}) collective-permute-start(bf16[512,128]{1,0:T(8,128)(2,1)S(1)} %get-tuple-element.52), channel_id=1, source_target_pairs={{0,2},{2,0},{1,3},{3,1},{4,6},{6,4},{5,7},{7,5},{8,10},{10,8},{9,1... | collective-permute-start | bytes 393224 | tf_op jit(solution)/shard_map/ppermute | solution.py:290
  31.6 8.1 %collective-permute-start.13 = (bf16[512,128]{1,0:T(8,128)(2,1)S(1)}, bf16[512,128]{1,0:T(8,128)(2,1)S(1)}, u32[]{:S(2)}, u32[]{:S(2)}) collective-permute-start(bf16[512,128]{1,0:T(8,128)(2,1)S(1)} %get-tuple-element.44), channel_id=1, source_target_pairs={{0,3},{1,2},{2,1},{3,0},{4,7},{5,6},{6,5},{7,4},{8,11},{9,10},{10,... | collective-permute-start | bytes 393224 | tf_op jit(solution)/shard_map/ppermute | solution.py:352
  33.4 1.3 %collective-permute-start.9 = (bf16[128,256]{1,0:T(8,128)(2,1)S(1)}, bf16[128,256]{1,0:T(8,128)(2,1)S(1)}, u32[]{:S(2)}, u32[]{:S(2)}) collective-permute-start(bf16[128,256]{1,0:T(8,128)(2,1)S(1)} %get-tuple-element.48), channel_id=1, source_target_pairs={{0,1},{1,0},{2,3},{3,2},{4,5},{5,4},{6,7},{7,6},{8,9},{9,8},{10,11... | collective-permute-start | bytes 196616 | tf_op jit(solution)/shard_map/ppermute | solution.py:290
  33.5 3.0 %copy-start.1 = (bf16[4096,256]{1,0:T(8,128)(2,1)S(1)}, bf16[4096,256]{1,0:T(8,128)(2,1)}, u32[]{:S(2)}) copy-start(bf16[4096,256]{1,0:T(8,128)(2,1)} %w_ref.3) | copy-start | bytes 6291460
  33.5 1.4 %collective-permute-start.10 = (bf16[128,256]{1,0:T(8,128)(2,1)S(1)}, bf16[128,256]{1,0:T(8,128)(2,1)S(1)}, u32[]{:S(2)}, u32[]{:S(2)}) collective-permute-start(bf16[128,256]{1,0:T(8,128)(2,1)S(1)} %get-tuple-element.49), channel_id=1, source_target_pairs={{0,1},{1,0},{2,3},{3,2},{4,5},{5,4},{6,7},{7,6},{8,9},{9,8},{10,11... | collective-permute-start | bytes 196616 | tf_op jit(solution)/shard_map/ppermute | solution.py:290
  35.9 9.3 %collective-permute-start.18 = (bf16[256,512]{1,0:T(8,128)(2,1)S(1)}, bf16[256,512]{1,0:T(8,128)(2,1)S(1)}, u32[]{:S(2)}, u32[]{:S(2)}) collective-permute-start(bf16[256,512]{1,0:T(8,128)(2,1)S(1)} %get-tuple-element.50), channel_id=1, source_target_pairs={{0,4},{4,0},{8,12},{12,8},{1,5},{5,1},{9,13},{13,9},{2,6},{6,2},{1... | collective-permute-start | bytes 786440 | tf_op jit(solution)/shard_map/ppermute | solution.py:365
  39.7 12.1 %copy-start.5 = (bf16[512,256]{1,0:T(8,128)(2,1)S(1)}, bf16[512,256]{1,0:T(8,128)(2,1)}, u32[]{:S(2)}) copy-start(bf16[512,256]{1,0:T(8,128)(2,1)} %get-tuple-element.37.kf_ref.refs_6_) | copy-start | bytes 786436
  40.3 10.0 %collective-permute-start.15 = (bf16[512,128]{1,0:T(8,128)(2,1)S(1)}, bf16[512,128]{1,0:T(8,128)(2,1)S(1)}, u32[]{:S(2)}, u32[]{:S(2)}) collective-permute-start(bf16[512,128]{1,0:T(8,128)(2,1)S(1)} %get-tuple-element.60.refs_1_), channel_id=1, source_target_pairs={{0,8},{4,12},{8,0},{12,4},{1,9},{5,13},{9,1},{13,5},{2,10},{6,14},... | collective-permute-start | bytes 393224 | tf_op jit(solution)/shard_map/ppermute | solution.py:379
  42.7 7.6 %collective-permute-start.14 = (bf16[512,128]{1,0:T(8,128)(2,1)S(1)}, bf16[512,128]{1,0:T(8,128)(2,1)S(1)}, u32[]{:S(2)}, u32[]{:S(2)}) collective-permute-start(bf16[512,128]{1,0:T(8,128)(2,1)S(1)} %get-tuple-element.60.refs_1_), channel_id=1, source_target_pairs={{0,4},{4,0},{8,12},{12,8},{1,5},{5,1},{9,13},{13,9},{2,6},{6,2},{1... | collective-permute-start | bytes 393224 | tf_op jit(solution)/shard_map/ppermute | solution.py:380
  42.7 22.2 %collective-permute-start.17 = (bf16[256,512]{1,0:T(8,128)(2,1)S(1)}, bf16[256,512]{1,0:T(8,128)(2,1)S(1)}, u32[]{:S(2)}, u32[]{:S(2)}) collective-permute-start(bf16[256,512]{1,0:T(8,128)(2,1)S(1)} %pair.2.mine_ref), channel_id=1, source_target_pairs={{2,10},{6,14},{8,0},{12,4},{3,11},{7,15},{9,1},{13,5},{18,26},{22,... | collective-permute-start | bytes 786440 | tf_op jit(solution)/shard_map/ppermute | solution.py:411
  45.2 19.6 %collective-permute-start.20 = (bf16[256,512]{1,0:T(8,128)(2,1)S(1)}, bf16[256,512]{1,0:T(8,128)(2,1)S(1)}, u32[]{:S(2)}, u32[]{:S(2)}) collective-permute-start(bf16[256,512]{1,0:T(8,128)(2,1)S(1)} %pair.3), channel_id=1, source_target_pairs={{0,2},{4,6},{10,8},{14,12},{1,3},{5,7},{11,9},{15,13},{16,18},{20,... | collective-permute-start | bytes 786440 | tf_op jit(solution)/shard_map/ppermute | solution.py:413
  46.5 25.5 %collective-permute-start.19 = (bf16[256,512]{1,0:T(8,128)(2,1)S(1)}, bf16[256,512]{1,0:T(8,128)(2,1)S(1)}, u32[]{:S(2)}, u32[]{:S(2)}) collective-permute-start(bf16[256,512]{1,0:T(8,128)(2,1)S(1)} %pair.3), channel_id=1, source_target_pairs={{2,8},{6,12},{8,2},{12,6},{3,9},{7,13},{9,3},{13,7},{18,24},{22,28... | collective-permute-start | bytes 786440 | tf_op jit(solution)/shard_map/ppermute | solution.py:412
  50.3 12.7 %collective-permute-start.16 = (bf16[512,128]{1,0:T(8,128)(2,1)S(1)}, bf16[512,128]{1,0:T(8,128)(2,1)S(1)}, u32[]{:S(2)}, u32[]{:S(2)}) collective-permute-start(bf16[512,128]{1,0:T(8,128)(2,1)S(1)} %collective-permute-done.15.refs_3_), channel_id=1, source_target_pairs={{0,4},{4,0},{8,12},{12,8},{1,5},{5,1},{9,13},{13,9},{2,6},{6,2},{1... | collective-permute-start | bytes 393224 | tf_op jit(solution)/shard_map/ppermute | solution.py:381
  51.8 11.2 %copy-start.3 = (bf16[1,512,256]{2,1,0:T(8,128)(2,1)S(1)}, bf16[1,512,256]{2,1,0:T(8,128)(2,1)}, u32[]{:S(2)}) copy-start(bf16[1,512,256]{2,1,0:T(8,128)(2,1)} %param.7) | copy-start | bytes 786436

commit v6 on v5

--- a/solution.py
+++ b/solution.py
@@ -115,9 +115,17 @@
 
 
 def split_body(x_ref, *outs):
-    rows = outs[0].shape[0]
-    for i, out in enumerate(outs):
-        out[...] = x_ref[i * rows : (i + 1) * rows, :]
+    at = 0
+    for out in outs:
+        out[...] = x_ref[at : at + out.shape[0], :]
+        at += out.shape[0]
+
+
+def join_body(*refs):
+    *parts, out_ref = refs
+    rows = parts[0].shape[0]
+    for i, part in enumerate(parts):
+        out_ref[i * rows : (i + 1) * rows, :] = part[...]
 
 
 def causal():
@@ -144,7 +152,7 @@
 
 
 def in_order(z, s):
-    return 0
+    return s
 
 
 def by_shift(z, s):
@@ -153,7 +161,11 @@
 
 
 def by_flip(z, s):
-    return lax.bitwise_xor(z, jnp.int32(s))
+    return lax.bitwise_xor(z, jnp.int32((0, 2, 1, 3)[s]))
+
+
+def views(parts, rows):
+    return [p.at[i * rows : (i + 1) * rows] for p in parts for i in range(p.shape[0] // rows)]
 
 
 def numer_body(dims, np_, *refs):
@@ -165,8 +177,8 @@
         n, h = divmod(i, heads)
         query_block = z * nb + n
         total = jnp.zeros((DH, DH), F32)
-        for s, part in enumerate(parts):
-            for b in range(part.shape[0] // (heads * DH)):
+        for s, part in enumerate(views(parts, nb * heads * DH)):
+            for b in range(nb):
                 times = count(lay_ref, h, query_block, owner_of(z, s) * nb + b)
                 total = total + times * part[mat(b * heads + h), :].astype(F32)
         carried = total.astype(BF16)
@@ -215,8 +227,8 @@
         n, h = divmod(i, heads)
         key_block = z * nb + n
         total = jnp.zeros((DH, DH), F32)
-        for s, part in enumerate(parts):
-            for b in range(part.shape[0] // (heads * DH)):
+        for s, part in enumerate(views(parts, nb * heads * DH)):
+            for b in range(nb):
                 times = count(lay_ref, h, owner_of(z, s) * nb + b, key_block)
                 total = total + times * part[mat(b * heads + h), :].astype(F32)
         sg = total.astype(BF16)
@@ -254,32 +266,41 @@
     sib_ref[...] = mm(og_sib_ref[...], w_ref[...], NN).astype(BF16)
 
 
-def weight_body(attn_ref, og_ref, og_sib_ref, *refs):
-    *sib_refs, give_ref, keep_ref = refs
-    step = sib_refs[0].shape[0]
-    rows = give_ref.shape[1]
+def weight_body(n_out, attn_ref, og_ref, og_sib_ref, *refs):
+    sibs, outs = refs[:-n_out], refs[-n_out:]
+    rows = outs[0].shape[1]
+    pieces = len(outs) // 2
     parity, core = lax.rem(lax.axis_index("seq"), 2), lax.axis_index("dp")
-
-    def part(pair):
+    for which, pair in enumerate((1 - parity, parity)):
         at = pl.ds(pl.multiple_of((2 * pair + core) * rows, rows), rows)
         total = mm(attn_ref[...], og_ref[:, at], TN)
-        for i, sib in enumerate(sib_refs):
-            total = total + mm(sib[...], og_sib_ref[i * step : (i + 1) * step, at], TN)
-        return total
-
-    give_ref[...] = part(1 - parity).astype(BF16)
-    keep_ref[...] = part(parity)
+        row = 0
+        for sib in sibs:
+            total = total + mm(sib[...], og_sib_ref[row : row + sib.shape[0], at], TN)
+            row += sib.shape[0]
+        for i in range(pieces):
+            out = outs[which * pieces + i]
+            size = out.shape[0]
+            out[...] = total[i * size : (i + 1) * size, :].astype(out.dtype)
 
 
 def pair_body(keep_ref, got_ref, out_ref):
     out_ref[...] = (keep_ref[...] + got_ref[...].astype(F32)).astype(BF16)
 
 
-def final_body(mine_ref, a_ref, b_ref, c_ref, out_ref):
+def cross_body(i, keep_ref, got_ref, mine_ref, send_ref, stay_ref):
     home = lax.axis_index("seq") // 2 == lax.axis_index("head")
-    mine = jnp.where(home, mine_ref[...].astype(F32), 0.0)
-    total = mine + a_ref[...].astype(F32) + b_ref[...].astype(F32) + c_ref[...].astype(F32)
-    out_ref[...] = total.T
+    cross = (keep_ref[...].astype(F32) + got_ref[...].astype(F32)).astype(BF16)
+    mine = mine_ref[mat(i), :]
+    send_ref[...] = jnp.where(home, cross, mine)
+    stay_ref[...] = jnp.where(home, mine, cross)
+
+
+def final_body(*refs):
+    *got, out_ref = refs
+    for i in range(len(got) // 2):
+        total = got[2 * i][...].astype(F32) + got[2 * i + 1][...].astype(F32)
+        out_ref[:, mat(i)] = total.T
 
 
 def after(x, *deps):
@@ -334,6 +355,13 @@
     if not paired:
         og = lax.all_gather(og, "head", axis=1, tiled=True)
         d_own = jnp.dot(og, out_weight, preferred_element_type=F32)
+    if paired:
+        column = sds((tokens, DH), BF16)
+        d_same, d_sib = call(other_body, (column, column), (after(og, qf), og_sib, w_other), 0, "other")
+        across = [(h * 2 + c, (1 - h) * 2 + 1 - c) for h in range(2) for c in range(2)]
+        intra = after(intra, d_sib)
+        d_same = swap(d_same, "head")
+        d_sib = lax.ppermute(d_sib, ("head", "dp"), across)
     carried, num, attn = call(
         functools.partial(numer_body, (nb, heads, first_owner), len(parts)),
         (mats, flat, rows16),
@@ -343,29 +371,9 @@
     )
     if paired:
         attn_other = swap(attn, "head")
-        column = sds((tokens, DH), BF16)
-        sib_late = after(og_sib, attn)
-        d_same, d_sib = call(other_body, (column, column), (og, sib_late, w_other), 0, "other")
-        across = [(h * 2 + c, (1 - h) * 2 + 1 - c) for h in range(2) for c in range(2)]
-        d_sib_sent = d_sib
-        d_same = swap(d_same, "head")
-        d_sib = lax.ppermute(d_sib, ("head", "dp"), across)
-        block = (cols, width // 4)
-        outs = (sds(block, BF16), sds(block, F32))
-        neighbours = [(0, 1), (1, 0), (2, 3), (3, 2)]
-        give_a, keep_a = call(weight_body, outs, (attn, og, og_sib, swap(attn, "dp")), 0, "weight")
-        got_a = lax.ppermute(give_a, "seq", neighbours)
-        attn_other = after(attn_other, give_a, d_sib_sent)
-        quarter = sds((tokens // 4, cols), BF16)
-        pieces = call(split_body, (quarter,) * 4, (attn_other,), 0, "split")
-        pieces = [swap(piece, "dp") for piece in pieces]
-        give_b, keep_b = call(
-            weight_body, outs, (attn_other, og, og_sib, *pieces), 0, "weight"
-        )
-        got_b = lax.ppermute(give_b, "seq", neighbours)
-        d_own = own_partial(after(og, give_b), out_weight)
-        (mine,) = call(pair_body, (sds(keep_a.shape, BF16),), (keep_a, got_a), 0, "pair")
-        d_parts = (d_own, after(d_same, give_b, mine), d_sib)
+        attn_sib = swap(attn, "dp")
+        d_own = own_partial(after(og, attn), out_weight)
+        d_parts = (d_own, d_same, d_sib)
     else:
         d_parts = (d_own,)
     dnum, cg = call(
@@ -376,10 +384,39 @@
         "dnum",
     )
     if paired:
+        neighbours = [(0, 1), (1, 0), (2, 3), (3, 2)]
         two = lax.ppermute(cg, "seq", [(i, i ^ 2) for i in range(4)])
-        one = lax.ppermute(cg, "seq", neighbours)
-        cparts = [cg, one, two, lax.ppermute(after(two, one), "seq", neighbours)]
+        block, half = (cols, width // 4), sds((DH, width // 4), BF16)
+        give, keep = call(
+            functools.partial(weight_body, 2),
+            (sds(block, BF16), sds(block, F32)),
+            (after(attn, cg), og, og_sib, attn_sib),
+            0,
+            "weight",
+        )
+        got = lax.ppermute(give, "seq", neighbours)
+        attn_other = after(attn_other, give)
+        third = tokens // 48 * 16
+        sizes = (third, third, tokens - 2 * third)
+        cuts = call(split_body, tuple(sds((n, cols), BF16) for n in sizes), (attn_other,), 0, "split")
+        pieces = call(
+            functools.partial(weight_body, 2 * heads),
+            (half,) * (2 * heads),
+            (attn_other, og, og_sib, *[swap(cut, "dp") for cut in cuts]),
+            0,
+            "weight",
+        )
+        give_b, keep_b = pieces[:heads], pieces[heads:]
+        beside = [((s ^ 1) * 2 + 1 - h, s * 2 + h) for s in range(4) for h in range(2)]
+        crossed = [
+            (swap(k, "head"), lax.ppermute(g, ("seq", "head"), beside)) for k, g in zip(keep_b, give_b)
+        ]
+        (joined,) = call(
+            join_body, (sds((2 * cg.shape[0], DH), BF16),), (cg, after(two, give_b[0])), 0, "join"
+        )
+        cparts = [cg, two, lax.ppermute(joined, "seq", neighbours)]
         second_owner = by_flip
+        (mine,) = call(pair_body, (sds(block, BF16),), (keep, got), 0, "pair")
     else:
         cparts, second_owner = gather_parts(cg, seq_size), first_owner
     dq, dkp, dvp = call(
@@ -397,24 +434,11 @@
         "key",
     )
     if paired:
-        (cross,) = call(pair_body, (sds(keep_b.shape, BF16),), (keep_b, got_b), 0, "pair")
-        to_line, to_side, to_both = [], [], []
-        for s in range(4):
-            for h in range(2):
-                if s // 2 == h:
-                    to_side.append((s * 2 + h, s * 2 + 1 - h))
-                else:
-                    to_line.append((s * 2 + h, (s ^ 2) * 2 + h))
-                    to_both.append((s * 2 + h, (s ^ 2) * 2 + 1 - h))
-        axes = ("seq", "head")
-        arrived = (
-            lax.ppermute(mine, axes, to_line),
-            lax.ppermute(cross, axes, to_both),
-            lax.ppermute(cross, axes, to_side),
-        )
-        (weight_grad,) = call(
-            final_body, (sds(mine.shape[::-1], F32),), (mine, *arrived), 0, "final"
-        )
+        sums = []
+        for i, (k, g) in enumerate(crossed):
+            send, stay = call(functools.partial(cross_body, i), (half, half), (k, g, mine), 0, "cross")
+            sums += [stay, lax.ppermute(send, "seq", [(s, s ^ 2) for s in range(4)])]
+        (weight_grad,) = call(final_body, (sds(block[::-1], F32),), tuple(sums), 0, "final")
     else:
         weight_grad = lax.psum_scatter(
             lax.dot_general(og, attn, TN, preferred_element_type=F32).astype(BF16),

time: 73.3 us -> 65.6 us (0.89)
  the two profiles are of different devices: /device:TPU:3 before, /device:TPU:0 now
where the time goes in v6:
time: 65.6 us; the launch traced here: 65.4 us
  starting transfers between devices  29.5 us (45%)
  waiting for transfers between devices  19.1 us (29%)
  Pallas kernels  14.7 us (22%)
  local copies, waits for them, and re-layouts  1.35 us (2%)
  between operations  0.85 us (1%)
    ppermute x10, waiting for transfers between devices, swap(): return lax.ppermute(x, axis, [(0, 1), (1, 0)])  13.3 us
    pallas_call x14, Pallas kernels, call(): pl.pallas_call(body, out_shape=outs, in_specs=[SM if a.dtype == jnp.int32...  11 us
    ppermute x10, starting transfers between devices, swap(): return lax.ppermute(x, axis, [(0, 1), (1, 0)])  8.55 us
    ppermute x2, starting transfers between devices, per_device(): lax.ppermute(g, ('seq', 'head'), beside)  6 us
    ppermute x2, waiting for transfers between devices, per_device(): sums += [stay, lax.ppermute(send, 'seq', [(s, s ^ 2) for s in range(4)])]  5.71 us
    ppermute x3, starting transfers between devices, gather_parts(): parts.append(lax.ppermute(x, 'seq', pairs))  5.51 us
    ppermute x2, starting transfers between devices, per_device(): sums += [stay, lax.ppermute(send, 'seq', [(s, s ^ 2) for s in range(4)])]  4.12 us
    pallas_call x1, Pallas kernels, begin(): pl.pallas_call(begin_body, out_shape=(sds((tokens, cols), BF16), sds((cou...  2.95 us
  transfers between devices with their start and end apart: 21, of which 8 were waited for; matrix products, arithmetic and copies ran while one was open for 0% of the time, Pallas kernels for 21%

profile of v6, /device:TPU:0, one launch (start us, length us, event | category | flops | bytes accessed | tf_op | source)
XLA Modules:
  0.0 65.4 jit_solution(8737241743247050902)
XLA Ops:
  1.2 3.0 %begin.1 = (bf16[512,256]{1,0:T(8,128)(2,1)}, bf16[512,128]{1,0:T(8,128)(2,1)}, bf16[2048,128]{1,0:T(8,128)(2,1)}) custom-call(bf16[512,256]{1,0:T(8,128)(2,1)} %bitcast.18, bf16[512,256]{1,0:T(8,128)(2,1)} %bitcast.14, bf16[4096,256]{1,0:T(8,128)(2,1)} %w_ref.3), custom_call_target="tpu_custom_call" | custom-call | flops 1 | bytes 1 | tf_op jit(solution)/shard_map/begin/pallas_call | solution.py:96
  4.1 2.7 %collective-permute-start.4 = (bf16[2048,128]{1,0:T(8,128)(2,1)}, bf16[2048,128]{1,0:T(8,128)(2,1)S(1)}, u32[]{:S(2)}, u32[]{:S(2)}) collective-permute-start(bf16[2048,128]{1,0:T(8,128)(2,1)} %get-tuple-element.47), channel_id=1, source_target_pairs={{0,2},{2,0},{1,3},{3,1},{4,6},{6,4},{5,7},{7,5},{8,10},{10,8},{9,1... | collective-permute-start | bytes 1572872 | tf_op jit(solution)/shard_map/ppermute | solution.py:311
  6.9 1.6 %collective-permute-start = (bf16[512,128]{1,0:T(8,128)(2,1)}, bf16[512,128]{1,0:T(8,128)(2,1)S(1)}, u32[]{:S(2)}, u32[]{:S(2)}) collective-permute-start(bf16[512,128]{1,0:T(8,128)(2,1)} %get-tuple-element.42.refs_1_), channel_id=1, source_target_pairs={{0,4},{4,8},{8,12},{12,0},{1,5},{5,9},{9,13},{13,1},{2,6},{6,10},{... | collective-permute-start | bytes 393224 | tf_op jit(solution)/shard_map/ppermute | solution.py:320
  8.4 2.6 %collective-permute-start.1 = (bf16[512,128]{1,0:T(8,128)(2,1)}, bf16[512,128]{1,0:T(8,128)(2,1)S(1)}, u32[]{:S(2)}, u32[]{:S(2)}) collective-permute-start(bf16[512,128]{1,0:T(8,128)(2,1)} %get-tuple-element.42.refs_1_), channel_id=1, source_target_pairs={{0,8},{4,12},{8,0},{12,4},{1,9},{5,13},{9,1},{13,5},{2,10},{6,14},... | collective-permute-start | bytes 393224 | tf_op jit(solution)/shard_map/ppermute | solution.py:320
  11.0 1.3 %collective-permute-start.2 = (bf16[512,128]{1,0:T(8,128)(2,1)}, bf16[512,128]{1,0:T(8,128)(2,1)S(1)}, u32[]{:S(2)}, u32[]{:S(2)}) collective-permute-start(bf16[512,128]{1,0:T(8,128)(2,1)} %get-tuple-element.42.refs_1_), channel_id=1, source_target_pairs={{0,12},{4,0},{8,4},{12,8},{1,13},{5,1},{9,5},{13,9},{2,14},{6,2},{... | collective-permute-start | bytes 393224 | tf_op jit(solution)/shard_map/ppermute | solution.py:320
  12.4 0.9 %copy-done.4 = bf16[512,256]{1,0:T(8,128)(2,1)S(1)} copy-done((bf16[512,256]{1,0:T(8,128)(2,1)S(1)}, bf16[512,256]{1,0:T(8,128)(2,1)}, u32[]{:S(2)}) %copy-start.4) | copy-done | bytes 262168
  13.3 0.7 %scores.1 = (bf16[512,256]{1,0:T(8,128)(2,1)S(1)}, bf16[1024,256]{1,0:T(8,128)(2,1)S(1)}, f32[512,256]{1,0:T(8,128)S(1)}) custom-call(bf16[512,256]{1,0:T(8,128)(2,1)S(1)} %bitcast.20, bf16[512,256]{1,0:T(8,128)(2,1)S(1)} %copy-done.4, bf16[512,256]{1,0:T(8,128)(2,1)S(1)} %bitcast.15), custom_call_target="tpu_custom_call" | custom-call | flops 1 | bytes 1 | tf_op jit(solution)/shard_map/scores/pallas_call | solution.py:45
  14.0 5.5 %collective-permute-done.4.w_ref = bf16[2048,128]{1,0:T(8,128)(2,1)S(1)} collective-permute-done((bf16[2048,128]{1,0:T(8,128)(2,1)}, bf16[2048,128]{1,0:T(8,128)(2,1)S(1)}, u32[]{:S(2)}, u32[]{:S(2)}) %collective-permute-start.4) | collective-permute-done | bytes 524320 | tf_op jit(solution)/shard_map/ppermute | solution.py:311
  19.5 1.2 %other.1 = (bf16[512,128]{1,0:T(8,128)(2,1)S(1)}, bf16[512,128]{1,0:T(8,128)(2,1)S(1)}) custom-call(bf16[512,2048]{1,0:T(8,128)(2,1)S(1)} %bitcast.10, bf16[512,2048]{1,0:T(8,128)(2,1)S(1)} %collective-permute-done.3.og_sib_ref, bf16[2048,128]{1,0:T(8,128)(2,1)S(1)} %collective-permute-done.4.w_ref), custom_call_target="tpu_custom_call" | custom-call | flops 1 | bytes 1 | tf_op jit(solution)/shard_map/other/pallas_call | solution.py:45
  20.8 1.0 %collective-permute-start.6 = (bf16[512,128]{1,0:T(8,128)(2,1)S(1)}, bf16[512,128]{1,0:T(8,128)(2,1)S(1)}, u32[]{:S(2)}, u32[]{:S(2)}) collective-permute-start(bf16[512,128]{1,0:T(8,128)(2,1)S(1)} %get-tuple-element.48), channel_id=1, source_target_pairs={{0,3},{1,2},{2,1},{3,0},{4,7},{5,6},{6,5},{7,4},{8,11},{9,10},{10,... | collective-permute-start | bytes 393224 | tf_op jit(solution)/shard_map/ppermute | solution.py:364
  21.7 0.9 %collective-permute-start.5 = (bf16[512,128]{1,0:T(8,128)(2,1)S(1)}, bf16[512,128]{1,0:T(8,128)(2,1)S(1)}, u32[]{:S(2)}, u32[]{:S(2)}) collective-permute-start(bf16[512,128]{1,0:T(8,128)(2,1)S(1)} %get-tuple-element.52), channel_id=1, source_target_pairs={{0,2},{2,0},{1,3},{3,1},{4,6},{6,4},{5,7},{7,5},{8,10},{10,8},{9,1... | collective-permute-start | bytes 393224 | tf_op jit(solution)/shard_map/ppermute | solution.py:311
  22.7 1.8 %numer.1 = (bf16[512,128]{1,0:T(8,128)(2,1)S(1)}, f32[512,256]{1,0:T(8,128)S(1)}, bf16[512,256]{1,0:T(8,128)(2,1)}) custom-call(s32[2,4,8]{2,1,0:T(4,128)S(1)} %bitcast.23, bf16[512,128]{1,0:T(8,128)(2,1)S(1)} %copy-done.10, bf16[512,128]{1,0:T(8,128)(2,1)S(1)} %collective-permute-done.refs_2_, bf16[512,128]{1,0:T(8,128)(2,1)S(1)} %collective-permute-done.1.refs_3_, ...), custom_call_target="tpu_custom_call" | custom-call | flops 99999997952 | bytes 1 | tf_op jit(solution)/shard_map/numer/pallas_call | solution.py:45
  24.6 1.7 %collective-permute-start.8 = (bf16[512,256]{1,0:T(8,128)(2,1)}, bf16[512,256]{1,0:T(8,128)(2,1)S(1)}, u32[]{:S(2)}, u32[]{:S(2)}) collective-permute-start(bf16[512,256]{1,0:T(8,128)(2,1)} %get-tuple-element.59.attn_ref), channel_id=1, source_target_pairs={{0,2},{2,0},{1,3},{3,1},{4,6},{6,4},{5,7},{7,5},{8,10},{10,8},{9,1... | collective-permute-start | bytes 786440 | tf_op jit(solution)/shard_map/ppermute | solution.py:311
  26.3 0.8 %own_partial.1.refs_0_ = f32[512,256]{1,0:T(8,128)S(1)} custom-call(bf16[512,2048]{1,0:T(8,128)(2,1)S(1)} %bitcast.11, bf16[4096,256]{1,0:T(8,128)(2,1)S(1)} %copy-done.1), custom_call_target="tpu_custom_call" | custom-call | flops 1 | bytes 1 | tf_op jit(solution)/shard_map/own_partial/pallas_call | solution.py:252
  27.1 2.6 %collective-permute-done.5.refs_1_ = bf16[512,128]{1,0:T(8,128)(2,1)S(1)} collective-permute-done((bf16[512,128]{1,0:T(8,128)(2,1)S(1)}, bf16[512,128]{1,0:T(8,128)(2,1)S(1)}, u32[]{:S(2)}, u32[]{:S(2)}) %collective-permute-start.5) | collective-permute-done | bytes 131104 | tf_op jit(solution)/shard_map/ppermute | solution.py:311
  30.7 0.7 %weight.2 = (bf16[256,512]{1,0:T(8,128)(2,1)S(1)}, f32[256,512]{1,0:T(8,128)S(1)}) custom-call(bf16[512,256]{1,0:T(8,128)(2,1)S(1)} %copy-done.7, bf16[512,2048]{1,0:T(8,128)(2,1)S(1)} %bitcast.12, bf16[512,2048]{1,0:T(8,128)(2,1)S(1)} %collective-permute-done.3.og_sib_ref, bf16[512,256]{1,0:T(8,128)(2,1)S(1)} %collective-permute-done.9.refs_0_), custom_call_target="tpu_custom_call" | custom-call | flops 1 | bytes 1 | tf_op jit(solution)/shard_map/weight/pallas_call | solution.py:45
  31.4 1.6 %collective-permute-start.16 = (bf16[256,512]{1,0:T(8,128)(2,1)S(1)}, bf16[256,512]{1,0:T(8,128)(2,1)S(1)}, u32[]{:S(2)}, u32[]{:S(2)}) collective-permute-start(bf16[256,512]{1,0:T(8,128)(2,1)S(1)} %get-tuple-element.60), channel_id=1, source_target_pairs={{0,4},{4,0},{8,12},{12,8},{1,5},{5,1},{9,13},{13,9},{2,6},{6,2},{1... | collective-permute-start | bytes 786440 | tf_op jit(solution)/shard_map/ppermute | solution.py:397
  33.1 2.6 %collective-permute-start.7 = (bf16[512,128]{1,0:T(8,128)(2,1)S(1)}, bf16[512,128]{1,0:T(8,128)(2,1)S(1)}, u32[]{:S(2)}, u32[]{:S(2)}) collective-permute-start(bf16[512,128]{1,0:T(8,128)(2,1)S(1)} %get-tuple-element.58.refs_0_.refs_1_), channel_id=1, source_target_pairs={{0,8},{4,12},{8,0},{12,4},{1,9},{5,13},{9,1},{13,5},{2,10},{6,14},... | collective-permute-start | bytes 393224 | tf_op jit(solution)/shard_map/ppermute | solution.py:388
  36.3 0.8 %collective-permute-done.10.refs_0_ = bf16[160,256]{1,0:T(8,128)(2,1)S(1)} collective-permute-done((bf16[160,256]{1,0:T(8,128)(2,1)S(1)}, bf16[160,256]{1,0:T(8,128)(2,1)S(1)}, u32[]{:S(2)}, u32[]{:S(2)}) %collective-permute-start.10) | collective-permute-done | bytes 81952 | tf_op jit(solution)/shard_map/ppermute | solution.py:311
  37.5 0.9 %weight.3 = (bf16[128,512]{1,0:T(8,128)(2,1)S(1)}, bf16[128,512]{1,0:T(8,128)(2,1)S(1)}, bf16[128,512]{1,0:T(8,128)(2,1)S(1)}, bf16[128,512]{1,0:T(8,128)(2,1)S(1)}) custom-call(bf16[512,256]{1,0:T(8,128)(2,1)S(1)} %collective-permute-done.8.x_ref.attn_ref, bf16[512,2048]{1,0:T(8,128)(2,1)S(1)} %bitcast.13, ...), custom_call_target="tpu_custom_call" | custom-call | flops 1 | bytes 1 | tf_op jit(solution)/shard_map/weight/pallas_call | solution.py:45
  38.4 1.0 %collective-permute-start.18 = (bf16[128,512]{1,0:T(8,128)(2,1)S(1)}, bf16[128,512]{1,0:T(8,128)(2,1)S(1)}, u32[]{:S(2)}, u32[]{:S(2)}) collective-permute-start(bf16[128,512]{1,0:T(8,128)(2,1)S(1)} %get-tuple-element.75), channel_id=1, source_target_pairs={{0,2},{2,0},{1,3},{3,1},{4,6},{6,4},{5,7},{7,5},{8,10},{10,8},{9,1... | collective-permute-start | bytes 393224 | tf_op jit(solution)/shard_map/ppermute | solution.py:311
  39.4 1.8 %collective-permute-start.19 = (bf16[128,512]{1,0:T(8,128)(2,1)S(1)}, bf16[128,512]{1,0:T(8,128)(2,1)S(1)}, u32[]{:S(2)}, u32[]{:S(2)}) collective-permute-start(bf16[128,512]{1,0:T(8,128)(2,1)S(1)} %get-tuple-element.76), channel_id=1, source_target_pairs={{6,0},{4,2},{2,4},{0,6},{14,8},{12,10},{10,12},{8,14},{7,1},{5,3},... | collective-permute-start | bytes 393224 | tf_op jit(solution)/shard_map/ppermute | solution.py:412
  41.2 1.0 %collective-permute-start.14 = (bf16[128,512]{1,0:T(8,128)(2,1)S(1)}, bf16[128,512]{1,0:T(8,128)(2,1)S(1)}, u32[]{:S(2)}, u32[]{:S(2)}) collective-permute-start(bf16[128,512]{1,0:T(8,128)(2,1)S(1)} %get-tuple-element.71), channel_id=1, source_target_pairs={{0,2},{2,0},{1,3},{3,1},{4,6},{6,4},{5,7},{7,5},{8,10},{10,8},{9,1... | collective-permute-start | bytes 393224 | tf_op jit(solution)/shard_map/ppermute | solution.py:311
  42.2 4.2 %collective-permute-start.15 = (bf16[128,512]{1,0:T(8,128)(2,1)S(1)}, bf16[128,512]{1,0:T(8,128)(2,1)S(1)}, u32[]{:S(2)}, u32[]{:S(2)}) collective-permute-start(bf16[128,512]{1,0:T(8,128)(2,1)S(1)} %get-tuple-element.65), channel_id=1, source_target_pairs={{6,0},{4,2},{2,4},{0,6},{14,8},{12,10},{10,12},{8,14},{7,1},{5,3},... | collective-permute-start | bytes 393224 | tf_op jit(solution)/shard_map/ppermute | solution.py:412
  46.6 3.4 %collective-permute-done.18.keep_ref = bf16[128,512]{1,0:T(8,128)(2,1)S(1)} collective-permute-done((bf16[128,512]{1,0:T(8,128)(2,1)S(1)}, bf16[128,512]{1,0:T(8,128)(2,1)S(1)}, u32[]{:S(2)}, u32[]{:S(2)}) %collective-permute-start.18) | collective-permute-done | bytes 131104 | tf_op jit(solution)/shard_map/ppermute | solution.py:311
  50.1 1.8 %collective-permute-start.20 = (bf16[128,512]{1,0:T(8,128)(2,1)S(1)}, bf16[128,512]{1,0:T(8,128)(2,1)S(1)}, u32[]{:S(2)}, u32[]{:S(2)}) collective-permute-start(bf16[128,512]{1,0:T(8,128)(2,1)S(1)} %get-tuple-element.78), channel_id=1, source_target_pairs={{0,8},{4,12},{8,0},{12,4},{1,9},{5,13},{9,1},{13,5},{2,10},{6,14},... | collective-permute-start | bytes 393224 | tf_op jit(solution)/shard_map/ppermute | solution.py:440
  52.6 2.3 %collective-permute-start.17 = (bf16[128,512]{1,0:T(8,128)(2,1)S(1)}, bf16[128,512]{1,0:T(8,128)(2,1)S(1)}, u32[]{:S(2)}, u32[]{:S(2)}) collective-permute-start(bf16[128,512]{1,0:T(8,128)(2,1)S(1)} %get-tuple-element.74), channel_id=1, source_target_pairs={{0,8},{4,12},{8,0},{12,4},{1,9},{5,13},{9,1},{13,5},{2,10},{6,14},... | collective-permute-start | bytes 393224 | tf_op jit(solution)/shard_map/ppermute | solution.py:440
  54.9 1.9 %query.1 = (bf16[512,256]{1,0:T(8,128)(2,1)}, f32[512,256]{1,0:T(8,128)S(1)}, f32[512,256]{1,0:T(8,128)S(1)}) custom-call(bf16[512,256]{1,0:T(8,128)(2,1)S(1)} %bitcast.21, bf16[512,256]{1,0:T(8,128)(2,1)S(1)} %get-tuple-element.44.refs_5_.refs_4_.qf_ref, bf16[512,256]{1,0:T(8,128)(2,1)S(1)} %copy-done.5, bf16[512,256]{1,0:T(8,128)(2,1)S(1)} %bitcast.16, ...), custom_call_target="tpu_custom_call" | custom-call | flops 99999997952 | bytes 1 | tf_op jit(solution)/shard_map/query/pallas_call | solution.py:45
  56.8 1.9 %key.1 = (bf16[512,256]{1,0:T(8,128)(2,1)}, bf16[512,256]{1,0:T(8,128)(2,1)}) custom-call(s32[2,4,8]{2,1,0:T(4,128)S(1)} %bitcast.24, bf16[512,128]{1,0:T(8,128)(2,1)S(1)} %get-tuple-element.58.refs_0_.refs_1_, bf16[512,128]{1,0:T(8,128)(2,1)S(1)} %collective-permute-done.7.refs_1_.refs_2_, bf16[1024,128]{1,0:T(8,128)(2,1)S(1)} %collective-permute-done.13.refs_3_, ...), custom_call_target="tpu_custom_call" | custom-call | flops 1 | bytes 1 | tf_op jit(solution)/shard_map/key/pallas_call | solution.py:45
  58.7 3.7 %collective-permute-done.20.refs_3_ = bf16[128,512]{1,0:T(8,128)(2,1)S(1)} collective-permute-done((bf16[128,512]{1,0:T(8,128)(2,1)S(1)}, bf16[128,512]{1,0:T(8,128)(2,1)S(1)}, u32[]{:S(2)}, u32[]{:S(2)}) %collective-permute-start.20) | collective-permute-done | bytes 131104 | tf_op jit(solution)/shard_map/ppermute | solution.py:440
  62.5 2.0 %collective-permute-done.17.refs_1_ = bf16[128,512]{1,0:T(8,128)(2,1)S(1)} collective-permute-done((bf16[128,512]{1,0:T(8,128)(2,1)S(1)}, bf16[128,512]{1,0:T(8,128)(2,1)S(1)}, u32[]{:S(2)}, u32[]{:S(2)}) %collective-permute-start.17) | collective-permute-done | bytes 131104 | tf_op jit(solution)/shard_map/ppermute | solution.py:440
  64.4 1.0 %final.1 = f32[512,256]{1,0:T(8,128)} custom-call(bf16[128,512]{1,0:T(8,128)(2,1)S(1)} %get-tuple-element.73.refs_0_, bf16[128,512]{1,0:T(8,128)(2,1)S(1)} %collective-permute-done.17.refs_1_, bf16[128,512]{1,0:T(8,128)(2,1)S(1)} %get-tuple-element.77.refs_2_, bf16[128,512]{1,0:T(8,128)(2,1)S(1)} %collective-permute-done.20.refs_3_), custom_call_target="tpu_custom_call" | custom-call | flops 1 | bytes 1 | tf_op jit(solution)/shard_map/final/pallas_call | solution.py:45
  (48 shorter events, 3.5 us)
Async XLA Ops:
  0.6 18.9 %copy-start = (bf16[1,512,2048]{2,1,0:T(8,128)(2,1)S(1)}, bf16[1,512,2048]{2,1,0:T(8,128)(2,1)}, u32[]{:S(2)}) copy-start(bf16[1,512,2048]{2,1,0:T(8,128)(2,1)} %param.11) | copy-start | bytes 6291460
  0.6 11.7 %copy-start.2 = (bf16[1,512,256]{2,1,0:T(8,128)(2,1)S(1)}, bf16[1,512,256]{2,1,0:T(8,128)(2,1)}, u32[]{:S(2)}) copy-start(bf16[1,512,256]{2,1,0:T(8,128)(2,1)} %param.8) | copy-start | bytes 786436
  0.7 11.7 %copy-start.6 = (bf16[1,512,256]{2,1,0:T(8,128)(2,1)S(1)}, bf16[1,512,256]{2,1,0:T(8,128)(2,1)}, u32[]{:S(2)}) copy-start(bf16[1,512,256]{2,1,0:T(8,128)(2,1)} %param.6) | copy-start | bytes 786436
  0.7 18.9 %collective-permute-start.3 = (bf16[512,2048]{1,0:T(8,128)(2,1)}, bf16[512,2048]{1,0:T(8,128)(2,1)S(1)}, u32[]{:S(2)}, u32[]{:S(2)}) collective-permute-start(bf16[512,2048]{1,0:T(8,128)(2,1)} %bitcast.9), channel_id=1, source_target_pairs={{0,1},{1,0},{2,3},{3,2},{4,5},{5,4},{6,7},{7,6},{8,9},{9,8},{10,11... | collective-permute-start | bytes 6291464 | tf_op jit(solution)/shard_map/ppermute | solution.py:311
  4.1 15.4 %collective-permute-start.4 = (bf16[2048,128]{1,0:T(8,128)(2,1)}, bf16[2048,128]{1,0:T(8,128)(2,1)S(1)}, u32[]{:S(2)}, u32[]{:S(2)}) collective-permute-start(bf16[2048,128]{1,0:T(8,128)(2,1)} %get-tuple-element.47), channel_id=1, source_target_pairs={{0,2},{2,0},{1,3},{3,1},{4,6},{6,4},{5,7},{7,5},{8,10},{10,8},{9,1... | collective-permute-start | bytes 1572872 | tf_op jit(solution)/shard_map/ppermute | solution.py:311
  6.9 15.8 %collective-permute-start = (bf16[512,128]{1,0:T(8,128)(2,1)}, bf16[512,128]{1,0:T(8,128)(2,1)S(1)}, u32[]{:S(2)}, u32[]{:S(2)}) collective-permute-start(bf16[512,128]{1,0:T(8,128)(2,1)} %get-tuple-element.42.refs_1_), channel_id=1, source_target_pairs={{0,4},{4,8},{8,12},{12,0},{1,5},{5,9},{9,13},{13,1},{2,6},{6,10},{... | collective-permute-start | bytes 393224 | tf_op jit(solution)/shard_map/ppermute | solution.py:320
  8.4 14.2 %collective-permute-start.1 = (bf16[512,128]{1,0:T(8,128)(2,1)}, bf16[512,128]{1,0:T(8,128)(2,1)S(1)}, u32[]{:S(2)}, u32[]{:S(2)}) collective-permute-start(bf16[512,128]{1,0:T(8,128)(2,1)} %get-tuple-element.42.refs_1_), channel_id=1, source_target_pairs={{0,8},{4,12},{8,0},{12,4},{1,9},{5,13},{9,1},{13,5},{2,10},{6,14},... | collective-permute-start | bytes 393224 | tf_op jit(solution)/shard_map/ppermute | solution.py:320
  11.0 11.6 %collective-permute-start.2 = (bf16[512,128]{1,0:T(8,128)(2,1)}, bf16[512,128]{1,0:T(8,128)(2,1)S(1)}, u32[]{:S(2)}, u32[]{:S(2)}) collective-permute-start(bf16[512,128]{1,0:T(8,128)(2,1)} %get-tuple-element.42.refs_1_), channel_id=1, source_target_pairs={{0,12},{4,0},{8,4},{12,8},{1,13},{5,1},{9,5},{13,9},{2,14},{6,2},{... | collective-permute-start | bytes 393224 | tf_op jit(solution)/shard_map/ppermute | solution.py:320
  12.4 1.0 %copy-start.4 = (bf16[512,256]{1,0:T(8,128)(2,1)S(1)}, bf16[512,256]{1,0:T(8,128)(2,1)}, u32[]{:S(2)}) copy-start(bf16[512,256]{1,0:T(8,128)(2,1)} %get-tuple-element.43.kf_ref.refs_5_) | copy-start | bytes 786436
  14.0 8.7 %copy-start.8 = (s32[2,8,4]{1,2,0:T(4,128)S(1)}, s32[2,8,4]{1,2,0:T(4,128)}, u32[]{:S(2)}) copy-start(s32[2,8,4]{1,2,0:T(4,128)} %param.9) | copy-start | bytes 772
  14.0 8.7 %copy-start.10 = (bf16[512,128]{1,0:T(8,128)(2,1)S(1)}, bf16[512,128]{1,0:T(8,128)(2,1)}, u32[]{:S(2)}) copy-start(bf16[512,128]{1,0:T(8,128)(2,1)} %get-tuple-element.42.refs_1_) | copy-start | bytes 393220
  20.8 6.4 %collective-permute-start.6 = (bf16[512,128]{1,0:T(8,128)(2,1)S(1)}, bf16[512,128]{1,0:T(8,128)(2,1)S(1)}, u32[]{:S(2)}, u32[]{:S(2)}) collective-permute-start(bf16[512,128]{1,0:T(8,128)(2,1)S(1)} %get-tuple-element.48), channel_id=1, source_target_pairs={{0,3},{1,2},{2,1},{3,0},{4,7},{5,6},{6,5},{7,4},{8,11},{9,10},{10,... | collective-permute-start | bytes 393224 | tf_op jit(solution)/shard_map/ppermute | solution.py:364
  21.7 8.0 %collective-permute-start.5 = (bf16[512,128]{1,0:T(8,128)(2,1)S(1)}, bf16[512,128]{1,0:T(8,128)(2,1)S(1)}, u32[]{:S(2)}, u32[]{:S(2)}) collective-permute-start(bf16[512,128]{1,0:T(8,128)(2,1)S(1)} %get-tuple-element.52), channel_id=1, source_target_pairs={{0,2},{2,0},{1,3},{3,1},{4,6},{6,4},{5,7},{7,5},{8,10},{10,8},{9,1... | collective-permute-start | bytes 393224 | tf_op jit(solution)/shard_map/ppermute | solution.py:311
  22.7 3.6 %copy-start.1 = (bf16[4096,256]{1,0:T(8,128)(2,1)S(1)}, bf16[4096,256]{1,0:T(8,128)(2,1)}, u32[]{:S(2)}) copy-start(bf16[4096,256]{1,0:T(8,128)(2,1)} %w_ref.3) | copy-start | bytes 6291460
  24.5 5.8 %collective-permute-start.9 = (bf16[512,256]{1,0:T(8,128)(2,1)}, bf16[512,256]{1,0:T(8,128)(2,1)S(1)}, u32[]{:S(2)}, u32[]{:S(2)}) collective-permute-start(bf16[512,256]{1,0:T(8,128)(2,1)} %get-tuple-element.59.attn_ref), channel_id=1, source_target_pairs={{0,1},{1,0},{2,3},{3,2},{4,5},{5,4},{6,7},{7,6},{8,9},{9,8},{10,11... | collective-permute-start | bytes 786440 | tf_op jit(solution)/shard_map/ppermute | solution.py:311
  24.6 11.0 %collective-permute-start.8 = (bf16[512,256]{1,0:T(8,128)(2,1)}, bf16[512,256]{1,0:T(8,128)(2,1)S(1)}, u32[]{:S(2)}, u32[]{:S(2)}) collective-permute-start(bf16[512,256]{1,0:T(8,128)(2,1)} %get-tuple-element.59.attn_ref), channel_id=1, source_target_pairs={{0,2},{2,0},{1,3},{3,1},{4,6},{6,4},{5,7},{7,5},{8,10},{10,8},{9,1... | collective-permute-start | bytes 786440 | tf_op jit(solution)/shard_map/ppermute | solution.py:311
  29.7 1.0 %copy-start.7 = (bf16[512,256]{1,0:T(8,128)(2,1)S(1)}, bf16[512,256]{1,0:T(8,128)(2,1)}, u32[]{:S(2)}) copy-start(bf16[512,256]{1,0:T(8,128)(2,1)} %get-tuple-element.59.attn_ref) | copy-start | bytes 786436
  31.4 15.0 %collective-permute-start.16 = (bf16[256,512]{1,0:T(8,128)(2,1)S(1)}, bf16[256,512]{1,0:T(8,128)(2,1)S(1)}, u32[]{:S(2)}, u32[]{:S(2)}) collective-permute-start(bf16[256,512]{1,0:T(8,128)(2,1)S(1)} %get-tuple-element.60), channel_id=1, source_target_pairs={{0,4},{4,0},{8,12},{12,8},{1,5},{5,1},{9,13},{13,9},{2,6},{6,2},{1... | collective-permute-start | bytes 786440 | tf_op jit(solution)/shard_map/ppermute | solution.py:397
  33.1 9.1 %collective-permute-start.7 = (bf16[512,128]{1,0:T(8,128)(2,1)S(1)}, bf16[512,128]{1,0:T(8,128)(2,1)S(1)}, u32[]{:S(2)}, u32[]{:S(2)}) collective-permute-start(bf16[512,128]{1,0:T(8,128)(2,1)S(1)} %get-tuple-element.58.refs_0_.refs_1_), channel_id=1, source_target_pairs={{0,8},{4,12},{8,0},{12,4},{1,9},{5,13},{9,1},{13,5},{2,10},{6,14},... | collective-permute-start | bytes 393224 | tf_op jit(solution)/shard_map/ppermute | solution.py:388
  35.7 1.9 %collective-permute-start.12 = (bf16[192,256]{1,0:T(8,128)(2,1)S(1)}, bf16[192,256]{1,0:T(8,128)(2,1)S(1)}, u32[]{:S(2)}, u32[]{:S(2)}) collective-permute-start(bf16[192,256]{1,0:T(8,128)(2,1)S(1)} %get-tuple-element.64), channel_id=1, source_target_pairs={{0,1},{1,0},{2,3},{3,2},{4,5},{5,4},{6,7},{7,6},{8,9},{9,8},{10,11... | collective-permute-start | bytes 294920 | tf_op jit(solution)/shard_map/ppermute | solution.py:311
  35.8 1.4 %collective-permute-start.10 = (bf16[160,256]{1,0:T(8,128)(2,1)S(1)}, bf16[160,256]{1,0:T(8,128)(2,1)S(1)}, u32[]{:S(2)}, u32[]{:S(2)}) collective-permute-start(bf16[160,256]{1,0:T(8,128)(2,1)S(1)} %get-tuple-element.62), channel_id=1, source_target_pairs={{0,1},{1,0},{2,3},{3,2},{4,5},{5,4},{6,7},{7,6},{8,9},{9,8},{10,11... | collective-permute-start | bytes 245768 | tf_op jit(solution)/shard_map/ppermute | solution.py:311
  36.3 1.3 %collective-permute-start.11 = (bf16[160,256]{1,0:T(8,128)(2,1)S(1)}, bf16[160,256]{1,0:T(8,128)(2,1)S(1)}, u32[]{:S(2)}, u32[]{:S(2)}) collective-permute-start(bf16[160,256]{1,0:T(8,128)(2,1)S(1)} %get-tuple-element.63), channel_id=1, source_target_pairs={{0,1},{1,0},{2,3},{3,2},{4,5},{5,4},{6,7},{7,6},{8,9},{9,8},{10,11... | collective-permute-start | bytes 245768 | tf_op jit(solution)/shard_map/ppermute | solution.py:311
  38.4 16.4 %copy-start.5 = (bf16[512,256]{1,0:T(8,128)(2,1)S(1)}, bf16[512,256]{1,0:T(8,128)(2,1)}, u32[]{:S(2)}) copy-start(bf16[512,256]{1,0:T(8,128)(2,1)} %get-tuple-element.43.kf_ref.refs_5_) | copy-start | bytes 786436
  38.4 11.6 %collective-permute-start.18 = (bf16[128,512]{1,0:T(8,128)(2,1)S(1)}, bf16[128,512]{1,0:T(8,128)(2,1)S(1)}, u32[]{:S(2)}, u32[]{:S(2)}) collective-permute-start(bf16[128,512]{1,0:T(8,128)(2,1)S(1)} %get-tuple-element.75), channel_id=1, source_target_pairs={{0,2},{2,0},{1,3},{3,1},{4,6},{6,4},{5,7},{7,5},{8,10},{10,8},{9,1... | collective-permute-start | bytes 393224 | tf_op jit(solution)/shard_map/ppermute | solution.py:311
  39.4 10.6 %collective-permute-start.19 = (bf16[128,512]{1,0:T(8,128)(2,1)S(1)}, bf16[128,512]{1,0:T(8,128)(2,1)S(1)}, u32[]{:S(2)}, u32[]{:S(2)}) collective-permute-start(bf16[128,512]{1,0:T(8,128)(2,1)S(1)} %get-tuple-element.76), channel_id=1, source_target_pairs={{6,0},{4,2},{2,4},{0,6},{14,8},{12,10},{10,12},{8,14},{7,1},{5,3},... | collective-permute-start | bytes 393224 | tf_op jit(solution)/shard_map/ppermute | solution.py:412
  41.2 11.3 %collective-permute-start.14 = (bf16[128,512]{1,0:T(8,128)(2,1)S(1)}, bf16[128,512]{1,0:T(8,128)(2,1)S(1)}, u32[]{:S(2)}, u32[]{:S(2)}) collective-permute-start(bf16[128,512]{1,0:T(8,128)(2,1)S(1)} %get-tuple-element.71), channel_id=1, source_target_pairs={{0,2},{2,0},{1,3},{3,1},{4,6},{6,4},{5,7},{7,5},{8,10},{10,8},{9,1... | collective-permute-start | bytes 393224 | tf_op jit(solution)/shard_map/ppermute | solution.py:311
  42.2 10.3 %collective-permute-start.15 = (bf16[128,512]{1,0:T(8,128)(2,1)S(1)}, bf16[128,512]{1,0:T(8,128)(2,1)S(1)}, u32[]{:S(2)}, u32[]{:S(2)}) collective-permute-start(bf16[128,512]{1,0:T(8,128)(2,1)S(1)} %get-tuple-element.65), channel_id=1, source_target_pairs={{6,0},{4,2},{2,4},{0,6},{14,8},{12,10},{10,12},{8,14},{7,1},{5,3},... | collective-permute-start | bytes 393224 | tf_op jit(solution)/shard_map/ppermute | solution.py:412
  46.4 10.4 %collective-permute-start.13 = (bf16[1024,128]{1,0:T(8,128)(2,1)S(1)}, bf16[1024,128]{1,0:T(8,128)(2,1)S(1)}, u32[]{:S(2)}, u32[]{:S(2)}) collective-permute-start(bf16[1024,128]{1,0:T(8,128)(2,1)S(1)} %join.1), channel_id=1, source_target_pairs={{0,4},{4,0},{8,12},{12,8},{1,5},{5,1},{9,13},{13,9},{2,6},{6,2},{1... | collective-permute-start | bytes 786440 | tf_op jit(solution)/shard_map/ppermute | solution.py:417
  50.1 12.4 %collective-permute-start.20 = (bf16[128,512]{1,0:T(8,128)(2,1)S(1)}, bf16[128,512]{1,0:T(8,128)(2,1)S(1)}, u32[]{:S(2)}, u32[]{:S(2)}) collective-permute-start(bf16[128,512]{1,0:T(8,128)(2,1)S(1)} %get-tuple-element.78), channel_id=1, source_target_pairs={{0,8},{4,12},{8,0},{12,4},{1,9},{5,13},{9,1},{13,5},{2,10},{6,14},... | collective-permute-start | bytes 393224 | tf_op jit(solution)/shard_map/ppermute | solution.py:440
  52.6 11.9 %collective-permute-start.17 = (bf16[128,512]{1,0:T(8,128)(2,1)S(1)}, bf16[128,512]{1,0:T(8,128)(2,1)S(1)}, u32[]{:S(2)}, u32[]{:S(2)}) collective-permute-start(bf16[128,512]{1,0:T(8,128)(2,1)S(1)} %get-tuple-element.74), channel_id=1, source_target_pairs={{0,8},{4,12},{8,0},{12,4},{1,9},{5,13},{9,1},{13,5},{2,10},{6,14},... | collective-permute-start | bytes 393224 | tf_op jit(solution)/shard_map/ppermute | solution.py:440
  54.9 1.9 %copy-start.3 = (bf16[1,512,256]{2,1,0:T(8,128)(2,1)S(1)}, bf16[1,512,256]{2,1,0:T(8,128)(2,1)}, u32[]{:S(2)}) copy-start(bf16[1,512,256]{2,1,0:T(8,128)(2,1)} %param.7) | copy-start | bytes 786436
  54.9 2.0 %copy-start.9 = (s32[2,8,4]{1,2,0:T(4,128)S(1)}, s32[2,8,4]{1,2,0:T(4,128)}, u32[]{:S(2)}) copy-start(s32[2,8,4]{1,2,0:T(4,128)} %param.9) | copy-start | bytes 772

commit v7 on v6

--- a/solution.py
+++ b/solution.py
@@ -70,48 +70,56 @@
         st_ref[mat(i), :] = mm(kf, v_ref[r, c], TN).astype(BF16)
 
 
-def begin_body(k_ref, v_ref, w_ref, kf_ref, st_ref, far_ref, k_in, v_in, far_in, sems):
+def far_body(w_ref, far_ref, sem):
     width, cols = far_ref.shape
     rows = pl.ds(pl.multiple_of((1 - lax.axis_index("head")) * width, width), width)
     lanes = pl.ds(pl.multiple_of(lax.axis_index("dp") * cols, cols), cols)
-    far_copy = pltpu.make_async_copy(w_ref.at[rows, lanes], far_in, sems.at[0])
-    k_copy = pltpu.make_async_copy(k_ref, k_in, sems.at[1])
-    v_copy = pltpu.make_async_copy(v_ref, v_in, sems.at[2])
+    copy = pltpu.make_async_copy(w_ref.at[rows, lanes], far_ref, sem)
+    copy.start()
+    copy.wait()
+
+
+def far_rows(w, width):
+    return pl.pallas_call(
+        far_body,
+        out_shape=sds((width, DH), BF16),
+        in_specs=[pl.BlockSpec(memory_space=pl.ANY)],
+        out_specs=VM,
+        scratch_shapes=[pltpu.SemaphoreType.DMA],
+        name="far",
+        compiler_params=pltpu.CompilerParams(vmem_limit_bytes=BEGIN),
+        cost_estimate=SHORT,
+    )(w)
+
+
+def begin_body(k_ref, v_ref, kf_ref, st_ref, k_in, v_in, sems):
+    k_copy = pltpu.make_async_copy(k_ref, k_in, sems.at[0])
+    v_copy = pltpu.make_async_copy(v_ref, v_in, sems.at[1])
     k_copy.start()
     v_copy.start()
-    far_copy.start()
     k_copy.wait()
     v_copy.wait()
     states_body(k_in, v_in, kf_ref, st_ref)
-    far_copy.wait()
-    out_copy = pltpu.make_async_copy(far_in, far_ref, sems.at[3])
-    out_copy.start()
-    out_copy.wait()
-
-
-def begin(k, v, w, width):
+
+
+def begin(k, v):
     tokens, cols = k.shape
     count = tokens // BLK * (cols // DH)
     hbm = pl.BlockSpec(memory_space=pl.ANY)
     return pl.pallas_call(
         begin_body,
-        out_shape=(
-            sds((tokens, cols), BF16),
-            sds((count * DH, DH), BF16),
-            sds((width, DH), BF16),
-        ),
-        in_specs=[hbm, hbm, hbm],
-        out_specs=[VM, VM, hbm],
+        out_shape=(sds((tokens, cols), BF16), sds((count * DH, DH), BF16)),
+        in_specs=[hbm, hbm],
+        out_specs=[VM, VM],
         scratch_shapes=[
             pltpu.VMEM((tokens, cols), BF16),
             pltpu.VMEM((tokens, cols), BF16),
-            pltpu.VMEM((width, DH), BF16),
-            pltpu.SemaphoreType.DMA((4,)),
+            pltpu.SemaphoreType.DMA((2,)),
         ],
         name="begin",
         compiler_params=pltpu.CompilerParams(vmem_limit_bytes=BEGIN),
         cost_estimate=SHORT,
-    )(k, v, w)
+    )(k, v)
 
 
 def split_body(x_ref, *outs):
@@ -119,13 +127,6 @@
     for out in outs:
         out[...] = x_ref[at : at + out.shape[0], :]
         at += out.shape[0]
-
-
-def join_body(*refs):
-    *parts, out_ref = refs
-    rows = parts[0].shape[0]
-    for i, part in enumerate(parts):
-        out_ref[i * rows : (i + 1) * rows, :] = part[...]
 
 
 def causal():
@@ -266,26 +267,25 @@
     sib_ref[...] = mm(og_sib_ref[...], w_ref[...], NN).astype(BF16)
 
 
-def weight_body(n_out, attn_ref, og_ref, og_sib_ref, *refs):
-    sibs, outs = refs[:-n_out], refs[-n_out:]
+def weight_body(cols, attn_ref, og_ref, og_sib_ref, *refs):
+    sibs, outs = refs[:-2], refs[-2:]
     rows = outs[0].shape[1]
-    pieces = len(outs) // 2
     parity, core = lax.rem(lax.axis_index("seq"), 2), lax.axis_index("dp")
     for which, pair in enumerate((1 - parity, parity)):
         at = pl.ds(pl.multiple_of((2 * pair + core) * rows, rows), rows)
-        total = mm(attn_ref[...], og_ref[:, at], TN)
+        total = mm(attn_ref[:, cols], og_ref[:, at], TN)
         row = 0
         for sib in sibs:
-            total = total + mm(sib[...], og_sib_ref[row : row + sib.shape[0], at], TN)
+            total = total + mm(sib[:, cols], og_sib_ref[row : row + sib.shape[0], at], TN)
             row += sib.shape[0]
-        for i in range(pieces):
-            out = outs[which * pieces + i]
-            size = out.shape[0]
-            out[...] = total[i * size : (i + 1) * size, :].astype(out.dtype)
-
-
-def pair_body(keep_ref, got_ref, out_ref):
+        outs[which][...] = total.astype(outs[which].dtype)
+
+
+def pair_body(keep_ref, got_ref, cg_ref, two_ref, out_ref, joined_ref):
     out_ref[...] = (keep_ref[...] + got_ref[...].astype(F32)).astype(BF16)
+    rows = cg_ref.shape[0]
+    joined_ref[:rows, :] = cg_ref[...]
+    joined_ref[rows:, :] = two_ref[...]
 
 
 def cross_body(i, keep_ref, got_ref, mine_ref, send_ref, stay_ref):
@@ -339,8 +339,9 @@
 
     if paired:
         width = og.shape[1]
-        kf, st, far = begin(k, v, out_weight, width)
+        far = far_rows(out_weight, width)
         w_other = swap(far, "head")
+        kf, st = begin(after(k, far), v)
         og_sib = swap(og, "dp")
     else:
         kf, st = call(states_body, (rows16, mats), (k, v), unit, "states")
@@ -388,7 +389,7 @@
         two = lax.ppermute(cg, "seq", [(i, i ^ 2) for i in range(4)])
         block, half = (cols, width // 4), sds((DH, width // 4), BF16)
         give, keep = call(
-            functools.partial(weight_body, 2),
+            functools.partial(weight_body, slice(None)),
             (sds(block, BF16), sds(block, F32)),
             (after(attn, cg), og, og_sib, attn_sib),
             0,
@@ -399,24 +400,33 @@
         third = tokens // 48 * 16
         sizes = (third, third, tokens - 2 * third)
         cuts = call(split_body, tuple(sds((n, cols), BF16) for n in sizes), (attn_other,), 0, "split")
-        pieces = call(
-            functools.partial(weight_body, 2 * heads),
-            (half,) * (2 * heads),
-            (attn_other, og, og_sib, *[swap(cut, "dp") for cut in cuts]),
+        cuts = [swap(cut, "dp") for cut in cuts]
+        beside = [((s ^ 1) * 2 + 1 - h, s * 2 + h) for s in range(4) for h in range(2)]
+
+        def cross_piece(i, *deps):
+            give, keep = call(
+                functools.partial(weight_body, mat(i)),
+                (half, half),
+                (after(attn_other, *deps), og, og_sib, *cuts),
+                0,
+                "weight",
+            )
+            return give, (swap(keep, "head"), lax.ppermute(give, ("seq", "head"), beside))
+
+        give_b, first_crossed = cross_piece(0)
+        mine, joined = call(
+            pair_body,
+            (sds(block, BF16), sds((2 * cg.shape[0], DH), BF16)),
+            (keep, got, cg, two),
             0,
-            "weight",
+            "pair",
         )
-        give_b, keep_b = pieces[:heads], pieces[heads:]
-        beside = [((s ^ 1) * 2 + 1 - h, s * 2 + h) for s in range(4) for h in range(2)]
-        crossed = [
-            (swap(k, "head"), lax.ppermute(g, ("seq", "head"), beside)) for k, g in zip(keep_b, give_b)
-        ]
-        (joined,) = call(
-            join_body, (sds((2 * cg.shape[0], DH), BF16),), (cg, after(two, give_b[0])), 0, "join"
-        )
+        crossed = [first_crossed]
+        for i in range(1, heads):
+            give_b, piece = cross_piece(i, mine)
+            crossed.append(piece)
         cparts = [cg, two, lax.ppermute(joined, "seq", neighbours)]
         second_owner = by_flip
-        (mine,) = call(pair_body, (sds(block, BF16),), (keep, got), 0, "pair")
     else:
         cparts, second_owner = gather_parts(cg, seq_size), first_owner
     dq, dkp, dvp = call(

time: 65.6 us -> 63.9 us (0.974)
  waiting for transfers between devices: 19.1 us -> 14.9 us
  starting transfers between devices: 29.5 us -> 30.7 us
  Pallas kernels: 14.7 us -> 15.8 us
    ppermute x2, waiting for transfers between devices: 5.71 us -> 0.01 us  [per_device(): sums += [stay, lax.ppermute(send, 'seq', [(s, s ^ 2) for s in range(4)])]]
    ppermute x10, waiting for transfers between devices: 13.3 us -> 8.6 us  [swap(): return lax.ppermute(x, axis, [(0, 1), (1, 0)])]
    ppermute x1, waiting for transfers between devices: 0.01 us -> 4.56 us  [per_device(): cparts = [cg, two, lax.ppermute(joined, 'seq', neighbours)]]
    pallas_call x0 -> x1, Pallas kernels: none -> 1.84 us  [far_rows(): pl.pallas_call(far_body, out_shape=sds((width, DH), BF16), in_specs=[pl.B...]
    ppermute x1, waiting for transfers between devices: 0.01 us -> 1.54 us  [per_device(): two = lax.ppermute(cg, 'seq', [(i, i ^ 2) for i in range(4)])]
    ppermute x2, starting transfers between devices: 6 us -> 4.78 us  [cross_piece(): lax.ppermute(give, ('seq', 'head'), beside)]
    ppermute x1, starting transfers between devices: 0.07 us -> 0.99 us  [per_device(): cparts = [cg, two, lax.ppermute(joined, 'seq', neighbours)]]
    pallas_call x1, Pallas kernels: 2.95 us -> 2.06 us  [begin(): pl.pallas_call(begin_body, out_shape=(sds((tokens, cols), BF16), sds((cou...]
  transfers between devices with their start and end apart: 21 -> 21, of which waited for: 8 -> 8; matrix products, arithmetic and copies ran while one was open for 0% -> 0% of each run, Pallas kernels for 21% -> 23%
where the time goes in v7:
time: 63.9 us; the launch traced here: 63.7 us
  starting transfers between devices  30.7 us (48%)
  Pallas kernels  15.8 us (25%)
  waiting for transfers between devices  14.9 us (23%)
  local copies, waits for them, and re-layouts  1.36 us (2%)
  between operations  0.84 us (1%)
    pallas_call x14, Pallas kernels, call(): pl.pallas_call(body, out_shape=outs, in_specs=[SM if a.dtype == jnp.int32...  11.2 us
    ppermute x10, starting transfers between devices, swap(): return lax.ppermute(x, axis, [(0, 1), (1, 0)])  9.39 us
    ppermute x10, waiting for transfers between devices, swap(): return lax.ppermute(x, axis, [(0, 1), (1, 0)])  8.6 us
    ppermute x3, starting transfers between devices, gather_parts(): parts.append(lax.ppermute(x, 'seq', pairs))  5.57 us
    ppermute x2, starting transfers between devices, per_device(): sums += [stay, lax.ppermute(send, 'seq', [(s, s ^ 2) for s in range(4)])]  4.78 us
    ppermute x2, starting transfers between devices, cross_piece(): lax.ppermute(give, ('seq', 'head'), beside)  4.78 us
    ppermute x1, waiting for transfers between devices, per_device(): cparts = [cg, two, lax.ppermute(joined, 'seq', neighbours)]  4.56 us
    ppermute x1, starting transfers between devices, per_device(): two = lax.ppermute(cg, 'seq', [(i, i ^ 2) for i in range(4)])  2.58 us
  transfers between devices with their start and end apart: 21, of which 8 were waited for; matrix products, arithmetic and copies ran while one was open for 0% of the time, Pallas kernels for 23%

profile of v7, /device:TPU:0, one launch (start us, length us, event | category | flops | bytes accessed | tf_op | source)
XLA Modules:
  0.0 63.7 jit_solution(7886266140410863331)
XLA Ops:
  1.2 1.8 %far.1 = bf16[2048,128]{1,0:T(8,128)(2,1)} custom-call(bf16[4096,256]{1,0:T(8,128)(2,1)} %w_ref.3), custom_call_target="tpu_custom_call" | custom-call | flops 1 | bytes 1 | tf_op jit(solution)/shard_map/far/pallas_call | solution.py:83
  3.0 2.7 %collective-permute-start.4 = (bf16[2048,128]{1,0:T(8,128)(2,1)}, bf16[2048,128]{1,0:T(8,128)(2,1)S(1)}, u32[]{:S(2)}, u32[]{:S(2)}) collective-permute-start(bf16[2048,128]{1,0:T(8,128)(2,1)} %far.1), channel_id=1, source_target_pairs={{0,2},{2,0},{1,3},{3,1},{4,6},{6,4},{5,7},{7,5},{8,10},{10,8},{9,1... | collective-permute-start | bytes 1572872 | tf_op jit(solution)/shard_map/ppermute | solution.py:311
  5.8 2.1 %begin.1 = (bf16[512,256]{1,0:T(8,128)(2,1)}, bf16[512,128]{1,0:T(8,128)(2,1)}) custom-call(bf16[512,256]{1,0:T(8,128)(2,1)} %bitcast.19, bf16[512,256]{1,0:T(8,128)(2,1)} %bitcast.15), custom_call_target="tpu_custom_call" | custom-call | flops 1 | bytes 1 | tf_op jit(solution)/shard_map/begin/pallas_call | solution.py:109
  7.8 1.6 %collective-permute-start = (bf16[512,128]{1,0:T(8,128)(2,1)}, bf16[512,128]{1,0:T(8,128)(2,1)S(1)}, u32[]{:S(2)}, u32[]{:S(2)}) collective-permute-start(bf16[512,128]{1,0:T(8,128)(2,1)} %get-tuple-element.45.refs_1_), channel_id=1, source_target_pairs={{0,4},{4,8},{8,12},{12,0},{1,5},{5,9},{9,13},{13,1},{2,6},{6,10},{... | collective-permute-start | bytes 393224 | tf_op jit(solution)/shard_map/ppermute | solution.py:320
  9.5 2.6 %collective-permute-start.1 = (bf16[512,128]{1,0:T(8,128)(2,1)}, bf16[512,128]{1,0:T(8,128)(2,1)S(1)}, u32[]{:S(2)}, u32[]{:S(2)}) collective-permute-start(bf16[512,128]{1,0:T(8,128)(2,1)} %get-tuple-element.45.refs_1_), channel_id=1, source_target_pairs={{0,8},{4,12},{8,0},{12,4},{1,9},{5,13},{9,1},{13,5},{2,10},{6,14},... | collective-permute-start | bytes 393224 | tf_op jit(solution)/shard_map/ppermute | solution.py:320
  12.0 1.3 %collective-permute-start.2 = (bf16[512,128]{1,0:T(8,128)(2,1)}, bf16[512,128]{1,0:T(8,128)(2,1)S(1)}, u32[]{:S(2)}, u32[]{:S(2)}) collective-permute-start(bf16[512,128]{1,0:T(8,128)(2,1)} %get-tuple-element.45.refs_1_), channel_id=1, source_target_pairs={{0,12},{4,0},{8,4},{12,8},{1,13},{5,1},{9,5},{13,9},{2,14},{6,2},{... | collective-permute-start | bytes 393224 | tf_op jit(solution)/shard_map/ppermute | solution.py:320
  13.4 0.9 %copy-done.3 = bf16[512,256]{1,0:T(8,128)(2,1)S(1)} copy-done((bf16[512,256]{1,0:T(8,128)(2,1)S(1)}, bf16[512,256]{1,0:T(8,128)(2,1)}, u32[]{:S(2)}) %copy-start.3) | copy-done | bytes 262168
  15.0 3.4 %collective-permute-done.4.w_ref = bf16[2048,128]{1,0:T(8,128)(2,1)S(1)} collective-permute-done((bf16[2048,128]{1,0:T(8,128)(2,1)}, bf16[2048,128]{1,0:T(8,128)(2,1)S(1)}, u32[]{:S(2)}, u32[]{:S(2)}) %collective-permute-start.4) | collective-permute-done | bytes 524320 | tf_op jit(solution)/shard_map/ppermute | solution.py:311
  18.4 1.2 %other.1 = (bf16[512,128]{1,0:T(8,128)(2,1)S(1)}, bf16[512,128]{1,0:T(8,128)(2,1)S(1)}) custom-call(bf16[512,2048]{1,0:T(8,128)(2,1)S(1)} %bitcast.10, bf16[512,2048]{1,0:T(8,128)(2,1)S(1)} %collective-permute-done.3.og_sib_ref, bf16[2048,128]{1,0:T(8,128)(2,1)S(1)} %collective-permute-done.4.w_ref), custom_call_target="tpu_custom_call" | custom-call | flops 1 | bytes 1 | tf_op jit(solution)/shard_map/other/pallas_call | solution.py:45
  19.7 1.0 %collective-permute-start.6 = (bf16[512,128]{1,0:T(8,128)(2,1)S(1)}, bf16[512,128]{1,0:T(8,128)(2,1)S(1)}, u32[]{:S(2)}, u32[]{:S(2)}) collective-permute-start(bf16[512,128]{1,0:T(8,128)(2,1)S(1)} %get-tuple-element.50), channel_id=1, source_target_pairs={{0,3},{1,2},{2,1},{3,0},{4,7},{5,6},{6,5},{7,4},{8,11},{9,10},{10,... | collective-permute-start | bytes 393224 | tf_op jit(solution)/shard_map/ppermute | solution.py:365
  20.6 0.9 %collective-permute-start.5 = (bf16[512,128]{1,0:T(8,128)(2,1)S(1)}, bf16[512,128]{1,0:T(8,128)(2,1)S(1)}, u32[]{:S(2)}, u32[]{:S(2)}) collective-permute-start(bf16[512,128]{1,0:T(8,128)(2,1)S(1)} %get-tuple-element.54), channel_id=1, source_target_pairs={{0,2},{2,0},{1,3},{3,1},{4,6},{6,4},{5,7},{7,5},{8,10},{10,8},{9,1... | collective-permute-start | bytes 393224 | tf_op jit(solution)/shard_map/ppermute | solution.py:311
  21.6 1.8 %numer.1 = (bf16[512,128]{1,0:T(8,128)(2,1)S(1)}, f32[512,256]{1,0:T(8,128)S(1)}, bf16[512,256]{1,0:T(8,128)(2,1)}) custom-call(s32[2,4,8]{2,1,0:T(4,128)S(1)} %bitcast.24, bf16[512,128]{1,0:T(8,128)(2,1)S(1)} %copy-done.10, bf16[512,128]{1,0:T(8,128)(2,1)S(1)} %collective-permute-done.refs_2_, bf16[512,128]{1,0:T(8,128)(2,1)S(1)} %collective-permute-done.1.refs_3_, ...), custom_call_target="tpu_custom_call" | custom-call | flops 99999997952 | bytes 1 | tf_op jit(solution)/shard_map/numer/pallas_call | solution.py:45
  23.5 1.7 %collective-permute-start.11 = (bf16[512,256]{1,0:T(8,128)(2,1)}, bf16[512,256]{1,0:T(8,128)(2,1)S(1)}, u32[]{:S(2)}, u32[]{:S(2)}) collective-permute-start(bf16[512,256]{1,0:T(8,128)(2,1)} %get-tuple-element.61.attn_ref), channel_id=1, source_target_pairs={{0,2},{2,0},{1,3},{3,1},{4,6},{6,4},{5,7},{7,5},{8,10},{10,8},{9,1... | collective-permute-start | bytes 786440 | tf_op jit(solution)/shard_map/ppermute | solution.py:311
  25.2 0.8 %own_partial.1.refs_0_ = f32[512,256]{1,0:T(8,128)S(1)} custom-call(bf16[512,2048]{1,0:T(8,128)(2,1)S(1)} %bitcast.11, bf16[4096,256]{1,0:T(8,128)(2,1)S(1)} %copy-done.1), custom_call_target="tpu_custom_call" | custom-call | flops 1 | bytes 1 | tf_op jit(solution)/shard_map/own_partial/pallas_call | solution.py:253
  26.0 2.6 %collective-permute-done.5.refs_1_ = bf16[512,128]{1,0:T(8,128)(2,1)S(1)} collective-permute-done((bf16[512,128]{1,0:T(8,128)(2,1)S(1)}, bf16[512,128]{1,0:T(8,128)(2,1)S(1)}, u32[]{:S(2)}, u32[]{:S(2)}) %collective-permute-start.5) | collective-permute-done | bytes 131104 | tf_op jit(solution)/shard_map/ppermute | solution.py:311
  29.6 0.7 %weight.3 = (bf16[256,512]{1,0:T(8,128)(2,1)S(1)}, f32[256,512]{1,0:T(8,128)S(1)}) custom-call(bf16[512,256]{1,0:T(8,128)(2,1)S(1)} %copy-done.7, bf16[512,2048]{1,0:T(8,128)(2,1)S(1)} %bitcast.12, bf16[512,2048]{1,0:T(8,128)(2,1)S(1)} %collective-permute-done.3.og_sib_ref, bf16[512,256]{1,0:T(8,128)(2,1)S(1)} %collective-permute-done.8.refs_0_), custom_call_target="tpu_custom_call" | custom-call | flops 1 | bytes 1 | tf_op jit(solution)/shard_map/weight/pallas_call | solution.py:45
  30.3 1.6 %collective-permute-start.9 = (bf16[256,512]{1,0:T(8,128)(2,1)S(1)}, bf16[256,512]{1,0:T(8,128)(2,1)S(1)}, u32[]{:S(2)}, u32[]{:S(2)}) collective-permute-start(bf16[256,512]{1,0:T(8,128)(2,1)S(1)} %get-tuple-element.63), channel_id=1, source_target_pairs={{0,4},{4,0},{8,12},{12,8},{1,5},{5,1},{9,13},{13,9},{2,6},{6,2},{1... | collective-permute-start | bytes 786440 | tf_op jit(solution)/shard_map/ppermute | solution.py:398
  32.0 2.6 %collective-permute-start.7 = (bf16[512,128]{1,0:T(8,128)(2,1)S(1)}, bf16[512,128]{1,0:T(8,128)(2,1)S(1)}, u32[]{:S(2)}, u32[]{:S(2)}) collective-permute-start(bf16[512,128]{1,0:T(8,128)(2,1)S(1)} %get-tuple-element.60.cg_ref.refs_1_), channel_id=1, source_target_pairs={{0,8},{4,12},{8,0},{12,4},{1,9},{5,13},{9,1},{13,5},{2,10},{6,14},... | collective-permute-start | bytes 393224 | tf_op jit(solution)/shard_map/ppermute | solution.py:389
  35.2 0.8 %collective-permute-done.12.refs_0_ = bf16[160,256]{1,0:T(8,128)(2,1)S(1)} collective-permute-done((bf16[160,256]{1,0:T(8,128)(2,1)S(1)}, bf16[160,256]{1,0:T(8,128)(2,1)S(1)}, u32[]{:S(2)}, u32[]{:S(2)}) %collective-permute-start.12) | collective-permute-done | bytes 81952 | tf_op jit(solution)/shard_map/ppermute | solution.py:311
  37.0 1.0 %collective-permute-start.15 = (bf16[128,512]{1,0:T(8,128)(2,1)S(1)}, bf16[128,512]{1,0:T(8,128)(2,1)S(1)}, u32[]{:S(2)}, u32[]{:S(2)}) collective-permute-start(bf16[128,512]{1,0:T(8,128)(2,1)S(1)} %get-tuple-element.73), channel_id=1, source_target_pairs={{0,2},{2,0},{1,3},{3,1},{4,6},{6,4},{5,7},{7,5},{8,10},{10,8},{9,1... | collective-permute-start | bytes 393224 | tf_op jit(solution)/shard_map/ppermute | solution.py:311
  37.9 1.8 %collective-permute-start.16 = (bf16[128,512]{1,0:T(8,128)(2,1)S(1)}, bf16[128,512]{1,0:T(8,128)(2,1)S(1)}, u32[]{:S(2)}, u32[]{:S(2)}) collective-permute-start(bf16[128,512]{1,0:T(8,128)(2,1)S(1)} %get-tuple-element.74), channel_id=1, source_target_pairs={{6,0},{4,2},{2,4},{0,6},{14,8},{12,10},{10,12},{8,14},{7,1},{5,3},... | collective-permute-start | bytes 393224 | tf_op jit(solution)/shard_map/ppermute | solution.py:414
  39.7 1.5 %collective-permute-done.7.two_ref.refs_2_ = bf16[512,128]{1,0:T(8,128)(2,1)S(1)} collective-permute-done((bf16[512,128]{1,0:T(8,128)(2,1)S(1)}, bf16[512,128]{1,0:T(8,128)(2,1)S(1)}, u32[]{:S(2)}, u32[]{:S(2)}) %collective-permute-start.7) | collective-permute-done | bytes 131104 | tf_op jit(solution)/shard_map/ppermute | solution.py:389
  42.1 1.8 %collective-permute-start.18 = (bf16[128,512]{1,0:T(8,128)(2,1)S(1)}, bf16[128,512]{1,0:T(8,128)(2,1)S(1)}, u32[]{:S(2)}, u32[]{:S(2)}) collective-permute-start(bf16[128,512]{1,0:T(8,128)(2,1)S(1)} %get-tuple-element.79), channel_id=1, source_target_pairs={{0,2},{2,0},{1,3},{3,1},{4,6},{6,4},{5,7},{7,5},{8,10},{10,8},{9,1... | collective-permute-start | bytes 393224 | tf_op jit(solution)/shard_map/ppermute | solution.py:311
  43.9 3.0 %collective-permute-start.19 = (bf16[128,512]{1,0:T(8,128)(2,1)S(1)}, bf16[128,512]{1,0:T(8,128)(2,1)S(1)}, u32[]{:S(2)}, u32[]{:S(2)}) collective-permute-start(bf16[128,512]{1,0:T(8,128)(2,1)S(1)} %get-tuple-element.80), channel_id=1, source_target_pairs={{6,0},{4,2},{2,4},{0,6},{14,8},{12,10},{10,12},{8,14},{7,1},{5,3},... | collective-permute-start | bytes 393224 | tf_op jit(solution)/shard_map/ppermute | solution.py:414
  47.0 1.6 %collective-permute-start.17 = (bf16[128,512]{1,0:T(8,128)(2,1)S(1)}, bf16[128,512]{1,0:T(8,128)(2,1)S(1)}, u32[]{:S(2)}, u32[]{:S(2)}) collective-permute-start(bf16[128,512]{1,0:T(8,128)(2,1)S(1)} %get-tuple-element.77), channel_id=1, source_target_pairs={{0,8},{4,12},{8,0},{12,4},{1,9},{5,13},{9,1},{13,5},{2,10},{6,14},... | collective-permute-start | bytes 393224 | tf_op jit(solution)/shard_map/ppermute | solution.py:450
  48.6 1.0 %collective-permute-start.10 = (bf16[1024,128]{1,0:T(8,128)(2,1)S(1)}, bf16[1024,128]{1,0:T(8,128)(2,1)S(1)}, u32[]{:S(2)}, u32[]{:S(2)}) collective-permute-start(bf16[1024,128]{1,0:T(8,128)(2,1)S(1)} %get-tuple-element.64), channel_id=1, source_target_pairs={{0,4},{4,0},{8,12},{12,8},{1,5},{5,1},{9,13},{13,9},{2,6},{6,2},{1... | collective-permute-start | bytes 786440 | tf_op jit(solution)/shard_map/ppermute | solution.py:428
  49.6 1.4 %collective-permute-done.18.keep_ref = bf16[128,512]{1,0:T(8,128)(2,1)S(1)} collective-permute-done((bf16[128,512]{1,0:T(8,128)(2,1)S(1)}, bf16[128,512]{1,0:T(8,128)(2,1)S(1)}, u32[]{:S(2)}, u32[]{:S(2)}) %collective-permute-start.18) | collective-permute-done | bytes 131104 | tf_op jit(solution)/shard_map/ppermute | solution.py:311
  51.1 3.2 %collective-permute-start.20 = (bf16[128,512]{1,0:T(8,128)(2,1)S(1)}, bf16[128,512]{1,0:T(8,128)(2,1)S(1)}, u32[]{:S(2)}, u32[]{:S(2)}) collective-permute-start(bf16[128,512]{1,0:T(8,128)(2,1)S(1)} %get-tuple-element.82), channel_id=1, source_target_pairs={{0,8},{4,12},{8,0},{12,4},{1,9},{5,13},{9,1},{13,5},{2,10},{6,14},... | collective-permute-start | bytes 393224 | tf_op jit(solution)/shard_map/ppermute | solution.py:450
  54.3 1.9 %query.1 = (bf16[512,256]{1,0:T(8,128)(2,1)}, f32[512,256]{1,0:T(8,128)S(1)}, f32[512,256]{1,0:T(8,128)S(1)}) custom-call(bf16[512,256]{1,0:T(8,128)(2,1)S(1)} %bitcast.22, bf16[512,256]{1,0:T(8,128)(2,1)S(1)} %get-tuple-element.47.refs_5_.refs_4_.qf_ref, bf16[512,256]{1,0:T(8,128)(2,1)S(1)} %copy-done.4, bf16[512,256]{1,0:T(8,128)(2,1)S(1)} %bitcast.17, ...), custom_call_target="tpu_custom_call" | custom-call | flops 99999997952 | bytes 1 | tf_op jit(solution)/shard_map/query/pallas_call | solution.py:45
  56.2 4.6 %collective-permute-done.10.refs_3_ = bf16[1024,128]{1,0:T(8,128)(2,1)S(1)} collective-permute-done((bf16[1024,128]{1,0:T(8,128)(2,1)S(1)}, bf16[1024,128]{1,0:T(8,128)(2,1)S(1)}, u32[]{:S(2)}, u32[]{:S(2)}) %collective-permute-start.10) | collective-permute-done | bytes 262176 | tf_op jit(solution)/shard_map/ppermute | solution.py:428
  60.8 1.9 %key.1 = (bf16[512,256]{1,0:T(8,128)(2,1)}, bf16[512,256]{1,0:T(8,128)(2,1)}) custom-call(s32[2,4,8]{2,1,0:T(4,128)S(1)} %bitcast.25, bf16[512,128]{1,0:T(8,128)(2,1)S(1)} %get-tuple-element.60.cg_ref.refs_1_, bf16[512,128]{1,0:T(8,128)(2,1)S(1)} %collective-permute-done.7.two_ref.refs_2_, bf16[1024,128]{1,0:T(8,128)(2,1)S(1)} %collective-permute-done.10.refs_3_, ...), custom_call_target="tpu_custom_call" | custom-call | flops 1 | bytes 1 | tf_op jit(solution)/shard_map/key/pallas_call | solution.py:45
  62.7 1.0 %final.1 = f32[512,256]{1,0:T(8,128)} custom-call(bf16[128,512]{1,0:T(8,128)(2,1)S(1)} %get-tuple-element.76.refs_0_, bf16[128,512]{1,0:T(8,128)(2,1)S(1)} %collective-permute-done.17.refs_1_, bf16[128,512]{1,0:T(8,128)(2,1)S(1)} %get-tuple-element.81.refs_2_, bf16[128,512]{1,0:T(8,128)(2,1)S(1)} %collective-permute-done.20.refs_3_), custom_call_target="tpu_custom_call" | custom-call | flops 1 | bytes 1 | tf_op jit(solution)/shard_map/final/pallas_call | solution.py:45
  (49 shorter events, 4.8 us)
Async XLA Ops:
  0.6 17.8 %copy-start = (bf16[1,512,2048]{2,1,0:T(8,128)(2,1)S(1)}, bf16[1,512,2048]{2,1,0:T(8,128)(2,1)}, u32[]{:S(2)}) copy-start(bf16[1,512,2048]{2,1,0:T(8,128)(2,1)} %param.11) | copy-start | bytes 6291460
  0.6 12.8 %copy-start.2 = (bf16[1,512,256]{2,1,0:T(8,128)(2,1)S(1)}, bf16[1,512,256]{2,1,0:T(8,128)(2,1)}, u32[]{:S(2)}) copy-start(bf16[1,512,256]{2,1,0:T(8,128)(2,1)} %param.8) | copy-start | bytes 786436
  0.7 12.7 %copy-start.6 = (bf16[1,512,256]{2,1,0:T(8,128)(2,1)S(1)}, bf16[1,512,256]{2,1,0:T(8,128)(2,1)}, u32[]{:S(2)}) copy-start(bf16[1,512,256]{2,1,0:T(8,128)(2,1)} %param.6) | copy-start | bytes 786436
  0.7 17.7 %collective-permute-start.3 = (bf16[512,2048]{1,0:T(8,128)(2,1)}, bf16[512,2048]{1,0:T(8,128)(2,1)S(1)}, u32[]{:S(2)}, u32[]{:S(2)}) collective-permute-start(bf16[512,2048]{1,0:T(8,128)(2,1)} %bitcast.9), channel_id=1, source_target_pairs={{0,1},{1,0},{2,3},{3,2},{4,5},{5,4},{6,7},{7,6},{8,9},{9,8},{10,11... | collective-permute-start | bytes 6291464 | tf_op jit(solution)/shard_map/ppermute | solution.py:311
  3.0 15.4 %collective-permute-start.4 = (bf16[2048,128]{1,0:T(8,128)(2,1)}, bf16[2048,128]{1,0:T(8,128)(2,1)S(1)}, u32[]{:S(2)}, u32[]{:S(2)}) collective-permute-start(bf16[2048,128]{1,0:T(8,128)(2,1)} %far.1), channel_id=1, source_target_pairs={{0,2},{2,0},{1,3},{3,1},{4,6},{6,4},{5,7},{7,5},{8,10},{10,8},{9,1... | collective-permute-start | bytes 1572872 | tf_op jit(solution)/shard_map/ppermute | solution.py:311
  7.8 13.7 %collective-permute-start = (bf16[512,128]{1,0:T(8,128)(2,1)}, bf16[512,128]{1,0:T(8,128)(2,1)S(1)}, u32[]{:S(2)}, u32[]{:S(2)}) collective-permute-start(bf16[512,128]{1,0:T(8,128)(2,1)} %get-tuple-element.45.refs_1_), channel_id=1, source_target_pairs={{0,4},{4,8},{8,12},{12,0},{1,5},{5,9},{9,13},{13,1},{2,6},{6,10},{... | collective-permute-start | bytes 393224 | tf_op jit(solution)/shard_map/ppermute | solution.py:320
  9.5 12.1 %collective-permute-start.1 = (bf16[512,128]{1,0:T(8,128)(2,1)}, bf16[512,128]{1,0:T(8,128)(2,1)S(1)}, u32[]{:S(2)}, u32[]{:S(2)}) collective-permute-start(bf16[512,128]{1,0:T(8,128)(2,1)} %get-tuple-element.45.refs_1_), channel_id=1, source_target_pairs={{0,8},{4,12},{8,0},{12,4},{1,9},{5,13},{9,1},{13,5},{2,10},{6,14},... | collective-permute-start | bytes 393224 | tf_op jit(solution)/shard_map/ppermute | solution.py:320
  12.0 9.5 %collective-permute-start.2 = (bf16[512,128]{1,0:T(8,128)(2,1)}, bf16[512,128]{1,0:T(8,128)(2,1)S(1)}, u32[]{:S(2)}, u32[]{:S(2)}) collective-permute-start(bf16[512,128]{1,0:T(8,128)(2,1)} %get-tuple-element.45.refs_1_), channel_id=1, source_target_pairs={{0,12},{4,0},{8,4},{12,8},{1,13},{5,1},{9,5},{13,9},{2,14},{6,2},{... | collective-permute-start | bytes 393224 | tf_op jit(solution)/shard_map/ppermute | solution.py:320
  13.4 1.0 %copy-start.3 = (bf16[512,256]{1,0:T(8,128)(2,1)S(1)}, bf16[512,256]{1,0:T(8,128)(2,1)}, u32[]{:S(2)}) copy-start(bf16[512,256]{1,0:T(8,128)(2,1)} %get-tuple-element.46.kf_ref.refs_5_) | copy-start | bytes 786436
  15.0 6.5 %copy-start.8 = (s32[2,8,4]{1,2,0:T(4,128)S(1)}, s32[2,8,4]{1,2,0:T(4,128)}, u32[]{:S(2)}) copy-start(s32[2,8,4]{1,2,0:T(4,128)} %param.9) | copy-start | bytes 772
  15.0 6.5 %copy-start.10 = (bf16[512,128]{1,0:T(8,128)(2,1)S(1)}, bf16[512,128]{1,0:T(8,128)(2,1)}, u32[]{:S(2)}) copy-start(bf16[512,128]{1,0:T(8,128)(2,1)} %get-tuple-element.45.refs_1_) | copy-start | bytes 393220
  19.7 6.4 %collective-permute-start.6 = (bf16[512,128]{1,0:T(8,128)(2,1)S(1)}, bf16[512,128]{1,0:T(8,128)(2,1)S(1)}, u32[]{:S(2)}, u32[]{:S(2)}) collective-permute-start(bf16[512,128]{1,0:T(8,128)(2,1)S(1)} %get-tuple-element.50), channel_id=1, source_target_pairs={{0,3},{1,2},{2,1},{3,0},{4,7},{5,6},{6,5},{7,4},{8,11},{9,10},{10,... | collective-permute-start | bytes 393224 | tf_op jit(solution)/shard_map/ppermute | solution.py:365
  20.6 8.0 %collective-permute-start.5 = (bf16[512,128]{1,0:T(8,128)(2,1)S(1)}, bf16[512,128]{1,0:T(8,128)(2,1)S(1)}, u32[]{:S(2)}, u32[]{:S(2)}) collective-permute-start(bf16[512,128]{1,0:T(8,128)(2,1)S(1)} %get-tuple-element.54), channel_id=1, source_target_pairs={{0,2},{2,0},{1,3},{3,1},{4,6},{6,4},{5,7},{7,5},{8,10},{10,8},{9,1... | collective-permute-start | bytes 393224 | tf_op jit(solution)/shard_map/ppermute | solution.py:311
  21.6 3.6 %copy-start.1 = (bf16[4096,256]{1,0:T(8,128)(2,1)S(1)}, bf16[4096,256]{1,0:T(8,128)(2,1)}, u32[]{:S(2)}) copy-start(bf16[4096,256]{1,0:T(8,128)(2,1)} %w_ref.3) | copy-start | bytes 6291460
  23.4 5.8 %collective-permute-start.8 = (bf16[512,256]{1,0:T(8,128)(2,1)}, bf16[512,256]{1,0:T(8,128)(2,1)S(1)}, u32[]{:S(2)}, u32[]{:S(2)}) collective-permute-start(bf16[512,256]{1,0:T(8,128)(2,1)} %get-tuple-element.61.attn_ref), channel_id=1, source_target_pairs={{0,1},{1,0},{2,3},{3,2},{4,5},{5,4},{6,7},{7,6},{8,9},{9,8},{10,11... | collective-permute-start | bytes 786440 | tf_op jit(solution)/shard_map/ppermute | solution.py:311
  23.5 11.0 %collective-permute-start.11 = (bf16[512,256]{1,0:T(8,128)(2,1)}, bf16[512,256]{1,0:T(8,128)(2,1)S(1)}, u32[]{:S(2)}, u32[]{:S(2)}) collective-permute-start(bf16[512,256]{1,0:T(8,128)(2,1)} %get-tuple-element.61.attn_ref), channel_id=1, source_target_pairs={{0,2},{2,0},{1,3},{3,1},{4,6},{6,4},{5,7},{7,5},{8,10},{10,8},{9,1... | collective-permute-start | bytes 786440 | tf_op jit(solution)/shard_map/ppermute | solution.py:311
  28.6 1.0 %copy-start.7 = (bf16[512,256]{1,0:T(8,128)(2,1)S(1)}, bf16[512,256]{1,0:T(8,128)(2,1)}, u32[]{:S(2)}) copy-start(bf16[512,256]{1,0:T(8,128)(2,1)} %get-tuple-element.61.attn_ref) | copy-start | bytes 786436
  30.3 11.2 %collective-permute-start.9 = (bf16[256,512]{1,0:T(8,128)(2,1)S(1)}, bf16[256,512]{1,0:T(8,128)(2,1)S(1)}, u32[]{:S(2)}, u32[]{:S(2)}) collective-permute-start(bf16[256,512]{1,0:T(8,128)(2,1)S(1)} %get-tuple-element.63), channel_id=1, source_target_pairs={{0,4},{4,0},{8,12},{12,8},{1,5},{5,1},{9,13},{13,9},{2,6},{6,2},{1... | collective-permute-start | bytes 786440 | tf_op jit(solution)/shard_map/ppermute | solution.py:398
  32.0 9.3 %collective-permute-start.7 = (bf16[512,128]{1,0:T(8,128)(2,1)S(1)}, bf16[512,128]{1,0:T(8,128)(2,1)S(1)}, u32[]{:S(2)}, u32[]{:S(2)}) collective-permute-start(bf16[512,128]{1,0:T(8,128)(2,1)S(1)} %get-tuple-element.60.cg_ref.refs_1_), channel_id=1, source_target_pairs={{0,8},{4,12},{8,0},{12,4},{1,9},{5,13},{9,1},{13,5},{2,10},{6,14},... | collective-permute-start | bytes 393224 | tf_op jit(solution)/shard_map/ppermute | solution.py:389
  34.6 1.9 %collective-permute-start.14 = (bf16[192,256]{1,0:T(8,128)(2,1)S(1)}, bf16[192,256]{1,0:T(8,128)(2,1)S(1)}, u32[]{:S(2)}, u32[]{:S(2)}) collective-permute-start(bf16[192,256]{1,0:T(8,128)(2,1)S(1)} %get-tuple-element.72), channel_id=1, source_target_pairs={{0,1},{1,0},{2,3},{3,2},{4,5},{5,4},{6,7},{7,6},{8,9},{9,8},{10,11... | collective-permute-start | bytes 294920 | tf_op jit(solution)/shard_map/ppermute | solution.py:311
  34.6 1.4 %collective-permute-start.12 = (bf16[160,256]{1,0:T(8,128)(2,1)S(1)}, bf16[160,256]{1,0:T(8,128)(2,1)S(1)}, u32[]{:S(2)}, u32[]{:S(2)}) collective-permute-start(bf16[160,256]{1,0:T(8,128)(2,1)S(1)} %get-tuple-element.70), channel_id=1, source_target_pairs={{0,1},{1,0},{2,3},{3,2},{4,5},{5,4},{6,7},{7,6},{8,9},{9,8},{10,11... | collective-permute-start | bytes 245768 | tf_op jit(solution)/shard_map/ppermute | solution.py:311
  35.1 1.3 %collective-permute-start.13 = (bf16[160,256]{1,0:T(8,128)(2,1)S(1)}, bf16[160,256]{1,0:T(8,128)(2,1)S(1)}, u32[]{:S(2)}, u32[]{:S(2)}) collective-permute-start(bf16[160,256]{1,0:T(8,128)(2,1)S(1)} %get-tuple-element.71), channel_id=1, source_target_pairs={{0,1},{1,0},{2,3},{3,2},{4,5},{5,4},{6,7},{7,6},{8,9},{9,8},{10,11... | collective-permute-start | bytes 245768 | tf_op jit(solution)/shard_map/ppermute | solution.py:311
  37.0 10.0 %collective-permute-start.15 = (bf16[128,512]{1,0:T(8,128)(2,1)S(1)}, bf16[128,512]{1,0:T(8,128)(2,1)S(1)}, u32[]{:S(2)}, u32[]{:S(2)}) collective-permute-start(bf16[128,512]{1,0:T(8,128)(2,1)S(1)} %get-tuple-element.73), channel_id=1, source_target_pairs={{0,2},{2,0},{1,3},{3,1},{4,6},{6,4},{5,7},{7,5},{8,10},{10,8},{9,1... | collective-permute-start | bytes 393224 | tf_op jit(solution)/shard_map/ppermute | solution.py:311
  37.9 9.0 %collective-permute-start.16 = (bf16[128,512]{1,0:T(8,128)(2,1)S(1)}, bf16[128,512]{1,0:T(8,128)(2,1)S(1)}, u32[]{:S(2)}, u32[]{:S(2)}) collective-permute-start(bf16[128,512]{1,0:T(8,128)(2,1)S(1)} %get-tuple-element.74), channel_id=1, source_target_pairs={{6,0},{4,2},{2,4},{0,6},{14,8},{12,10},{10,12},{8,14},{7,1},{5,3},... | collective-permute-start | bytes 393224 | tf_op jit(solution)/shard_map/ppermute | solution.py:414
  41.6 12.7 %copy-start.4 = (bf16[512,256]{1,0:T(8,128)(2,1)S(1)}, bf16[512,256]{1,0:T(8,128)(2,1)}, u32[]{:S(2)}) copy-start(bf16[512,256]{1,0:T(8,128)(2,1)} %get-tuple-element.46.kf_ref.refs_5_) | copy-start | bytes 786436
  42.1 8.9 %collective-permute-start.18 = (bf16[128,512]{1,0:T(8,128)(2,1)S(1)}, bf16[128,512]{1,0:T(8,128)(2,1)S(1)}, u32[]{:S(2)}, u32[]{:S(2)}) collective-permute-start(bf16[128,512]{1,0:T(8,128)(2,1)S(1)} %get-tuple-element.79), channel_id=1, source_target_pairs={{0,2},{2,0},{1,3},{3,1},{4,6},{6,4},{5,7},{7,5},{8,10},{10,8},{9,1... | collective-permute-start | bytes 393224 | tf_op jit(solution)/shard_map/ppermute | solution.py:311
  43.9 7.1 %collective-permute-start.19 = (bf16[128,512]{1,0:T(8,128)(2,1)S(1)}, bf16[128,512]{1,0:T(8,128)(2,1)S(1)}, u32[]{:S(2)}, u32[]{:S(2)}) collective-permute-start(bf16[128,512]{1,0:T(8,128)(2,1)S(1)} %get-tuple-element.80), channel_id=1, source_target_pairs={{6,0},{4,2},{2,4},{0,6},{14,8},{12,10},{10,12},{8,14},{7,1},{5,3},... | collective-permute-start | bytes 393224 | tf_op jit(solution)/shard_map/ppermute | solution.py:414
  47.0 15.7 %collective-permute-start.17 = (bf16[128,512]{1,0:T(8,128)(2,1)S(1)}, bf16[128,512]{1,0:T(8,128)(2,1)S(1)}, u32[]{:S(2)}, u32[]{:S(2)}) collective-permute-start(bf16[128,512]{1,0:T(8,128)(2,1)S(1)} %get-tuple-element.77), channel_id=1, source_target_pairs={{0,8},{4,12},{8,0},{12,4},{1,9},{5,13},{9,1},{13,5},{2,10},{6,14},... | collective-permute-start | bytes 393224 | tf_op jit(solution)/shard_map/ppermute | solution.py:450
  48.6 12.2 %collective-permute-start.10 = (bf16[1024,128]{1,0:T(8,128)(2,1)S(1)}, bf16[1024,128]{1,0:T(8,128)(2,1)S(1)}, u32[]{:S(2)}, u32[]{:S(2)}) collective-permute-start(bf16[1024,128]{1,0:T(8,128)(2,1)S(1)} %get-tuple-element.64), channel_id=1, source_target_pairs={{0,4},{4,0},{8,12},{12,8},{1,5},{5,1},{9,13},{13,9},{2,6},{6,2},{1... | collective-permute-start | bytes 786440 | tf_op jit(solution)/shard_map/ppermute | solution.py:428
  51.1 11.6 %collective-permute-start.20 = (bf16[128,512]{1,0:T(8,128)(2,1)S(1)}, bf16[128,512]{1,0:T(8,128)(2,1)S(1)}, u32[]{:S(2)}, u32[]{:S(2)}) collective-permute-start(bf16[128,512]{1,0:T(8,128)(2,1)S(1)} %get-tuple-element.82), channel_id=1, source_target_pairs={{0,8},{4,12},{8,0},{12,4},{1,9},{5,13},{9,1},{13,5},{2,10},{6,14},... | collective-permute-start | bytes 393224 | tf_op jit(solution)/shard_map/ppermute | solution.py:450
  54.3 6.5 %copy-start.5 = (bf16[1,512,256]{2,1,0:T(8,128)(2,1)S(1)}, bf16[1,512,256]{2,1,0:T(8,128)(2,1)}, u32[]{:S(2)}) copy-start(bf16[1,512,256]{2,1,0:T(8,128)(2,1)} %param.7) | copy-start | bytes 786436
  54.3 6.5 %copy-start.9 = (s32[2,8,4]{1,2,0:T(4,128)S(1)}, s32[2,8,4]{1,2,0:T(4,128)}, u32[]{:S(2)}) copy-start(s32[2,8,4]{1,2,0:T(4,128)} %param.9) | copy-start | bytes 772

commit v8 on v7

--- a/solution.py
+++ b/solution.py
@@ -208,7 +208,9 @@
         cg_ref[mat(i), :] = mm(qf_ref[r, c], dnum, TN).astype(BF16)
 
 
-def query_body(q_ref, qf_ref, kf_ref, v_ref, dnum_ref, carried_ref, sc_ref, dq_ref, dk_ref, dv_ref):
+def query_body(q_ref, qf_ref, kf_ref, v_ref, dnum_ref, carried_ref, sc_ref, attn_ref, *outs):
+    dq_ref, dk_ref, dv_ref, attn_out_ref = outs
+    attn_out_ref[...] = attn_ref[...]
     keep = causal()
     for i, r, c in tiles(q_ref.shape[0], q_ref.shape[1] // DH):
         dnum = dnum_ref[r, c]
@@ -429,24 +431,18 @@
         second_owner = by_flip
     else:
         cparts, second_owner = gather_parts(cg, seq_size), first_owner
-    dq, dkp, dvp = call(
+    dq, dkp, dvp, attn_out = call(
         query_body,
-        (rows16, flat, flat),
-        (q, qf, kf, v, dnum, carried, sc),
+        (rows16, flat, flat, rows16),
+        (q, qf, kf, v, dnum, carried, sc, attn),
         9 * unit,
         "query",
     )
-    dk, dv = call(
-        functools.partial(key_body, (nb, heads, second_owner), len(cparts)),
-        (rows16, rows16),
-        (lay, *cparts, k, kf, v, dkp, dvp),
-        2 * unit,
-        "key",
-    )
     if paired:
         sums = []
-        for i, (k, g) in enumerate(crossed):
-            send, stay = call(functools.partial(cross_body, i), (half, half), (k, g, mine), 0, "cross")
+        for i, (straight, diagonal) in enumerate(crossed):
+            send, stay = call(functools.partial(cross_body, i), (half, half), (straight, diagonal, mine), 0, "cross")
+            mine = after(mine, send)
             sums += [stay, lax.ppermute(send, "seq", [(s, s ^ 2) for s in range(4)])]
         (weight_grad,) = call(final_body, (sds(block[::-1], F32),), tuple(sums), 0, "final")
     else:
@@ -456,7 +452,16 @@
             scatter_dimension=0,
             tiled=True,
         ).astype(F32)
-    return attn[None], dq[None], dk[None], dv[None], weight_grad
+    if paired:
+        dkp = after(dkp, weight_grad)
+    dk, dv = call(
+        functools.partial(key_body, (nb, heads, second_owner), len(cparts)),
+        (rows16, rows16),
+        (lay, *cparts, k, kf, v, dkp, dvp),
+        2 * unit,
+        "key",
+    )
+    return attn_out[None], dq[None], dk[None], dv[None], weight_grad
 
 
 def solution(mesh):

time: 63.9 us -> 63.1 us (0.987)
    ppermute x1, waiting for transfers between devices: 4.56 us -> 0.01 us  [per_device(): cparts = [cg, two, lax.ppermute(joined, 'seq', neighbours)]]
    ppermute x2, waiting for transfers between devices: 0.01 us -> 4.47 us  [per_device(): sums += [stay, lax.ppermute(send, 'seq', [(s, s ^ 2) for s in range(4)])]]
    ppermute x1, waiting for transfers between devices: 1.54 us -> 0.83 us  [per_device(): two = lax.ppermute(cg, 'seq', [(i, i ^ 2) for i in range(4)])]
    unnamed x22 -> x20, local copies, waits for them, and re-layouts: 1.36 us -> 1 us
  transfers between devices with their start and end apart: 21 -> 21, of which waited for: 8 -> 8; matrix products, arithmetic and copies ran while one was open for 0% -> 0% of each run, Pallas kernels for 23% -> 21%
where the time goes in v8:
time: 63.1 us; the launch traced here: 62.9 us
  starting transfers between devices  30.9 us (49%)
  Pallas kernels  15.2 us (24%)
  waiting for transfers between devices  15 us (24%)
  local copies, waits for them, and re-layouts  1 us (2%)
  between operations  0.84 us (1%)
    pallas_call x14, Pallas kernels, call(): pl.pallas_call(body, out_shape=outs, in_specs=[SM if a.dtype == jnp.int32...  10.5 us
    ppermute x10, starting transfers between devices, swap(): return lax.ppermute(x, axis, [(0, 1), (1, 0)])  9.57 us
    ppermute x10, waiting for transfers between devices, swap(): return lax.ppermute(x, axis, [(0, 1), (1, 0)])  9.09 us
    ppermute x3, starting transfers between devices, gather_parts(): parts.append(lax.ppermute(x, 'seq', pairs))  5.57 us
    ppermute x2, starting transfers between devices, cross_piece(): lax.ppermute(give, ('seq', 'head'), beside)  4.68 us
    ppermute x2, waiting for transfers between devices, per_device(): sums += [stay, lax.ppermute(send, 'seq', [(s, s ^ 2) for s in range(4)])]  4.47 us
    ppermute x2, starting transfers between devices, per_device(): sums += [stay, lax.ppermute(send, 'seq', [(s, s ^ 2) for s in range(4)])]  4.34 us
    ppermute x1, starting transfers between devices, per_device(): two = lax.ppermute(cg, 'seq', [(i, i ^ 2) for i in range(4)])  2.59 us
  transfers between devices with their start and end apart: 21, of which 8 were waited for; matrix products, arithmetic and copies ran while one was open for 0% of the time, Pallas kernels for 21%

profile of v8, /device:TPU:0, one launch (start us, length us, event | category | flops | bytes accessed | tf_op | source)
XLA Modules:
  0.0 62.9 jit_solution(11970969887548000487)
XLA Ops:
  1.2 1.8 %far.1 = bf16[2048,128]{1,0:T(8,128)(2,1)} custom-call(bf16[4096,256]{1,0:T(8,128)(2,1)} %w_ref.3), custom_call_target="tpu_custom_call" | custom-call | flops 1 | bytes 1 | tf_op jit(solution)/shard_map/far/pallas_call | solution.py:83
  3.0 2.7 %collective-permute-start.4 = (bf16[2048,128]{1,0:T(8,128)(2,1)}, bf16[2048,128]{1,0:T(8,128)(2,1)S(1)}, u32[]{:S(2)}, u32[]{:S(2)}) collective-permute-start(bf16[2048,128]{1,0:T(8,128)(2,1)} %far.1), channel_id=1, source_target_pairs={{0,2},{2,0},{1,3},{3,1},{4,6},{6,4},{5,7},{7,5},{8,10},{10,8},{9,1... | collective-permute-start | bytes 1572872 | tf_op jit(solution)/shard_map/ppermute | solution.py:313
  5.8 2.1 %begin.1 = (bf16[512,256]{1,0:T(8,128)(2,1)}, bf16[512,128]{1,0:T(8,128)(2,1)}) custom-call(bf16[512,256]{1,0:T(8,128)(2,1)} %bitcast.19, bf16[512,256]{1,0:T(8,128)(2,1)} %bitcast.15), custom_call_target="tpu_custom_call" | custom-call | flops 1 | bytes 1 | tf_op jit(solution)/shard_map/begin/pallas_call | solution.py:109
  7.8 1.6 %collective-permute-start = (bf16[512,128]{1,0:T(8,128)(2,1)}, bf16[512,128]{1,0:T(8,128)(2,1)S(1)}, u32[]{:S(2)}, u32[]{:S(2)}) collective-permute-start(bf16[512,128]{1,0:T(8,128)(2,1)} %get-tuple-element.50.refs_1_), channel_id=1, source_target_pairs={{0,4},{4,8},{8,12},{12,0},{1,5},{5,9},{9,13},{13,1},{2,6},{6,10},{... | collective-permute-start | bytes 393224 | tf_op jit(solution)/shard_map/ppermute | solution.py:322
  9.5 2.6 %collective-permute-start.1 = (bf16[512,128]{1,0:T(8,128)(2,1)}, bf16[512,128]{1,0:T(8,128)(2,1)S(1)}, u32[]{:S(2)}, u32[]{:S(2)}) collective-permute-start(bf16[512,128]{1,0:T(8,128)(2,1)} %get-tuple-element.50.refs_1_), channel_id=1, source_target_pairs={{0,8},{4,12},{8,0},{12,4},{1,9},{5,13},{9,1},{13,5},{2,10},{6,14},... | collective-permute-start | bytes 393224 | tf_op jit(solution)/shard_map/ppermute | solution.py:322
  12.0 1.3 %collective-permute-start.2 = (bf16[512,128]{1,0:T(8,128)(2,1)}, bf16[512,128]{1,0:T(8,128)(2,1)S(1)}, u32[]{:S(2)}, u32[]{:S(2)}) collective-permute-start(bf16[512,128]{1,0:T(8,128)(2,1)} %get-tuple-element.50.refs_1_), channel_id=1, source_target_pairs={{0,12},{4,0},{8,4},{12,8},{1,13},{5,1},{9,5},{13,9},{2,14},{6,2},{... | collective-permute-start | bytes 393224 | tf_op jit(solution)/shard_map/ppermute | solution.py:322
  13.4 0.9 %copy-done.3 = bf16[512,256]{1,0:T(8,128)(2,1)S(1)} copy-done((bf16[512,256]{1,0:T(8,128)(2,1)S(1)}, bf16[512,256]{1,0:T(8,128)(2,1)}, u32[]{:S(2)}) %copy-start.3) | copy-done | bytes 262168
  15.0 3.4 %collective-permute-done.4.w_ref = bf16[2048,128]{1,0:T(8,128)(2,1)S(1)} collective-permute-done((bf16[2048,128]{1,0:T(8,128)(2,1)}, bf16[2048,128]{1,0:T(8,128)(2,1)S(1)}, u32[]{:S(2)}, u32[]{:S(2)}) %collective-permute-start.4) | collective-permute-done | bytes 524320 | tf_op jit(solution)/shard_map/ppermute | solution.py:313
  18.4 1.2 %other.1 = (bf16[512,128]{1,0:T(8,128)(2,1)S(1)}, bf16[512,128]{1,0:T(8,128)(2,1)S(1)}) custom-call(bf16[512,2048]{1,0:T(8,128)(2,1)S(1)} %bitcast.10, bf16[512,2048]{1,0:T(8,128)(2,1)S(1)} %collective-permute-done.3.og_sib_ref, bf16[2048,128]{1,0:T(8,128)(2,1)S(1)} %collective-permute-done.4.w_ref), custom_call_target="tpu_custom_call" | custom-call | flops 1 | bytes 1 | tf_op jit(solution)/shard_map/other/pallas_call | solution.py:45
  19.7 1.0 %collective-permute-start.6 = (bf16[512,128]{1,0:T(8,128)(2,1)S(1)}, bf16[512,128]{1,0:T(8,128)(2,1)S(1)}, u32[]{:S(2)}, u32[]{:S(2)}) collective-permute-start(bf16[512,128]{1,0:T(8,128)(2,1)S(1)} %get-tuple-element.53), channel_id=1, source_target_pairs={{0,3},{1,2},{2,1},{3,0},{4,7},{5,6},{6,5},{7,4},{8,11},{9,10},{10,... | collective-permute-start | bytes 393224 | tf_op jit(solution)/shard_map/ppermute | solution.py:367
  20.6 0.9 %collective-permute-start.5 = (bf16[512,128]{1,0:T(8,128)(2,1)S(1)}, bf16[512,128]{1,0:T(8,128)(2,1)S(1)}, u32[]{:S(2)}, u32[]{:S(2)}) collective-permute-start(bf16[512,128]{1,0:T(8,128)(2,1)S(1)} %get-tuple-element.57), channel_id=1, source_target_pairs={{0,2},{2,0},{1,3},{3,1},{4,6},{6,4},{5,7},{7,5},{8,10},{10,8},{9,1... | collective-permute-start | bytes 393224 | tf_op jit(solution)/shard_map/ppermute | solution.py:313
  21.6 1.1 %numer.1 = (bf16[512,128]{1,0:T(8,128)(2,1)S(1)}, f32[512,256]{1,0:T(8,128)S(1)}, bf16[512,256]{1,0:T(8,128)(2,1)S(1)}) custom-call(s32[2,4,8]{2,1,0:T(4,128)S(1)} %bitcast.23, bf16[512,128]{1,0:T(8,128)(2,1)S(1)} %copy-done.9, bf16[512,128]{1,0:T(8,128)(2,1)S(1)} %collective-permute-done.refs_2_, bf16[512,128]{1,0:T(8,128)(2,1)S(1)} %collective-permute-done.1.refs_3_, ...), custom_call_target="tpu_custom_call" | custom-call | flops 99999997952 | bytes 1 | tf_op jit(solution)/shard_map/numer/pallas_call | solution.py:45
  22.9 1.7 %collective-permute-start.11 = (bf16[512,256]{1,0:T(8,128)(2,1)S(1)}, bf16[512,256]{1,0:T(8,128)(2,1)S(1)}, u32[]{:S(2)}, u32[]{:S(2)}) collective-permute-start(bf16[512,256]{1,0:T(8,128)(2,1)S(1)} %get-tuple-element.65.attn_ref), channel_id=1, source_target_pairs={{0,2},{2,0},{1,3},{3,1},{4,6},{6,4},{5,7},{7,5},{8,10},{10,8},{9,1... | collective-permute-start | bytes 786440 | tf_op jit(solution)/shard_map/ppermute | solution.py:313
  24.6 0.8 %own_partial.1.refs_0_ = f32[512,256]{1,0:T(8,128)S(1)} custom-call(bf16[512,2048]{1,0:T(8,128)(2,1)S(1)} %bitcast.11, bf16[4096,256]{1,0:T(8,128)(2,1)S(1)} %copy-done.1), custom_call_target="tpu_custom_call" | custom-call | flops 1 | bytes 1 | tf_op jit(solution)/shard_map/own_partial/pallas_call | solution.py:255
  25.4 3.2 %collective-permute-done.5.refs_1_ = bf16[512,128]{1,0:T(8,128)(2,1)S(1)} collective-permute-done((bf16[512,128]{1,0:T(8,128)(2,1)S(1)}, bf16[512,128]{1,0:T(8,128)(2,1)S(1)}, u32[]{:S(2)}, u32[]{:S(2)}) %collective-permute-start.5) | collective-permute-done | bytes 131104 | tf_op jit(solution)/shard_map/ppermute | solution.py:313
  29.2 0.7 %weight.3 = (bf16[256,512]{1,0:T(8,128)(2,1)S(1)}, f32[256,512]{1,0:T(8,128)S(1)}) custom-call(bf16[512,256]{1,0:T(8,128)(2,1)S(1)} %get-tuple-element.65.attn_ref, bf16[512,2048]{1,0:T(8,128)(2,1)S(1)} %bitcast.12, bf16[512,2048]{1,0:T(8,128)(2,1)S(1)} %collective-permute-done.3.og_sib_ref, bf16[512,256]{1,0:T(8,128)(2,1)S(1)} %collective-permute-done.8.refs_0_), custom_call_target="tpu_custom_call" | custom-call | flops 1 | bytes 1 | tf_op jit(solution)/shard_map/weight/pallas_call | solution.py:45
  30.0 1.6 %collective-permute-start.9 = (bf16[256,512]{1,0:T(8,128)(2,1)S(1)}, bf16[256,512]{1,0:T(8,128)(2,1)S(1)}, u32[]{:S(2)}, u32[]{:S(2)}) collective-permute-start(bf16[256,512]{1,0:T(8,128)(2,1)S(1)} %get-tuple-element.67), channel_id=1, source_target_pairs={{0,4},{4,0},{8,12},{12,8},{1,5},{5,1},{9,13},{13,9},{2,6},{6,2},{1... | collective-permute-start | bytes 786440 | tf_op jit(solution)/shard_map/ppermute | solution.py:400
  31.6 2.6 %collective-permute-start.7 = (bf16[512,128]{1,0:T(8,128)(2,1)S(1)}, bf16[512,128]{1,0:T(8,128)(2,1)S(1)}, u32[]{:S(2)}, u32[]{:S(2)}) collective-permute-start(bf16[512,128]{1,0:T(8,128)(2,1)S(1)} %get-tuple-element.64.cg_ref.refs_1_), channel_id=1, source_target_pairs={{0,8},{4,12},{8,0},{12,4},{1,9},{5,13},{9,1},{13,5},{2,10},{6,14},... | collective-permute-start | bytes 393224 | tf_op jit(solution)/shard_map/ppermute | solution.py:391
  34.9 0.8 %collective-permute-done.12.refs_0_ = bf16[160,256]{1,0:T(8,128)(2,1)S(1)} collective-permute-done((bf16[160,256]{1,0:T(8,128)(2,1)S(1)}, bf16[160,256]{1,0:T(8,128)(2,1)S(1)}, u32[]{:S(2)}, u32[]{:S(2)}) %collective-permute-start.12) | collective-permute-done | bytes 81952 | tf_op jit(solution)/shard_map/ppermute | solution.py:313
  36.6 1.1 %collective-permute-start.15 = (bf16[128,512]{1,0:T(8,128)(2,1)S(1)}, bf16[128,512]{1,0:T(8,128)(2,1)S(1)}, u32[]{:S(2)}, u32[]{:S(2)}) collective-permute-start(bf16[128,512]{1,0:T(8,128)(2,1)S(1)} %get-tuple-element.74), channel_id=1, source_target_pairs={{0,2},{2,0},{1,3},{3,1},{4,6},{6,4},{5,7},{7,5},{8,10},{10,8},{9,1... | collective-permute-start | bytes 393224 | tf_op jit(solution)/shard_map/ppermute | solution.py:313
  37.7 2.1 %collective-permute-start.16 = (bf16[128,512]{1,0:T(8,128)(2,1)S(1)}, bf16[128,512]{1,0:T(8,128)(2,1)S(1)}, u32[]{:S(2)}, u32[]{:S(2)}) collective-permute-start(bf16[128,512]{1,0:T(8,128)(2,1)S(1)} %get-tuple-element.75), channel_id=1, source_target_pairs={{6,0},{4,2},{2,4},{0,6},{14,8},{12,10},{10,12},{8,14},{7,1},{5,3},... | collective-permute-start | bytes 393224 | tf_op jit(solution)/shard_map/ppermute | solution.py:416
  39.7 0.8 %collective-permute-done.7.two_ref.refs_2_ = bf16[512,128]{1,0:T(8,128)(2,1)S(1)} collective-permute-done((bf16[512,128]{1,0:T(8,128)(2,1)S(1)}, bf16[512,128]{1,0:T(8,128)(2,1)S(1)}, u32[]{:S(2)}, u32[]{:S(2)}) %collective-permute-start.7) | collective-permute-done | bytes 131104 | tf_op jit(solution)/shard_map/ppermute | solution.py:391
  41.7 1.8 %collective-permute-start.18 = (bf16[128,512]{1,0:T(8,128)(2,1)S(1)}, bf16[128,512]{1,0:T(8,128)(2,1)S(1)}, u32[]{:S(2)}, u32[]{:S(2)}) collective-permute-start(bf16[128,512]{1,0:T(8,128)(2,1)S(1)} %get-tuple-element.80), channel_id=1, source_target_pairs={{0,2},{2,0},{1,3},{3,1},{4,6},{6,4},{5,7},{7,5},{8,10},{10,8},{9,1... | collective-permute-start | bytes 393224 | tf_op jit(solution)/shard_map/ppermute | solution.py:313
  43.6 2.6 %collective-permute-start.19 = (bf16[128,512]{1,0:T(8,128)(2,1)S(1)}, bf16[128,512]{1,0:T(8,128)(2,1)S(1)}, u32[]{:S(2)}, u32[]{:S(2)}) collective-permute-start(bf16[128,512]{1,0:T(8,128)(2,1)S(1)} %get-tuple-element.81), channel_id=1, source_target_pairs={{6,0},{4,2},{2,4},{0,6},{14,8},{12,10},{10,12},{8,14},{7,1},{5,3},... | collective-permute-start | bytes 393224 | tf_op jit(solution)/shard_map/ppermute | solution.py:416
  46.3 1.6 %collective-permute-start.17 = (bf16[128,512]{1,0:T(8,128)(2,1)S(1)}, bf16[128,512]{1,0:T(8,128)(2,1)S(1)}, u32[]{:S(2)}, u32[]{:S(2)}) collective-permute-start(bf16[128,512]{1,0:T(8,128)(2,1)S(1)} %get-tuple-element.78), channel_id=1, source_target_pairs={{0,8},{4,12},{8,0},{12,4},{1,9},{5,13},{9,1},{13,5},{2,10},{6,14},... | collective-permute-start | bytes 393224 | tf_op jit(solution)/shard_map/ppermute | solution.py:446
  47.9 1.5 %collective-permute-start.10 = (bf16[1024,128]{1,0:T(8,128)(2,1)S(1)}, bf16[1024,128]{1,0:T(8,128)(2,1)S(1)}, u32[]{:S(2)}, u32[]{:S(2)}) collective-permute-start(bf16[1024,128]{1,0:T(8,128)(2,1)S(1)} %get-tuple-element.68), channel_id=1, source_target_pairs={{0,4},{4,0},{8,12},{12,8},{1,5},{5,1},{9,13},{13,9},{2,6},{6,2},{1... | collective-permute-start | bytes 786440 | tf_op jit(solution)/shard_map/ppermute | solution.py:430
  49.4 1.3 %collective-permute-done.18.keep_ref = bf16[128,512]{1,0:T(8,128)(2,1)S(1)} collective-permute-done((bf16[128,512]{1,0:T(8,128)(2,1)S(1)}, bf16[128,512]{1,0:T(8,128)(2,1)S(1)}, u32[]{:S(2)}, u32[]{:S(2)}) %collective-permute-start.18) | collective-permute-done | bytes 131104 | tf_op jit(solution)/shard_map/ppermute | solution.py:313
  50.8 2.7 %collective-permute-start.20 = (bf16[128,512]{1,0:T(8,128)(2,1)S(1)}, bf16[128,512]{1,0:T(8,128)(2,1)S(1)}, u32[]{:S(2)}, u32[]{:S(2)}) collective-permute-start(bf16[128,512]{1,0:T(8,128)(2,1)S(1)} %get-tuple-element.84), channel_id=1, source_target_pairs={{0,8},{4,12},{8,0},{12,4},{1,9},{5,13},{9,1},{13,5},{2,10},{6,14},... | collective-permute-start | bytes 393224 | tf_op jit(solution)/shard_map/ppermute | solution.py:446
  53.5 2.0 %query.1 = (bf16[512,256]{1,0:T(8,128)(2,1)}, f32[512,256]{1,0:T(8,128)S(1)}, f32[512,256]{1,0:T(8,128)S(1)}, bf16[512,256]{1,0:T(8,128)(2,1)}) custom-call(bf16[512,256]{1,0:T(8,128)(2,1)S(1)} %bitcast.22, bf16[512,256]{1,0:T(8,128)(2,1)S(1)} %get-tuple-element.49.refs_5_.refs_4_.qf_ref, bf16[512,256]{1,0:T(8,128)(2,1)S(1)} %copy-done.4, ...), custom_call_target="tpu_custom_call" | custom-call | flops 99999997952 | bytes 1 | tf_op jit(solution)/shard_map/query/pallas_call | solution.py:45
  55.5 4.5 %collective-permute-done.20.refs_3_ = bf16[128,512]{1,0:T(8,128)(2,1)S(1)} collective-permute-done((bf16[128,512]{1,0:T(8,128)(2,1)S(1)}, bf16[128,512]{1,0:T(8,128)(2,1)S(1)}, u32[]{:S(2)}, u32[]{:S(2)}) %collective-permute-start.20) | collective-permute-done | bytes 131104 | tf_op jit(solution)/shard_map/ppermute | solution.py:446
  60.0 1.0 %final.1 = f32[512,256]{1,0:T(8,128)} custom-call(bf16[128,512]{1,0:T(8,128)(2,1)S(1)} %get-tuple-element.77.refs_0_, bf16[128,512]{1,0:T(8,128)(2,1)S(1)} %collective-permute-done.17.refs_1_, bf16[128,512]{1,0:T(8,128)(2,1)S(1)} %get-tuple-element.83.refs_2_, bf16[128,512]{1,0:T(8,128)(2,1)S(1)} %collective-permute-done.20.refs_3_), custom_call_target="tpu_custom_call" | custom-call | flops 1 | bytes 1 | tf_op jit(solution)/shard_map/final/pallas_call | solution.py:45
  61.0 1.9 %key.1 = (bf16[512,256]{1,0:T(8,128)(2,1)}, bf16[512,256]{1,0:T(8,128)(2,1)}) custom-call(s32[2,4,8]{2,1,0:T(4,128)S(1)} %bitcast.24, bf16[512,128]{1,0:T(8,128)(2,1)S(1)} %get-tuple-element.64.cg_ref.refs_1_, bf16[512,128]{1,0:T(8,128)(2,1)S(1)} %collective-permute-done.7.two_ref.refs_2_, bf16[1024,128]{1,0:T(8,128)(2,1)S(1)} %collective-permute-done.10.refs_3_, ...), custom_call_target="tpu_custom_call" | custom-call | flops 1 | bytes 1 | tf_op jit(solution)/shard_map/key/pallas_call | solution.py:45
  (47 shorter events, 4.8 us)
Async XLA Ops:
  0.6 17.8 %copy-start = (bf16[1,512,2048]{2,1,0:T(8,128)(2,1)S(1)}, bf16[1,512,2048]{2,1,0:T(8,128)(2,1)}, u32[]{:S(2)}) copy-start(bf16[1,512,2048]{2,1,0:T(8,128)(2,1)} %param.11) | copy-start | bytes 6291460
  0.6 12.8 %copy-start.2 = (bf16[1,512,256]{2,1,0:T(8,128)(2,1)S(1)}, bf16[1,512,256]{2,1,0:T(8,128)(2,1)}, u32[]{:S(2)}) copy-start(bf16[1,512,256]{2,1,0:T(8,128)(2,1)} %param.8) | copy-start | bytes 786436
  0.7 12.7 %copy-start.6 = (bf16[1,512,256]{2,1,0:T(8,128)(2,1)S(1)}, bf16[1,512,256]{2,1,0:T(8,128)(2,1)}, u32[]{:S(2)}) copy-start(bf16[1,512,256]{2,1,0:T(8,128)(2,1)} %param.6) | copy-start | bytes 786436
  0.7 17.7 %collective-permute-start.3 = (bf16[512,2048]{1,0:T(8,128)(2,1)}, bf16[512,2048]{1,0:T(8,128)(2,1)S(1)}, u32[]{:S(2)}, u32[]{:S(2)}) collective-permute-start(bf16[512,2048]{1,0:T(8,128)(2,1)} %bitcast.9), channel_id=1, source_target_pairs={{0,1},{1,0},{2,3},{3,2},{4,5},{5,4},{6,7},{7,6},{8,9},{9,8},{10,11... | collective-permute-start | bytes 6291464 | tf_op jit(solution)/shard_map/ppermute | solution.py:313
  3.0 15.4 %collective-permute-start.4 = (bf16[2048,128]{1,0:T(8,128)(2,1)}, bf16[2048,128]{1,0:T(8,128)(2,1)S(1)}, u32[]{:S(2)}, u32[]{:S(2)}) collective-permute-start(bf16[2048,128]{1,0:T(8,128)(2,1)} %far.1), channel_id=1, source_target_pairs={{0,2},{2,0},{1,3},{3,1},{4,6},{6,4},{5,7},{7,5},{8,10},{10,8},{9,1... | collective-permute-start | bytes 1572872 | tf_op jit(solution)/shard_map/ppermute | solution.py:313
  7.8 13.7 %collective-permute-start = (bf16[512,128]{1,0:T(8,128)(2,1)}, bf16[512,128]{1,0:T(8,128)(2,1)S(1)}, u32[]{:S(2)}, u32[]{:S(2)}) collective-permute-start(bf16[512,128]{1,0:T(8,128)(2,1)} %get-tuple-element.50.refs_1_), channel_id=1, source_target_pairs={{0,4},{4,8},{8,12},{12,0},{1,5},{5,9},{9,13},{13,1},{2,6},{6,10},{... | collective-permute-start | bytes 393224 | tf_op jit(solution)/shard_map/ppermute | solution.py:322
  9.5 12.1 %collective-permute-start.1 = (bf16[512,128]{1,0:T(8,128)(2,1)}, bf16[512,128]{1,0:T(8,128)(2,1)S(1)}, u32[]{:S(2)}, u32[]{:S(2)}) collective-permute-start(bf16[512,128]{1,0:T(8,128)(2,1)} %get-tuple-element.50.refs_1_), channel_id=1, source_target_pairs={{0,8},{4,12},{8,0},{12,4},{1,9},{5,13},{9,1},{13,5},{2,10},{6,14},... | collective-permute-start | bytes 393224 | tf_op jit(solution)/shard_map/ppermute | solution.py:322
  12.0 9.5 %collective-permute-start.2 = (bf16[512,128]{1,0:T(8,128)(2,1)}, bf16[512,128]{1,0:T(8,128)(2,1)S(1)}, u32[]{:S(2)}, u32[]{:S(2)}) collective-permute-start(bf16[512,128]{1,0:T(8,128)(2,1)} %get-tuple-element.50.refs_1_), channel_id=1, source_target_pairs={{0,12},{4,0},{8,4},{12,8},{1,13},{5,1},{9,5},{13,9},{2,14},{6,2},{... | collective-permute-start | bytes 393224 | tf_op jit(solution)/shard_map/ppermute | solution.py:322
  13.4 1.0 %copy-start.3 = (bf16[512,256]{1,0:T(8,128)(2,1)S(1)}, bf16[512,256]{1,0:T(8,128)(2,1)}, u32[]{:S(2)}) copy-start(bf16[512,256]{1,0:T(8,128)(2,1)} %get-tuple-element.48.kf_ref.refs_5_) | copy-start | bytes 786436
  15.0 6.5 %copy-start.7 = (s32[2,8,4]{1,2,0:T(4,128)S(1)}, s32[2,8,4]{1,2,0:T(4,128)}, u32[]{:S(2)}) copy-start(s32[2,8,4]{1,2,0:T(4,128)} %param.9) | copy-start | bytes 772
  15.0 6.5 %copy-start.9 = (bf16[512,128]{1,0:T(8,128)(2,1)S(1)}, bf16[512,128]{1,0:T(8,128)(2,1)}, u32[]{:S(2)}) copy-start(bf16[512,128]{1,0:T(8,128)(2,1)} %get-tuple-element.50.refs_1_) | copy-start | bytes 393220
  19.7 9.0 %collective-permute-start.6 = (bf16[512,128]{1,0:T(8,128)(2,1)S(1)}, bf16[512,128]{1,0:T(8,128)(2,1)S(1)}, u32[]{:S(2)}, u32[]{:S(2)}) collective-permute-start(bf16[512,128]{1,0:T(8,128)(2,1)S(1)} %get-tuple-element.53), channel_id=1, source_target_pairs={{0,3},{1,2},{2,1},{3,0},{4,7},{5,6},{6,5},{7,4},{8,11},{9,10},{10,... | collective-permute-start | bytes 393224 | tf_op jit(solution)/shard_map/ppermute | solution.py:367
  20.6 8.0 %collective-permute-start.5 = (bf16[512,128]{1,0:T(8,128)(2,1)S(1)}, bf16[512,128]{1,0:T(8,128)(2,1)S(1)}, u32[]{:S(2)}, u32[]{:S(2)}) collective-permute-start(bf16[512,128]{1,0:T(8,128)(2,1)S(1)} %get-tuple-element.57), channel_id=1, source_target_pairs={{0,2},{2,0},{1,3},{3,1},{4,6},{6,4},{5,7},{7,5},{8,10},{10,8},{9,1... | collective-permute-start | bytes 393224 | tf_op jit(solution)/shard_map/ppermute | solution.py:313
  21.6 3.0 %copy-start.1 = (bf16[4096,256]{1,0:T(8,128)(2,1)S(1)}, bf16[4096,256]{1,0:T(8,128)(2,1)}, u32[]{:S(2)}) copy-start(bf16[4096,256]{1,0:T(8,128)(2,1)} %w_ref.3) | copy-start | bytes 6291460
  22.7 6.5 %collective-permute-start.8 = (bf16[512,256]{1,0:T(8,128)(2,1)S(1)}, bf16[512,256]{1,0:T(8,128)(2,1)S(1)}, u32[]{:S(2)}, u32[]{:S(2)}) collective-permute-start(bf16[512,256]{1,0:T(8,128)(2,1)S(1)} %get-tuple-element.65.attn_ref), channel_id=1, source_target_pairs={{0,1},{1,0},{2,3},{3,2},{4,5},{5,4},{6,7},{7,6},{8,9},{9,8},{10,11... | collective-permute-start | bytes 786440 | tf_op jit(solution)/shard_map/ppermute | solution.py:313
  22.9 11.3 %collective-permute-start.11 = (bf16[512,256]{1,0:T(8,128)(2,1)S(1)}, bf16[512,256]{1,0:T(8,128)(2,1)S(1)}, u32[]{:S(2)}, u32[]{:S(2)}) collective-permute-start(bf16[512,256]{1,0:T(8,128)(2,1)S(1)} %get-tuple-element.65.attn_ref), channel_id=1, source_target_pairs={{0,2},{2,0},{1,3},{3,1},{4,6},{6,4},{5,7},{7,5},{8,10},{10,8},{9,1... | collective-permute-start | bytes 786440 | tf_op jit(solution)/shard_map/ppermute | solution.py:313
  30.0 11.2 %collective-permute-start.9 = (bf16[256,512]{1,0:T(8,128)(2,1)S(1)}, bf16[256,512]{1,0:T(8,128)(2,1)S(1)}, u32[]{:S(2)}, u32[]{:S(2)}) collective-permute-start(bf16[256,512]{1,0:T(8,128)(2,1)S(1)} %get-tuple-element.67), channel_id=1, source_target_pairs={{0,4},{4,0},{8,12},{12,8},{1,5},{5,1},{9,13},{13,9},{2,6},{6,2},{1... | collective-permute-start | bytes 786440 | tf_op jit(solution)/shard_map/ppermute | solution.py:400
  31.6 9.0 %collective-permute-start.7 = (bf16[512,128]{1,0:T(8,128)(2,1)S(1)}, bf16[512,128]{1,0:T(8,128)(2,1)S(1)}, u32[]{:S(2)}, u32[]{:S(2)}) collective-permute-start(bf16[512,128]{1,0:T(8,128)(2,1)S(1)} %get-tuple-element.64.cg_ref.refs_1_), channel_id=1, source_target_pairs={{0,8},{4,12},{8,0},{12,4},{1,9},{5,13},{9,1},{13,5},{2,10},{6,14},... | collective-permute-start | bytes 393224 | tf_op jit(solution)/shard_map/ppermute | solution.py:391
  34.2 1.9 %collective-permute-start.14 = (bf16[192,256]{1,0:T(8,128)(2,1)S(1)}, bf16[192,256]{1,0:T(8,128)(2,1)S(1)}, u32[]{:S(2)}, u32[]{:S(2)}) collective-permute-start(bf16[192,256]{1,0:T(8,128)(2,1)S(1)} %get-tuple-element.73), channel_id=1, source_target_pairs={{0,1},{1,0},{2,3},{3,2},{4,5},{5,4},{6,7},{7,6},{8,9},{9,8},{10,11... | collective-permute-start | bytes 294920 | tf_op jit(solution)/shard_map/ppermute | solution.py:313
  34.3 1.4 %collective-permute-start.12 = (bf16[160,256]{1,0:T(8,128)(2,1)S(1)}, bf16[160,256]{1,0:T(8,128)(2,1)S(1)}, u32[]{:S(2)}, u32[]{:S(2)}) collective-permute-start(bf16[160,256]{1,0:T(8,128)(2,1)S(1)} %get-tuple-element.71), channel_id=1, source_target_pairs={{0,1},{1,0},{2,3},{3,2},{4,5},{5,4},{6,7},{7,6},{8,9},{9,8},{10,11... | collective-permute-start | bytes 245768 | tf_op jit(solution)/shard_map/ppermute | solution.py:313
  34.8 1.3 %collective-permute-start.13 = (bf16[160,256]{1,0:T(8,128)(2,1)S(1)}, bf16[160,256]{1,0:T(8,128)(2,1)S(1)}, u32[]{:S(2)}, u32[]{:S(2)}) collective-permute-start(bf16[160,256]{1,0:T(8,128)(2,1)S(1)} %get-tuple-element.72), channel_id=1, source_target_pairs={{0,1},{1,0},{2,3},{3,2},{4,5},{5,4},{6,7},{7,6},{8,9},{9,8},{10,11... | collective-permute-start | bytes 245768 | tf_op jit(solution)/shard_map/ppermute | solution.py:313
  36.6 9.6 %collective-permute-start.15 = (bf16[128,512]{1,0:T(8,128)(2,1)S(1)}, bf16[128,512]{1,0:T(8,128)(2,1)S(1)}, u32[]{:S(2)}, u32[]{:S(2)}) collective-permute-start(bf16[128,512]{1,0:T(8,128)(2,1)S(1)} %get-tuple-element.74), channel_id=1, source_target_pairs={{0,2},{2,0},{1,3},{3,1},{4,6},{6,4},{5,7},{7,5},{8,10},{10,8},{9,1... | collective-permute-start | bytes 393224 | tf_op jit(solution)/shard_map/ppermute | solution.py:313
  37.7 8.5 %collective-permute-start.16 = (bf16[128,512]{1,0:T(8,128)(2,1)S(1)}, bf16[128,512]{1,0:T(8,128)(2,1)S(1)}, u32[]{:S(2)}, u32[]{:S(2)}) collective-permute-start(bf16[128,512]{1,0:T(8,128)(2,1)S(1)} %get-tuple-element.75), channel_id=1, source_target_pairs={{6,0},{4,2},{2,4},{0,6},{14,8},{12,10},{10,12},{8,14},{7,1},{5,3},... | collective-permute-start | bytes 393224 | tf_op jit(solution)/shard_map/ppermute | solution.py:416
  41.2 12.3 %copy-start.4 = (bf16[512,256]{1,0:T(8,128)(2,1)S(1)}, bf16[512,256]{1,0:T(8,128)(2,1)}, u32[]{:S(2)}) copy-start(bf16[512,256]{1,0:T(8,128)(2,1)} %get-tuple-element.48.kf_ref.refs_5_) | copy-start | bytes 786436
  41.7 9.0 %collective-permute-start.18 = (bf16[128,512]{1,0:T(8,128)(2,1)S(1)}, bf16[128,512]{1,0:T(8,128)(2,1)S(1)}, u32[]{:S(2)}, u32[]{:S(2)}) collective-permute-start(bf16[128,512]{1,0:T(8,128)(2,1)S(1)} %get-tuple-element.80), channel_id=1, source_target_pairs={{0,2},{2,0},{1,3},{3,1},{4,6},{6,4},{5,7},{7,5},{8,10},{10,8},{9,1... | collective-permute-start | bytes 393224 | tf_op jit(solution)/shard_map/ppermute | solution.py:313
  43.6 7.1 %collective-permute-start.19 = (bf16[128,512]{1,0:T(8,128)(2,1)S(1)}, bf16[128,512]{1,0:T(8,128)(2,1)S(1)}, u32[]{:S(2)}, u32[]{:S(2)}) collective-permute-start(bf16[128,512]{1,0:T(8,128)(2,1)S(1)} %get-tuple-element.81), channel_id=1, source_target_pairs={{6,0},{4,2},{2,4},{0,6},{14,8},{12,10},{10,12},{8,14},{7,1},{5,3},... | collective-permute-start | bytes 393224 | tf_op jit(solution)/shard_map/ppermute | solution.py:416
  46.3 9.2 %collective-permute-start.17 = (bf16[128,512]{1,0:T(8,128)(2,1)S(1)}, bf16[128,512]{1,0:T(8,128)(2,1)S(1)}, u32[]{:S(2)}, u32[]{:S(2)}) collective-permute-start(bf16[128,512]{1,0:T(8,128)(2,1)S(1)} %get-tuple-element.78), channel_id=1, source_target_pairs={{0,8},{4,12},{8,0},{12,4},{1,9},{5,13},{9,1},{13,5},{2,10},{6,14},... | collective-permute-start | bytes 393224 | tf_op jit(solution)/shard_map/ppermute | solution.py:446
  47.9 13.1 %collective-permute-start.10 = (bf16[1024,128]{1,0:T(8,128)(2,1)S(1)}, bf16[1024,128]{1,0:T(8,128)(2,1)S(1)}, u32[]{:S(2)}, u32[]{:S(2)}) collective-permute-start(bf16[1024,128]{1,0:T(8,128)(2,1)S(1)} %get-tuple-element.68), channel_id=1, source_target_pairs={{0,4},{4,0},{8,12},{12,8},{1,5},{5,1},{9,13},{13,9},{2,6},{6,2},{1... | collective-permute-start | bytes 786440 | tf_op jit(solution)/shard_map/ppermute | solution.py:430
  50.8 9.2 %collective-permute-start.20 = (bf16[128,512]{1,0:T(8,128)(2,1)S(1)}, bf16[128,512]{1,0:T(8,128)(2,1)S(1)}, u32[]{:S(2)}, u32[]{:S(2)}) collective-permute-start(bf16[128,512]{1,0:T(8,128)(2,1)S(1)} %get-tuple-element.84), channel_id=1, source_target_pairs={{0,8},{4,12},{8,0},{12,4},{1,9},{5,13},{9,1},{13,5},{2,10},{6,14},... | collective-permute-start | bytes 393224 | tf_op jit(solution)/shard_map/ppermute | solution.py:446
  53.5 7.5 %copy-start.5 = (bf16[1,512,256]{2,1,0:T(8,128)(2,1)S(1)}, bf16[1,512,256]{2,1,0:T(8,128)(2,1)}, u32[]{:S(2)}) copy-start(bf16[1,512,256]{2,1,0:T(8,128)(2,1)} %param.7) | copy-start | bytes 786436
  53.5 7.5 %copy-start.8 = (s32[2,8,4]{1,2,0:T(4,128)S(1)}, s32[2,8,4]{1,2,0:T(4,128)}, u32[]{:S(2)}) copy-start(s32[2,8,4]{1,2,0:T(4,128)} %param.9) | copy-start | bytes 772

commit v9 on v8

--- a/solution.py
+++ b/solution.py
@@ -11,7 +11,8 @@
 BLK = 256
 EPS = 1e-06
 LIMIT = 16 << 20
-BEGIN = 56 << 20
+BEGIN = 52 << 20
+FAR = 4
 SHORT = pl.CostEstimate(flops=1, bytes_accessed=1, transcendentals=0)
 LONG = pl.CostEstimate(flops=10**11, bytes_accessed=1, transcendentals=0)
 F32 = jnp.float32
@@ -39,14 +40,21 @@
     return jnp.where(x > 0, 1.0, jnp.exp(jnp.minimum(x, 0.0)))
 
 
-def call(body, outs, ins, flops, name):
+def streamed(outs, streams):
+    if not streams:
+        return []
+    return [pltpu.VMEM(o.shape, o.dtype) for o in outs] + [pltpu.SemaphoreType.DMA((streams,))]
+
+
+def call(body, outs, ins, flops, name, streams=0):
     read = sum(a.size * a.dtype.itemsize for a in ins)
     wrote = sum(s.size * s.dtype.itemsize for s in outs)
     return pl.pallas_call(
         body,
         out_shape=outs,
         in_specs=[SM if a.dtype == jnp.int32 else VM for a in ins],
-        out_specs=[VM] * len(outs),
+        out_specs=[pl.BlockSpec(memory_space=pl.ANY) if streams else VM] * len(outs),
+        scratch_shapes=streamed(outs, streams),
         name=name,
         compiler_params=pltpu.CompilerParams(vmem_limit_bytes=LIMIT),
         cost_estimate=LONG if name in ("query", "dnum", "numer") else SHORT,
@@ -70,13 +78,20 @@
         st_ref[mat(i), :] = mm(kf, v_ref[r, c], TN).astype(BF16)
 
 
-def far_body(w_ref, far_ref, sem):
+def far_body(w_ref, far_ref, sems):
     width, cols = far_ref.shape
-    rows = pl.ds(pl.multiple_of((1 - lax.axis_index("head")) * width, width), width)
+    first = (1 - lax.axis_index("head")) * width
     lanes = pl.ds(pl.multiple_of(lax.axis_index("dp") * cols, cols), cols)
-    copy = pltpu.make_async_copy(w_ref.at[rows, lanes], far_ref, sem)
-    copy.start()
-    copy.wait()
+    copies = []
+    for i in range(FAR):
+        size = width // FAR
+        rows = pl.ds(pl.multiple_of(first + i * size, size), size)
+        into = far_ref.at[i * size : (i + 1) * size]
+        copies.append(pltpu.make_async_copy(w_ref.at[rows, lanes], into, sems.at[i]))
+    for copy in copies:
+        copy.start()
+    for copy in copies:
+        copy.wait()
 
 
 def far_rows(w, width):
@@ -85,7 +100,7 @@
         out_shape=sds((width, DH), BF16),
         in_specs=[pl.BlockSpec(memory_space=pl.ANY)],
         out_specs=VM,
-        scratch_shapes=[pltpu.SemaphoreType.DMA],
+        scratch_shapes=[pltpu.SemaphoreType.DMA((FAR,))],
         name="far",
         compiler_params=pltpu.CompilerParams(vmem_limit_bytes=BEGIN),
         cost_estimate=SHORT,
@@ -224,7 +239,8 @@
 def key_body(dims, np_, *refs):
     nb, heads, owner_of = dims
     lay_ref, *parts = refs[: 1 + np_]
-    k_ref, kf_ref, v_ref, dkp_ref, dvp_ref, dk_ref, dv_ref = refs[1 + np_ :]
+    k_ref, kf_ref, v_ref, dkp_ref, dvp_ref, dk_out, dv_out, dk_ref, dv_ref, sems = refs[1 + np_ :]
+    copies = []
     z = lax.axis_index("seq")
     for i, r, c in tiles(k_ref.shape[0], heads):
         n, h = divmod(i, heads)
@@ -238,6 +254,12 @@
         dk = mm(v_ref[r, c], sg, NT) + dkp_ref[r, c]
         dk_ref[r, c] = (dk * slope(k_ref[r, c].astype(F32))).astype(BF16)
         dv_ref[r, c] = (mm(kf_ref[r, c], sg, NN) + dvp_ref[r, c]).astype(BF16)
+        if h == heads - 1:
+            for at, (ref, out) in enumerate(((dk_ref, dk_out), (dv_ref, dv_out))):
+                copies.append(pltpu.make_async_copy(ref.at[r, :], out.at[r, :], sems.at[2 * n + at]))
+                copies[-1].start()
+    for copy in copies:
+        copy.wait()
 
 
 def own_body(og_ref, w_ref, out_ref, w_in, sem):
@@ -299,10 +321,16 @@
 
 
 def final_body(*refs):
-    *got, out_ref = refs
-    for i in range(len(got) // 2):
-        total = got[2 * i][...].astype(F32) + got[2 * i + 1][...].astype(F32)
-        out_ref[:, mat(i)] = total.T
+    *got, out_ref, total_ref, sems = refs
+    copies = []
+    for j in range(total_ref.shape[0] // DH):
+        for i in range(len(got) // 2):
+            total = got[2 * i][:, mat(j)].astype(F32) + got[2 * i + 1][:, mat(j)].astype(F32)
+            total_ref[mat(j), mat(i)] = total.T
+        copies.append(pltpu.make_async_copy(total_ref.at[mat(j), :], out_ref.at[mat(j), :], sems.at[j]))
+        copies[-1].start()
+    for copy in copies:
+        copy.wait()
 
 
 def after(x, *deps):
@@ -444,7 +472,7 @@
             send, stay = call(functools.partial(cross_body, i), (half, half), (straight, diagonal, mine), 0, "cross")
             mine = after(mine, send)
             sums += [stay, lax.ppermute(send, "seq", [(s, s ^ 2) for s in range(4)])]
-        (weight_grad,) = call(final_body, (sds(block[::-1], F32),), tuple(sums), 0, "final")
+        (weight_grad,) = call(final_body, (sds(block[::-1], F32),), tuple(sums), 0, "final", block[1] // DH)
     else:
         weight_grad = lax.psum_scatter(
             lax.dot_general(og, attn, TN, preferred_element_type=F32).astype(BF16),
@@ -460,6 +488,7 @@
         (lay, *cparts, k, kf, v, dkp, dvp),
         2 * unit,
         "key",
+        2 * nb,
     )
     return attn_out[None], dq[None], dk[None], dv[None], weight_grad
 

time: 63.1 us -> 62.2 us (0.986)
  Pallas kernels: 15.2 us -> 12.8 us
  waiting for transfers between devices: 15 us -> 17.4 us
  local copies, waits for them, and re-layouts: 1 us -> 0.03 us
    ppermute x10, waiting for transfers between devices: 9.09 us -> 11.5 us  [swap(): return lax.ppermute(x, axis, [(0, 1), (1, 0)])]
    pallas_call x1, Pallas kernels: 2.06 us -> 0.41 us  [begin(): pl.pallas_call(begin_body, out_shape=(sds((tokens, cols), BF16), sds((cou...]
    unnamed x20 -> x14, local copies, waits for them, and re-layouts: 1 us -> 0.03 us
    pallas_call x1, Pallas kernels: 1.84 us -> 1.13 us  [far_rows(): pl.pallas_call(far_body, out_shape=sds((width, DH), BF16), in_specs=[pl.B...]
  transfers between devices with their start and end apart: 21 -> 21, of which waited for: 8 -> 8; matrix products, arithmetic and copies ran while one was open for 0% -> 0% of each run, Pallas kernels for 21% -> 18%
where the time goes in v9:
time: 62.2 us; the launch traced here: 61.9 us
  starting transfers between devices  30.8 us (50%)
  waiting for transfers between devices  17.4 us (28%)
  Pallas kernels  12.8 us (21%)
  between operations  0.84 us (1%)
    ppermute x10, waiting for transfers between devices, swap(): return lax.ppermute(x, axis, [(0, 1), (1, 0)])  11.5 us
    pallas_call x14, Pallas kernels, call(): pl.pallas_call(body, out_shape=outs, in_specs=[SM if a.dtype == jnp.int32...  10.4 us
    ppermute x10, starting transfers between devices, swap(): return lax.ppermute(x, axis, [(0, 1), (1, 0)])  9.59 us
    ppermute x3, starting transfers between devices, gather_parts(): parts.append(lax.ppermute(x, 'seq', pairs))  5.57 us
    ppermute x2, starting transfers between devices, cross_piece(): lax.ppermute(give, ('seq', 'head'), beside)  4.6 us
    ppermute x2, waiting for transfers between devices, per_device(): sums += [stay, lax.ppermute(send, 'seq', [(s, s ^ 2) for s in range(4)])]  4.43 us
    ppermute x2, starting transfers between devices, per_device(): sums += [stay, lax.ppermute(send, 'seq', [(s, s ^ 2) for s in range(4)])]  4.39 us
    ppermute x1, starting transfers between devices, per_device(): two = lax.ppermute(cg, 'seq', [(i, i ^ 2) for i in range(4)])  2.59 us
  transfers between devices with their start and end apart: 21, of which 8 were waited for; matrix products, arithmetic and copies ran while one was open for 0% of the time, Pallas kernels for 18%

profile of v9, /device:TPU:0, one launch (start us, length us, event | category | flops | bytes accessed | tf_op | source)
XLA Modules:
  0.0 61.9 jit_solution(6160931059864389263)
XLA Ops:
  1.2 1.1 %far.1 = bf16[2048,128]{1,0:T(8,128)(2,1)S(1)} custom-call(bf16[4096,256]{1,0:T(8,128)(2,1)} %w_ref.3), custom_call_target="tpu_custom_call" | custom-call | flops 1 | bytes 1 | tf_op jit(solution)/shard_map/far/pallas_call | solution.py:98
  2.3 2.7 %collective-permute-start.4 = (bf16[2048,128]{1,0:T(8,128)(2,1)S(1)}, bf16[2048,128]{1,0:T(8,128)(2,1)S(1)}, u32[]{:S(2)}, u32[]{:S(2)}) collective-permute-start(bf16[2048,128]{1,0:T(8,128)(2,1)S(1)} %far.1), channel_id=1, source_target_pairs={{0,2},{2,0},{1,3},{3,1},{4,6},{6,4},{5,7},{7,5},{8,10},{10,8},{9,1... | collective-permute-start | bytes 1572872 | tf_op jit(solution)/shard_map/ppermute | solution.py:341
  5.5 1.6 %collective-permute-start = (bf16[512,128]{1,0:T(8,128)(2,1)S(1)}, bf16[512,128]{1,0:T(8,128)(2,1)S(1)}, u32[]{:S(2)}, u32[]{:S(2)}) collective-permute-start(bf16[512,128]{1,0:T(8,128)(2,1)S(1)} %get-tuple-element.50.refs_1_), channel_id=1, source_target_pairs={{0,4},{4,8},{8,12},{12,0},{1,5},{5,9},{9,13},{13,1},{2,6},{6,10},{... | collective-permute-start | bytes 393224 | tf_op jit(solution)/shard_map/ppermute | solution.py:350
  7.1 2.6 %collective-permute-start.1 = (bf16[512,128]{1,0:T(8,128)(2,1)S(1)}, bf16[512,128]{1,0:T(8,128)(2,1)S(1)}, u32[]{:S(2)}, u32[]{:S(2)}) collective-permute-start(bf16[512,128]{1,0:T(8,128)(2,1)S(1)} %get-tuple-element.50.refs_1_), channel_id=1, source_target_pairs={{0,8},{4,12},{8,0},{12,4},{1,9},{5,13},{9,1},{13,5},{2,10},{6,14},... | collective-permute-start | bytes 393224 | tf_op jit(solution)/shard_map/ppermute | solution.py:350
  9.7 1.3 %collective-permute-start.2 = (bf16[512,128]{1,0:T(8,128)(2,1)S(1)}, bf16[512,128]{1,0:T(8,128)(2,1)S(1)}, u32[]{:S(2)}, u32[]{:S(2)}) collective-permute-start(bf16[512,128]{1,0:T(8,128)(2,1)S(1)} %get-tuple-element.50.refs_1_), channel_id=1, source_target_pairs={{0,12},{4,0},{8,4},{12,8},{1,13},{5,1},{9,5},{13,9},{2,14},{6,2},{... | collective-permute-start | bytes 393224 | tf_op jit(solution)/shard_map/ppermute | solution.py:350
  11.1 0.7 %scores.1 = (bf16[512,256]{1,0:T(8,128)(2,1)S(1)}, bf16[1024,256]{1,0:T(8,128)(2,1)S(1)}, f32[512,256]{1,0:T(8,128)S(1)}) custom-call(bf16[512,256]{1,0:T(8,128)(2,1)S(1)} %bitcast.21, bf16[512,256]{1,0:T(8,128)(2,1)S(1)} %get-tuple-element.48.kf_ref.refs_5_, bf16[512,256]{1,0:T(8,128)(2,1)S(1)} %bitcast.16), custom_call_target="tpu_custom_call" | custom-call | flops 1 | bytes 1 | tf_op jit(solution)/shard_map/scores/pallas_call | solution.py:52
  11.7 5.8 %collective-permute-done.4.w_ref = bf16[2048,128]{1,0:T(8,128)(2,1)S(1)} collective-permute-done((bf16[2048,128]{1,0:T(8,128)(2,1)S(1)}, bf16[2048,128]{1,0:T(8,128)(2,1)S(1)}, u32[]{:S(2)}, u32[]{:S(2)}) %collective-permute-start.4) | collective-permute-done | bytes 524320 | tf_op jit(solution)/shard_map/ppermute | solution.py:341
  17.5 1.2 %other.1 = (bf16[512,128]{1,0:T(8,128)(2,1)S(1)}, bf16[512,128]{1,0:T(8,128)(2,1)S(1)}) custom-call(bf16[512,2048]{1,0:T(8,128)(2,1)S(1)} %bitcast.10, bf16[512,2048]{1,0:T(8,128)(2,1)S(1)} %collective-permute-done.3.og_sib_ref, bf16[2048,128]{1,0:T(8,128)(2,1)S(1)} %collective-permute-done.4.w_ref), custom_call_target="tpu_custom_call" | custom-call | flops 1 | bytes 1 | tf_op jit(solution)/shard_map/other/pallas_call | solution.py:52
  18.8 1.0 %collective-permute-start.6 = (bf16[512,128]{1,0:T(8,128)(2,1)S(1)}, bf16[512,128]{1,0:T(8,128)(2,1)S(1)}, u32[]{:S(2)}, u32[]{:S(2)}) collective-permute-start(bf16[512,128]{1,0:T(8,128)(2,1)S(1)} %get-tuple-element.53), channel_id=1, source_target_pairs={{0,3},{1,2},{2,1},{3,0},{4,7},{5,6},{6,5},{7,4},{8,11},{9,10},{10,... | collective-permute-start | bytes 393224 | tf_op jit(solution)/shard_map/ppermute | solution.py:395
  19.7 0.9 %collective-permute-start.5 = (bf16[512,128]{1,0:T(8,128)(2,1)S(1)}, bf16[512,128]{1,0:T(8,128)(2,1)S(1)}, u32[]{:S(2)}, u32[]{:S(2)}) collective-permute-start(bf16[512,128]{1,0:T(8,128)(2,1)S(1)} %get-tuple-element.57), channel_id=1, source_target_pairs={{0,2},{2,0},{1,3},{3,1},{4,6},{6,4},{5,7},{7,5},{8,10},{10,8},{9,1... | collective-permute-start | bytes 393224 | tf_op jit(solution)/shard_map/ppermute | solution.py:341
  20.7 1.1 %numer.1 = (bf16[512,128]{1,0:T(8,128)(2,1)S(1)}, f32[512,256]{1,0:T(8,128)S(1)}, bf16[512,256]{1,0:T(8,128)(2,1)S(1)}) custom-call(s32[2,4,8]{2,1,0:T(4,128)S(1)} %bitcast.23, bf16[512,128]{1,0:T(8,128)(2,1)S(1)} %get-tuple-element.50.refs_1_, bf16[512,128]{1,0:T(8,128)(2,1)S(1)} %collective-permute-done.refs_2_, ...), custom_call_target="tpu_custom_call" | custom-call | flops 99999997952 | bytes 1 | tf_op jit(solution)/shard_map/numer/pallas_call | solution.py:52
  22.0 1.7 %collective-permute-start.11 = (bf16[512,256]{1,0:T(8,128)(2,1)S(1)}, bf16[512,256]{1,0:T(8,128)(2,1)S(1)}, u32[]{:S(2)}, u32[]{:S(2)}) collective-permute-start(bf16[512,256]{1,0:T(8,128)(2,1)S(1)} %get-tuple-element.65.attn_ref), channel_id=1, source_target_pairs={{0,2},{2,0},{1,3},{3,1},{4,6},{6,4},{5,7},{7,5},{8,10},{10,8},{9,1... | collective-permute-start | bytes 786440 | tf_op jit(solution)/shard_map/ppermute | solution.py:341
  23.7 0.8 %own_partial.1.refs_0_ = f32[512,256]{1,0:T(8,128)S(1)} custom-call(bf16[512,2048]{1,0:T(8,128)(2,1)S(1)} %bitcast.11, bf16[4096,256]{1,0:T(8,128)(2,1)S(1)} %copy-done.1), custom_call_target="tpu_custom_call" | custom-call | flops 1 | bytes 1 | tf_op jit(solution)/shard_map/own_partial/pallas_call | solution.py:277
  24.5 3.2 %collective-permute-done.5.refs_1_ = bf16[512,128]{1,0:T(8,128)(2,1)S(1)} collective-permute-done((bf16[512,128]{1,0:T(8,128)(2,1)S(1)}, bf16[512,128]{1,0:T(8,128)(2,1)S(1)}, u32[]{:S(2)}, u32[]{:S(2)}) %collective-permute-start.5) | collective-permute-done | bytes 131104 | tf_op jit(solution)/shard_map/ppermute | solution.py:341
  28.3 0.7 %weight.3 = (bf16[256,512]{1,0:T(8,128)(2,1)S(1)}, f32[256,512]{1,0:T(8,128)S(1)}) custom-call(bf16[512,256]{1,0:T(8,128)(2,1)S(1)} %get-tuple-element.65.attn_ref, bf16[512,2048]{1,0:T(8,128)(2,1)S(1)} %bitcast.12, bf16[512,2048]{1,0:T(8,128)(2,1)S(1)} %collective-permute-done.3.og_sib_ref, bf16[512,256]{1,0:T(8,128)(2,1)S(1)} %collective-permute-done.8.refs_0_), custom_call_target="tpu_custom_call" | custom-call | flops 1 | bytes 1 | tf_op jit(solution)/shard_map/weight/pallas_call | solution.py:52
  29.1 1.6 %collective-permute-start.9 = (bf16[256,512]{1,0:T(8,128)(2,1)S(1)}, bf16[256,512]{1,0:T(8,128)(2,1)S(1)}, u32[]{:S(2)}, u32[]{:S(2)}) collective-permute-start(bf16[256,512]{1,0:T(8,128)(2,1)S(1)} %get-tuple-element.67), channel_id=1, source_target_pairs={{0,4},{4,0},{8,12},{12,8},{1,5},{5,1},{9,13},{13,9},{2,6},{6,2},{1... | collective-permute-start | bytes 786440 | tf_op jit(solution)/shard_map/ppermute | solution.py:428
  30.7 2.6 %collective-permute-start.7 = (bf16[512,128]{1,0:T(8,128)(2,1)S(1)}, bf16[512,128]{1,0:T(8,128)(2,1)S(1)}, u32[]{:S(2)}, u32[]{:S(2)}) collective-permute-start(bf16[512,128]{1,0:T(8,128)(2,1)S(1)} %get-tuple-element.64.cg_ref.refs_1_), channel_id=1, source_target_pairs={{0,8},{4,12},{8,0},{12,4},{1,9},{5,13},{9,1},{13,5},{2,10},{6,14},... | collective-permute-start | bytes 393224 | tf_op jit(solution)/shard_map/ppermute | solution.py:419
  34.0 0.8 %collective-permute-done.12.refs_0_ = bf16[160,256]{1,0:T(8,128)(2,1)S(1)} collective-permute-done((bf16[160,256]{1,0:T(8,128)(2,1)S(1)}, bf16[160,256]{1,0:T(8,128)(2,1)S(1)}, u32[]{:S(2)}, u32[]{:S(2)}) %collective-permute-start.12) | collective-permute-done | bytes 81952 | tf_op jit(solution)/shard_map/ppermute | solution.py:341
  35.8 1.1 %collective-permute-start.15 = (bf16[128,512]{1,0:T(8,128)(2,1)S(1)}, bf16[128,512]{1,0:T(8,128)(2,1)S(1)}, u32[]{:S(2)}, u32[]{:S(2)}) collective-permute-start(bf16[128,512]{1,0:T(8,128)(2,1)S(1)} %get-tuple-element.74), channel_id=1, source_target_pairs={{0,2},{2,0},{1,3},{3,1},{4,6},{6,4},{5,7},{7,5},{8,10},{10,8},{9,1... | collective-permute-start | bytes 393224 | tf_op jit(solution)/shard_map/ppermute | solution.py:341
  36.8 2.0 %collective-permute-start.16 = (bf16[128,512]{1,0:T(8,128)(2,1)S(1)}, bf16[128,512]{1,0:T(8,128)(2,1)S(1)}, u32[]{:S(2)}, u32[]{:S(2)}) collective-permute-start(bf16[128,512]{1,0:T(8,128)(2,1)S(1)} %get-tuple-element.75), channel_id=1, source_target_pairs={{6,0},{4,2},{2,4},{0,6},{14,8},{12,10},{10,12},{8,14},{7,1},{5,3},... | collective-permute-start | bytes 393224 | tf_op jit(solution)/shard_map/ppermute | solution.py:444
  38.8 0.8 %collective-permute-done.7.two_ref.refs_2_ = bf16[512,128]{1,0:T(8,128)(2,1)S(1)} collective-permute-done((bf16[512,128]{1,0:T(8,128)(2,1)S(1)}, bf16[512,128]{1,0:T(8,128)(2,1)S(1)}, u32[]{:S(2)}, u32[]{:S(2)}) %collective-permute-start.7) | collective-permute-done | bytes 131104 | tf_op jit(solution)/shard_map/ppermute | solution.py:419
  39.7 0.6 collective-permute-done.9.got_ref
  40.9 1.9 %collective-permute-start.18 = (bf16[128,512]{1,0:T(8,128)(2,1)S(1)}, bf16[128,512]{1,0:T(8,128)(2,1)S(1)}, u32[]{:S(2)}, u32[]{:S(2)}) collective-permute-start(bf16[128,512]{1,0:T(8,128)(2,1)S(1)} %get-tuple-element.80), channel_id=1, source_target_pairs={{0,2},{2,0},{1,3},{3,1},{4,6},{6,4},{5,7},{7,5},{8,10},{10,8},{9,1... | collective-permute-start | bytes 393224 | tf_op jit(solution)/shard_map/ppermute | solution.py:341
  42.7 2.6 %collective-permute-start.19 = (bf16[128,512]{1,0:T(8,128)(2,1)S(1)}, bf16[128,512]{1,0:T(8,128)(2,1)S(1)}, u32[]{:S(2)}, u32[]{:S(2)}) collective-permute-start(bf16[128,512]{1,0:T(8,128)(2,1)S(1)} %get-tuple-element.81), channel_id=1, source_target_pairs={{6,0},{4,2},{2,4},{0,6},{14,8},{12,10},{10,12},{8,14},{7,1},{5,3},... | collective-permute-start | bytes 393224 | tf_op jit(solution)/shard_map/ppermute | solution.py:444
  45.4 1.6 %collective-permute-start.17 = (bf16[128,512]{1,0:T(8,128)(2,1)S(1)}, bf16[128,512]{1,0:T(8,128)(2,1)S(1)}, u32[]{:S(2)}, u32[]{:S(2)}) collective-permute-start(bf16[128,512]{1,0:T(8,128)(2,1)S(1)} %get-tuple-element.78), channel_id=1, source_target_pairs={{0,8},{4,12},{8,0},{12,4},{1,9},{5,13},{9,1},{13,5},{2,10},{6,14},... | collective-permute-start | bytes 393224 | tf_op jit(solution)/shard_map/ppermute | solution.py:474
  47.0 1.5 %collective-permute-start.10 = (bf16[1024,128]{1,0:T(8,128)(2,1)S(1)}, bf16[1024,128]{1,0:T(8,128)(2,1)S(1)}, u32[]{:S(2)}, u32[]{:S(2)}) collective-permute-start(bf16[1024,128]{1,0:T(8,128)(2,1)S(1)} %get-tuple-element.68), channel_id=1, source_target_pairs={{0,4},{4,0},{8,12},{12,8},{1,5},{5,1},{9,13},{13,9},{2,6},{6,2},{1... | collective-permute-start | bytes 786440 | tf_op jit(solution)/shard_map/ppermute | solution.py:458
  48.5 1.3 %collective-permute-done.18.keep_ref = bf16[128,512]{1,0:T(8,128)(2,1)S(1)} collective-permute-done((bf16[128,512]{1,0:T(8,128)(2,1)S(1)}, bf16[128,512]{1,0:T(8,128)(2,1)S(1)}, u32[]{:S(2)}, u32[]{:S(2)}) %collective-permute-start.18) | collective-permute-done | bytes 131104 | tf_op jit(solution)/shard_map/ppermute | solution.py:341
  49.9 2.7 %collective-permute-start.20 = (bf16[128,512]{1,0:T(8,128)(2,1)S(1)}, bf16[128,512]{1,0:T(8,128)(2,1)S(1)}, u32[]{:S(2)}, u32[]{:S(2)}) collective-permute-start(bf16[128,512]{1,0:T(8,128)(2,1)S(1)} %get-tuple-element.84), channel_id=1, source_target_pairs={{0,8},{4,12},{8,0},{12,4},{1,9},{5,13},{9,1},{13,5},{2,10},{6,14},... | collective-permute-start | bytes 393224 | tf_op jit(solution)/shard_map/ppermute | solution.py:474
  52.6 2.0 %query.1 = (bf16[512,256]{1,0:T(8,128)(2,1)}, f32[512,256]{1,0:T(8,128)S(1)}, f32[512,256]{1,0:T(8,128)S(1)}, bf16[512,256]{1,0:T(8,128)(2,1)}) custom-call(bf16[512,256]{1,0:T(8,128)(2,1)S(1)} %bitcast.22, bf16[512,256]{1,0:T(8,128)(2,1)S(1)} %get-tuple-element.49.refs_5_.refs_4_.qf_ref, bf16[512,256]{1,0:T(8,128)(2,1)S(1)} %get-tuple-element.48.kf_ref.refs_5_, ...), custom_call_target="tpu_custom_call" | custom-call | flops 99999997952 | bytes 1 | tf_op jit(solution)/shard_map/query/pallas_call | solution.py:52
  54.6 4.4 %collective-permute-done.20.refs_3_ = bf16[128,512]{1,0:T(8,128)(2,1)S(1)} collective-permute-done((bf16[128,512]{1,0:T(8,128)(2,1)S(1)}, bf16[128,512]{1,0:T(8,128)(2,1)S(1)}, u32[]{:S(2)}, u32[]{:S(2)}) %collective-permute-start.20) | collective-permute-done | bytes 131104 | tf_op jit(solution)/shard_map/ppermute | solution.py:474
  59.1 0.9 %final.1 = f32[512,256]{1,0:T(8,128)} custom-call(bf16[128,512]{1,0:T(8,128)(2,1)S(1)} %get-tuple-element.77.refs_0_, bf16[128,512]{1,0:T(8,128)(2,1)S(1)} %collective-permute-done.17.refs_1_, bf16[128,512]{1,0:T(8,128)(2,1)S(1)} %get-tuple-element.83.refs_2_, bf16[128,512]{1,0:T(8,128)(2,1)S(1)} %collective-permute-done.20.refs_3_), custom_call_target="tpu_custom_call" | custom-call | flops 1 | bytes 1 | tf_op jit(solution)/shard_map/final/pallas_call | solution.py:52
  60.0 1.8 %key.1 = (bf16[512,256]{1,0:T(8,128)(2,1)}, bf16[512,256]{1,0:T(8,128)(2,1)}) custom-call(s32[2,4,8]{2,1,0:T(4,128)S(1)} %bitcast.24, bf16[512,128]{1,0:T(8,128)(2,1)S(1)} %get-tuple-element.64.cg_ref.refs_1_, bf16[512,128]{1,0:T(8,128)(2,1)S(1)} %collective-permute-done.7.two_ref.refs_2_, bf16[1024,128]{1,0:T(8,128)(2,1)S(1)} %collective-permute-done.10.refs_3_, ...), custom_call_target="tpu_custom_call" | custom-call | flops 1 | bytes 1 | tf_op jit(solution)/shard_map/key/pallas_call | solution.py:52
  (41 shorter events, 4.0 us)
Async XLA Ops:
  0.6 16.9 %copy-start = (bf16[1,512,2048]{2,1,0:T(8,128)(2,1)S(1)}, bf16[1,512,2048]{2,1,0:T(8,128)(2,1)}, u32[]{:S(2)}) copy-start(bf16[1,512,2048]{2,1,0:T(8,128)(2,1)} %param.11) | copy-start | bytes 6291460
  0.6 4.4 %copy-start.3 = (bf16[1,512,256]{2,1,0:T(8,128)(2,1)S(1)}, bf16[1,512,256]{2,1,0:T(8,128)(2,1)}, u32[]{:S(2)}) copy-start(bf16[1,512,256]{2,1,0:T(8,128)(2,1)} %param.7) | copy-start | bytes 786436
  0.7 4.4 %copy-start.2 = (bf16[1,512,256]{2,1,0:T(8,128)(2,1)S(1)}, bf16[1,512,256]{2,1,0:T(8,128)(2,1)}, u32[]{:S(2)}) copy-start(bf16[1,512,256]{2,1,0:T(8,128)(2,1)} %param.8) | copy-start | bytes 786436
  0.7 10.4 %copy-start.4 = (bf16[1,512,256]{2,1,0:T(8,128)(2,1)S(1)}, bf16[1,512,256]{2,1,0:T(8,128)(2,1)}, u32[]{:S(2)}) copy-start(bf16[1,512,256]{2,1,0:T(8,128)(2,1)} %param.6) | copy-start | bytes 786436
  0.7 16.9 %collective-permute-start.3 = (bf16[512,2048]{1,0:T(8,128)(2,1)}, bf16[512,2048]{1,0:T(8,128)(2,1)S(1)}, u32[]{:S(2)}, u32[]{:S(2)}) collective-permute-start(bf16[512,2048]{1,0:T(8,128)(2,1)} %bitcast.9), channel_id=1, source_target_pairs={{0,1},{1,0},{2,3},{3,2},{4,5},{5,4},{6,7},{7,6},{8,9},{9,8},{10,11... | collective-permute-start | bytes 6291464 | tf_op jit(solution)/shard_map/ppermute | solution.py:341
  2.3 15.2 %collective-permute-start.4 = (bf16[2048,128]{1,0:T(8,128)(2,1)S(1)}, bf16[2048,128]{1,0:T(8,128)(2,1)S(1)}, u32[]{:S(2)}, u32[]{:S(2)}) collective-permute-start(bf16[2048,128]{1,0:T(8,128)(2,1)S(1)} %far.1), channel_id=1, source_target_pairs={{0,2},{2,0},{1,3},{3,1},{4,6},{6,4},{5,7},{7,5},{8,10},{10,8},{9,1... | collective-permute-start | bytes 1572872 | tf_op jit(solution)/shard_map/ppermute | solution.py:341
  5.5 15.2 %collective-permute-start = (bf16[512,128]{1,0:T(8,128)(2,1)S(1)}, bf16[512,128]{1,0:T(8,128)(2,1)S(1)}, u32[]{:S(2)}, u32[]{:S(2)}) collective-permute-start(bf16[512,128]{1,0:T(8,128)(2,1)S(1)} %get-tuple-element.50.refs_1_), channel_id=1, source_target_pairs={{0,4},{4,8},{8,12},{12,0},{1,5},{5,9},{9,13},{13,1},{2,6},{6,10},{... | collective-permute-start | bytes 393224 | tf_op jit(solution)/shard_map/ppermute | solution.py:350
  7.1 13.5 %collective-permute-start.1 = (bf16[512,128]{1,0:T(8,128)(2,1)S(1)}, bf16[512,128]{1,0:T(8,128)(2,1)S(1)}, u32[]{:S(2)}, u32[]{:S(2)}) collective-permute-start(bf16[512,128]{1,0:T(8,128)(2,1)S(1)} %get-tuple-element.50.refs_1_), channel_id=1, source_target_pairs={{0,8},{4,12},{8,0},{12,4},{1,9},{5,13},{9,1},{13,5},{2,10},{6,14},... | collective-permute-start | bytes 393224 | tf_op jit(solution)/shard_map/ppermute | solution.py:350
  9.7 11.0 %collective-permute-start.2 = (bf16[512,128]{1,0:T(8,128)(2,1)S(1)}, bf16[512,128]{1,0:T(8,128)(2,1)S(1)}, u32[]{:S(2)}, u32[]{:S(2)}) collective-permute-start(bf16[512,128]{1,0:T(8,128)(2,1)S(1)} %get-tuple-element.50.refs_1_), channel_id=1, source_target_pairs={{0,12},{4,0},{8,4},{12,8},{1,13},{5,1},{9,5},{13,9},{2,14},{6,2},{... | collective-permute-start | bytes 393224 | tf_op jit(solution)/shard_map/ppermute | solution.py:350
  11.7 8.9 %copy-start.5 = (s32[2,8,4]{1,2,0:T(4,128)S(1)}, s32[2,8,4]{1,2,0:T(4,128)}, u32[]{:S(2)}) copy-start(s32[2,8,4]{1,2,0:T(4,128)} %param.9) | copy-start | bytes 772
  18.8 9.0 %collective-permute-start.6 = (bf16[512,128]{1,0:T(8,128)(2,1)S(1)}, bf16[512,128]{1,0:T(8,128)(2,1)S(1)}, u32[]{:S(2)}, u32[]{:S(2)}) collective-permute-start(bf16[512,128]{1,0:T(8,128)(2,1)S(1)} %get-tuple-element.53), channel_id=1, source_target_pairs={{0,3},{1,2},{2,1},{3,0},{4,7},{5,6},{6,5},{7,4},{8,11},{9,10},{10,... | collective-permute-start | bytes 393224 | tf_op jit(solution)/shard_map/ppermute | solution.py:395
  19.7 8.0 %collective-permute-start.5 = (bf16[512,128]{1,0:T(8,128)(2,1)S(1)}, bf16[512,128]{1,0:T(8,128)(2,1)S(1)}, u32[]{:S(2)}, u32[]{:S(2)}) collective-permute-start(bf16[512,128]{1,0:T(8,128)(2,1)S(1)} %get-tuple-element.57), channel_id=1, source_target_pairs={{0,2},{2,0},{1,3},{3,1},{4,6},{6,4},{5,7},{7,5},{8,10},{10,8},{9,1... | collective-permute-start | bytes 393224 | tf_op jit(solution)/shard_map/ppermute | solution.py:341
  20.7 3.0 %copy-start.1 = (bf16[4096,256]{1,0:T(8,128)(2,1)S(1)}, bf16[4096,256]{1,0:T(8,128)(2,1)}, u32[]{:S(2)}) copy-start(bf16[4096,256]{1,0:T(8,128)(2,1)} %w_ref.3) | copy-start | bytes 6291460
  21.8 6.5 %collective-permute-start.8 = (bf16[512,256]{1,0:T(8,128)(2,1)S(1)}, bf16[512,256]{1,0:T(8,128)(2,1)S(1)}, u32[]{:S(2)}, u32[]{:S(2)}) collective-permute-start(bf16[512,256]{1,0:T(8,128)(2,1)S(1)} %get-tuple-element.65.attn_ref), channel_id=1, source_target_pairs={{0,1},{1,0},{2,3},{3,2},{4,5},{5,4},{6,7},{7,6},{8,9},{9,8},{10,11... | collective-permute-start | bytes 786440 | tf_op jit(solution)/shard_map/ppermute | solution.py:341
  22.0 11.3 %collective-permute-start.11 = (bf16[512,256]{1,0:T(8,128)(2,1)S(1)}, bf16[512,256]{1,0:T(8,128)(2,1)S(1)}, u32[]{:S(2)}, u32[]{:S(2)}) collective-permute-start(bf16[512,256]{1,0:T(8,128)(2,1)S(1)} %get-tuple-element.65.attn_ref), channel_id=1, source_target_pairs={{0,2},{2,0},{1,3},{3,1},{4,6},{6,4},{5,7},{7,5},{8,10},{10,8},{9,1... | collective-permute-start | bytes 786440 | tf_op jit(solution)/shard_map/ppermute | solution.py:341
  29.1 11.2 %collective-permute-start.9 = (bf16[256,512]{1,0:T(8,128)(2,1)S(1)}, bf16[256,512]{1,0:T(8,128)(2,1)S(1)}, u32[]{:S(2)}, u32[]{:S(2)}) collective-permute-start(bf16[256,512]{1,0:T(8,128)(2,1)S(1)} %get-tuple-element.67), channel_id=1, source_target_pairs={{0,4},{4,0},{8,12},{12,8},{1,5},{5,1},{9,13},{13,9},{2,6},{6,2},{1... | collective-permute-start | bytes 786440 | tf_op jit(solution)/shard_map/ppermute | solution.py:428
  30.7 8.9 %collective-permute-start.7 = (bf16[512,128]{1,0:T(8,128)(2,1)S(1)}, bf16[512,128]{1,0:T(8,128)(2,1)S(1)}, u32[]{:S(2)}, u32[]{:S(2)}) collective-permute-start(bf16[512,128]{1,0:T(8,128)(2,1)S(1)} %get-tuple-element.64.cg_ref.refs_1_), channel_id=1, source_target_pairs={{0,8},{4,12},{8,0},{12,4},{1,9},{5,13},{9,1},{13,5},{2,10},{6,14},... | collective-permute-start | bytes 393224 | tf_op jit(solution)/shard_map/ppermute | solution.py:419
  33.3 1.9 %collective-permute-start.14 = (bf16[192,256]{1,0:T(8,128)(2,1)S(1)}, bf16[192,256]{1,0:T(8,128)(2,1)S(1)}, u32[]{:S(2)}, u32[]{:S(2)}) collective-permute-start(bf16[192,256]{1,0:T(8,128)(2,1)S(1)} %get-tuple-element.73), channel_id=1, source_target_pairs={{0,1},{1,0},{2,3},{3,2},{4,5},{5,4},{6,7},{7,6},{8,9},{9,8},{10,11... | collective-permute-start | bytes 294920 | tf_op jit(solution)/shard_map/ppermute | solution.py:341
  33.4 1.4 %collective-permute-start.12 = (bf16[160,256]{1,0:T(8,128)(2,1)S(1)}, bf16[160,256]{1,0:T(8,128)(2,1)S(1)}, u32[]{:S(2)}, u32[]{:S(2)}) collective-permute-start(bf16[160,256]{1,0:T(8,128)(2,1)S(1)} %get-tuple-element.71), channel_id=1, source_target_pairs={{0,1},{1,0},{2,3},{3,2},{4,5},{5,4},{6,7},{7,6},{8,9},{9,8},{10,11... | collective-permute-start | bytes 245768 | tf_op jit(solution)/shard_map/ppermute | solution.py:341
  33.9 1.3 %collective-permute-start.13 = (bf16[160,256]{1,0:T(8,128)(2,1)S(1)}, bf16[160,256]{1,0:T(8,128)(2,1)S(1)}, u32[]{:S(2)}, u32[]{:S(2)}) collective-permute-start(bf16[160,256]{1,0:T(8,128)(2,1)S(1)} %get-tuple-element.72), channel_id=1, source_target_pairs={{0,1},{1,0},{2,3},{3,2},{4,5},{5,4},{6,7},{7,6},{8,9},{9,8},{10,11... | collective-permute-start | bytes 245768 | tf_op jit(solution)/shard_map/ppermute | solution.py:341
  35.8 9.6 %collective-permute-start.15 = (bf16[128,512]{1,0:T(8,128)(2,1)S(1)}, bf16[128,512]{1,0:T(8,128)(2,1)S(1)}, u32[]{:S(2)}, u32[]{:S(2)}) collective-permute-start(bf16[128,512]{1,0:T(8,128)(2,1)S(1)} %get-tuple-element.74), channel_id=1, source_target_pairs={{0,2},{2,0},{1,3},{3,1},{4,6},{6,4},{5,7},{7,5},{8,10},{10,8},{9,1... | collective-permute-start | bytes 393224 | tf_op jit(solution)/shard_map/ppermute | solution.py:341
  36.8 8.5 %collective-permute-start.16 = (bf16[128,512]{1,0:T(8,128)(2,1)S(1)}, bf16[128,512]{1,0:T(8,128)(2,1)S(1)}, u32[]{:S(2)}, u32[]{:S(2)}) collective-permute-start(bf16[128,512]{1,0:T(8,128)(2,1)S(1)} %get-tuple-element.75), channel_id=1, source_target_pairs={{6,0},{4,2},{2,4},{0,6},{14,8},{12,10},{10,12},{8,14},{7,1},{5,3},... | collective-permute-start | bytes 393224 | tf_op jit(solution)/shard_map/ppermute | solution.py:444
  40.9 8.9 %collective-permute-start.18 = (bf16[128,512]{1,0:T(8,128)(2,1)S(1)}, bf16[128,512]{1,0:T(8,128)(2,1)S(1)}, u32[]{:S(2)}, u32[]{:S(2)}) collective-permute-start(bf16[128,512]{1,0:T(8,128)(2,1)S(1)} %get-tuple-element.80), channel_id=1, source_target_pairs={{0,2},{2,0},{1,3},{3,1},{4,6},{6,4},{5,7},{7,5},{8,10},{10,8},{9,1... | collective-permute-start | bytes 393224 | tf_op jit(solution)/shard_map/ppermute | solution.py:341
  42.7 7.1 %collective-permute-start.19 = (bf16[128,512]{1,0:T(8,128)(2,1)S(1)}, bf16[128,512]{1,0:T(8,128)(2,1)S(1)}, u32[]{:S(2)}, u32[]{:S(2)}) collective-permute-start(bf16[128,512]{1,0:T(8,128)(2,1)S(1)} %get-tuple-element.81), channel_id=1, source_target_pairs={{6,0},{4,2},{2,4},{0,6},{14,8},{12,10},{10,12},{8,14},{7,1},{5,3},... | collective-permute-start | bytes 393224 | tf_op jit(solution)/shard_map/ppermute | solution.py:444
  45.4 9.3 %collective-permute-start.17 = (bf16[128,512]{1,0:T(8,128)(2,1)S(1)}, bf16[128,512]{1,0:T(8,128)(2,1)S(1)}, u32[]{:S(2)}, u32[]{:S(2)}) collective-permute-start(bf16[128,512]{1,0:T(8,128)(2,1)S(1)} %get-tuple-element.78), channel_id=1, source_target_pairs={{0,8},{4,12},{8,0},{12,4},{1,9},{5,13},{9,1},{13,5},{2,10},{6,14},... | collective-permute-start | bytes 393224 | tf_op jit(solution)/shard_map/ppermute | solution.py:474
  47.0 13.0 %collective-permute-start.10 = (bf16[1024,128]{1,0:T(8,128)(2,1)S(1)}, bf16[1024,128]{1,0:T(8,128)(2,1)S(1)}, u32[]{:S(2)}, u32[]{:S(2)}) collective-permute-start(bf16[1024,128]{1,0:T(8,128)(2,1)S(1)} %get-tuple-element.68), channel_id=1, source_target_pairs={{0,4},{4,0},{8,12},{12,8},{1,5},{5,1},{9,13},{13,9},{2,6},{6,2},{1... | collective-permute-start | bytes 786440 | tf_op jit(solution)/shard_map/ppermute | solution.py:458
  49.9 9.2 %collective-permute-start.20 = (bf16[128,512]{1,0:T(8,128)(2,1)S(1)}, bf16[128,512]{1,0:T(8,128)(2,1)S(1)}, u32[]{:S(2)}, u32[]{:S(2)}) collective-permute-start(bf16[128,512]{1,0:T(8,128)(2,1)S(1)} %get-tuple-element.84), channel_id=1, source_target_pairs={{0,8},{4,12},{8,0},{12,4},{1,9},{5,13},{9,1},{13,5},{2,10},{6,14},... | collective-permute-start | bytes 393224 | tf_op jit(solution)/shard_map/ppermute | solution.py:474
  52.6 7.4 %copy-start.6 = (s32[2,8,4]{1,2,0:T(4,128)S(1)}, s32[2,8,4]{1,2,0:T(4,128)}, u32[]{:S(2)}) copy-start(s32[2,8,4]{1,2,0:T(4,128)} %param.9) | copy-start | bytes 772

commit v10 on v9

--- a/solution.py
+++ b/solution.py
@@ -57,7 +57,7 @@
         scratch_shapes=streamed(outs, streams),
         name=name,
         compiler_params=pltpu.CompilerParams(vmem_limit_bytes=LIMIT),
-        cost_estimate=LONG if name in ("query", "dnum", "numer") else SHORT,
+        cost_estimate=LONG if name in ("query", "dnum") else SHORT,
     )(*ins)
 
 

time: 62.2 us -> 61.1 us (0.982)
  waiting for transfers between devices: 17.4 us -> 14.6 us
  starting transfers between devices: 30.8 us -> 32.1 us
    ppermute x10, waiting for transfers between devices: 11.5 us -> 7.66 us  [swap(): return lax.ppermute(x, axis, [(0, 1), (1, 0)])]
    ppermute x1, waiting for transfers between devices: 0.01 us -> 2.56 us  [per_device(): d_sib = lax.ppermute(d_sib, ('head', 'dp'), across)]
    ppermute x2, waiting for transfers between devices: 4.43 us -> 2.65 us  [per_device(): sums += [stay, lax.ppermute(send, 'seq', [(s, s ^ 2) for s in range(4)])]]
    ppermute x2, starting transfers between devices: 4.6 us -> 5.76 us  [cross_piece(): lax.ppermute(give, ('seq', 'head'), beside)]
    ppermute x2, starting transfers between devices: 4.39 us -> 5.48 us  [per_device(): sums += [stay, lax.ppermute(send, 'seq', [(s, s ^ 2) for s in range(4)])]]
    ppermute x1, starting transfers between devices: 0.97 us -> 0.01 us  [per_device(): d_sib = lax.ppermute(d_sib, ('head', 'dp'), across)]
where the time goes in v10:
time: 61.1 us; the launch traced here: 60.3 us
  starting transfers between devices  32.1 us (53%)
  waiting for transfers between devices  14.6 us (24%)
  Pallas kernels  12.8 us (21%)
  between operations  0.87 us (1%)
    pallas_call x14, Pallas kernels, call(): pl.pallas_call(body, out_shape=outs, in_specs=[SM if a.dtype == jnp.int32...  10.4 us
    ppermute x10, starting transfers between devices, swap(): return lax.ppermute(x, axis, [(0, 1), (1, 0)])  9.45 us
    ppermute x10, waiting for transfers between devices, swap(): return lax.ppermute(x, axis, [(0, 1), (1, 0)])  7.66 us
    ppermute x2, starting transfers between devices, cross_piece(): lax.ppermute(give, ('seq', 'head'), beside)  5.76 us
    ppermute x3, starting transfers between devices, gather_parts(): parts.append(lax.ppermute(x, 'seq', pairs))  5.57 us
    ppermute x2, starting transfers between devices, per_device(): sums += [stay, lax.ppermute(send, 'seq', [(s, s ^ 2) for s in range(4)])]  5.48 us
    ppermute x2, waiting for transfers between devices, per_device(): sums += [stay, lax.ppermute(send, 'seq', [(s, s ^ 2) for s in range(4)])]  2.65 us
    ppermute x1, starting transfers between devices, per_device(): two = lax.ppermute(cg, 'seq', [(i, i ^ 2) for i in range(4)])  2.59 us
  transfers between devices with their start and end apart: 21, of which 8 were waited for; matrix products, arithmetic and copies ran while one was open for 0% of the time, Pallas kernels for 18%

profile of v10, /device:TPU:0, one launch (start us, length us, event | category | flops | bytes accessed | tf_op | source)
XLA Modules:
  0.0 60.3 jit_solution(8546712579267941556)
XLA Ops:
  1.2 1.1 %far.1 = bf16[2048,128]{1,0:T(8,128)(2,1)S(1)} custom-call(bf16[4096,256]{1,0:T(8,128)(2,1)} %w_ref.3), custom_call_target="tpu_custom_call" | custom-call | flops 1 | bytes 1 | tf_op jit(solution)/shard_map/far/pallas_call | solution.py:98
  2.3 2.7 %collective-permute-start.4 = (bf16[2048,128]{1,0:T(8,128)(2,1)S(1)}, bf16[2048,128]{1,0:T(8,128)(2,1)S(1)}, u32[]{:S(2)}, u32[]{:S(2)}) collective-permute-start(bf16[2048,128]{1,0:T(8,128)(2,1)S(1)} %far.1), channel_id=1, source_target_pairs={{0,2},{2,0},{1,3},{3,1},{4,6},{6,4},{5,7},{7,5},{8,10},{10,8},{9,1... | collective-permute-start | bytes 1572872 | tf_op jit(solution)/shard_map/ppermute | solution.py:341
  5.5 1.6 %collective-permute-start = (bf16[512,128]{1,0:T(8,128)(2,1)S(1)}, bf16[512,128]{1,0:T(8,128)(2,1)S(1)}, u32[]{:S(2)}, u32[]{:S(2)}) collective-permute-start(bf16[512,128]{1,0:T(8,128)(2,1)S(1)} %get-tuple-element.50.refs_1_), channel_id=1, source_target_pairs={{0,4},{4,8},{8,12},{12,0},{1,5},{5,9},{9,13},{13,1},{2,6},{6,10},{... | collective-permute-start | bytes 393224 | tf_op jit(solution)/shard_map/ppermute | solution.py:350
  7.1 2.6 %collective-permute-start.1 = (bf16[512,128]{1,0:T(8,128)(2,1)S(1)}, bf16[512,128]{1,0:T(8,128)(2,1)S(1)}, u32[]{:S(2)}, u32[]{:S(2)}) collective-permute-start(bf16[512,128]{1,0:T(8,128)(2,1)S(1)} %get-tuple-element.50.refs_1_), channel_id=1, source_target_pairs={{0,8},{4,12},{8,0},{12,4},{1,9},{5,13},{9,1},{13,5},{2,10},{6,14},... | collective-permute-start | bytes 393224 | tf_op jit(solution)/shard_map/ppermute | solution.py:350
  9.7 1.3 %collective-permute-start.2 = (bf16[512,128]{1,0:T(8,128)(2,1)S(1)}, bf16[512,128]{1,0:T(8,128)(2,1)S(1)}, u32[]{:S(2)}, u32[]{:S(2)}) collective-permute-start(bf16[512,128]{1,0:T(8,128)(2,1)S(1)} %get-tuple-element.50.refs_1_), channel_id=1, source_target_pairs={{0,12},{4,0},{8,4},{12,8},{1,13},{5,1},{9,5},{13,9},{2,14},{6,2},{... | collective-permute-start | bytes 393224 | tf_op jit(solution)/shard_map/ppermute | solution.py:350
  11.1 0.7 %scores.1 = (bf16[512,256]{1,0:T(8,128)(2,1)S(1)}, bf16[1024,256]{1,0:T(8,128)(2,1)S(1)}, f32[512,256]{1,0:T(8,128)S(1)}) custom-call(bf16[512,256]{1,0:T(8,128)(2,1)S(1)} %bitcast.21, bf16[512,256]{1,0:T(8,128)(2,1)S(1)} %get-tuple-element.48.kf_ref.refs_5_, bf16[512,256]{1,0:T(8,128)(2,1)S(1)} %bitcast.16), custom_call_target="tpu_custom_call" | custom-call | flops 1 | bytes 1 | tf_op jit(solution)/shard_map/scores/pallas_call | solution.py:52
  11.8 5.8 %collective-permute-done.4.w_ref = bf16[2048,128]{1,0:T(8,128)(2,1)S(1)} collective-permute-done((bf16[2048,128]{1,0:T(8,128)(2,1)S(1)}, bf16[2048,128]{1,0:T(8,128)(2,1)S(1)}, u32[]{:S(2)}, u32[]{:S(2)}) %collective-permute-start.4) | collective-permute-done | bytes 524320 | tf_op jit(solution)/shard_map/ppermute | solution.py:341
  17.5 1.2 %other.1 = (bf16[512,128]{1,0:T(8,128)(2,1)S(1)}, bf16[512,128]{1,0:T(8,128)(2,1)S(1)}) custom-call(bf16[512,2048]{1,0:T(8,128)(2,1)S(1)} %bitcast.10, bf16[512,2048]{1,0:T(8,128)(2,1)S(1)} %collective-permute-done.3.og_sib_ref, bf16[2048,128]{1,0:T(8,128)(2,1)S(1)} %collective-permute-done.4.w_ref), custom_call_target="tpu_custom_call" | custom-call | flops 1 | bytes 1 | tf_op jit(solution)/shard_map/other/pallas_call | solution.py:52
  18.8 1.8 %collective-permute-start.5 = (bf16[512,128]{1,0:T(8,128)(2,1)S(1)}, bf16[512,128]{1,0:T(8,128)(2,1)S(1)}, u32[]{:S(2)}, u32[]{:S(2)}) collective-permute-start(bf16[512,128]{1,0:T(8,128)(2,1)S(1)} %get-tuple-element.57), channel_id=1, source_target_pairs={{0,2},{2,0},{1,3},{3,1},{4,6},{6,4},{5,7},{7,5},{8,10},{10,8},{9,1... | collective-permute-start | bytes 393224 | tf_op jit(solution)/shard_map/ppermute | solution.py:341
  20.6 1.1 %numer.1 = (bf16[512,128]{1,0:T(8,128)(2,1)S(1)}, f32[512,256]{1,0:T(8,128)S(1)}, bf16[512,256]{1,0:T(8,128)(2,1)S(1)}) custom-call(s32[2,4,8]{2,1,0:T(4,128)S(1)} %bitcast.23, bf16[512,128]{1,0:T(8,128)(2,1)S(1)} %get-tuple-element.50.refs_1_, bf16[512,128]{1,0:T(8,128)(2,1)S(1)} %collective-permute-done.refs_2_, ...), custom_call_target="tpu_custom_call" | custom-call | flops 1 | bytes 1 | tf_op jit(solution)/shard_map/numer/pallas_call | solution.py:52
  22.2 1.7 %collective-permute-start.11 = (bf16[512,256]{1,0:T(8,128)(2,1)S(1)}, bf16[512,256]{1,0:T(8,128)(2,1)S(1)}, u32[]{:S(2)}, u32[]{:S(2)}) collective-permute-start(bf16[512,256]{1,0:T(8,128)(2,1)S(1)} %get-tuple-element.65.attn_ref), channel_id=1, source_target_pairs={{0,2},{2,0},{1,3},{3,1},{4,6},{6,4},{5,7},{7,5},{8,10},{10,8},{9,1... | collective-permute-start | bytes 786440 | tf_op jit(solution)/shard_map/ppermute | solution.py:341
  24.0 0.8 %own_partial.1.refs_0_ = f32[512,256]{1,0:T(8,128)S(1)} custom-call(bf16[512,2048]{1,0:T(8,128)(2,1)S(1)} %bitcast.11, bf16[4096,256]{1,0:T(8,128)(2,1)S(1)} %copy-done.1), custom_call_target="tpu_custom_call" | custom-call | flops 1 | bytes 1 | tf_op jit(solution)/shard_map/own_partial/pallas_call | solution.py:277
  24.8 2.6 %collective-permute-done.6.refs_2_ = bf16[512,128]{1,0:T(8,128)(2,1)S(1)} collective-permute-done((bf16[512,128]{1,0:T(8,128)(2,1)S(1)}, bf16[512,128]{1,0:T(8,128)(2,1)S(1)}, u32[]{:S(2)}, u32[]{:S(2)}) %collective-permute-start.6) | collective-permute-done | bytes 131104 | tf_op jit(solution)/shard_map/ppermute | solution.py:395
  27.3 0.6 dnum.1
  27.9 0.7 %weight.3 = (bf16[256,512]{1,0:T(8,128)(2,1)S(1)}, f32[256,512]{1,0:T(8,128)S(1)}) custom-call(bf16[512,256]{1,0:T(8,128)(2,1)S(1)} %get-tuple-element.65.attn_ref, bf16[512,2048]{1,0:T(8,128)(2,1)S(1)} %bitcast.12, bf16[512,2048]{1,0:T(8,128)(2,1)S(1)} %collective-permute-done.3.og_sib_ref, bf16[512,256]{1,0:T(8,128)(2,1)S(1)} %collective-permute-done.8.refs_0_), custom_call_target="tpu_custom_call" | custom-call | flops 1 | bytes 1 | tf_op jit(solution)/shard_map/weight/pallas_call | solution.py:52
  28.7 1.6 %collective-permute-start.9 = (bf16[256,512]{1,0:T(8,128)(2,1)S(1)}, bf16[256,512]{1,0:T(8,128)(2,1)S(1)}, u32[]{:S(2)}, u32[]{:S(2)}) collective-permute-start(bf16[256,512]{1,0:T(8,128)(2,1)S(1)} %get-tuple-element.67), channel_id=1, source_target_pairs={{0,4},{4,0},{8,12},{12,8},{1,5},{5,1},{9,13},{13,9},{2,6},{6,2},{1... | collective-permute-start | bytes 786440 | tf_op jit(solution)/shard_map/ppermute | solution.py:428
  30.3 2.6 %collective-permute-start.7 = (bf16[512,128]{1,0:T(8,128)(2,1)S(1)}, bf16[512,128]{1,0:T(8,128)(2,1)S(1)}, u32[]{:S(2)}, u32[]{:S(2)}) collective-permute-start(bf16[512,128]{1,0:T(8,128)(2,1)S(1)} %get-tuple-element.64.cg_ref.refs_1_), channel_id=1, source_target_pairs={{0,8},{4,12},{8,0},{12,4},{1,9},{5,13},{9,1},{13,5},{2,10},{6,14},... | collective-permute-start | bytes 393224 | tf_op jit(solution)/shard_map/ppermute | solution.py:419
  33.6 0.8 %collective-permute-done.12.refs_0_ = bf16[160,256]{1,0:T(8,128)(2,1)S(1)} collective-permute-done((bf16[160,256]{1,0:T(8,128)(2,1)S(1)}, bf16[160,256]{1,0:T(8,128)(2,1)S(1)}, u32[]{:S(2)}, u32[]{:S(2)}) %collective-permute-start.12) | collective-permute-done | bytes 81952 | tf_op jit(solution)/shard_map/ppermute | solution.py:341
  34.8 0.6 weight.4
  35.3 1.5 %collective-permute-start.15 = (bf16[128,512]{1,0:T(8,128)(2,1)S(1)}, bf16[128,512]{1,0:T(8,128)(2,1)S(1)}, u32[]{:S(2)}, u32[]{:S(2)}) collective-permute-start(bf16[128,512]{1,0:T(8,128)(2,1)S(1)} %get-tuple-element.74), channel_id=1, source_target_pairs={{0,2},{2,0},{1,3},{3,1},{4,6},{6,4},{5,7},{7,5},{8,10},{10,8},{9,1... | collective-permute-start | bytes 393224 | tf_op jit(solution)/shard_map/ppermute | solution.py:341
  36.8 1.2 %collective-permute-start.16 = (bf16[128,512]{1,0:T(8,128)(2,1)S(1)}, bf16[128,512]{1,0:T(8,128)(2,1)S(1)}, u32[]{:S(2)}, u32[]{:S(2)}) collective-permute-start(bf16[128,512]{1,0:T(8,128)(2,1)S(1)} %get-tuple-element.75), channel_id=1, source_target_pairs={{6,0},{4,2},{2,4},{0,6},{14,8},{12,10},{10,12},{8,14},{7,1},{5,3},... | collective-permute-start | bytes 393224 | tf_op jit(solution)/shard_map/ppermute | solution.py:444
  38.0 1.3 %collective-permute-done.7.two_ref.refs_2_ = bf16[512,128]{1,0:T(8,128)(2,1)S(1)} collective-permute-done((bf16[512,128]{1,0:T(8,128)(2,1)S(1)}, bf16[512,128]{1,0:T(8,128)(2,1)S(1)}, u32[]{:S(2)}, u32[]{:S(2)}) %collective-permute-start.7) | collective-permute-done | bytes 131104 | tf_op jit(solution)/shard_map/ppermute | solution.py:419
  39.8 0.6 weight.5
  40.4 4.6 %collective-permute-start.19 = (bf16[128,512]{1,0:T(8,128)(2,1)S(1)}, bf16[128,512]{1,0:T(8,128)(2,1)S(1)}, u32[]{:S(2)}, u32[]{:S(2)}) collective-permute-start(bf16[128,512]{1,0:T(8,128)(2,1)S(1)} %get-tuple-element.81), channel_id=1, source_target_pairs={{6,0},{4,2},{2,4},{0,6},{14,8},{12,10},{10,12},{8,14},{7,1},{5,3},... | collective-permute-start | bytes 393224 | tf_op jit(solution)/shard_map/ppermute | solution.py:444
  45.1 2.1 %collective-permute-start.17 = (bf16[128,512]{1,0:T(8,128)(2,1)S(1)}, bf16[128,512]{1,0:T(8,128)(2,1)S(1)}, u32[]{:S(2)}, u32[]{:S(2)}) collective-permute-start(bf16[128,512]{1,0:T(8,128)(2,1)S(1)} %get-tuple-element.78), channel_id=1, source_target_pairs={{0,8},{4,12},{8,0},{12,4},{1,9},{5,13},{9,1},{13,5},{2,10},{6,14},... | collective-permute-start | bytes 393224 | tf_op jit(solution)/shard_map/ppermute | solution.py:474
  47.1 1.6 %collective-permute-start.10 = (bf16[1024,128]{1,0:T(8,128)(2,1)S(1)}, bf16[1024,128]{1,0:T(8,128)(2,1)S(1)}, u32[]{:S(2)}, u32[]{:S(2)}) collective-permute-start(bf16[1024,128]{1,0:T(8,128)(2,1)S(1)} %get-tuple-element.68), channel_id=1, source_target_pairs={{0,4},{4,0},{8,12},{12,8},{1,5},{5,1},{9,13},{13,9},{2,6},{6,2},{1... | collective-permute-start | bytes 786440 | tf_op jit(solution)/shard_map/ppermute | solution.py:458
  48.7 0.7 %collective-permute-done.18.keep_ref = bf16[128,512]{1,0:T(8,128)(2,1)S(1)} collective-permute-done((bf16[128,512]{1,0:T(8,128)(2,1)S(1)}, bf16[128,512]{1,0:T(8,128)(2,1)S(1)}, u32[]{:S(2)}, u32[]{:S(2)}) %collective-permute-start.18) | collective-permute-done | bytes 131104 | tf_op jit(solution)/shard_map/ppermute | solution.py:341
  49.5 3.4 %collective-permute-start.20 = (bf16[128,512]{1,0:T(8,128)(2,1)S(1)}, bf16[128,512]{1,0:T(8,128)(2,1)S(1)}, u32[]{:S(2)}, u32[]{:S(2)}) collective-permute-start(bf16[128,512]{1,0:T(8,128)(2,1)S(1)} %get-tuple-element.84), channel_id=1, source_target_pairs={{0,8},{4,12},{8,0},{12,4},{1,9},{5,13},{9,1},{13,5},{2,10},{6,14},... | collective-permute-start | bytes 393224 | tf_op jit(solution)/shard_map/ppermute | solution.py:474
  52.9 2.0 %query.1 = (bf16[512,256]{1,0:T(8,128)(2,1)}, f32[512,256]{1,0:T(8,128)S(1)}, f32[512,256]{1,0:T(8,128)S(1)}, bf16[512,256]{1,0:T(8,128)(2,1)}) custom-call(bf16[512,256]{1,0:T(8,128)(2,1)S(1)} %bitcast.22, bf16[512,256]{1,0:T(8,128)(2,1)S(1)} %get-tuple-element.49.refs_5_.refs_4_.qf_ref, bf16[512,256]{1,0:T(8,128)(2,1)S(1)} %get-tuple-element.48.kf_ref.refs_5_, ...), custom_call_target="tpu_custom_call" | custom-call | flops 99999997952 | bytes 1 | tf_op jit(solution)/shard_map/query/pallas_call | solution.py:52
  54.9 2.6 %collective-permute-done.20.refs_3_ = bf16[128,512]{1,0:T(8,128)(2,1)S(1)} collective-permute-done((bf16[128,512]{1,0:T(8,128)(2,1)S(1)}, bf16[128,512]{1,0:T(8,128)(2,1)S(1)}, u32[]{:S(2)}, u32[]{:S(2)}) %collective-permute-start.20) | collective-permute-done | bytes 131104 | tf_op jit(solution)/shard_map/ppermute | solution.py:474
  57.5 0.9 %final.1 = f32[512,256]{1,0:T(8,128)} custom-call(bf16[128,512]{1,0:T(8,128)(2,1)S(1)} %get-tuple-element.77.refs_0_, bf16[128,512]{1,0:T(8,128)(2,1)S(1)} %collective-permute-done.17.refs_1_, bf16[128,512]{1,0:T(8,128)(2,1)S(1)} %get-tuple-element.83.refs_2_, bf16[128,512]{1,0:T(8,128)(2,1)S(1)} %collective-permute-done.20.refs_3_), custom_call_target="tpu_custom_call" | custom-call | flops 1 | bytes 1 | tf_op jit(solution)/shard_map/final/pallas_call | solution.py:52
  58.5 1.8 %key.1 = (bf16[512,256]{1,0:T(8,128)(2,1)}, bf16[512,256]{1,0:T(8,128)(2,1)}) custom-call(s32[2,4,8]{2,1,0:T(4,128)S(1)} %bitcast.24, bf16[512,128]{1,0:T(8,128)(2,1)S(1)} %get-tuple-element.64.cg_ref.refs_1_, bf16[512,128]{1,0:T(8,128)(2,1)S(1)} %collective-permute-done.7.two_ref.refs_2_, bf16[1024,128]{1,0:T(8,128)(2,1)S(1)} %collective-permute-done.10.refs_3_, ...), custom_call_target="tpu_custom_call" | custom-call | flops 1 | bytes 1 | tf_op jit(solution)/shard_map/key/pallas_call | solution.py:52
  (41 shorter events, 3.1 us)
Async XLA Ops:
  0.6 16.9 %copy-start = (bf16[1,512,2048]{2,1,0:T(8,128)(2,1)S(1)}, bf16[1,512,2048]{2,1,0:T(8,128)(2,1)}, u32[]{:S(2)}) copy-start(bf16[1,512,2048]{2,1,0:T(8,128)(2,1)} %param.11) | copy-start | bytes 6291460
  0.6 4.4 %copy-start.3 = (bf16[1,512,256]{2,1,0:T(8,128)(2,1)S(1)}, bf16[1,512,256]{2,1,0:T(8,128)(2,1)}, u32[]{:S(2)}) copy-start(bf16[1,512,256]{2,1,0:T(8,128)(2,1)} %param.7) | copy-start | bytes 786436
  0.7 4.4 %copy-start.2 = (bf16[1,512,256]{2,1,0:T(8,128)(2,1)S(1)}, bf16[1,512,256]{2,1,0:T(8,128)(2,1)}, u32[]{:S(2)}) copy-start(bf16[1,512,256]{2,1,0:T(8,128)(2,1)} %param.8) | copy-start | bytes 786436
  0.7 10.4 %copy-start.4 = (bf16[1,512,256]{2,1,0:T(8,128)(2,1)S(1)}, bf16[1,512,256]{2,1,0:T(8,128)(2,1)}, u32[]{:S(2)}) copy-start(bf16[1,512,256]{2,1,0:T(8,128)(2,1)} %param.6) | copy-start | bytes 786436
  0.7 16.9 %collective-permute-start.3 = (bf16[512,2048]{1,0:T(8,128)(2,1)}, bf16[512,2048]{1,0:T(8,128)(2,1)S(1)}, u32[]{:S(2)}, u32[]{:S(2)}) collective-permute-start(bf16[512,2048]{1,0:T(8,128)(2,1)} %bitcast.9), channel_id=1, source_target_pairs={{0,1},{1,0},{2,3},{3,2},{4,5},{5,4},{6,7},{7,6},{8,9},{9,8},{10,11... | collective-permute-start | bytes 6291464 | tf_op jit(solution)/shard_map/ppermute | solution.py:341
  2.3 15.2 %collective-permute-start.4 = (bf16[2048,128]{1,0:T(8,128)(2,1)S(1)}, bf16[2048,128]{1,0:T(8,128)(2,1)S(1)}, u32[]{:S(2)}, u32[]{:S(2)}) collective-permute-start(bf16[2048,128]{1,0:T(8,128)(2,1)S(1)} %far.1), channel_id=1, source_target_pairs={{0,2},{2,0},{1,3},{3,1},{4,6},{6,4},{5,7},{7,5},{8,10},{10,8},{9,1... | collective-permute-start | bytes 1572872 | tf_op jit(solution)/shard_map/ppermute | solution.py:341
  5.5 15.1 %collective-permute-start = (bf16[512,128]{1,0:T(8,128)(2,1)S(1)}, bf16[512,128]{1,0:T(8,128)(2,1)S(1)}, u32[]{:S(2)}, u32[]{:S(2)}) collective-permute-start(bf16[512,128]{1,0:T(8,128)(2,1)S(1)} %get-tuple-element.50.refs_1_), channel_id=1, source_target_pairs={{0,4},{4,8},{8,12},{12,0},{1,5},{5,9},{9,13},{13,1},{2,6},{6,10},{... | collective-permute-start | bytes 393224 | tf_op jit(solution)/shard_map/ppermute | solution.py:350
  7.1 13.5 %collective-permute-start.1 = (bf16[512,128]{1,0:T(8,128)(2,1)S(1)}, bf16[512,128]{1,0:T(8,128)(2,1)S(1)}, u32[]{:S(2)}, u32[]{:S(2)}) collective-permute-start(bf16[512,128]{1,0:T(8,128)(2,1)S(1)} %get-tuple-element.50.refs_1_), channel_id=1, source_target_pairs={{0,8},{4,12},{8,0},{12,4},{1,9},{5,13},{9,1},{13,5},{2,10},{6,14},... | collective-permute-start | bytes 393224 | tf_op jit(solution)/shard_map/ppermute | solution.py:350
  9.7 10.9 %collective-permute-start.2 = (bf16[512,128]{1,0:T(8,128)(2,1)S(1)}, bf16[512,128]{1,0:T(8,128)(2,1)S(1)}, u32[]{:S(2)}, u32[]{:S(2)}) collective-permute-start(bf16[512,128]{1,0:T(8,128)(2,1)S(1)} %get-tuple-element.50.refs_1_), channel_id=1, source_target_pairs={{0,12},{4,0},{8,4},{12,8},{1,13},{5,1},{9,5},{13,9},{2,14},{6,2},{... | collective-permute-start | bytes 393224 | tf_op jit(solution)/shard_map/ppermute | solution.py:350
  11.7 8.9 %copy-start.5 = (s32[2,8,4]{1,2,0:T(4,128)S(1)}, s32[2,8,4]{1,2,0:T(4,128)}, u32[]{:S(2)}) copy-start(s32[2,8,4]{1,2,0:T(4,128)} %param.9) | copy-start | bytes 772
  11.7 12.2 %copy-start.1 = (bf16[4096,256]{1,0:T(8,128)(2,1)S(1)}, bf16[4096,256]{1,0:T(8,128)(2,1)}, u32[]{:S(2)}) copy-start(bf16[4096,256]{1,0:T(8,128)(2,1)} %w_ref.3) | copy-start | bytes 6291460
  18.8 6.0 %collective-permute-start.5 = (bf16[512,128]{1,0:T(8,128)(2,1)S(1)}, bf16[512,128]{1,0:T(8,128)(2,1)S(1)}, u32[]{:S(2)}, u32[]{:S(2)}) collective-permute-start(bf16[512,128]{1,0:T(8,128)(2,1)S(1)} %get-tuple-element.57), channel_id=1, source_target_pairs={{0,2},{2,0},{1,3},{3,1},{4,6},{6,4},{5,7},{7,5},{8,10},{10,8},{9,1... | collective-permute-start | bytes 393224 | tf_op jit(solution)/shard_map/ppermute | solution.py:341
  20.6 6.8 %collective-permute-start.6 = (bf16[512,128]{1,0:T(8,128)(2,1)S(1)}, bf16[512,128]{1,0:T(8,128)(2,1)S(1)}, u32[]{:S(2)}, u32[]{:S(2)}) collective-permute-start(bf16[512,128]{1,0:T(8,128)(2,1)S(1)} %get-tuple-element.53), channel_id=1, source_target_pairs={{0,3},{1,2},{2,1},{3,0},{4,7},{5,6},{6,5},{7,4},{8,11},{9,10},{10,... | collective-permute-start | bytes 393224 | tf_op jit(solution)/shard_map/ppermute | solution.py:395
  21.8 6.2 %collective-permute-start.8 = (bf16[512,256]{1,0:T(8,128)(2,1)S(1)}, bf16[512,256]{1,0:T(8,128)(2,1)S(1)}, u32[]{:S(2)}, u32[]{:S(2)}) collective-permute-start(bf16[512,256]{1,0:T(8,128)(2,1)S(1)} %get-tuple-element.65.attn_ref), channel_id=1, source_target_pairs={{0,1},{1,0},{2,3},{3,2},{4,5},{5,4},{6,7},{7,6},{8,9},{9,8},{10,11... | collective-permute-start | bytes 786440 | tf_op jit(solution)/shard_map/ppermute | solution.py:341
  22.2 10.7 %collective-permute-start.11 = (bf16[512,256]{1,0:T(8,128)(2,1)S(1)}, bf16[512,256]{1,0:T(8,128)(2,1)S(1)}, u32[]{:S(2)}, u32[]{:S(2)}) collective-permute-start(bf16[512,256]{1,0:T(8,128)(2,1)S(1)} %get-tuple-element.65.attn_ref), channel_id=1, source_target_pairs={{0,2},{2,0},{1,3},{3,1},{4,6},{6,4},{5,7},{7,5},{8,10},{10,8},{9,1... | collective-permute-start | bytes 786440 | tf_op jit(solution)/shard_map/ppermute | solution.py:341
  28.7 11.1 %collective-permute-start.9 = (bf16[256,512]{1,0:T(8,128)(2,1)S(1)}, bf16[256,512]{1,0:T(8,128)(2,1)S(1)}, u32[]{:S(2)}, u32[]{:S(2)}) collective-permute-start(bf16[256,512]{1,0:T(8,128)(2,1)S(1)} %get-tuple-element.67), channel_id=1, source_target_pairs={{0,4},{4,0},{8,12},{12,8},{1,5},{5,1},{9,13},{13,9},{2,6},{6,2},{1... | collective-permute-start | bytes 786440 | tf_op jit(solution)/shard_map/ppermute | solution.py:428
  30.3 9.0 %collective-permute-start.7 = (bf16[512,128]{1,0:T(8,128)(2,1)S(1)}, bf16[512,128]{1,0:T(8,128)(2,1)S(1)}, u32[]{:S(2)}, u32[]{:S(2)}) collective-permute-start(bf16[512,128]{1,0:T(8,128)(2,1)S(1)} %get-tuple-element.64.cg_ref.refs_1_), channel_id=1, source_target_pairs={{0,8},{4,12},{8,0},{12,4},{1,9},{5,13},{9,1},{13,5},{2,10},{6,14},... | collective-permute-start | bytes 393224 | tf_op jit(solution)/shard_map/ppermute | solution.py:419
  32.9 1.9 %collective-permute-start.14 = (bf16[192,256]{1,0:T(8,128)(2,1)S(1)}, bf16[192,256]{1,0:T(8,128)(2,1)S(1)}, u32[]{:S(2)}, u32[]{:S(2)}) collective-permute-start(bf16[192,256]{1,0:T(8,128)(2,1)S(1)} %get-tuple-element.73), channel_id=1, source_target_pairs={{0,1},{1,0},{2,3},{3,2},{4,5},{5,4},{6,7},{7,6},{8,9},{9,8},{10,11... | collective-permute-start | bytes 294920 | tf_op jit(solution)/shard_map/ppermute | solution.py:341
  33.0 1.4 %collective-permute-start.12 = (bf16[160,256]{1,0:T(8,128)(2,1)S(1)}, bf16[160,256]{1,0:T(8,128)(2,1)S(1)}, u32[]{:S(2)}, u32[]{:S(2)}) collective-permute-start(bf16[160,256]{1,0:T(8,128)(2,1)S(1)} %get-tuple-element.71), channel_id=1, source_target_pairs={{0,1},{1,0},{2,3},{3,2},{4,5},{5,4},{6,7},{7,6},{8,9},{9,8},{10,11... | collective-permute-start | bytes 245768 | tf_op jit(solution)/shard_map/ppermute | solution.py:341
  33.5 1.3 %collective-permute-start.13 = (bf16[160,256]{1,0:T(8,128)(2,1)S(1)}, bf16[160,256]{1,0:T(8,128)(2,1)S(1)}, u32[]{:S(2)}, u32[]{:S(2)}) collective-permute-start(bf16[160,256]{1,0:T(8,128)(2,1)S(1)} %get-tuple-element.72), channel_id=1, source_target_pairs={{0,1},{1,0},{2,3},{3,2},{4,5},{5,4},{6,7},{7,6},{8,9},{9,8},{10,11... | collective-permute-start | bytes 245768 | tf_op jit(solution)/shard_map/ppermute | solution.py:341
  35.3 9.6 %collective-permute-start.15 = (bf16[128,512]{1,0:T(8,128)(2,1)S(1)}, bf16[128,512]{1,0:T(8,128)(2,1)S(1)}, u32[]{:S(2)}, u32[]{:S(2)}) collective-permute-start(bf16[128,512]{1,0:T(8,128)(2,1)S(1)} %get-tuple-element.74), channel_id=1, source_target_pairs={{0,2},{2,0},{1,3},{3,1},{4,6},{6,4},{5,7},{7,5},{8,10},{10,8},{9,1... | collective-permute-start | bytes 393224 | tf_op jit(solution)/shard_map/ppermute | solution.py:341
  36.8 8.2 %collective-permute-start.16 = (bf16[128,512]{1,0:T(8,128)(2,1)S(1)}, bf16[128,512]{1,0:T(8,128)(2,1)S(1)}, u32[]{:S(2)}, u32[]{:S(2)}) collective-permute-start(bf16[128,512]{1,0:T(8,128)(2,1)S(1)} %get-tuple-element.75), channel_id=1, source_target_pairs={{6,0},{4,2},{2,4},{0,6},{14,8},{12,10},{10,12},{8,14},{7,1},{5,3},... | collective-permute-start | bytes 393224 | tf_op jit(solution)/shard_map/ppermute | solution.py:444
  40.3 9.0 %collective-permute-start.18 = (bf16[128,512]{1,0:T(8,128)(2,1)S(1)}, bf16[128,512]{1,0:T(8,128)(2,1)S(1)}, u32[]{:S(2)}, u32[]{:S(2)}) collective-permute-start(bf16[128,512]{1,0:T(8,128)(2,1)S(1)} %get-tuple-element.80), channel_id=1, source_target_pairs={{0,2},{2,0},{1,3},{3,1},{4,6},{6,4},{5,7},{7,5},{8,10},{10,8},{9,1... | collective-permute-start | bytes 393224 | tf_op jit(solution)/shard_map/ppermute | solution.py:341
  40.4 9.0 %collective-permute-start.19 = (bf16[128,512]{1,0:T(8,128)(2,1)S(1)}, bf16[128,512]{1,0:T(8,128)(2,1)S(1)}, u32[]{:S(2)}, u32[]{:S(2)}) collective-permute-start(bf16[128,512]{1,0:T(8,128)(2,1)S(1)} %get-tuple-element.81), channel_id=1, source_target_pairs={{6,0},{4,2},{2,4},{0,6},{14,8},{12,10},{10,12},{8,14},{7,1},{5,3},... | collective-permute-start | bytes 393224 | tf_op jit(solution)/shard_map/ppermute | solution.py:444
  45.1 9.8 %collective-permute-start.17 = (bf16[128,512]{1,0:T(8,128)(2,1)S(1)}, bf16[128,512]{1,0:T(8,128)(2,1)S(1)}, u32[]{:S(2)}, u32[]{:S(2)}) collective-permute-start(bf16[128,512]{1,0:T(8,128)(2,1)S(1)} %get-tuple-element.78), channel_id=1, source_target_pairs={{0,8},{4,12},{8,0},{12,4},{1,9},{5,13},{9,1},{13,5},{2,10},{6,14},... | collective-permute-start | bytes 393224 | tf_op jit(solution)/shard_map/ppermute | solution.py:474
  47.1 11.3 %collective-permute-start.10 = (bf16[1024,128]{1,0:T(8,128)(2,1)S(1)}, bf16[1024,128]{1,0:T(8,128)(2,1)S(1)}, u32[]{:S(2)}, u32[]{:S(2)}) collective-permute-start(bf16[1024,128]{1,0:T(8,128)(2,1)S(1)} %get-tuple-element.68), channel_id=1, source_target_pairs={{0,4},{4,0},{8,12},{12,8},{1,5},{5,1},{9,13},{13,9},{2,6},{6,2},{1... | collective-permute-start | bytes 786440 | tf_op jit(solution)/shard_map/ppermute | solution.py:458
  49.5 8.1 %collective-permute-start.20 = (bf16[128,512]{1,0:T(8,128)(2,1)S(1)}, bf16[128,512]{1,0:T(8,128)(2,1)S(1)}, u32[]{:S(2)}, u32[]{:S(2)}) collective-permute-start(bf16[128,512]{1,0:T(8,128)(2,1)S(1)} %get-tuple-element.84), channel_id=1, source_target_pairs={{0,8},{4,12},{8,0},{12,4},{1,9},{5,13},{9,1},{13,5},{2,10},{6,14},... | collective-permute-start | bytes 393224 | tf_op jit(solution)/shard_map/ppermute | solution.py:474
  52.9 5.6 %copy-start.6 = (s32[2,8,4]{1,2,0:T(4,128)S(1)}, s32[2,8,4]{1,2,0:T(4,128)}, u32[]{:S(2)}) copy-start(s32[2,8,4]{1,2,0:T(4,128)} %param.9) | copy-start | bytes 772

commit v11 on v10

--- a/solution.py
+++ b/solution.py
@@ -10,7 +10,7 @@
 DH = 128
 BLK = 256
 EPS = 1e-06
-LIMIT = 16 << 20
+LIMIT = 10 << 20
 BEGIN = 52 << 20
 FAR = 4
 SHORT = pl.CostEstimate(flops=1, bytes_accessed=1, transcendentals=0)

time: 61.1 us -> 61.1 us (level)
  no operation moved by 1% of the time
where the time goes in v11:
time: 61.1 us; the launch traced here: 60.3 us
  starting transfers between devices  32.1 us (53%)
  waiting for transfers between devices  14.6 us (24%)
  Pallas kernels  12.8 us (21%)
  between operations  0.87 us (1%)
    pallas_call x14, Pallas kernels, call(): pl.pallas_call(body, out_shape=outs, in_specs=[SM if a.dtype == jnp.int32...  10.4 us
    ppermute x10, starting transfers between devices, swap(): return lax.ppermute(x, axis, [(0, 1), (1, 0)])  9.45 us
    ppermute x10, waiting for transfers between devices, swap(): return lax.ppermute(x, axis, [(0, 1), (1, 0)])  7.66 us
    ppermute x2, starting transfers between devices, cross_piece(): lax.ppermute(give, ('seq', 'head'), beside)  5.76 us
    ppermute x3, starting transfers between devices, gather_parts(): parts.append(lax.ppermute(x, 'seq', pairs))  5.57 us
    ppermute x2, starting transfers between devices, per_device(): sums += [stay, lax.ppermute(send, 'seq', [(s, s ^ 2) for s in range(4)])]  5.48 us
    ppermute x2, waiting for transfers between devices, per_device(): sums += [stay, lax.ppermute(send, 'seq', [(s, s ^ 2) for s in range(4)])]  2.65 us
    ppermute x1, starting transfers between devices, per_device(): two = lax.ppermute(cg, 'seq', [(i, i ^ 2) for i in range(4)])  2.59 us
  transfers between devices with their start and end apart: 21, of which 8 were waited for; matrix products, arithmetic and copies ran while one was open for 0% of the time, Pallas kernels for 18%

profile of v11, /device:TPU:0, one launch (start us, length us, event | category | flops | bytes accessed | tf_op | source)
XLA Modules:
  0.0 60.3 jit_solution(6002416400911840873)
XLA Ops:
  1.2 1.1 %far.1 = bf16[2048,128]{1,0:T(8,128)(2,1)S(1)} custom-call(bf16[4096,256]{1,0:T(8,128)(2,1)} %w_ref.3), custom_call_target="tpu_custom_call" | custom-call | flops 1 | bytes 1 | tf_op jit(solution)/shard_map/far/pallas_call | solution.py:98
  2.3 2.7 %collective-permute-start.4 = (bf16[2048,128]{1,0:T(8,128)(2,1)S(1)}, bf16[2048,128]{1,0:T(8,128)(2,1)S(1)}, u32[]{:S(2)}, u32[]{:S(2)}) collective-permute-start(bf16[2048,128]{1,0:T(8,128)(2,1)S(1)} %far.1), channel_id=1, source_target_pairs={{0,2},{2,0},{1,3},{3,1},{4,6},{6,4},{5,7},{7,5},{8,10},{10,8},{9,1... | collective-permute-start | bytes 1572872 | tf_op jit(solution)/shard_map/ppermute | solution.py:341
  5.5 1.6 %collective-permute-start = (bf16[512,128]{1,0:T(8,128)(2,1)S(1)}, bf16[512,128]{1,0:T(8,128)(2,1)S(1)}, u32[]{:S(2)}, u32[]{:S(2)}) collective-permute-start(bf16[512,128]{1,0:T(8,128)(2,1)S(1)} %get-tuple-element.50.refs_1_), channel_id=1, source_target_pairs={{0,4},{4,8},{8,12},{12,0},{1,5},{5,9},{9,13},{13,1},{2,6},{6,10},{... | collective-permute-start | bytes 393224 | tf_op jit(solution)/shard_map/ppermute | solution.py:350
  7.1 2.6 %collective-permute-start.1 = (bf16[512,128]{1,0:T(8,128)(2,1)S(1)}, bf16[512,128]{1,0:T(8,128)(2,1)S(1)}, u32[]{:S(2)}, u32[]{:S(2)}) collective-permute-start(bf16[512,128]{1,0:T(8,128)(2,1)S(1)} %get-tuple-element.50.refs_1_), channel_id=1, source_target_pairs={{0,8},{4,12},{8,0},{12,4},{1,9},{5,13},{9,1},{13,5},{2,10},{6,14},... | collective-permute-start | bytes 393224 | tf_op jit(solution)/shard_map/ppermute | solution.py:350
  9.7 1.3 %collective-permute-start.2 = (bf16[512,128]{1,0:T(8,128)(2,1)S(1)}, bf16[512,128]{1,0:T(8,128)(2,1)S(1)}, u32[]{:S(2)}, u32[]{:S(2)}) collective-permute-start(bf16[512,128]{1,0:T(8,128)(2,1)S(1)} %get-tuple-element.50.refs_1_), channel_id=1, source_target_pairs={{0,12},{4,0},{8,4},{12,8},{1,13},{5,1},{9,5},{13,9},{2,14},{6,2},{... | collective-permute-start | bytes 393224 | tf_op jit(solution)/shard_map/ppermute | solution.py:350
  11.1 0.7 %scores.1 = (bf16[512,256]{1,0:T(8,128)(2,1)S(1)}, bf16[1024,256]{1,0:T(8,128)(2,1)S(1)}, f32[512,256]{1,0:T(8,128)S(1)}) custom-call(bf16[512,256]{1,0:T(8,128)(2,1)S(1)} %bitcast.21, bf16[512,256]{1,0:T(8,128)(2,1)S(1)} %get-tuple-element.48.kf_ref.refs_5_, bf16[512,256]{1,0:T(8,128)(2,1)S(1)} %bitcast.16), custom_call_target="tpu_custom_call" | custom-call | flops 1 | bytes 1 | tf_op jit(solution)/shard_map/scores/pallas_call | solution.py:52
  11.8 5.8 %collective-permute-done.4.w_ref = bf16[2048,128]{1,0:T(8,128)(2,1)S(1)} collective-permute-done((bf16[2048,128]{1,0:T(8,128)(2,1)S(1)}, bf16[2048,128]{1,0:T(8,128)(2,1)S(1)}, u32[]{:S(2)}, u32[]{:S(2)}) %collective-permute-start.4) | collective-permute-done | bytes 524320 | tf_op jit(solution)/shard_map/ppermute | solution.py:341
  17.5 1.2 %other.1 = (bf16[512,128]{1,0:T(8,128)(2,1)S(1)}, bf16[512,128]{1,0:T(8,128)(2,1)S(1)}) custom-call(bf16[512,2048]{1,0:T(8,128)(2,1)S(1)} %bitcast.10, bf16[512,2048]{1,0:T(8,128)(2,1)S(1)} %collective-permute-done.3.og_sib_ref, bf16[2048,128]{1,0:T(8,128)(2,1)S(1)} %collective-permute-done.4.w_ref), custom_call_target="tpu_custom_call" | custom-call | flops 1 | bytes 1 | tf_op jit(solution)/shard_map/other/pallas_call | solution.py:52
  18.8 1.8 %collective-permute-start.5 = (bf16[512,128]{1,0:T(8,128)(2,1)S(1)}, bf16[512,128]{1,0:T(8,128)(2,1)S(1)}, u32[]{:S(2)}, u32[]{:S(2)}) collective-permute-start(bf16[512,128]{1,0:T(8,128)(2,1)S(1)} %get-tuple-element.57), channel_id=1, source_target_pairs={{0,2},{2,0},{1,3},{3,1},{4,6},{6,4},{5,7},{7,5},{8,10},{10,8},{9,1... | collective-permute-start | bytes 393224 | tf_op jit(solution)/shard_map/ppermute | solution.py:341
  20.6 1.1 %numer.1 = (bf16[512,128]{1,0:T(8,128)(2,1)S(1)}, f32[512,256]{1,0:T(8,128)S(1)}, bf16[512,256]{1,0:T(8,128)(2,1)S(1)}) custom-call(s32[2,4,8]{2,1,0:T(4,128)S(1)} %bitcast.23, bf16[512,128]{1,0:T(8,128)(2,1)S(1)} %get-tuple-element.50.refs_1_, bf16[512,128]{1,0:T(8,128)(2,1)S(1)} %collective-permute-done.refs_2_, ...), custom_call_target="tpu_custom_call" | custom-call | flops 1 | bytes 1 | tf_op jit(solution)/shard_map/numer/pallas_call | solution.py:52
  22.2 1.7 %collective-permute-start.11 = (bf16[512,256]{1,0:T(8,128)(2,1)S(1)}, bf16[512,256]{1,0:T(8,128)(2,1)S(1)}, u32[]{:S(2)}, u32[]{:S(2)}) collective-permute-start(bf16[512,256]{1,0:T(8,128)(2,1)S(1)} %get-tuple-element.65.attn_ref), channel_id=1, source_target_pairs={{0,2},{2,0},{1,3},{3,1},{4,6},{6,4},{5,7},{7,5},{8,10},{10,8},{9,1... | collective-permute-start | bytes 786440 | tf_op jit(solution)/shard_map/ppermute | solution.py:341
  24.0 0.8 %own_partial.1.refs_0_ = f32[512,256]{1,0:T(8,128)S(1)} custom-call(bf16[512,2048]{1,0:T(8,128)(2,1)S(1)} %bitcast.11, bf16[4096,256]{1,0:T(8,128)(2,1)S(1)} %copy-done.1), custom_call_target="tpu_custom_call" | custom-call | flops 1 | bytes 1 | tf_op jit(solution)/shard_map/own_partial/pallas_call | solution.py:277
  24.8 2.6 %collective-permute-done.6.refs_2_ = bf16[512,128]{1,0:T(8,128)(2,1)S(1)} collective-permute-done((bf16[512,128]{1,0:T(8,128)(2,1)S(1)}, bf16[512,128]{1,0:T(8,128)(2,1)S(1)}, u32[]{:S(2)}, u32[]{:S(2)}) %collective-permute-start.6) | collective-permute-done | bytes 131104 | tf_op jit(solution)/shard_map/ppermute | solution.py:395
  27.3 0.6 dnum.1
  27.9 0.7 %weight.3 = (bf16[256,512]{1,0:T(8,128)(2,1)S(1)}, f32[256,512]{1,0:T(8,128)S(1)}) custom-call(bf16[512,256]{1,0:T(8,128)(2,1)S(1)} %get-tuple-element.65.attn_ref, bf16[512,2048]{1,0:T(8,128)(2,1)S(1)} %bitcast.12, bf16[512,2048]{1,0:T(8,128)(2,1)S(1)} %collective-permute-done.3.og_sib_ref, bf16[512,256]{1,0:T(8,128)(2,1)S(1)} %collective-permute-done.8.refs_0_), custom_call_target="tpu_custom_call" | custom-call | flops 1 | bytes 1 | tf_op jit(solution)/shard_map/weight/pallas_call | solution.py:52
  28.7 1.6 %collective-permute-start.9 = (bf16[256,512]{1,0:T(8,128)(2,1)S(1)}, bf16[256,512]{1,0:T(8,128)(2,1)S(1)}, u32[]{:S(2)}, u32[]{:S(2)}) collective-permute-start(bf16[256,512]{1,0:T(8,128)(2,1)S(1)} %get-tuple-element.67), channel_id=1, source_target_pairs={{0,4},{4,0},{8,12},{12,8},{1,5},{5,1},{9,13},{13,9},{2,6},{6,2},{1... | collective-permute-start | bytes 786440 | tf_op jit(solution)/shard_map/ppermute | solution.py:428
  30.3 2.6 %collective-permute-start.7 = (bf16[512,128]{1,0:T(8,128)(2,1)S(1)}, bf16[512,128]{1,0:T(8,128)(2,1)S(1)}, u32[]{:S(2)}, u32[]{:S(2)}) collective-permute-start(bf16[512,128]{1,0:T(8,128)(2,1)S(1)} %get-tuple-element.64.cg_ref.refs_1_), channel_id=1, source_target_pairs={{0,8},{4,12},{8,0},{12,4},{1,9},{5,13},{9,1},{13,5},{2,10},{6,14},... | collective-permute-start | bytes 393224 | tf_op jit(solution)/shard_map/ppermute | solution.py:419
  33.6 0.8 %collective-permute-done.12.refs_0_ = bf16[160,256]{1,0:T(8,128)(2,1)S(1)} collective-permute-done((bf16[160,256]{1,0:T(8,128)(2,1)S(1)}, bf16[160,256]{1,0:T(8,128)(2,1)S(1)}, u32[]{:S(2)}, u32[]{:S(2)}) %collective-permute-start.12) | collective-permute-done | bytes 81952 | tf_op jit(solution)/shard_map/ppermute | solution.py:341
  34.8 0.6 weight.4
  35.3 1.5 %collective-permute-start.15 = (bf16[128,512]{1,0:T(8,128)(2,1)S(1)}, bf16[128,512]{1,0:T(8,128)(2,1)S(1)}, u32[]{:S(2)}, u32[]{:S(2)}) collective-permute-start(bf16[128,512]{1,0:T(8,128)(2,1)S(1)} %get-tuple-element.74), channel_id=1, source_target_pairs={{0,2},{2,0},{1,3},{3,1},{4,6},{6,4},{5,7},{7,5},{8,10},{10,8},{9,1... | collective-permute-start | bytes 393224 | tf_op jit(solution)/shard_map/ppermute | solution.py:341
  36.8 1.2 %collective-permute-start.16 = (bf16[128,512]{1,0:T(8,128)(2,1)S(1)}, bf16[128,512]{1,0:T(8,128)(2,1)S(1)}, u32[]{:S(2)}, u32[]{:S(2)}) collective-permute-start(bf16[128,512]{1,0:T(8,128)(2,1)S(1)} %get-tuple-element.75), channel_id=1, source_target_pairs={{6,0},{4,2},{2,4},{0,6},{14,8},{12,10},{10,12},{8,14},{7,1},{5,3},... | collective-permute-start | bytes 393224 | tf_op jit(solution)/shard_map/ppermute | solution.py:444
  38.0 1.3 %collective-permute-done.7.two_ref.refs_2_ = bf16[512,128]{1,0:T(8,128)(2,1)S(1)} collective-permute-done((bf16[512,128]{1,0:T(8,128)(2,1)S(1)}, bf16[512,128]{1,0:T(8,128)(2,1)S(1)}, u32[]{:S(2)}, u32[]{:S(2)}) %collective-permute-start.7) | collective-permute-done | bytes 131104 | tf_op jit(solution)/shard_map/ppermute | solution.py:419
  39.8 0.6 weight.5
  40.4 4.6 %collective-permute-start.19 = (bf16[128,512]{1,0:T(8,128)(2,1)S(1)}, bf16[128,512]{1,0:T(8,128)(2,1)S(1)}, u32[]{:S(2)}, u32[]{:S(2)}) collective-permute-start(bf16[128,512]{1,0:T(8,128)(2,1)S(1)} %get-tuple-element.81), channel_id=1, source_target_pairs={{6,0},{4,2},{2,4},{0,6},{14,8},{12,10},{10,12},{8,14},{7,1},{5,3},... | collective-permute-start | bytes 393224 | tf_op jit(solution)/shard_map/ppermute | solution.py:444
  45.1 2.1 %collective-permute-start.17 = (bf16[128,512]{1,0:T(8,128)(2,1)S(1)}, bf16[128,512]{1,0:T(8,128)(2,1)S(1)}, u32[]{:S(2)}, u32[]{:S(2)}) collective-permute-start(bf16[128,512]{1,0:T(8,128)(2,1)S(1)} %get-tuple-element.78), channel_id=1, source_target_pairs={{0,8},{4,12},{8,0},{12,4},{1,9},{5,13},{9,1},{13,5},{2,10},{6,14},... | collective-permute-start | bytes 393224 | tf_op jit(solution)/shard_map/ppermute | solution.py:474
  47.1 1.6 %collective-permute-start.10 = (bf16[1024,128]{1,0:T(8,128)(2,1)S(1)}, bf16[1024,128]{1,0:T(8,128)(2,1)S(1)}, u32[]{:S(2)}, u32[]{:S(2)}) collective-permute-start(bf16[1024,128]{1,0:T(8,128)(2,1)S(1)} %get-tuple-element.68), channel_id=1, source_target_pairs={{0,4},{4,0},{8,12},{12,8},{1,5},{5,1},{9,13},{13,9},{2,6},{6,2},{1... | collective-permute-start | bytes 786440 | tf_op jit(solution)/shard_map/ppermute | solution.py:458
  48.7 0.7 %collective-permute-done.18.keep_ref = bf16[128,512]{1,0:T(8,128)(2,1)S(1)} collective-permute-done((bf16[128,512]{1,0:T(8,128)(2,1)S(1)}, bf16[128,512]{1,0:T(8,128)(2,1)S(1)}, u32[]{:S(2)}, u32[]{:S(2)}) %collective-permute-start.18) | collective-permute-done | bytes 131104 | tf_op jit(solution)/shard_map/ppermute | solution.py:341
  49.5 3.4 %collective-permute-start.20 = (bf16[128,512]{1,0:T(8,128)(2,1)S(1)}, bf16[128,512]{1,0:T(8,128)(2,1)S(1)}, u32[]{:S(2)}, u32[]{:S(2)}) collective-permute-start(bf16[128,512]{1,0:T(8,128)(2,1)S(1)} %get-tuple-element.84), channel_id=1, source_target_pairs={{0,8},{4,12},{8,0},{12,4},{1,9},{5,13},{9,1},{13,5},{2,10},{6,14},... | collective-permute-start | bytes 393224 | tf_op jit(solution)/shard_map/ppermute | solution.py:474
  52.9 2.0 %query.1 = (bf16[512,256]{1,0:T(8,128)(2,1)}, f32[512,256]{1,0:T(8,128)S(1)}, f32[512,256]{1,0:T(8,128)S(1)}, bf16[512,256]{1,0:T(8,128)(2,1)}) custom-call(bf16[512,256]{1,0:T(8,128)(2,1)S(1)} %bitcast.22, bf16[512,256]{1,0:T(8,128)(2,1)S(1)} %get-tuple-element.49.refs_5_.refs_4_.qf_ref, bf16[512,256]{1,0:T(8,128)(2,1)S(1)} %get-tuple-element.48.kf_ref.refs_5_, ...), custom_call_target="tpu_custom_call" | custom-call | flops 99999997952 | bytes 1 | tf_op jit(solution)/shard_map/query/pallas_call | solution.py:52
  54.9 2.6 %collective-permute-done.20.refs_3_ = bf16[128,512]{1,0:T(8,128)(2,1)S(1)} collective-permute-done((bf16[128,512]{1,0:T(8,128)(2,1)S(1)}, bf16[128,512]{1,0:T(8,128)(2,1)S(1)}, u32[]{:S(2)}, u32[]{:S(2)}) %collective-permute-start.20) | collective-permute-done | bytes 131104 | tf_op jit(solution)/shard_map/ppermute | solution.py:474
  57.5 0.9 %final.1 = f32[512,256]{1,0:T(8,128)} custom-call(bf16[128,512]{1,0:T(8,128)(2,1)S(1)} %get-tuple-element.77.refs_0_, bf16[128,512]{1,0:T(8,128)(2,1)S(1)} %collective-permute-done.17.refs_1_, bf16[128,512]{1,0:T(8,128)(2,1)S(1)} %get-tuple-element.83.refs_2_, bf16[128,512]{1,0:T(8,128)(2,1)S(1)} %collective-permute-done.20.refs_3_), custom_call_target="tpu_custom_call" | custom-call | flops 1 | bytes 1 | tf_op jit(solution)/shard_map/final/pallas_call | solution.py:52
  58.5 1.8 %key.1 = (bf16[512,256]{1,0:T(8,128)(2,1)}, bf16[512,256]{1,0:T(8,128)(2,1)}) custom-call(s32[2,4,8]{2,1,0:T(4,128)S(1)} %bitcast.24, bf16[512,128]{1,0:T(8,128)(2,1)S(1)} %get-tuple-element.64.cg_ref.refs_1_, bf16[512,128]{1,0:T(8,128)(2,1)S(1)} %collective-permute-done.7.two_ref.refs_2_, bf16[1024,128]{1,0:T(8,128)(2,1)S(1)} %collective-permute-done.10.refs_3_, ...), custom_call_target="tpu_custom_call" | custom-call | flops 1 | bytes 1 | tf_op jit(solution)/shard_map/key/pallas_call | solution.py:52
  (41 shorter events, 3.1 us)
Async XLA Ops:
  0.6 16.9 %copy-start = (bf16[1,512,2048]{2,1,0:T(8,128)(2,1)S(1)}, bf16[1,512,2048]{2,1,0:T(8,128)(2,1)}, u32[]{:S(2)}) copy-start(bf16[1,512,2048]{2,1,0:T(8,128)(2,1)} %param.11) | copy-start | bytes 6291460
  0.6 4.4 %copy-start.3 = (bf16[1,512,256]{2,1,0:T(8,128)(2,1)S(1)}, bf16[1,512,256]{2,1,0:T(8,128)(2,1)}, u32[]{:S(2)}) copy-start(bf16[1,512,256]{2,1,0:T(8,128)(2,1)} %param.7) | copy-start | bytes 786436
  0.7 4.4 %copy-start.2 = (bf16[1,512,256]{2,1,0:T(8,128)(2,1)S(1)}, bf16[1,512,256]{2,1,0:T(8,128)(2,1)}, u32[]{:S(2)}) copy-start(bf16[1,512,256]{2,1,0:T(8,128)(2,1)} %param.8) | copy-start | bytes 786436
  0.7 10.4 %copy-start.4 = (bf16[1,512,256]{2,1,0:T(8,128)(2,1)S(1)}, bf16[1,512,256]{2,1,0:T(8,128)(2,1)}, u32[]{:S(2)}) copy-start(bf16[1,512,256]{2,1,0:T(8,128)(2,1)} %param.6) | copy-start | bytes 786436
  0.7 16.9 %collective-permute-start.3 = (bf16[512,2048]{1,0:T(8,128)(2,1)}, bf16[512,2048]{1,0:T(8,128)(2,1)S(1)}, u32[]{:S(2)}, u32[]{:S(2)}) collective-permute-start(bf16[512,2048]{1,0:T(8,128)(2,1)} %bitcast.9), channel_id=1, source_target_pairs={{0,1},{1,0},{2,3},{3,2},{4,5},{5,4},{6,7},{7,6},{8,9},{9,8},{10,11... | collective-permute-start | bytes 6291464 | tf_op jit(solution)/shard_map/ppermute | solution.py:341
  2.3 15.2 %collective-permute-start.4 = (bf16[2048,128]{1,0:T(8,128)(2,1)S(1)}, bf16[2048,128]{1,0:T(8,128)(2,1)S(1)}, u32[]{:S(2)}, u32[]{:S(2)}) collective-permute-start(bf16[2048,128]{1,0:T(8,128)(2,1)S(1)} %far.1), channel_id=1, source_target_pairs={{0,2},{2,0},{1,3},{3,1},{4,6},{6,4},{5,7},{7,5},{8,10},{10,8},{9,1... | collective-permute-start | bytes 1572872 | tf_op jit(solution)/shard_map/ppermute | solution.py:341
  5.5 15.1 %collective-permute-start = (bf16[512,128]{1,0:T(8,128)(2,1)S(1)}, bf16[512,128]{1,0:T(8,128)(2,1)S(1)}, u32[]{:S(2)}, u32[]{:S(2)}) collective-permute-start(bf16[512,128]{1,0:T(8,128)(2,1)S(1)} %get-tuple-element.50.refs_1_), channel_id=1, source_target_pairs={{0,4},{4,8},{8,12},{12,0},{1,5},{5,9},{9,13},{13,1},{2,6},{6,10},{... | collective-permute-start | bytes 393224 | tf_op jit(solution)/shard_map/ppermute | solution.py:350
  7.1 13.5 %collective-permute-start.1 = (bf16[512,128]{1,0:T(8,128)(2,1)S(1)}, bf16[512,128]{1,0:T(8,128)(2,1)S(1)}, u32[]{:S(2)}, u32[]{:S(2)}) collective-permute-start(bf16[512,128]{1,0:T(8,128)(2,1)S(1)} %get-tuple-element.50.refs_1_), channel_id=1, source_target_pairs={{0,8},{4,12},{8,0},{12,4},{1,9},{5,13},{9,1},{13,5},{2,10},{6,14},... | collective-permute-start | bytes 393224 | tf_op jit(solution)/shard_map/ppermute | solution.py:350
  9.7 10.9 %collective-permute-start.2 = (bf16[512,128]{1,0:T(8,128)(2,1)S(1)}, bf16[512,128]{1,0:T(8,128)(2,1)S(1)}, u32[]{:S(2)}, u32[]{:S(2)}) collective-permute-start(bf16[512,128]{1,0:T(8,128)(2,1)S(1)} %get-tuple-element.50.refs_1_), channel_id=1, source_target_pairs={{0,12},{4,0},{8,4},{12,8},{1,13},{5,1},{9,5},{13,9},{2,14},{6,2},{... | collective-permute-start | bytes 393224 | tf_op jit(solution)/shard_map/ppermute | solution.py:350
  11.7 8.9 %copy-start.5 = (s32[2,8,4]{1,2,0:T(4,128)S(1)}, s32[2,8,4]{1,2,0:T(4,128)}, u32[]{:S(2)}) copy-start(s32[2,8,4]{1,2,0:T(4,128)} %param.9) | copy-start | bytes 772
  11.7 12.2 %copy-start.1 = (bf16[4096,256]{1,0:T(8,128)(2,1)S(1)}, bf16[4096,256]{1,0:T(8,128)(2,1)}, u32[]{:S(2)}) copy-start(bf16[4096,256]{1,0:T(8,128)(2,1)} %w_ref.3) | copy-start | bytes 6291460
  18.8 6.0 %collective-permute-start.5 = (bf16[512,128]{1,0:T(8,128)(2,1)S(1)}, bf16[512,128]{1,0:T(8,128)(2,1)S(1)}, u32[]{:S(2)}, u32[]{:S(2)}) collective-permute-start(bf16[512,128]{1,0:T(8,128)(2,1)S(1)} %get-tuple-element.57), channel_id=1, source_target_pairs={{0,2},{2,0},{1,3},{3,1},{4,6},{6,4},{5,7},{7,5},{8,10},{10,8},{9,1... | collective-permute-start | bytes 393224 | tf_op jit(solution)/shard_map/ppermute | solution.py:341
  20.6 6.8 %collective-permute-start.6 = (bf16[512,128]{1,0:T(8,128)(2,1)S(1)}, bf16[512,128]{1,0:T(8,128)(2,1)S(1)}, u32[]{:S(2)}, u32[]{:S(2)}) collective-permute-start(bf16[512,128]{1,0:T(8,128)(2,1)S(1)} %get-tuple-element.53), channel_id=1, source_target_pairs={{0,3},{1,2},{2,1},{3,0},{4,7},{5,6},{6,5},{7,4},{8,11},{9,10},{10,... | collective-permute-start | bytes 393224 | tf_op jit(solution)/shard_map/ppermute | solution.py:395
  21.8 6.2 %collective-permute-start.8 = (bf16[512,256]{1,0:T(8,128)(2,1)S(1)}, bf16[512,256]{1,0:T(8,128)(2,1)S(1)}, u32[]{:S(2)}, u32[]{:S(2)}) collective-permute-start(bf16[512,256]{1,0:T(8,128)(2,1)S(1)} %get-tuple-element.65.attn_ref), channel_id=1, source_target_pairs={{0,1},{1,0},{2,3},{3,2},{4,5},{5,4},{6,7},{7,6},{8,9},{9,8},{10,11... | collective-permute-start | bytes 786440 | tf_op jit(solution)/shard_map/ppermute | solution.py:341
  22.2 10.7 %collective-permute-start.11 = (bf16[512,256]{1,0:T(8,128)(2,1)S(1)}, bf16[512,256]{1,0:T(8,128)(2,1)S(1)}, u32[]{:S(2)}, u32[]{:S(2)}) collective-permute-start(bf16[512,256]{1,0:T(8,128)(2,1)S(1)} %get-tuple-element.65.attn_ref), channel_id=1, source_target_pairs={{0,2},{2,0},{1,3},{3,1},{4,6},{6,4},{5,7},{7,5},{8,10},{10,8},{9,1... | collective-permute-start | bytes 786440 | tf_op jit(solution)/shard_map/ppermute | solution.py:341
  28.7 11.1 %collective-permute-start.9 = (bf16[256,512]{1,0:T(8,128)(2,1)S(1)}, bf16[256,512]{1,0:T(8,128)(2,1)S(1)}, u32[]{:S(2)}, u32[]{:S(2)}) collective-permute-start(bf16[256,512]{1,0:T(8,128)(2,1)S(1)} %get-tuple-element.67), channel_id=1, source_target_pairs={{0,4},{4,0},{8,12},{12,8},{1,5},{5,1},{9,13},{13,9},{2,6},{6,2},{1... | collective-permute-start | bytes 786440 | tf_op jit(solution)/shard_map/ppermute | solution.py:428
  30.3 9.0 %collective-permute-start.7 = (bf16[512,128]{1,0:T(8,128)(2,1)S(1)}, bf16[512,128]{1,0:T(8,128)(2,1)S(1)}, u32[]{:S(2)}, u32[]{:S(2)}) collective-permute-start(bf16[512,128]{1,0:T(8,128)(2,1)S(1)} %get-tuple-element.64.cg_ref.refs_1_), channel_id=1, source_target_pairs={{0,8},{4,12},{8,0},{12,4},{1,9},{5,13},{9,1},{13,5},{2,10},{6,14},... | collective-permute-start | bytes 393224 | tf_op jit(solution)/shard_map/ppermute | solution.py:419
  32.9 1.9 %collective-permute-start.14 = (bf16[192,256]{1,0:T(8,128)(2,1)S(1)}, bf16[192,256]{1,0:T(8,128)(2,1)S(1)}, u32[]{:S(2)}, u32[]{:S(2)}) collective-permute-start(bf16[192,256]{1,0:T(8,128)(2,1)S(1)} %get-tuple-element.73), channel_id=1, source_target_pairs={{0,1},{1,0},{2,3},{3,2},{4,5},{5,4},{6,7},{7,6},{8,9},{9,8},{10,11... | collective-permute-start | bytes 294920 | tf_op jit(solution)/shard_map/ppermute | solution.py:341
  33.0 1.4 %collective-permute-start.12 = (bf16[160,256]{1,0:T(8,128)(2,1)S(1)}, bf16[160,256]{1,0:T(8,128)(2,1)S(1)}, u32[]{:S(2)}, u32[]{:S(2)}) collective-permute-start(bf16[160,256]{1,0:T(8,128)(2,1)S(1)} %get-tuple-element.71), channel_id=1, source_target_pairs={{0,1},{1,0},{2,3},{3,2},{4,5},{5,4},{6,7},{7,6},{8,9},{9,8},{10,11... | collective-permute-start | bytes 245768 | tf_op jit(solution)/shard_map/ppermute | solution.py:341
  33.5 1.3 %collective-permute-start.13 = (bf16[160,256]{1,0:T(8,128)(2,1)S(1)}, bf16[160,256]{1,0:T(8,128)(2,1)S(1)}, u32[]{:S(2)}, u32[]{:S(2)}) collective-permute-start(bf16[160,256]{1,0:T(8,128)(2,1)S(1)} %get-tuple-element.72), channel_id=1, source_target_pairs={{0,1},{1,0},{2,3},{3,2},{4,5},{5,4},{6,7},{7,6},{8,9},{9,8},{10,11... | collective-permute-start | bytes 245768 | tf_op jit(solution)/shard_map/ppermute | solution.py:341
  35.3 9.6 %collective-permute-start.15 = (bf16[128,512]{1,0:T(8,128)(2,1)S(1)}, bf16[128,512]{1,0:T(8,128)(2,1)S(1)}, u32[]{:S(2)}, u32[]{:S(2)}) collective-permute-start(bf16[128,512]{1,0:T(8,128)(2,1)S(1)} %get-tuple-element.74), channel_id=1, source_target_pairs={{0,2},{2,0},{1,3},{3,1},{4,6},{6,4},{5,7},{7,5},{8,10},{10,8},{9,1... | collective-permute-start | bytes 393224 | tf_op jit(solution)/shard_map/ppermute | solution.py:341
  36.8 8.2 %collective-permute-start.16 = (bf16[128,512]{1,0:T(8,128)(2,1)S(1)}, bf16[128,512]{1,0:T(8,128)(2,1)S(1)}, u32[]{:S(2)}, u32[]{:S(2)}) collective-permute-start(bf16[128,512]{1,0:T(8,128)(2,1)S(1)} %get-tuple-element.75), channel_id=1, source_target_pairs={{6,0},{4,2},{2,4},{0,6},{14,8},{12,10},{10,12},{8,14},{7,1},{5,3},... | collective-permute-start | bytes 393224 | tf_op jit(solution)/shard_map/ppermute | solution.py:444
  40.3 9.0 %collective-permute-start.18 = (bf16[128,512]{1,0:T(8,128)(2,1)S(1)}, bf16[128,512]{1,0:T(8,128)(2,1)S(1)}, u32[]{:S(2)}, u32[]{:S(2)}) collective-permute-start(bf16[128,512]{1,0:T(8,128)(2,1)S(1)} %get-tuple-element.80), channel_id=1, source_target_pairs={{0,2},{2,0},{1,3},{3,1},{4,6},{6,4},{5,7},{7,5},{8,10},{10,8},{9,1... | collective-permute-start | bytes 393224 | tf_op jit(solution)/shard_map/ppermute | solution.py:341
  40.4 9.0 %collective-permute-start.19 = (bf16[128,512]{1,0:T(8,128)(2,1)S(1)}, bf16[128,512]{1,0:T(8,128)(2,1)S(1)}, u32[]{:S(2)}, u32[]{:S(2)}) collective-permute-start(bf16[128,512]{1,0:T(8,128)(2,1)S(1)} %get-tuple-element.81), channel_id=1, source_target_pairs={{6,0},{4,2},{2,4},{0,6},{14,8},{12,10},{10,12},{8,14},{7,1},{5,3},... | collective-permute-start | bytes 393224 | tf_op jit(solution)/shard_map/ppermute | solution.py:444
  45.1 9.8 %collective-permute-start.17 = (bf16[128,512]{1,0:T(8,128)(2,1)S(1)}, bf16[128,512]{1,0:T(8,128)(2,1)S(1)}, u32[]{:S(2)}, u32[]{:S(2)}) collective-permute-start(bf16[128,512]{1,0:T(8,128)(2,1)S(1)} %get-tuple-element.78), channel_id=1, source_target_pairs={{0,8},{4,12},{8,0},{12,4},{1,9},{5,13},{9,1},{13,5},{2,10},{6,14},... | collective-permute-start | bytes 393224 | tf_op jit(solution)/shard_map/ppermute | solution.py:474
  47.1 11.3 %collective-permute-start.10 = (bf16[1024,128]{1,0:T(8,128)(2,1)S(1)}, bf16[1024,128]{1,0:T(8,128)(2,1)S(1)}, u32[]{:S(2)}, u32[]{:S(2)}) collective-permute-start(bf16[1024,128]{1,0:T(8,128)(2,1)S(1)} %get-tuple-element.68), channel_id=1, source_target_pairs={{0,4},{4,0},{8,12},{12,8},{1,5},{5,1},{9,13},{13,9},{2,6},{6,2},{1... | collective-permute-start | bytes 786440 | tf_op jit(solution)/shard_map/ppermute | solution.py:458
  49.5 8.1 %collective-permute-start.20 = (bf16[128,512]{1,0:T(8,128)(2,1)S(1)}, bf16[128,512]{1,0:T(8,128)(2,1)S(1)}, u32[]{:S(2)}, u32[]{:S(2)}) collective-permute-start(bf16[128,512]{1,0:T(8,128)(2,1)S(1)} %get-tuple-element.84), channel_id=1, source_target_pairs={{0,8},{4,12},{8,0},{12,4},{1,9},{5,13},{9,1},{13,5},{2,10},{6,14},... | collective-permute-start | bytes 393224 | tf_op jit(solution)/shard_map/ppermute | solution.py:474
  52.9 5.6 %copy-start.6 = (s32[2,8,4]{1,2,0:T(4,128)S(1)}, s32[2,8,4]{1,2,0:T(4,128)}, u32[]{:S(2)}) copy-start(s32[2,8,4]{1,2,0:T(4,128)} %param.9) | copy-start | bytes 772
